TPU v7x, 32 devices: a whole 2x2x4 slice. The times are simulated.
32 devices in a mesh: row: 4 (over y, core), seq: 8 (over z, x).
Axes of the slice: x: 2, y: 2, z: 4, core: 2. Of those that a mesh axis runs over, the one named last changes fastest.
Arguments:
- tokens: bfloat16 [4, 2048, 1024], P('row', 'seq'), may hold values from -6 to 6
- cotangent: bfloat16 [4, 2048, 1024], P('row', 'seq'), may hold values from -6 to 6
- pair_lengths: int32 [4, 8], P('row'), may hold values from 1 to 513, 2048 in all within a row
- prefix_key: bfloat16 [64, 1024], replicated, may hold values from -6 to 6
- prefix_value: bfloat16 [64, 1024], replicated, may hold values from -6 to 6
- w_query: bfloat16 [1024, 1024], P('row'), may hold values from -0.1875 to 0.1875
- b_query: bfloat16 [1024], replicated, may hold values from -0.59765625 to 0.59765625
- w_key: bfloat16 [1024, 1024], P('row'), may hold values from -0.1875 to 0.1875
- w_value: bfloat16 [1024, 1024], P('row'), may hold values from -0.1875 to 0.1875
- b_value: bfloat16 [1024], replicated, may hold values from -0.29882812 to 0.29882812
- w_out: bfloat16 [1024, 1024], P('row'), may hold values from -1 to 1
- b_out: bfloat16 [1024], replicated, may hold values from -0.59765625 to 0.59765625
- gain_attn: bfloat16 [1024], replicated, may hold values from 0.5 to 1.5
- shift_attn: bfloat16 [1024], replicated, may hold values from -0.59765625 to 0.59765625
- w_up: bfloat16 [1024, 4096], P('row'), may hold values from -0.1875 to 0.1875
- b_up: bfloat16 [4096], replicated, may hold values from -0.59765625 to 0.59765625
- w_down: bfloat16 [4096, 1024], P('row'), may hold values from -0.09375 to 0.09375
- b_down: bfloat16 [1024], replicated, may hold values from -0.59765625 to 0.59765625
- gain_ffn: bfloat16 [1024], replicated, may hold values from 0.5 to 1.5
- shift_ffn: bfloat16 [1024], replicated, may hold values from -0.59765625 to 0.59765625
Outputs:
- out_tokens: bfloat16 [4, 2048, 1024], P('row', 'seq')
- grad_tokens: bfloat16 [4, 2048, 1024], P('row', 'seq')
- grad_prefix_key: float32 [64, 1024], replicated
- grad_prefix_value: float32 [64, 1024], replicated
Inputs may be any that keep to these rules, and one draw needn't show every extreme that they name: `pair_lengths`: each row's 8 pair lengths sum to 2048; in each row the longest pair has exactly 513 tokens.
All inputs are finite; a program needn't handle non-finite values.
Results may differ from a plain program's by a relative error of at most 0.02.
Values may be sent and summed in bfloat16 or wider, within the bound.
No kernel may reach another device: no remote copies, remote signals or barrier semaphores. Data moves between devices by JAX's collectives and lax.ppermute only.
A program may use at most 192 MiB of HBM per device.

v0:
```python
import jax
import jax.numpy as jnp
from jax import lax
from jax.sharding import PartitionSpec as P

HEADS = 16
HEAD_DIM = 64
REACH = 2


ln_eps = 1e-05
masked_fill = -1e30


def shifted(block, axis, distance):
    devices = range(lax.axis_size(axis))
    route = [(i - distance, i) for i in devices if i - distance in devices]
    return lax.ppermute(block, axis, route)


def shortened(value):
    return jax.tree.map(lambda a: a.astype(jnp.bfloat16) if a.dtype == jnp.float32 else a, value)


def layer_norm(field, gain_vec, shift_vec):
    average = jnp.mean(field, axis=-1, keepdims=True)
    centred = field - average
    variance = jnp.mean(centred * centred, axis=-1, keepdims=True)
    return centred * lax.rsqrt(variance + ln_eps) * gain_vec + shift_vec


def segment_ids(pair_ends, first_pos, tok_count, row_length):
    places = first_pos + jnp.arange(tok_count, dtype=jnp.int32)
    inside = (places >= 0) & (places < row_length)
    labels = jnp.sum((places[:, None] >= pair_ends[None, :]).astype(jnp.int32), axis=1)
    return jnp.where(inside, labels, -1)


def block_scores(queries, key_block, key_labels, query_labels, score_scale):
    scores = (
        jnp.einsum("qhd,khd->hqk", queries, key_block, preferred_element_type=jnp.float32)
        * score_scale
    )
    if key_labels is None:
        return scores
    allowed = query_labels[:, None] == key_labels[None, :]
    return jnp.where(allowed[None], scores, masked_fill)


def per_device(
    tokens,
    cotangent,
    pair_lengths,
    prefix_key,
    prefix_value,
    w_query,
    b_query,
    w_key,
    w_value,
    b_value,
    w_out,
    b_out,
    gain_attn,
    shift_attn,
    w_up,
    b_up,
    w_down,
    b_down,
    gain_ffn,
    shift_ffn,
):
    gathered = (
        lax.all_gather(w_query, "row", axis=0, tiled=True),
        lax.all_gather(w_key, "row", axis=0, tiled=True),
        lax.all_gather(w_value, "row", axis=0, tiled=True),
        lax.all_gather(w_out, "row", axis=0, tiled=True),
        lax.all_gather(w_up, "row", axis=0, tiled=True),
        lax.all_gather(w_down, "row", axis=0, tiled=True),
    )
    full_query, full_key, full_value, full_out, full_up, full_down = gathered
    inputs = tokens[0]
    tok_count = inputs.shape[0]
    width_model = inputs.shape[1]
    score_scale = HEAD_DIM ** (-0.5)
    position_index = lax.axis_index("seq")
    row_length = tok_count * lax.axis_size("seq")
    pair_ends = jnp.cumsum(pair_lengths[0])
    own_first = position_index * tok_count
    query_labels = segment_ids(pair_ends, own_first, tok_count, row_length)
    head_shape = (tok_count, HEADS, HEAD_DIM)
    query_proj = (
        jnp.dot(inputs, full_query, preferred_element_type=jnp.float32)
        + b_query.astype(jnp.float32)
    ).astype(jnp.bfloat16)
    key_proj = jnp.dot(inputs, full_key, preferred_element_type=jnp.float32).astype(jnp.bfloat16)
    value_proj = (
        jnp.dot(inputs, full_value, preferred_element_type=jnp.float32)
        + b_value.astype(jnp.float32)
    ).astype(jnp.bfloat16)
    queries = query_proj.reshape(head_shape)
    keys_own = key_proj.reshape(head_shape)
    values_own = value_proj.reshape(head_shape)
    prefix_count = prefix_key.shape[0]
    prefix_keys = prefix_key.reshape(prefix_count, HEADS, HEAD_DIM)
    prefix_values = prefix_value.reshape(prefix_count, HEADS, HEAD_DIM)

    def token_blocks(lowers, uppers):
        listing = [(keys_own, values_own, query_labels)]
        for distance in range(1, REACH + 1):
            lower_pair = lowers[distance - 1]
            upper_pair = uppers[distance - 1]
            listing.append(
                (
                    lower_pair[0],
                    lower_pair[1],
                    segment_ids(pair_ends, own_first - distance * tok_count, tok_count, row_length),
                )
            )
            listing.append(
                (
                    upper_pair[0],
                    upper_pair[1],
                    segment_ids(pair_ends, own_first + distance * tok_count, tok_count, row_length),
                )
            )
        return listing

    lower_list = []
    moving = (keys_own, values_own)
    for repeat in range(REACH):
        moving = shifted((moving[0], moving[1]), "seq", 1)
        lower_list.append(moving)
    upper_list = []
    moving = (keys_own, values_own)
    for repeat in range(REACH):
        moving = shifted((moving[0], moving[1]), "seq", -1)
        upper_list.append(moving)
    blocks = token_blocks(lower_list, upper_list)
    prefix_scores = block_scores(queries, prefix_keys, None, None, score_scale)
    running_max = jnp.max(prefix_scores, axis=-1)
    prefix_exp = jnp.exp(prefix_scores - running_max[..., None])
    running_sum = jnp.sum(prefix_exp, axis=-1)
    attended = jnp.einsum(
        "hqk,khd->qhd",
        prefix_exp.astype(jnp.bfloat16),
        prefix_values,
        preferred_element_type=jnp.float32,
    )
    for key_block, value_block, key_labels in blocks:
        scores = block_scores(queries, key_block, key_labels, query_labels, score_scale)
        new_max = jnp.maximum(running_max, jnp.max(scores, axis=-1))
        factor = jnp.exp(running_max - new_max)
        block_exp = jnp.exp(scores - new_max[..., None])
        running_sum = running_sum * factor + jnp.sum(block_exp, axis=-1)
        attended = attended * factor.T[..., None] + jnp.einsum(
            "hqk,khd->qhd",
            block_exp.astype(jnp.bfloat16),
            value_block,
            preferred_element_type=jnp.float32,
        )
        running_max = new_max
    log_total = running_max + jnp.log(running_sum)
    attended = attended / running_sum.T[..., None]
    attended_low = attended.reshape(tok_count, width_model).astype(jnp.bfloat16)

    def softmax_of(scores):
        return jnp.exp(scores - log_total[..., None])

    branch_attn = jnp.dot(
        attended_low, full_out, preferred_element_type=jnp.float32
    ) + b_out.astype(jnp.float32)
    hidden_in = inputs.astype(jnp.float32) + branch_attn
    gain_one = gain_attn.astype(jnp.float32)
    shift_one = shift_attn.astype(jnp.float32)
    normed = layer_norm(hidden_in, gain_one, shift_one)
    pre_act = jnp.dot(
        normed.astype(jnp.bfloat16), full_up, preferred_element_type=jnp.float32
    ) + b_up.astype(jnp.float32)
    activated = jax.nn.gelu(pre_act, approximate=False).astype(jnp.bfloat16)
    summed = (
        normed
        + jnp.dot(activated, full_down, preferred_element_type=jnp.float32)
        + b_down.astype(jnp.float32)
    )
    gain_two = gain_ffn.astype(jnp.float32)
    shift_two = shift_ffn.astype(jnp.float32)
    result = layer_norm(summed, gain_two, shift_two)
    upstream = cotangent[0].astype(jnp.float32)
    unused_out, pull_norm = jax.vjp(lambda field: layer_norm(field, gain_two, shift_two), summed)
    grad_summed = pull_norm(upstream)[0]
    grad_act = jnp.dot(
        grad_summed.astype(jnp.bfloat16), full_down.T, preferred_element_type=jnp.float32
    )
    unused_gelu, pull_gelu = jax.vjp(lambda field: jax.nn.gelu(field, approximate=False), pre_act)
    grad_pre = pull_gelu(grad_act)[0].astype(jnp.bfloat16)
    grad_normed = grad_summed + jnp.dot(grad_pre, full_up.T, preferred_element_type=jnp.float32)
    unused_first, pull_first = jax.vjp(
        lambda field: layer_norm(field, gain_one, shift_one), hidden_in
    )
    grad_hidden = pull_first(grad_normed)[0]
    grad_attended = (
        jnp.dot(grad_hidden.astype(jnp.bfloat16), full_out.T, preferred_element_type=jnp.float32)
        .astype(jnp.bfloat16)
        .reshape(head_shape)
    )
    inner_sum = jnp.sum(grad_attended.astype(jnp.float32) * attended, axis=-1).T
    again_lower = []
    moving = (keys_own, values_own)
    for repeat in range(REACH):
        moving = shifted((moving[0], moving[1]), "seq", 1)
        again_lower.append(moving)
    again_upper = []
    moving = (keys_own, values_own)
    for repeat in range(REACH):
        moving = shifted((moving[0], moving[1]), "seq", -1)
        again_upper.append(moving)
    back_blocks = token_blocks(again_lower, again_upper)

    def grad_probs_of(value_block):
        return jnp.einsum(
            "qhd,khd->hqk", grad_attended, value_block, preferred_element_type=jnp.float32
        )

    def score_grads(probs, grad_probs):
        return (probs * (grad_probs - inner_sum[..., None])).astype(jnp.bfloat16)

    prefix_probs = softmax_of(prefix_scores)
    prefix_grad_scores = score_grads(prefix_probs, grad_probs_of(prefix_values))
    grad_queries = jnp.einsum(
        "hqk,khd->qhd", prefix_grad_scores, prefix_keys, preferred_element_type=jnp.float32
    )
    grad_pkey = (
        jnp.einsum("hqk,qhd->khd", prefix_grad_scores, queries, preferred_element_type=jnp.float32)
        * score_scale
    )
    grad_pvalue = jnp.einsum(
        "hqk,qhd->khd",
        prefix_probs.astype(jnp.bfloat16),
        grad_attended,
        preferred_element_type=jnp.float32,
    )
    block_grads = []
    for key_block, value_block, key_labels in back_blocks:
        probs = softmax_of(block_scores(queries, key_block, key_labels, query_labels, score_scale))
        grad_scores = score_grads(probs, grad_probs_of(value_block))
        grad_queries = grad_queries + jnp.einsum(
            "hqk,khd->qhd", grad_scores, key_block, preferred_element_type=jnp.float32
        )
        key_grad = (
            jnp.einsum("hqk,qhd->khd", grad_scores, queries, preferred_element_type=jnp.float32)
            * score_scale
        )
        value_grad = jnp.einsum(
            "hqk,qhd->khd",
            probs.astype(jnp.bfloat16),
            grad_attended,
            preferred_element_type=jnp.float32,
        )
        block_grads.append((key_grad, value_grad))
    empty_grads = (jnp.zeros(head_shape, jnp.float32), jnp.zeros(head_shape, jnp.float32))
    carried = empty_grads
    for distance in range(REACH, 0, -1):
        carried = jax.tree.map(jnp.add, carried, block_grads[2 * distance - 1])
        carried = jax.tree.map(
            lambda part, own: part.astype(own.dtype),
            shifted(shortened(carried), "seq", -1),
            carried,
        )
    from_higher = carried
    carried = empty_grads
    for distance in range(REACH, 0, -1):
        carried = jax.tree.map(jnp.add, carried, block_grads[2 * distance])
        carried = jax.tree.map(
            lambda part, own: part.astype(own.dtype), shifted(shortened(carried), "seq", 1), carried
        )
    grad_keys = (
        (block_grads[0][0] + from_higher[0] + carried[0])
        .reshape(tok_count, width_model)
        .astype(jnp.bfloat16)
    )
    grad_values = (
        (block_grads[0][1] + from_higher[1] + carried[1])
        .reshape(tok_count, width_model)
        .astype(jnp.bfloat16)
    )
    grad_query_low = (
        (grad_queries * score_scale).reshape(tok_count, width_model).astype(jnp.bfloat16)
    )
    grad_inputs = grad_hidden + jnp.dot(
        grad_query_low, full_query.T, preferred_element_type=jnp.float32
    )
    grad_inputs = grad_inputs + jnp.dot(grad_keys, full_key.T, preferred_element_type=jnp.float32)
    grad_inputs = grad_inputs + jnp.dot(
        grad_values, full_value.T, preferred_element_type=jnp.float32
    )
    prefix_sums = lax.psum(
        (
            grad_pkey.reshape(prefix_count, width_model),
            grad_pvalue.reshape(prefix_count, width_model),
        ),
        ("row", "seq"),
    )
    return (
        result.astype(jnp.bfloat16)[None],
        grad_inputs.astype(jnp.bfloat16)[None],
        prefix_sums[0],
        prefix_sums[1],
    )


def solution(mesh):
    placed = (
        P("row", "seq", None),
        P("row", "seq", None),
        P("row", None),
        P(),
        P(),
        P("row", None),
        P(),
        P("row", None),
        P("row", None),
        P(),
        P("row", None),
        P(),
        P(),
        P(),
        P("row", None),
        P(),
        P("row", None),
        P(),
        P(),
        P(),
    )
    return jax.shard_map(
        per_device,
        mesh=mesh,
        in_specs=placed,
        out_specs=(P("row", "seq", None), P("row", "seq", None), P(), P()),
        check_vma=False,
    )
```

profile of v0, /device:TPU:1, one launch (start us, length us, event | category | flops | bytes accessed | tf_op | source)
XLA Modules:
  0.0 469.0 jit_solution(14875585755988890551)
XLA Ops:
  16.0 18.8 %all-gather.9.cloned.1.call-done = bf16[1024,1024]{1,0:T(8,128)(2,1)} async-done(((bf16[256,1024]{1,0:T(8,128)(2,1)}), bf16[1024,1024]{1,0:T(8,128)(2,1)}) %all-gather.9.cloned.1.call-update) | async-done | bytes 2097168 | tf_op jit(solution)/shard_map/all_gather | solution.py:74
  34.8 2.3 convolution_convert_fusion.1
  37.3 1.3 collective-permute-start.2
  38.6 4.8 %collective-permute-start = (bf16[256,16,64]{0,2,1:T(8,128)(2,1)S(1)}, bf16[256,16,64]{0,2,1:T(8,128)(2,1)}, u32[]{:S(2)}, u32[]{:S(2)}) collective-permute-start(bf16[256,16,64]{0,2,1:T(8,128)(2,1)S(1)} %bitcast.310), channel_id=1, source_target_pairs={{0,1},{1,2},{2,3},{3,4},{4,5},{5,6},{6,7},{8,9},{9,10},{10,11},{11... | collective-permute-start | bytes 1572872 | tf_op jit(solution)/shard_map/ppermute | solution.py:18
  43.4 15.6 %all-gather.11.cloned.1.call-done = bf16[1024,1024]{1,0:T(8,128)(2,1)} async-done(((bf16[256,1024]{1,0:T(8,128)(2,1)}), bf16[1024,1024]{1,0:T(8,128)(2,1)}) %all-gather.11.cloned.1.call-update) | async-done | bytes 2097168 | tf_op jit(solution)/shard_map/all_gather | solution.py:75
  59.0 2.3 fusion.154
  62.3 1.3 collective-permute-start.3
  63.6 4.8 %collective-permute-start.1 = (bf16[256,16,64]{0,2,1:T(8,128)(2,1)}, bf16[256,16,64]{0,2,1:T(8,128)(2,1)}, u32[]{:S(2)}, u32[]{:S(2)}) collective-permute-start(bf16[256,16,64]{0,2,1:T(8,128)(2,1)} %bitcast.8), channel_id=1, source_target_pairs={{0,1},{1,2},{2,3},{3,4},{4,5},{5,6},{6,7},{8,9},{9,10},{10,11},{11... | collective-permute-start | bytes 1572872 | tf_op jit(solution)/shard_map/ppermute | solution.py:18
  68.4 14.8 %all-gather.7.cloned.1.call-done = bf16[1024,1024]{1,0:T(8,128)(2,1)} async-done(((bf16[256,1024]{1,0:T(8,128)(2,1)}), bf16[1024,1024]{1,0:T(8,128)(2,1)}) %all-gather.7.cloned.1.call-update) | async-done | bytes 2097168 | tf_op jit(solution)/shard_map/all_gather | solution.py:73
  83.2 2.3 fusion.153
  87.1 1.3 collective-permute-start.6
  88.4 4.0 collective-permute-start.4
  92.5 1.3 collective-permute-start.7
  93.8 4.8 %collective-permute-start.5 = (bf16[256,16,64]{0,2,1:T(8,128)(2,1)}, bf16[256,16,64]{0,2,1:T(8,128)(2,1)S(1)}, u32[]{:S(2)}, u32[]{:S(2)}) collective-permute-start(bf16[256,16,64]{0,2,1:T(8,128)(2,1)} %collective-permute-done.1), channel_id=1, source_target_pairs={{0,1},{1,2},{2,3},{3,4},{4,5},{5,6},{6,7},{8,9},{9,10},{10,11},{11... | collective-permute-start | bytes 1572872 | tf_op jit(solution)/shard_map/ppermute | solution.py:18
  98.6 1.9 fusion.22
  101.4 24.0 %collective-permute-done.4 = bf16[256,16,64]{0,2,1:T(8,128)(2,1)S(1)} collective-permute-done((bf16[256,16,64]{0,2,1:T(8,128)(2,1)}, bf16[256,16,64]{0,2,1:T(8,128)(2,1)S(1)}, u32[]{:S(2)}, u32[]{:S(2)}) %collective-permute-start.4) | collective-permute-done | bytes 524320 | tf_op jit(solution)/shard_map/ppermute | solution.py:18
  131.8 2.1 fusion.89
  134.0 2.1 fusion.95
  137.6 2.2 fusion.145
  140.7 2.3 fusion.248
  143.0 2.7 fusion.249
  146.0 20.9 %all-gather.15.cloned.1.call-done = bf16[1024,4096]{1,0:T(8,128)(2,1)} async-done(((bf16[256,4096]{1,0:T(8,128)(2,1)}), bf16[1024,4096]{1,0:T(8,128)(2,1)}) %all-gather.15.cloned.1.call-update) | async-done | bytes 8388624 | tf_op jit(solution)/shard_map/all_gather | solution.py:77
  167.0 7.8 %convolution_add_fusion = f32[256,4096]{1,0:T(8,128)} fusion(bf16[1024,4096]{1,0:T(8,128)(2,1)} %all-gather.15.cloned.1.call-done, f32[4096]{0:T(1024)S(1)} %copy-done.48, f32[256,1024]{1,0:T(8,128)S(1)} %get-tuple-element.50, f32[1024]{0:T(1024)S(1)} %copy-done.59, f32[1024]{0:T(1024)S(1)} %copy-done.58, f32[256]{0:T(256)S(1)} %fusion.210, ...), kind=kOutput, calls=%fused_computation.1 | convolution fusion | flops 2149842944 | bytes 13658112 | tf_op jit(solution)/shard_map/dot_general | solution.py:176
  174.8 51.9 %all-gather.17.cloned.1.call-done = bf16[4096,1024]{1,0:T(8,128)(2,1)} async-done(((bf16[1024,1024]{1,0:T(8,128)(2,1)}), bf16[4096,1024]{1,0:T(8,128)(2,1)}) %all-gather.17.cloned.1.call-update) | async-done | bytes 8388624 | tf_op jit(solution)/shard_map/all_gather | solution.py:78
  226.7 14.3 %fusion.250 = (f32[256]{0:T(256)S(1)}, f32[256,1024]{1,0:T(8,128)S(1)}) fusion(f32[1024]{0:T(1024)} %convert_element_type.254, bf16[4096,1024]{1,0:T(8,128)(2,1)} %all-gather.17.cloned.1.call-done, f32[256,4096]{1,0:T(8,128)} %convolution_add_fusion, f32[1024]{0:T(1024)} %convert_element_type.250, f32[1024]{0:T(1024)} %convert_element_type.249, ...), kind=kOutput, calls=%fused_computation.306 | convolution fusion | flops 2217475840 | bytes 14695424 | tf_op jit(solution)/shard_map/dot_general | solution.py:182
  243.8 24.5 %multiply_reduce_fusion.1 = (f32[256]{0:T(256)}, f32[256,1024]{1,0:T(8,128)}) fusion(f32[256,1024]{1,0:T(8,128)S(1)} %get-tuple-element.50, f32[256]{0:T(256)} %copy-done.49, f32[1024]{0:T(1024)} %convert_element_type.249, bf16[1024,4096]{1,0:T(8,128)(2,1)} %all-gather.15.cloned.1.call-done, f32[256,4096]{1,0:T(8,128)} %convolution_add_fusion, ...), kind=kOutput, calls=%fused_computation.195 | convolution fusion | flops 4376231936 | bytes 24655872 | tf_op jit(solution)/shard_map/dot_general | solution.py:196
  269.0 1.6 fusion.243
  271.6 2.3 convolution_convert_fusion
  275.3 4.4 fusion.168
  279.6 1.9 fusion.171
  282.0 2.0 fusion.104
  285.4 2.5 multiply_convert_fusion.4
  287.9 1.9 copy.145
  289.8 2.1 convolution_multiply_fusion.6
  292.0 1.9 copy.144
  293.9 3.8 multiply_convert_fusion
  297.7 1.6 fusion.166
  299.3 1.4 multiply_convert_fusion.1
  300.7 1.5 fusion.167
  302.3 1.3 collective-permute-start.8
  303.6 1.3 collective-permute-start.12
  304.9 5.4 %collective-permute-start.10 = (bf16[256,16,64]{0,2,1:T(8,128)(2,1)}, bf16[256,16,64]{0,2,1:T(8,128)(2,1)}, u32[]{:S(2)}, u32[]{:S(2)}) collective-permute-start(bf16[256,16,64]{0,2,1:T(8,128)(2,1)} %fusion.166), channel_id=1, source_target_pairs={{0,1},{1,2},{2,3},{3,4},{4,5},{5,6},{6,7},{8,9},{9,10},{10,11},{11... | collective-permute-start | bytes 1572872 | tf_op jit(solution)/shard_map/ppermute | solution.py:18
  310.3 4.5 collective-permute-start.14
  315.3 1.3 fusion.113
  316.6 2.2 convolution_bitcast_fusion
  318.9 3.8 multiply_convert_fusion.3
  322.7 2.6 multiply_convert_fusion.2
  325.8 1.8 fusion.119
  329.9 2.0 add_convert_fusion.11
  331.9 1.3 collective-permute-start.9
  333.1 8.4 %collective-permute-done.10 = bf16[256,16,64]{0,2,1:T(8,128)(2,1)} collective-permute-done((bf16[256,16,64]{0,2,1:T(8,128)(2,1)}, bf16[256,16,64]{0,2,1:T(8,128)(2,1)}, u32[]{:S(2)}, u32[]{:S(2)}) %collective-permute-start.10) | collective-permute-done | bytes 524320 | tf_op jit(solution)/shard_map/ppermute | solution.py:18
  341.5 1.8 add_convert_fusion.10
  343.3 4.1 collective-permute-start.11
  347.5 2.2 add_convert_fusion.8
  349.7 1.4 collective-permute-start.13
  351.1 13.5 %collective-permute-done.14 = bf16[256,16,64]{0,2,1:T(8,128)(2,1)} collective-permute-done((bf16[256,16,64]{0,2,1:T(8,128)(2,1)}, bf16[256,16,64]{0,2,1:T(8,128)(2,1)}, u32[]{:S(2)}, u32[]{:S(2)}) %collective-permute-start.14) | collective-permute-done | bytes 524320 | tf_op jit(solution)/shard_map/ppermute | solution.py:18
  364.6 2.1 add_convert_fusion.7
  366.8 4.3 collective-permute-start.15
  371.1 16.0 %collective-permute-done.11 = bf16[256,16,64]{0,2,1:T(8,128)(2,1)S(1)} collective-permute-done((bf16[256,16,64]{0,2,1:T(8,128)(2,1)S(1)}, bf16[256,16,64]{0,2,1:T(8,128)(2,1)S(1)}, u32[]{:S(2)}, u32[]{:S(2)}) %collective-permute-start.11) | collective-permute-done | bytes 524320 | tf_op jit(solution)/shard_map/ppermute | solution.py:18
  388.1 10.1 %collective-permute-done.15 = bf16[256,16,64]{0,2,1:T(8,128)(2,1)S(1)} collective-permute-done((bf16[256,16,64]{0,2,1:T(8,128)(2,1)S(1)}, bf16[256,16,64]{0,2,1:T(8,128)(2,1)S(1)}, u32[]{:S(2)}, u32[]{:S(2)}) %collective-permute-start.15) | collective-permute-done | bytes 524320 | tf_op jit(solution)/shard_map/ppermute | solution.py:18
  398.6 1.6 fusion.165
  400.1 58.4 %all-reduce.3.cloned.1.call-done = (f32[64,1024]{1,0:T(8,128)}, f32[64,1024]{1,0:T(8,128)}) async-done(((f32[64,1024]{1,0:T(8,128)}, f32[64,1024]{1,0:T(8,128)}), (f32[64,1024]{1,0:T(8,128)}, f32[64,1024]{1,0:T(8,128)})) %all-reduce.3.cloned.1.call-update) | async-done | bytes 524304 | tf_op jit(solution)/shard_map/psum | solution.py:296
  458.6 1.7 copy.178
  460.2 1.7 copy.179
  (233 shorter events, 33.2 us)
Async XLA Ops:
  7.2 5.9 %copy-start.63 = (bf16[1024]{0:T(1024)(128)(2,1)S(1)}, bf16[1024]{0:T(1024)(128)(2,1)}, u32[]{:S(2)}) copy-start(bf16[1024]{0:T(1024)(128)(2,1)} %param.26) | copy-start | bytes 6148
  7.2 5.9 %copy-start.64 = (bf16[1024]{0:T(1024)(128)(2,1)S(1)}, bf16[1024]{0:T(1024)(128)(2,1)}, u32[]{:S(2)}) copy-start(bf16[1024]{0:T(1024)(128)(2,1)} %param.29) | copy-start | bytes 6148
  7.2 5.9 %copy-start.65 = (bf16[1024]{0:T(1024)(128)(2,1)S(1)}, bf16[1024]{0:T(1024)(128)(2,1)}, u32[]{:S(2)}) copy-start(bf16[1024]{0:T(1024)(128)(2,1)} %param.31) | copy-start | bytes 6148
  7.2 5.9 %copy-start.66 = (bf16[1024]{0:T(1024)(128)(2,1)S(1)}, bf16[1024]{0:T(1024)(128)(2,1)}, u32[]{:S(2)}) copy-start(bf16[1024]{0:T(1024)(128)(2,1)} %param.37) | copy-start | bytes 6148
  7.2 6.5 %copy-start.67 = (bf16[1024]{0:T(1024)(128)(2,1)S(1)}, bf16[1024]{0:T(1024)(128)(2,1)}, u32[]{:S(2)}) copy-start(bf16[1024]{0:T(1024)(128)(2,1)} %param.39) | copy-start | bytes 6148
  7.2 7.1 %copy-start.52 = (bf16[4096]{0:T(1024)(128)(2,1)S(1)}, bf16[4096]{0:T(1024)(128)(2,1)}, u32[]{:S(2)}) copy-start(bf16[4096]{0:T(1024)(128)(2,1)} %param.35) | copy-start | bytes 24580
  7.3 7.7 %copy-start.41 = (bf16[64,1024]{1,0:T(8,128)(2,1)S(1)}, bf16[64,1024]{1,0:T(8,128)(2,1)}, u32[]{:S(2)}) copy-start(bf16[64,1024]{1,0:T(8,128)(2,1)} %param.24) | copy-start | bytes 393220
  7.3 7.9 %copy-start.42 = (bf16[64,1024]{1,0:T(8,128)(2,1)S(1)}, bf16[64,1024]{1,0:T(8,128)(2,1)}, u32[]{:S(2)}) copy-start(bf16[64,1024]{1,0:T(8,128)(2,1)} %param.23) | copy-start | bytes 393220
  7.3 8.1 %copy-start.71 = (s32[1,8]{1,0:T(1,128)S(1)}, s32[1,8]{1,0:T(1,128)}, u32[]{:S(2)}) copy-start(s32[1,8]{1,0:T(1,128)} %param.22) | copy-start | bytes 100
  7.3 27.5 %copy-start.40 = (bf16[1,256,1024]{2,1,0:T(8,128)(2,1)S(1)}, bf16[1,256,1024]{2,1,0:T(8,128)(2,1)}, u32[]{:S(2)}) copy-start(bf16[1,256,1024]{2,1,0:T(8,128)(2,1)} %param.20) | copy-start | bytes 1572868
  7.3 27.5 %all-gather.9.cloned.1.call-start = ((), (), s32[]{:S(2)}) async-start(), calls=%async_computation.1 | async-start | bytes 2621440 | tf_op jit(solution)/shard_map/all_gather | solution.py:74
  8.0 50.9 %all-gather.11.cloned.1.call-start = ((), (), s32[]{:S(2)}) async-start(), calls=%async_computation.2 | async-start | bytes 2621440 | tf_op jit(solution)/shard_map/all_gather | solution.py:75
  8.8 74.4 %all-gather.7.cloned.1.call-start = ((), (), s32[]{:S(2)}) async-start(), calls=%async_computation | async-start | bytes 2621440 | tf_op jit(solution)/shard_map/all_gather | solution.py:73
  9.5 133.5 %all-gather.13.cloned.1.call-start = ((), (), s32[]{:S(2)}) async-start(), calls=%async_computation.3 | async-start | bytes 2621440 | tf_op jit(solution)/shard_map/all_gather | solution.py:76
  10.1 156.9 %all-gather.15.cloned.1.call-start = ((), (), s32[]{:S(2)}) async-start(), calls=%async_computation.4 | async-start | bytes 10485760 | tf_op jit(solution)/shard_map/all_gather | solution.py:77
  10.7 216.0 %all-gather.17.cloned.1.call-start = ((), (), s32[]{:S(2)}) async-start(), calls=%async_computation.5 | async-start | bytes 10485760 | tf_op jit(solution)/shard_map/all_gather | solution.py:78
  11.3 447.3 %all-reduce.3.cloned.1.call-start = ((), (), s32[]{:S(2)}) async-start(), calls=%async_computation.6 | async-start | bytes 1048576 | tf_op jit(solution)/shard_map/psum | solution.py:296
  15.2 122.1 %copy-start.20 = (bf16[64,16,64]{2,1,0:T(8,128)(2,1)}, bf16[64,16,64]{2,1,0:T(8,128)(2,1)S(1)}, u32[]{:S(2)}) copy-start(bf16[64,16,64]{2,1,0:T(8,128)(2,1)S(1)} %reshape.437) | copy-start | bytes 393220
  16.0 115.9 %copy-start.38 = (pred[256,256]{0,1:T(8,128)(4,1)}, pred[256,256]{0,1:T(8,128)(4,1)S(1)}, u32[]{:S(2)}) copy-start(pred[256,256]{0,1:T(8,128)(4,1)S(1)} %get-tuple-element.30) | copy-start | bytes 196612
  16.0 120.2 %copy-start.36 = (pred[256,256]{0,1:T(8,128)(4,1)}, pred[256,256]{0,1:T(8,128)(4,1)S(1)}, u32[]{:S(2)}) copy-start(pred[256,256]{0,1:T(8,128)(4,1)S(1)} %get-tuple-element.33) | copy-start | bytes 196612
  16.0 124.1 %copy-start.33 = (pred[256,256]{0,1:T(8,128)(4,1)}, pred[256,256]{0,1:T(8,128)(4,1)S(1)}, u32[]{:S(2)}) copy-start(pred[256,256]{0,1:T(8,128)(4,1)S(1)} %get-tuple-element.32) | copy-start | bytes 196612
  37.3 48.9 %copy-start.14 = (bf16[256,1024]{0,1:T(8,128)(2,1)}, bf16[256,1024]{0,1:T(8,128)(2,1)S(1)}, u32[]{:S(2)}) copy-start(bf16[256,1024]{0,1:T(8,128)(2,1)S(1)} %copy.114) | copy-start | bytes 1572868
  37.3 49.8 %collective-permute-start.2 = (bf16[256,16,64]{0,2,1:T(8,128)(2,1)S(1)}, bf16[256,16,64]{0,2,1:T(8,128)(2,1)S(1)}, u32[]{:S(2)}, u32[]{:S(2)}) collective-permute-start(bf16[256,16,64]{0,2,1:T(8,128)(2,1)S(1)} %bitcast.309), channel_id=1, source_target_pairs={{1,0},{2,1},{3,2},{4,3},{5,4},{6,5},{7,6},{9,8},{10,9},{11,10},{12... | collective-permute-start | bytes 1572872 | tf_op jit(solution)/shard_map/ppermute | solution.py:18
  38.6 49.8 %collective-permute-start = (bf16[256,16,64]{0,2,1:T(8,128)(2,1)S(1)}, bf16[256,16,64]{0,2,1:T(8,128)(2,1)}, u32[]{:S(2)}, u32[]{:S(2)}) collective-permute-start(bf16[256,16,64]{0,2,1:T(8,128)(2,1)S(1)} %bitcast.310), channel_id=1, source_target_pairs={{0,1},{1,2},{2,3},{3,4},{4,5},{5,6},{6,7},{8,9},{9,10},{10,11},{11... | collective-permute-start | bytes 1572872 | tf_op jit(solution)/shard_map/ppermute | solution.py:18
  62.3 30.2 %collective-permute-start.3 = (bf16[256,16,64]{0,2,1:T(8,128)(2,1)}, bf16[256,16,64]{0,2,1:T(8,128)(2,1)}, u32[]{:S(2)}, u32[]{:S(2)}) collective-permute-start(bf16[256,16,64]{0,2,1:T(8,128)(2,1)} %bitcast.8), channel_id=1, source_target_pairs={{1,0},{2,1},{3,2},{4,3},{5,4},{6,5},{7,6},{9,8},{10,9},{11,10},{12... | collective-permute-start | bytes 1572872 | tf_op jit(solution)/shard_map/ppermute | solution.py:18
  63.6 30.2 %collective-permute-start.1 = (bf16[256,16,64]{0,2,1:T(8,128)(2,1)}, bf16[256,16,64]{0,2,1:T(8,128)(2,1)}, u32[]{:S(2)}, u32[]{:S(2)}) collective-permute-start(bf16[256,16,64]{0,2,1:T(8,128)(2,1)} %bitcast.8), channel_id=1, source_target_pairs={{0,1},{1,2},{2,3},{3,4},{4,5},{5,6},{6,7},{8,9},{9,10},{10,11},{11... | collective-permute-start | bytes 1572872 | tf_op jit(solution)/shard_map/ppermute | solution.py:18
  87.1 44.7 %copy-start.4 = (f32[16,256,256]{1,2,0:T(8,128)}, f32[16,256,256]{1,2,0:T(8,128)S(1)}, u32[]{:S(2)}) copy-start(f32[16,256,256]{1,2,0:T(8,128)S(1)} %get-tuple-element.46) | copy-start | bytes 12582916
  87.1 14.2 %copy-start.26 = (bf16[256,16,64]{0,2,1:T(8,128)(2,1)}, bf16[256,16,64]{0,2,1:T(8,128)(2,1)S(1)}, u32[]{:S(2)}) copy-start(bf16[256,16,64]{0,2,1:T(8,128)(2,1)S(1)} %collective-permute-done.2) | copy-start | bytes 1572868
  87.1 39.1 %collective-permute-start.6 = (bf16[256,16,64]{0,2,1:T(8,128)(2,1)S(1)}, bf16[256,16,64]{0,2,1:T(8,128)(2,1)S(1)}, u32[]{:S(2)}, u32[]{:S(2)}) collective-permute-start(bf16[256,16,64]{0,2,1:T(8,128)(2,1)S(1)} %collective-permute-done.2), channel_id=1, source_target_pairs={{1,0},{2,1},{3,2},{4,3},{5,4},{6,5},{7,6},{9,8},{10,9},{11,10},{12... | collective-permute-start | bytes 1572872 | tf_op jit(solution)/shard_map/ppermute | solution.py:18
  88.4 36.9 %collective-permute-start.4 = (bf16[256,16,64]{0,2,1:T(8,128)(2,1)}, bf16[256,16,64]{0,2,1:T(8,128)(2,1)S(1)}, u32[]{:S(2)}, u32[]{:S(2)}) collective-permute-start(bf16[256,16,64]{0,2,1:T(8,128)(2,1)} %collective-permute-done), channel_id=1, source_target_pairs={{0,1},{1,2},{2,3},{3,4},{4,5},{5,6},{6,7},{8,9},{9,10},{10,11},{11... | collective-permute-start | bytes 1572872 | tf_op jit(solution)/shard_map/ppermute | solution.py:18
  92.5 43.7 %collective-permute-start.7 = (bf16[256,16,64]{0,2,1:T(8,128)(2,1)}, bf16[256,16,64]{0,2,1:T(8,128)(2,1)S(1)}, u32[]{:S(2)}, u32[]{:S(2)}) collective-permute-start(bf16[256,16,64]{0,2,1:T(8,128)(2,1)} %collective-permute-done.3), channel_id=1, source_target_pairs={{1,0},{2,1},{3,2},{4,3},{5,4},{6,5},{7,6},{9,8},{10,9},{11,10},{12... | collective-permute-start | bytes 1572872 | tf_op jit(solution)/shard_map/ppermute | solution.py:18
  93.8 46.1 %collective-permute-start.5 = (bf16[256,16,64]{0,2,1:T(8,128)(2,1)}, bf16[256,16,64]{0,2,1:T(8,128)(2,1)S(1)}, u32[]{:S(2)}, u32[]{:S(2)}) collective-permute-start(bf16[256,16,64]{0,2,1:T(8,128)(2,1)} %collective-permute-done.1), channel_id=1, source_target_pairs={{0,1},{1,2},{2,3},{3,4},{4,5},{5,6},{6,7},{8,9},{9,10},{10,11},{11... | collective-permute-start | bytes 1572872 | tf_op jit(solution)/shard_map/ppermute | solution.py:18
  100.5 37.2 %copy-start = (f32[16,256,256]{1,2,0:T(8,128)}, f32[16,256,256]{1,2,0:T(8,128)S(1)}, u32[]{:S(2)}) copy-start(f32[16,256,256]{1,2,0:T(8,128)S(1)} %get-tuple-element.42) | copy-start | bytes 12582916
  101.4 32.7 %copy-start.2 = (f32[16,256,256]{1,2,0:T(8,128)}, f32[16,256,256]{1,2,0:T(8,128)S(1)}, u32[]{:S(2)}) copy-start(f32[16,256,256]{1,2,0:T(8,128)S(1)} %get-tuple-element.40) | copy-start | bytes 12582916
  126.2 14.0 %copy-start.6 = (f32[16,256,256]{1,2,0:T(8,128)}, f32[16,256,256]{1,2,0:T(8,128)S(1)}, u32[]{:S(2)}) copy-start(f32[16,256,256]{1,2,0:T(8,128)S(1)} %get-tuple-element.38) | copy-start | bytes 12582916
  127.1 9.1 %copy-start.9 = (f32[16,256,256]{1,2,0:T(8,128)}, f32[16,256,256]{1,2,0:T(8,128)S(1)}, u32[]{:S(2)}) copy-start(f32[16,256,256]{1,2,0:T(8,128)S(1)} %get-tuple-element.36) | copy-start | bytes 12582916
  143.0 24.0 %copy-start.48 = (f32[4096]{0:T(1024)S(1)}, f32[4096]{0:T(1024)}, u32[]{:S(2)}) copy-start(f32[4096]{0:T(1024)} %convert_element_type.252) | copy-start | bytes 49156
  143.0 24.0 %copy-start.58 = (f32[1024]{0:T(1024)S(1)}, f32[1024]{0:T(1024)}, u32[]{:S(2)}) copy-start(f32[1024]{0:T(1024)} %convert_element_type.249) | copy-start | bytes 12292
  143.0 24.0 %copy-start.59 = (f32[1024]{0:T(1024)S(1)}, f32[1024]{0:T(1024)}, u32[]{:S(2)}) copy-start(f32[1024]{0:T(1024)} %convert_element_type.250) | copy-start | bytes 12292
  145.7 21.3 %copy-start.49 = (f32[256]{0:T(256)}, f32[256]{0:T(256)S(1)}, u32[]{:S(2)}) copy-start(f32[256]{0:T(256)S(1)} %broadcast_multiply_fusion.1) | copy-start | bytes 3076
  146.0 21.0 %copy-start.51 = (f32[256]{0:T(256)}, f32[256]{0:T(256)S(1)}, u32[]{:S(2)}) copy-start(f32[256]{0:T(256)S(1)} %multiply_reduce_fusion.3) | copy-start | bytes 3076
  146.0 21.0 %copy-start.55 = (f32[256]{0:T(256)}, f32[256]{0:T(256)S(1)}, u32[]{:S(2)}) copy-start(f32[256]{0:T(256)S(1)} %fusion.210) | copy-start | bytes 3076
  174.8 66.2 %copy-start.25 = (bf16[1,256,1024]{2,1,0:T(8,128)(2,1)S(1)}, bf16[1,256,1024]{2,1,0:T(8,128)(2,1)}, u32[]{:S(2)}) copy-start(bf16[1,256,1024]{2,1,0:T(8,128)(2,1)} %param.21) | copy-start | bytes 1572868
  226.7 14.3 %copy-start.46 = (f32[1024]{0:T(1024)S(1)}, f32[1024]{0:T(1024)}, u32[]{:S(2)}) copy-start(f32[1024]{0:T(1024)} %convert_element_type.255) | copy-start | bytes 12292
  226.7 15.3 %copy-start.47 = (f32[1024]{0:T(1024)S(1)}, f32[1024]{0:T(1024)}, u32[]{:S(2)}) copy-start(f32[1024]{0:T(1024)} %convert_element_type.256) | copy-start | bytes 12292
  274.1 5.5 %copy-start.7 = (f32[16,256,256]{1,2,0:T(8,128)S(1)}, f32[16,256,256]{1,2,0:T(8,128)}, u32[]{:S(2)}) copy-start(f32[16,256,256]{1,2,0:T(8,128)} %copy-done.6) | copy-start | bytes 12582916
  274.2 5.5 %copy-start.34 = (pred[256,256]{0,1:T(8,128)(4,1)S(1)}, pred[256,256]{0,1:T(8,128)(4,1)}, u32[]{:S(2)}) copy-start(pred[256,256]{0,1:T(8,128)(4,1)} %copy-done.33) | copy-start | bytes 196612
  293.9 5.4 %copy-start.35 = (pred[256,256]{0,1:T(8,128)(4,1)S(1)}, pred[256,256]{0,1:T(8,128)(4,1)}, u32[]{:S(2)}) copy-start(pred[256,256]{0,1:T(8,128)(4,1)} %copy-done.33) | copy-start | bytes 196612
  293.9 5.4 %copy-start.44 = (f32[256,16]{0,1:T(8,128)S(1)}, f32[256,16]{0,1:T(8,128)}, u32[]{:S(2)}) copy-start(f32[256,16]{0,1:T(8,128)} %copy-done.43) | copy-start | bytes 49156
  293.9 5.4 %copy-start.70 = (bf16[256,16,64]{0,2,1:T(8,128)(2,1)S(1)}, bf16[256,16,64]{0,2,1:T(8,128)(2,1)}, u32[]{:S(2)}) copy-start(bf16[256,16,64]{0,2,1:T(8,128)(2,1)} %copy-done.69) | copy-start | bytes 1572868
  299.3 15.5 %copy-start.15 = (bf16[256,1024]{0,1:T(8,128)(2,1)S(1)}, bf16[256,1024]{0,1:T(8,128)(2,1)}, u32[]{:S(2)}) copy-start(bf16[256,1024]{0,1:T(8,128)(2,1)} %copy-done.14) | copy-start | bytes 1572868
  300.7 14.5 %copy-start.13 = (bf16[16,256,64]{1,2,0:T(8,128)(2,1)S(1)}, bf16[16,256,64]{1,2,0:T(8,128)(2,1)}, u32[]{:S(2)}) copy-start(bf16[16,256,64]{1,2,0:T(8,128)(2,1)} %fusion.152) | copy-start | bytes 1572868
  302.3 27.6 %collective-permute-start.8 = (bf16[256,16,64]{0,2,1:T(8,128)(2,1)}, bf16[256,16,64]{0,2,1:T(8,128)(2,1)}, u32[]{:S(2)}, u32[]{:S(2)}) collective-permute-start(bf16[256,16,64]{0,2,1:T(8,128)(2,1)} %fusion.167), channel_id=1, source_target_pairs={{1,0},{2,1},{3,2},{4,3},{5,4},{6,5},{7,6},{9,8},{10,9},{11,10},{12... | collective-permute-start | bytes 1572872 | tf_op jit(solution)/shard_map/ppermute | solution.py:18
  303.6 43.9 %collective-permute-start.12 = (bf16[256,16,64]{0,2,1:T(8,128)(2,1)}, bf16[256,16,64]{0,2,1:T(8,128)(2,1)}, u32[]{:S(2)}, u32[]{:S(2)}) collective-permute-start(bf16[256,16,64]{0,2,1:T(8,128)(2,1)} %fusion.171), channel_id=1, source_target_pairs={{1,0},{2,1},{3,2},{4,3},{5,4},{6,5},{7,6},{9,8},{10,9},{11,10},{12... | collective-permute-start | bytes 1572872 | tf_op jit(solution)/shard_map/ppermute | solution.py:18
  304.9 36.7 %collective-permute-start.10 = (bf16[256,16,64]{0,2,1:T(8,128)(2,1)}, bf16[256,16,64]{0,2,1:T(8,128)(2,1)}, u32[]{:S(2)}, u32[]{:S(2)}) collective-permute-start(bf16[256,16,64]{0,2,1:T(8,128)(2,1)} %fusion.166), channel_id=1, source_target_pairs={{0,1},{1,2},{2,3},{3,4},{4,5},{5,6},{6,7},{8,9},{9,10},{10,11},{11... | collective-permute-start | bytes 1572872 | tf_op jit(solution)/shard_map/ppermute | solution.py:18
  310.3 54.3 %collective-permute-start.14 = (bf16[256,16,64]{0,2,1:T(8,128)(2,1)}, bf16[256,16,64]{0,2,1:T(8,128)(2,1)}, u32[]{:S(2)}, u32[]{:S(2)}) collective-permute-start(bf16[256,16,64]{0,2,1:T(8,128)(2,1)} %fusion.168), channel_id=1, source_target_pairs={{0,1},{1,2},{2,3},{3,4},{4,5},{5,6},{6,7},{8,9},{9,10},{10,11},{11... | collective-permute-start | bytes 1572872 | tf_op jit(solution)/shard_map/ppermute | solution.py:18
  329.9 17.6 %copy-start.1 = (f32[16,256,256]{1,2,0:T(8,128)S(1)}, f32[16,256,256]{1,2,0:T(8,128)}, u32[]{:S(2)}) copy-start(f32[16,256,256]{1,2,0:T(8,128)} %copy-done) | copy-start | bytes 12582916
  331.9 39.2 %collective-permute-start.9 = (bf16[256,16,64]{0,2,1:T(8,128)(2,1)S(1)}, bf16[256,16,64]{0,2,1:T(8,128)(2,1)S(1)}, u32[]{:S(2)}, u32[]{:S(2)}) collective-permute-start(bf16[256,16,64]{0,2,1:T(8,128)(2,1)S(1)} %add_convert_fusion.11), channel_id=1, source_target_pairs={{1,0},{2,1},{3,2},{4,3},{5,4},{6,5},{7,6},{9,8},{10,9},{11,10},{12... | collective-permute-start | bytes 1572872 | tf_op jit(solution)/shard_map/ppermute | solution.py:18
  343.3 43.7 %collective-permute-start.11 = (bf16[256,16,64]{0,2,1:T(8,128)(2,1)S(1)}, bf16[256,16,64]{0,2,1:T(8,128)(2,1)S(1)}, u32[]{:S(2)}, u32[]{:S(2)}) collective-permute-start(bf16[256,16,64]{0,2,1:T(8,128)(2,1)S(1)} %add_convert_fusion.10), channel_id=1, source_target_pairs={{0,1},{1,2},{2,3},{3,4},{4,5},{5,6},{6,7},{8,9},{9,10},{10,11},{11... | collective-permute-start | bytes 1572872 | tf_op jit(solution)/shard_map/ppermute | solution.py:18
  349.7 37.7 %copy-start.24 = (bf16[1024,1024]{1,0:T(8,128)(2,1)S(1)}, bf16[1024,1024]{1,0:T(8,128)(2,1)}, u32[]{:S(2)}) copy-start(bf16[1024,1024]{1,0:T(8,128)(2,1)} %all-gather.9.cloned.1.call-done) | copy-start | bytes 6291460
  349.7 38.5 %collective-permute-start.13 = (bf16[256,16,64]{0,2,1:T(8,128)(2,1)S(1)}, bf16[256,16,64]{0,2,1:T(8,128)(2,1)S(1)}, u32[]{:S(2)}, u32[]{:S(2)}) collective-permute-start(bf16[256,16,64]{0,2,1:T(8,128)(2,1)S(1)} %add_convert_fusion.8), channel_id=1, source_target_pairs={{1,0},{2,1},{3,2},{4,3},{5,4},{6,5},{7,6},{9,8},{10,9},{11,10},{12... | collective-permute-start | bytes 1572872 | tf_op jit(solution)/shard_map/ppermute | solution.py:18
  366.8 31.5 %copy-start.32 = (f32[256,16,64]{0,2,1:T(8,128)S(1)}, f32[256,16,64]{0,2,1:T(8,128)}, u32[]{:S(2)}) copy-start(f32[256,16,64]{0,2,1:T(8,128)} %fusion.104) | copy-start | bytes 3145732
  366.8 31.5 %collective-permute-start.15 = (bf16[256,16,64]{0,2,1:T(8,128)(2,1)S(1)}, bf16[256,16,64]{0,2,1:T(8,128)(2,1)S(1)}, u32[]{:S(2)}, u32[]{:S(2)}) collective-permute-start(bf16[256,16,64]{0,2,1:T(8,128)(2,1)S(1)} %add_convert_fusion.7), channel_id=1, source_target_pairs={{0,1},{1,2},{2,3},{3,4},{4,5},{5,6},{6,7},{8,9},{9,10},{10,11},{11... | collective-permute-start | bytes 1572872 | tf_op jit(solution)/shard_map/ppermute | solution.py:18
  387.3 11.2 %copy-start.23 = (bf16[1024,1024]{1,0:T(8,128)(2,1)S(1)}, bf16[1024,1024]{1,0:T(8,128)(2,1)}, u32[]{:S(2)}) copy-start(bf16[1024,1024]{1,0:T(8,128)(2,1)} %all-gather.11.cloned.1.call-done) | copy-start | bytes 6291460
  (31 other events, 83.4 us)
Sparse Core Ops, SparseCore 0:
  9.7 25.0 all-gather.8
  36.4 22.5 all-gather.10
  60.6 22.5 all-gather.6
  84.6 22.5 all-gather.12
  108.6 58.3 all-gather.14
  168.4 58.2 all-gather.16
  316.7 141.8 all-reduce.2
where the time goes:
time: 476 us; the launch traced here: 469 us
  waiting for transfers between devices  256 us (54%)
  matrix products  123 us (26%)
  starting transfers between devices  47.4 us (10%)
  between operations  15.7 us (3%)
  other arithmetic  14.2 us (3%)
  local copies, waits for them, and re-layouts  12.6 us (3%)
    ppermute x16, waiting for transfers between devices, shifted(): return lax.ppermute(block, axis, route)  72 us
    psum x1, waiting for transfers between devices, per_device(): lax.psum((grad_pkey.reshape(prefix_count, width_model), grad_pvalue.resha...  58.4 us
    all_gather x1, waiting for transfers between devices, per_device(): lax.all_gather(w_down, 'row', axis=0, tiled=True)  51.9 us
    ppermute x16, starting transfers between devices, shifted(): return lax.ppermute(block, axis, route)  47.1 us
    dot_general x1, matrix products, per_device(): jnp.dot(grad_pre, full_up.T, preferred_element_type=jnp.float32)  24.5 us
    all_gather x1, waiting for transfers between devices, per_device(): lax.all_gather(w_up, 'row', axis=0, tiled=True)  20.9 us
    all_gather x1, waiting for transfers between devices, per_device(): lax.all_gather(w_key, 'row', axis=0, tiled=True)  18.8 us
    all_gather x1, waiting for transfers between devices, per_device(): lax.all_gather(w_value, 'row', axis=0, tiled=True)  15.6 us
  transfers between devices with their start and end apart: 23, of which 11 were waited for; matrix products, arithmetic and copies ran while one was open for 15% of the time, Pallas kernels for 0%

commit v1 on v0

v1 whole, which is shorter than its diff:
```python
import functools

import jax
import jax.numpy as jnp
from jax import lax
from jax.experimental import pallas as pl
from jax.experimental.pallas import tpu as pltpu
from jax.sharding import PartitionSpec as P

HEAD = 64
SCALE = HEAD**-0.5
LN_EPS = 1e-05
MASKED = -1e30
TILE = 256
CHUNK = 512

f32 = jnp.float32
bf16 = jnp.bfloat16
VM = pl.BlockSpec(memory_space=pltpu.VMEM)
SM = pl.BlockSpec(memory_space=pltpu.SMEM)
HB = pl.BlockSpec(memory_space=pl.ANY)


def shape_of(shape, kind):
    return jax.ShapeDtypeStruct(shape, kind)


def dot(a, b, ca=1, cb=0):
    return lax.dot_general(a, b, (((ca,), (cb,)), ((), ())), preferred_element_type=f32)


def row_at(offset, rows):
    return pl.ds(pl.multiple_of(offset, 64), rows)


def start_all(pairs, sems):
    made = [pltpu.make_async_copy(s, d, sems.at[i]) for i, (s, d) in enumerate(pairs)]
    for one in made:
        one.start()
    return made


def wait_all(made):
    for one in made:
        one.wait()


def normalised(v):
    centred = v - jnp.mean(v, axis=-1, keepdims=True)
    inv = lax.rsqrt(jnp.mean(centred * centred, axis=-1, keepdims=True) + LN_EPS)
    return centred * inv, inv


def norm_back(g, n, inv):
    return (g - jnp.mean(g, -1, keepdims=True) - n * jnp.mean(g * n, -1, keepdims=True)) * inv


def project_kernel(info, bq, bv, pk, pv, *rest, count, half):
    tok_in = rest[:6]
    own, mate = rest[6:9], rest[9:12]
    pieces = rest[12 : 12 + count]
    (q_ref, qt_ref, k_ref, kt_ref, v_ref, vt_ref, pk_ref, pkt_ref, pv_ref, pvt_ref, w_ref) = rest[
        12 + count : 23 + count
    ]
    tok, sem_x, sem_w = rest[23 + count :]
    core = info[0]
    tokens = tok_in[0].shape[0]
    width = tok.shape[1]
    pairs = []
    for i in range(6):
        slot = 2 * (i % 3) + (core if i < 3 else 1 - core)
        pairs.append((tok_in[i], tok.at[row_at(slot * tokens, tokens), :]))
    got_tok = start_all(pairs, sem_x)
    cols = pl.multiple_of(core * half, 128)
    got_w = []
    for i in (1, 2, 0):
        pairs = []
        for j, ref in enumerate((own[i], mate[i])):
            pairs.append((ref.at[:, pl.ds(cols, half)], w_ref.at[i, row_at(info[1 + j], ref.shape[0]), :]))
        for j, ref in enumerate(pieces):
            pairs.append(
                (
                    ref.at[:, pl.ds(i * width + cols, half)],
                    w_ref.at[i, row_at(info[3 + j], ref.shape[0]), :],
                )
            )
        got_w.append(start_all(pairs, sem_w.at[i]))
    pk_half, pv_half = pk[:, pl.ds(cols, half)], pv[:, pl.ds(cols, half)]
    pk_ref[...], pkt_ref[...] = pk_half, pk_half.astype(f32).T.astype(bf16)
    pv_ref[...], pvt_ref[...] = pv_half, pv_half.astype(f32).T.astype(bf16)
    wait_all(got_tok)
    bias_v = bv[:, pl.ds(cols, half)].astype(f32)
    bias_q = bq[:, pl.ds(cols, half)].astype(f32)
    blocks = k_ref.shape[0] // TILE
    wait_all(got_w[0])

    def key_block(b, carry):
        at = pl.ds(pl.multiple_of(b * TILE, TILE), TILE)
        full = dot(tok[at, :], w_ref[1])
        k_ref[at, :] = full.astype(bf16)
        kt_ref[:, at] = full.T.astype(bf16)
        return carry

    lax.fori_loop(0, blocks, key_block, 0)
    wait_all(got_w[1])

    def value_block(b, carry):
        at = pl.ds(pl.multiple_of(b * TILE, TILE), TILE)
        full = dot(tok[at, :], w_ref[2]) + bias_v
        v_ref[at, :] = full.astype(bf16)
        vt_ref[:, at] = full.T.astype(bf16)
        return carry

    lax.fori_loop(0, blocks, value_block, 0)
    wait_all(got_w[2])

    def query_block(b, carry):
        at = pl.ds(pl.multiple_of(b * TILE, TILE), TILE)
        src = pl.ds(pl.multiple_of(b * TILE + 2 * tokens, TILE), TILE)
        full = (dot(tok[src, :], w_ref[0]) + bias_q).astype(bf16).astype(f32) * SCALE
        q_ref[at, :] = full.astype(bf16)
        qt_ref[:, at] = full.T.astype(bf16)
        return carry

    lax.fori_loop(0, 2 * tokens // TILE, query_block, 0)


def project(info, bq, bv, pk, pv, toks, own, mate, pieces):
    tokens, width = toks[0].shape
    half = width // 2
    pre = pk.shape[0]
    n_q, n_k = 2 * tokens, 6 * tokens
    count = len(pieces)
    outs = [(n_q, half), (half, n_q), (n_k, half), (half, n_k), (n_k, half), (half, n_k)]
    outs += [(pre, half), (half, pre), (pre, half), (half, pre), (3, width, half)]
    return pl.pallas_call(
        functools.partial(project_kernel, count=count, half=half),
        out_shape=tuple(shape_of(s, bf16) for s in outs),
        in_specs=[SM] + [VM] * 4 + [HB] * (12 + count),
        out_specs=(VM,) * len(outs),
        scratch_shapes=[
            pltpu.VMEM((n_k, width), bf16),
            pltpu.SemaphoreType.DMA((6,)),
            pltpu.SemaphoreType.DMA((3, 2 + count)),
        ],
        compiler_params=pltpu.CompilerParams(vmem_limit_bytes=48 << 20),
        name="project",
    )(info, bq, bv, pk, pv, *toks, *own, *mate, *pieces)


def head_rows(ref, h, at):
    own = ref[pl.ds(h * HEAD, HEAD), at]
    zero = jnp.zeros_like(own)
    return jnp.concatenate([own, zero] if h % 2 == 0 else [zero, own], 0)


def head_cols(ref, h, at):
    block = ref[at, pl.ds((h // 2) * 2 * HEAD, 2 * HEAD)]
    lane = lax.broadcasted_iota(jnp.int32, block.shape, 1)
    return jnp.where((lane < HEAD) == (h % 2 == 0), block, jnp.zeros_like(block))


def pair_cols(h):
    return pl.ds((h // 2) * 2 * HEAD, 2 * HEAD)


def allowed_bias(k0, first, last):
    place = k0 + lax.broadcasted_iota(jnp.int32, (TILE, TILE), 0)
    return jnp.where((place >= first) & (place < last), 0.0, MASKED).astype(f32)


def forward_kernel(
    info, first, last, qt_ref, k_ref, vt_ref, pk_ref, pvt_ref, keep_ref, send_ref, ot_ref, lse_ref,
    stat, acc, bias, *, heads,
):
    tokens = keep_ref.shape[0]

    def one_query_tile(t, carry):
        at = pl.ds(pl.multiple_of(t * TILE, TILE), TILE)
        qs, qe = first[:, at], last[:, at]
        for h in range(heads):
            s = dot(pk_ref[:, pair_cols(h)], head_rows(qt_ref, h, at))
            top = jnp.max(s, axis=0, keepdims=True)
            p = jnp.exp(s - top)
            stat[pl.ds(h, 1), :] = top
            stat[pl.ds(heads + h, 1), :] = jnp.sum(p, axis=0, keepdims=True)
            acc[pl.ds(h * HEAD, HEAD), :] = dot(pvt_ref[pl.ds(h * HEAD, HEAD), :], p.astype(bf16))

        def one_key_tile(j, inner):
            k0 = pl.multiple_of(j * TILE, TILE)
            bias[...] = allowed_bias(k0, qs, qe)
            for h in range(heads):
                s = dot(k_ref[pl.ds(k0, TILE), pair_cols(h)], head_rows(qt_ref, h, at)) + bias[...]
                old = stat[pl.ds(h, 1), :]
                top = jnp.maximum(old, jnp.max(s, axis=0, keepdims=True))
                factor = jnp.exp(old - top)
                p = jnp.exp(s - top)
                stat[pl.ds(h, 1), :] = top
                stat[pl.ds(heads + h, 1), :] = stat[pl.ds(heads + h, 1), :] * factor + jnp.sum(
                    p, axis=0, keepdims=True
                )
                rows = pl.ds(h * HEAD, HEAD)
                acc[rows, :] = acc[rows, :] * factor + dot(
                    vt_ref[rows, pl.ds(k0, TILE)], p.astype(bf16)
                )
            return inner

        lax.fori_loop(info[1 + 2 * t], info[2 + 2 * t], one_key_tile, 0)
        for h in range(heads):
            rows = pl.ds(h * HEAD, HEAD)
            acc[rows, :] = acc[rows, :] / stat[pl.ds(heads + h, 1), :]
        ot_ref[:, at] = acc[...]
        lse_ref[:, at] = stat[pl.ds(0, heads), :] + jnp.log(stat[pl.ds(heads, heads), :])
        low = acc[...].T.astype(bf16)
        side = (t * TILE) // tokens
        rows = pl.ds(pl.multiple_of(t * TILE - side * tokens, TILE), TILE)

        @pl.when(side == info[0])
        def _():
            keep_ref[rows, :] = low

        @pl.when(side != info[0])
        def _():
            send_ref[rows, :] = low

        return carry

    lax.fori_loop(0, 2 * tokens // TILE, one_query_tile, 0)


def attend(info, first, last, qt, k, vt, pk, pvt):
    half, n_q = qt.shape
    heads = half // HEAD
    return pl.pallas_call(
        functools.partial(forward_kernel, heads=heads),
        out_shape=(
            shape_of((n_q // 2, half), bf16),
            shape_of((n_q // 2, half), bf16),
            shape_of((half, n_q), f32),
            shape_of((heads, n_q), f32),
        ),
        in_specs=[SM] + [VM] * 7,
        out_specs=(VM,) * 4,
        scratch_shapes=[
            pltpu.VMEM((2 * heads, TILE), f32),
            pltpu.VMEM((half, TILE), f32),
            pltpu.VMEM((TILE, TILE), f32),
        ],
        compiler_params=pltpu.CompilerParams(vmem_limit_bytes=40 << 20),
        name="attend",
    )(info, first, last, qt, k, vt, pk, pvt)


def tile_grads(h, k_b, v_b, kt_b, bias, qt_m, dot_m, q_m, do_m, lse, inner):
    s = dot(k_b, qt_m)
    if bias is not None:
        s = s + bias
    p = jnp.exp(s - lse)
    ds = (p * (dot(v_b, dot_m) - inner)).astype(bf16)
    return dot(p.astype(bf16), do_m), dot(ds, q_m), dot(kt_b, ds)


def sweep(ranges, at, first, last, refs, acc, heads):
    q_ref, qt_ref, k_ref, kt_ref, v_ref, do_ref, dot_ref, lse_ref, inner_ref, bias = refs
    dqt, dk, dv = acc
    qs, qe = first[:, at], last[:, at]

    def one_key_tile(j, carry):
        k0 = pl.multiple_of(j * TILE, TILE)
        r = pl.ds(k0, TILE)
        bias[...] = allowed_bias(k0, qs, qe)
        for h in range(heads):
            c, rows = pair_cols(h), pl.ds(h * HEAD, HEAD)
            gv, gk, gq = tile_grads(
                h, k_ref[r, c], v_ref[r, c], kt_ref[rows, r], bias[...], head_rows(qt_ref, h, at),
                head_rows(dot_ref, h, at), head_cols(q_ref, h, at), head_cols(do_ref, h, at),
                lse_ref[pl.ds(h, 1), at], inner_ref[pl.ds(h, 1), at],
            )
            dv[r, c] += gv
            dk[r, c] += gk
            dqt[rows, at] += gq
        return carry

    for lo, hi in ranges:
        lax.fori_loop(lo, hi, one_key_tile, 0)


def remote_grads_kernel(
    info, first, last, q_ref, qt_ref, k_ref, kt_ref, v_ref, pk_ref, pkt_ref, pv_ref, keep_in, recv_in,
    ot_ref, lse_ref, w_in, give_ref, keep_lo, keep_hi, pre_ref, dqt, do_s, dot_s, inner_s, dk, dv, bias,
    wsc, wsem, *, heads,
):
    copies = start_all([(w_in.at[1], wsc.at[0]), (w_in.at[2], wsc.at[1])], wsem)
    core = info[0]
    tokens = keep_in.shape[0]
    n_q, pre = q_ref.shape[0], pk_ref.shape[0]
    do_s[row_at(core * tokens, tokens), :] = keep_in[...]
    do_s[row_at((1 - core) * tokens, tokens), :] = recv_in[...]
    dk[...] = jnp.zeros_like(dk)
    dv[...] = jnp.zeros_like(dv)
    pre_ref[...] = jnp.zeros_like(pre_ref)

    def one_query_tile(t, carry):
        at = pl.ds(pl.multiple_of(t * TILE, TILE), TILE)
        dot_s[:, at] = do_s[at, :].astype(f32).T.astype(bf16)
        for h in range(heads):
            rows = pl.ds(h * HEAD, HEAD)
            inner_s[pl.ds(h, 1), at] = jnp.sum(
                dot_s[rows, at].astype(f32) * ot_ref[rows, at], axis=0, keepdims=True
            )
        for h in range(heads):
            c, rows = pair_cols(h), pl.ds(h * HEAD, HEAD)
            gv, gk, gq = tile_grads(
                h, pk_ref[:, c], pv_ref[:, c], pkt_ref[rows, :], None, head_rows(qt_ref, h, at),
                head_rows(dot_s, h, at), head_cols(q_ref, h, at), head_cols(do_s, h, at),
                lse_ref[pl.ds(h, 1), at], inner_s[pl.ds(h, 1), at],
            )
            pre_ref[pl.ds(0, pre), c] += gk
            pre_ref[pl.ds(pre, pre), c] += gv
            dqt[rows, at] = gq
        lo, hi = info[1 + 2 * t], info[2 + 2 * t]
        side = 2 * tokens // TILE
        refs = (q_ref, qt_ref, k_ref, kt_ref, v_ref, do_s, dot_s, lse_ref, inner_s, bias)
        ranges = ((lo, jnp.minimum(hi, side)), (jnp.maximum(lo, 2 * side), hi))
        sweep(ranges, at, first, last, refs, (dqt, dk, dv), heads)
        return carry

    lax.fori_loop(0, n_q // TILE, one_query_tile, 0)
    wait_all(copies)
    for i, keep in ((0, keep_lo), (1, keep_hi)):
        for mine in (True, False):
            block = core if mine else 1 - core
            r = row_at(i * 4 * tokens + block * tokens, tokens)
            out = dot(dk[r, :].astype(bf16), wsc[0], 1, 1) + dot(dv[r, :].astype(bf16), wsc[1], 1, 1)
            if mine:
                keep[...] = out
            else:
                give_ref[pl.ds(i * tokens, tokens), :] = out.astype(bf16)


def remote_grads(info, first, last, q, qt, k, kt, v, pk, pkt, pv, keep, recv, ot, lse, w):
    n_q, half = q.shape
    heads, tokens, width = half // HEAD, n_q // 2, w.shape[1]
    n_k, pre = k.shape[0], pk.shape[0]
    return pl.pallas_call(
        functools.partial(remote_grads_kernel, heads=heads),
        out_shape=(
            shape_of((2 * tokens, width), bf16),
            shape_of((tokens, width), f32),
            shape_of((tokens, width), f32),
            shape_of((2 * pre, half), f32),
            shape_of((half, n_q), f32),
            shape_of((n_q, half), bf16),
            shape_of((half, n_q), bf16),
            shape_of((heads, n_q), f32),
        ),
        in_specs=[SM] + [VM] * 14 + [HB],
        out_specs=(VM,) * 8,
        scratch_shapes=[
            pltpu.VMEM((n_k, half), f32),
            pltpu.VMEM((n_k, half), f32),
            pltpu.VMEM((TILE, TILE), f32),
            pltpu.VMEM((2, width, half), bf16),
            pltpu.SemaphoreType.DMA((2,)),
        ],
        compiler_params=pltpu.CompilerParams(vmem_limit_bytes=52 << 20),
        name="remote_grads",
    )(info, first, last, q, qt, k, kt, v, pk, pkt, pv, keep, recv, ot, lse, w)


def local_grads_kernel(
    info, first, last, q_ref, qt_ref, k_ref, kt_ref, v_ref, do_ref, dot_ref, lse_ref, inner_ref, dqt_in,
    gh_ref, w_in, keep_ref, give_ref, dqt, dk, dv, bias, wsc, wsem, *, heads,
):
    copies = start_all([(w_in, wsc)], wsem)
    core = info[0]
    n_q = q_ref.shape[0]
    tokens = n_q // 2
    dqt[...] = dqt_in[...]
    dk[...] = jnp.zeros_like(dk)
    dv[...] = jnp.zeros_like(dv)
    side = 2 * tokens // TILE

    def one_query_tile(t, carry):
        at = pl.ds(pl.multiple_of(t * TILE, TILE), TILE)
        lo, hi = info[1 + 2 * t], info[2 + 2 * t]
        refs = (q_ref, qt_ref, k_ref, kt_ref, v_ref, do_ref, dot_ref, lse_ref, inner_ref, bias)
        ranges = ((jnp.maximum(lo, side), jnp.minimum(hi, 2 * side)),)
        sweep(ranges, at, first, last, refs, (dqt, dk, dv), heads)
        return carry

    lax.fori_loop(0, n_q // TILE, one_query_tile, 0)
    wait_all(copies)
    for mine in (False, True):
        block = core if mine else 1 - core
        r = row_at(block * tokens, tokens)
        rk = row_at(block * tokens + n_q, tokens)
        dq = (dqt[:, r] * SCALE).T.astype(bf16)
        out = (
            dot(dq, wsc[0], 1, 1)
            + dot(dk[rk, :].astype(bf16), wsc[1], 1, 1)
            + dot(dv[rk, :].astype(bf16), wsc[2], 1, 1)
        )
        if mine:
            keep_ref[...] = out + gh_ref[...]
        else:
            give_ref[...] = out.astype(bf16)


def local_grads(info, first, last, q, qt, k, kt, v, do, dot_, lse, inner, dqt, gh, w):
    n_q, half = q.shape
    heads, tokens, width = half // HEAD, n_q // 2, w.shape[1]
    n_k = k.shape[0]
    return pl.pallas_call(
        functools.partial(local_grads_kernel, heads=heads),
        out_shape=(shape_of((tokens, width), f32), shape_of((tokens, width), bf16)),
        in_specs=[SM] + [VM] * 13 + [HB],
        out_specs=(VM,) * 2,
        scratch_shapes=[
            pltpu.VMEM((half, n_q), f32),
            pltpu.VMEM((n_k, half), f32),
            pltpu.VMEM((n_k, half), f32),
            pltpu.VMEM((TILE, TILE), f32),
            pltpu.VMEM((3, width, half), bf16),
            pltpu.SemaphoreType.DMA((1,)),
        ],
        compiler_params=pltpu.CompilerParams(vmem_limit_bytes=52 << 20),
        name="local_grads",
    )(info, first, last, q, qt, k, kt, v, do, dot_, lse, inner, dqt, gh, w)


def placed(refs, info, at, scale, dst, src_cols=None, dst_cols=None):
    pairs = []
    for i, ref in enumerate(refs):
        src = ref if src_cols is None else ref.at[:, src_cols]
        rows = row_at(info[at + i] * scale, ref.shape[0])
        pairs.append((src, dst.at[rows, :] if dst_cols is None else dst.at[rows, dst_cols]))
    return pairs


def out_pairs(parts, info, width, dst):
    return placed(parts[:2], info, 1, 1, dst) + placed(
        parts[2:], info, 3, 1, dst, pl.ds(3 * width, width)
    )


def up_kernel(info, own_att, got_att, tok, bo, ga, sa, bu, *rest, count):
    wo, wu = rest[:count], rest[count : 2 * count]
    nrm_ref, hat_ref, inv_ref, act_ref, slope_ref, wo_s, wu_s, sem_o, sem_u = rest[2 * count :]
    width, ff = wu_s.shape
    half = own_att.shape[1]
    got_o = start_all(out_pairs(wo, info, width, wo_s), sem_o)
    got_u = []
    for j in range(ff // width):
        cs = pl.ds(j * width, width)
        got_u.append(start_all(placed(wu, info, 1, 1, wu_s, cs, cs), sem_u.at[j]))
    core = info[0]
    wait_all(got_o)
    hidden = (
        tok[...].astype(f32)
        + dot(own_att[...], wo_s[row_at(core * half, half), :])
        + dot(got_att[...], wo_s[row_at((1 - core) * half, half), :])
        + bo[...].astype(f32)
    )
    hat, inv = normalised(hidden)
    hat_ref[...] = hat
    inv_ref[...] = jnp.broadcast_to(inv, inv_ref.shape)
    nrm = hat * ga[...].astype(f32) + sa[...].astype(f32)
    nrm_ref[...] = nrm
    low = nrm.astype(bf16)
    for j in range(ff // CHUNK):
        if (j * CHUNK) % width == 0:
            wait_all(got_u[j * CHUNK // width])
        cs = pl.ds(j * CHUNK, CHUNK)
        v = dot(low, wu_s[:, cs]) + bu[:, cs].astype(f32)
        phi = 0.5 + 0.5 * lax.erf(v * (0.5**0.5))
        act_ref[:, cs] = (v * phi).astype(bf16)
        slope_ref[:, cs] = (phi + v * (jnp.exp(v * v * -0.5) * 0.3989422804014327)).astype(bf16)


def up(info, own_att, got_att, tok, bo, ga, sa, bu, wo, wu):
    tokens, width = tok.shape
    ff, count = bu.shape[1], len(wo)
    return pl.pallas_call(
        functools.partial(up_kernel, count=count),
        out_shape=(
            shape_of((tokens, width), f32),
            shape_of((tokens, width), f32),
            shape_of((tokens, 128), f32),
            shape_of((tokens, ff), bf16),
            shape_of((tokens, ff), bf16),
        ),
        in_specs=[SM] + [VM] * 7 + [HB] * (2 * count),
        out_specs=(VM,) * 5,
        scratch_shapes=[
            pltpu.VMEM((width, width), bf16),
            pltpu.VMEM((width, ff), bf16),
            pltpu.SemaphoreType.DMA((count,)),
            pltpu.SemaphoreType.DMA((ff // width, count)),
        ],
        compiler_params=pltpu.CompilerParams(vmem_limit_bytes=50 << 20),
        name="up",
    )(info, own_att, got_att, tok, bo, ga, sa, bu, *wo, *wu)


def down_kernel(info, nrm_ref, hat_ref, inv_ref, act_ref, slope_ref, cot, bd, gf, sf, ga, *rest, count):
    wo, wu, wd = rest[:count], rest[count : 2 * count], rest[2 * count : 3 * count]
    out_ref, gh_ref, keep_ref, send_ref, wo_s, wu_s, wd_s, sem_o, sem_u, sem_d = rest[3 * count :]
    width, ff = wu_s.shape
    half = keep_ref.shape[1]
    got_d = start_all(placed(wd, info, 1, ff // width, wd_s), sem_d)
    got_u = start_all(placed(wu, info, 1, 1, wu_s), sem_u)
    got_o = start_all(out_pairs(wo, info, width, wo_s), sem_o)
    core = info[0]
    wait_all(got_d)
    summed = nrm_ref[...] + dot(act_ref[...], wd_s[...]) + bd[...].astype(f32)
    n, inv = normalised(summed)
    gain = gf[...].astype(f32)
    out_ref[...] = (n * gain + sf[...].astype(f32)).astype(bf16)
    gs = norm_back(cot[...].astype(f32) * gain, n, inv)
    low = gs.astype(bf16)
    wait_all(got_u)
    total = gs
    for j in range(ff // CHUNK):
        cs = pl.ds(j * CHUNK, CHUNK)
        gp = (dot(low, wd_s[cs, :], 1, 1) * slope_ref[:, cs].astype(f32)).astype(bf16)
        total = total + dot(gp, wu_s[:, cs], 1, 1)
    gh = norm_back(total * ga[...].astype(f32), hat_ref[...], inv_ref[:, :1])
    gh_ref[...] = gh
    gh_low = gh.astype(bf16)
    wait_all(got_o)
    send_ref[...] = dot(gh_low, wo_s[row_at((1 - core) * half, half), :], 1, 1).astype(bf16)
    keep_ref[...] = dot(gh_low, wo_s[row_at(core * half, half), :], 1, 1).astype(bf16)


def down(info, nrm, hat, inv, act, slope, cot, bd, gf, sf, ga, wo, wu, wd):
    tokens, width = nrm.shape
    ff, count = act.shape[1], len(wo)
    return pl.pallas_call(
        functools.partial(down_kernel, count=count),
        out_shape=(
            shape_of((tokens, width), bf16),
            shape_of((tokens, width), f32),
            shape_of((tokens, width // 2), bf16),
            shape_of((tokens, width // 2), bf16),
        ),
        in_specs=[SM] + [VM] * 10 + [HB] * (3 * count),
        out_specs=(VM,) * 4,
        scratch_shapes=[
            pltpu.VMEM((width, width), bf16),
            pltpu.VMEM((width, ff), bf16),
            pltpu.VMEM((ff, width), bf16),
            pltpu.SemaphoreType.DMA((count,)),
            pltpu.SemaphoreType.DMA((count,)),
            pltpu.SemaphoreType.DMA((count,)),
        ],
        compiler_params=pltpu.CompilerParams(vmem_limit_bytes=58 << 20),
        name="down",
    )(info, nrm, hat, inv, act, slope, cot, bd, gf, sf, ga, *wo, *wu, *wd)


def per_device(
    tokens, cotangent, pair_lengths, prefix_key, prefix_value, w_query, b_query, w_key, w_value, b_value,
    w_out, b_out, gain_attn, shift_attn, w_up, b_up, w_down, b_down, gain_ffn, shift_ffn,
):
    n_row, n_seq = lax.axis_size("row"), lax.axis_size("seq")
    r, s = lax.axis_index("row"), lax.axis_index("seq")
    core, x, zbit = r & 1, s & 1, (s >> 1) & 1
    tok_count, width = tokens.shape[1], tokens.shape[2]

    def by_core(a):
        return lax.ppermute(a, "row", [(i, i ^ 1) for i in range(n_row)])

    def by_y(a):
        return lax.ppermute(a, "row", [(i, i ^ 2) for i in range(n_row)])

    def by_seq(a, bit):
        return lax.ppermute(a, "seq", [(i, i ^ bit) for i in range(n_seq)])

    def swapped(a, shift):
        route = []
        for i in range(n_row):
            for j in range(n_seq):
                to = (j | 1) + 2 * shift - 1
                if 0 <= to < n_seq:
                    route.append((i * n_seq + j, ((i & ~1) | (j & 1)) * n_seq + to + (i & 1)))
        return lax.ppermute(a, ("row", "seq"), route)

    own = swapped(tokens[0], 0)
    below = lax.ppermute(own, "seq", [(j, j + 2) for j in range(n_seq - 2)])
    above = lax.ppermute(own, "seq", [(j + 2, j) for j in range(n_seq - 2)])
    toks = [below, own, above]
    toks = toks + [by_core(a) for a in toks]
    cot = swapped(cotangent[0], 0)

    h = x ^ zbit
    first_q, second_q = 2 * h + x, 2 * h + 1 - x

    def quarter(shards, which):
        rows = shards[0].shape[0] // 4
        cut = [lax.dynamic_slice_in_dim(a, which * rows, rows, 0) for a in shards]
        return cut[0] if len(cut) == 1 else jnp.concatenate(cut, 1)

    groups = ((w_query, w_key, w_value, w_out), (w_up,), (w_down,))
    gathered = []
    for shards in groups:
        one = by_y(quarter(shards, first_q))
        two = by_y(quarter(shards, second_q))
        got = [one, two, by_seq(one, 1), by_seq(one, 2)]
        gathered.append(got + [by_core(a) for a in got])
    mates = [by_core(a) for a in (w_query, w_key, w_value, w_out, w_up, w_down)]
    m = w_query.shape[0]
    offsets = [r * m, (r ^ 1) * m]
    for base in ((r ^ 2) * m, (r ^ 3) * m):
        for which in (first_q, second_q, 2 * (1 - h) + 1 - x, 2 * (1 - h) + x):
            offsets.append(base + which * (m // 4))

    theirs = by_core(pair_lengths)
    lengths = jnp.where(x == core, pair_lengths, theirs)[0]
    pairs = lengths.shape[0]
    later = jnp.arange(pairs)[:, None] >= jnp.arange(pairs)[None, :]
    ends = jnp.sum(jnp.where(later, lengths[None, :], 0), axis=1)
    base = (s // 2) * 2 * tok_count
    place = base + jnp.arange(2 * tok_count, dtype=jnp.int32)
    passed = ends[:, None] <= place[None, :]
    origin = base - 2 * tok_count
    first = jnp.max(jnp.where(passed, ends[:, None], 0), axis=0) - origin
    last = jnp.min(jnp.where(passed, n_seq * tok_count, ends[:, None]), axis=0) - origin
    bounds = jnp.stack([first[::TILE] // TILE, (last[TILE - 1 :: TILE] + TILE - 1) // TILE], 1)
    tile_info = jnp.concatenate([core[None], bounds.reshape(-1)]).astype(jnp.int32)
    info = jnp.stack([core] + offsets).astype(jnp.int32)
    first, last = first[None], last[None]

    def row(a):
        return a.reshape(1, -1)

    q, qt, k, kt, v, vt, pk, pkt, pv, pvt, w_half = project(
        info, row(b_query), row(b_value), prefix_key, prefix_value, toks,
        (w_query, w_key, w_value), mates[:3], gathered[0],
    )
    att_keep, att_send, ot, lse = attend(tile_info, first, last, qt, k, vt, pk, pvt)
    parts_o = [w_out, mates[3]] + gathered[0]
    parts_u = [w_up, mates[4]] + gathered[1]
    parts_d = [w_down, mates[5]] + gathered[2]
    nrm, hat, inv, act, slope = up(
        info, att_keep, by_core(att_send), own, row(b_out), row(gain_attn), row(shift_attn), row(b_up),
        parts_o, parts_u,
    )
    result, gh, ga_keep, ga_send = down(
        info, nrm, hat, inv, act, slope, cot, row(b_down), row(gain_ffn), row(shift_ffn), row(gain_attn),
        parts_o, parts_u, parts_d,
    )
    out_tokens = swapped(result, 0)
    give, keep_lo, keep_hi, pre, dqt, do, dot_, inner = remote_grads(
        tile_info, first, last, q, qt, k, kt, v, pk, pkt, pv, ga_keep, by_core(ga_send), ot, lse, w_half
    )
    got = by_core(give)
    low_part = swapped((keep_lo + got[:tok_count].astype(f32)).astype(bf16), -1)
    high_part = swapped((keep_hi + got[tok_count:].astype(f32)).astype(bf16), 1)

    def added(a, exchange):
        low = a.astype(bf16)
        return low.astype(f32) + exchange(low).astype(f32)

    pre = added(pre, by_y)
    bit = 1
    while bit < n_seq:
        pre = added(pre, functools.partial(by_seq, bit=bit))
        bit *= 2
    other = by_core(pre)
    pre = jnp.concatenate(
        [jnp.where(core == 0, pre, other), jnp.where(core == 0, other, pre)], axis=1
    )

    keep, give = local_grads(
        tile_info, first, last, q, qt, k, kt, v, do, dot_, lse, inner, dqt, gh, w_half
    )
    mine = swapped((keep + by_core(give).astype(f32)).astype(bf16), 0)
    grad_tokens = (mine.astype(f32) + low_part.astype(f32) + high_part.astype(f32)).astype(bf16)
    n_pre = prefix_key.shape[0]
    return out_tokens[None], grad_tokens[None], pre[:n_pre], pre[n_pre:]


def solution(mesh):
    both, split, whole = P("row", "seq", None), P("row", None), P()
    return jax.shard_map(
        per_device,
        mesh=mesh,
        in_specs=(
            both, both, split, whole, whole, split, whole, split, split, whole, split, whole, whole, whole,
            split, whole, split, whole, whole, whole,
        ),
        out_specs=(both, both, whole, whole),
        check_vma=False,
    )
```

time: 476 us -> 284 us (0.60); the launches traced: 469 us -> 282 us
  waiting for transfers between devices: 256 us -> 88.9 us
  matrix products: 123 us -> 0 us
  Pallas kernels: 0 us -> 83.6 us
  starting transfers between devices: 47.4 us -> 78.5 us
  between operations: 15.7 us -> 1.4 us
  local copies, waits for them, and re-layouts: 12.6 us -> 23.5 us
  other arithmetic: 14.2 us -> 6.25 us
    dot_general x47 -> x0, matrix products: 123 us -> none  [the longest x1 24.5 us: per_device(): jnp.dot(grad_pre, full_up.T, preferred_element_type=jnp.float32)]
    all_gather x6 -> x0, waiting for transfers between devices: 122 us -> none  [the longest x1 51.9 us: per_device(): lax.all_gather(w_down, 'row', axis=0, tiled=True)]
    pallas_call x0 -> x6, Pallas kernels: none -> 83.6 us  [the longest x1 19.6 us: down(): pl.pallas_call(functools.partial(down_kernel, count=count), out_shape=(sh...]
    psum x1 -> x0, waiting for transfers between devices: 58.4 us -> none  [per_device(): lax.psum((grad_pkey.reshape(prefix_count, width_model), grad_pvalue.resha...]
    ppermute x16 -> x51, starting transfers between devices: 47.1 us -> 78.5 us  [the longest x6 21.4 us: swapped(): return lax.ppermute(a, ('row', 'seq'), route)]
    ppermute x16 -> x51, waiting for transfers between devices: 72 us -> 88.9 us  [the longest x7 52.5 us: by_y(): return lax.ppermute(a, 'row', [(i, i ^ 2) for i in range(n_row)])]
    reduce_sum x12 -> x1, other arithmetic: 8.27 us -> 0.12 us  [per_device(): ends = jnp.sum(jnp.where(later, lengths[None, :], 0), axis=1)]
    dynamic_slice x0 -> x6, local copies, waits for them, and re-layouts: none -> 7.69 us  [quarter(): cut = [lax.dynamic_slice_in_dim(a, which * rows, rows, 0) for a in shards]]
  transfers between devices with their start and end apart: 23 -> 51, of which waited for: 11 -> 16; matrix products, arithmetic and copies ran while one was open for 15% -> 4% of each run, Pallas kernels for 0% -> 19%
where the time goes in v1:
time: 284 us; the launch traced here: 282 us
  waiting for transfers between devices  88.9 us (31%)
  Pallas kernels  83.6 us (29%)
  starting transfers between devices  78.5 us (28%)
  local copies, waits for them, and re-layouts  23.5 us (8%)
  other arithmetic  6.25 us (2%)
    ppermute x7, waiting for transfers between devices, by_y(): return lax.ppermute(a, 'row', [(i, i ^ 2) for i in range(n_row)])  52.5 us
    ppermute x6, starting transfers between devices, swapped(): return lax.ppermute(a, ('row', 'seq'), route)  21.4 us
    ppermute x9, starting transfers between devices, by_seq(): return lax.ppermute(a, 'seq', [(i, i ^ bit) for i in range(n_seq)])  20.9 us
    ppermute x27, starting transfers between devices, by_core(): return lax.ppermute(a, 'row', [(i, i ^ 1) for i in range(n_row)])  20 us
    pallas_call x1, Pallas kernels, down(): pl.pallas_call(functools.partial(down_kernel, count=count), out_shape=(sh...  19.6 us
    ppermute x9, waiting for transfers between devices, by_seq(): return lax.ppermute(a, 'seq', [(i, i ^ bit) for i in range(n_seq)])  15.8 us
    pallas_call x1, Pallas kernels, local_grads(): pl.pallas_call(functools.partial(local_grads_kernel, heads=heads), out_sh...  14.4 us
    unnamed x105, local copies, waits for them, and re-layouts  13.5 us
  transfers between devices with their start and end apart: 51, of which 16 were waited for; matrix products, arithmetic and copies ran while one was open for 4% of the time, Pallas kernels for 19%

profile of v1, /device:TPU:1, one launch (start us, length us, event | category | flops | bytes accessed | tf_op | source)
XLA Modules:
  0.0 282.2 jit_solution(6817680669557243250)
XLA Ops:
  0.7 1.1 constant_dynamic-slice_fusion.7
  1.8 1.0 constant_dynamic-slice_fusion.6
  2.8 1.0 constant_dynamic-slice_fusion.5
  4.9 2.1 collective-permute-start.10
  7.1 4.4 %collective-permute-start.1 = (bf16[256,1024]{1,0:T(8,128)(2,1)S(1)}, bf16[256,1024]{1,0:T(8,128)(2,1)S(1)}, u32[]{:S(2)}, u32[]{:S(2)}) collective-permute-start(bf16[256,1024]{1,0:T(8,128)(2,1)S(1)} %bitcast.31), channel_id=1, source_target_pairs={{0,0},{1,8},{2,2},{3,10},{4,4},{5,12},{6,6},{7,14},{8,1},{9,9},{10... | collective-permute-start | bytes 1572872 | tf_op jit(solution)/shard_map/ppermute | solution.py:587
  11.6 2.1 collective-permute-start.29
  13.8 1.1 collective-permute-done
  15.1 3.6 %collective-permute-done.10.rest_12_.rest_2_ = bf16[64,4096]{1,0:T(8,128)(2,1)S(1)} collective-permute-done((bf16[64,4096]{1,0:T(8,128)(2,1)S(1)}, bf16[64,4096]{1,0:T(8,128)(2,1)S(1)}, u32[]{:S(2)}, u32[]{:S(2)}) %collective-permute-start.10) | collective-permute-done | bytes 524320 | tf_op jit(solution)/shard_map/ppermute | solution.py:575
  18.7 2.1 collective-permute-start.8
  20.7 9.2 %collective-permute-done.11.rest_13_.rest_3_ = bf16[64,4096]{1,0:T(8,128)(2,1)S(1)} collective-permute-done((bf16[64,4096]{1,0:T(8,128)(2,1)S(1)}, bf16[64,4096]{1,0:T(8,128)(2,1)S(1)}, u32[]{:S(2)}, u32[]{:S(2)}) %collective-permute-start.11) | collective-permute-done | bytes 524320 | tf_op jit(solution)/shard_map/ppermute | solution.py:575
  29.9 1.2 collective-permute-start.9
  31.2 2.3 constant_dynamic-slice_fusion.2
  33.5 1.5 collective-permute-start.22
  34.9 1.3 constant_dynamic-slice_fusion
  36.4 1.4 collective-permute-start.32
  37.9 1.5 collective-permute-start.14
  39.4 7.5 %collective-permute-done.22.rest_13_ = bf16[64,4096]{1,0:T(8,128)(2,1)} collective-permute-done((bf16[64,4096]{1,0:T(8,128)(2,1)}, bf16[64,4096]{1,0:T(8,128)(2,1)}, u32[]{:S(2)}, u32[]{:S(2)}) %collective-permute-start.22) | collective-permute-done | bytes 524320 | tf_op jit(solution)/shard_map/ppermute | solution.py:575
  46.9 1.5 collective-permute-start.13
  48.4 9.7 %collective-permute-done.21.rest_12_ = bf16[64,4096]{1,0:T(8,128)(2,1)} collective-permute-done((bf16[64,4096]{1,0:T(8,128)(2,1)S(1)}, bf16[64,4096]{1,0:T(8,128)(2,1)}, u32[]{:S(2)}, u32[]{:S(2)}) %collective-permute-start.21) | collective-permute-done | bytes 524320 | tf_op jit(solution)/shard_map/ppermute | solution.py:575
  58.1 1.4 collective-permute-start.12
  59.5 9.8 %collective-permute-done.32.rest_23_ = bf16[256,1024]{1,0:T(8,128)(2,1)} collective-permute-done((bf16[256,1024]{1,0:T(8,128)(2,1)S(1)}, bf16[256,1024]{1,0:T(8,128)(2,1)}, u32[]{:S(2)}, u32[]{:S(2)}) %collective-permute-start.32) | collective-permute-done | bytes 524320 | tf_op jit(solution)/shard_map/ppermute | solution.py:575
  69.3 2.1 collective-permute-start.15
  71.5 9.1 %collective-permute-done.31.rest_22_ = bf16[256,1024]{1,0:T(8,128)(2,1)} collective-permute-done((bf16[256,1024]{1,0:T(8,128)(2,1)S(1)}, bf16[256,1024]{1,0:T(8,128)(2,1)}, u32[]{:S(2)}, u32[]{:S(2)}) %collective-permute-start.31) | collective-permute-done | bytes 524320 | tf_op jit(solution)/shard_map/ppermute | solution.py:575
  80.6 1.3 collective-permute-start.5
  81.8 1.3 collective-permute-start.3
  83.1 4.1 %collective-permute-start.2 = (bf16[256,1024]{1,0:T(8,128)(2,1)S(1)}, bf16[256,1024]{1,0:T(8,128)(2,1)S(1)}, u32[]{:S(2)}, u32[]{:S(2)}) collective-permute-start(bf16[256,1024]{1,0:T(8,128)(2,1)S(1)} %collective-permute-done.1.rest_1_.tok), channel_id=1, source_target_pairs={{0,2},{1,3},{2,4},{3,5},{4,6},{5,7},{8,10},{9,11},{10,12},{11,13},... | collective-permute-start | bytes 1572872 | tf_op jit(solution)/shard_map/ppermute | solution.py:590
  88.8 1.5 collective-permute-start.24
  90.3 7.1 %collective-permute-done.3.rest_2_ = bf16[256,1024]{1,0:T(8,128)(2,1)S(1)} collective-permute-done((bf16[256,1024]{1,0:T(8,128)(2,1)S(1)}, bf16[256,1024]{1,0:T(8,128)(2,1)S(1)}, u32[]{:S(2)}, u32[]{:S(2)}) %collective-permute-start.3) | collective-permute-done | bytes 524320 | tf_op jit(solution)/shard_map/ppermute | solution.py:591
  97.4 1.3 collective-permute-start.23
  98.7 1.5 collective-permute-start.20
  100.3 2.0 collective-permute-start.34
  102.2 1.1 collective-permute-start.17
  103.5 6.2 %collective-permute-done.24.rest_15_ = bf16[64,4096]{1,0:T(8,128)(2,1)S(1)} collective-permute-done((bf16[64,4096]{1,0:T(8,128)(2,1)}, bf16[64,4096]{1,0:T(8,128)(2,1)S(1)}, u32[]{:S(2)}, u32[]{:S(2)}) %collective-permute-start.24) | collective-permute-done | bytes 524320 | tf_op jit(solution)/shard_map/ppermute | solution.py:578
  109.6 1.7 collective-permute-start.30
  112.2 8.7 %collective-permute-done.34.rest_25_ = bf16[256,1024]{1,0:T(8,128)(2,1)} collective-permute-done((bf16[256,1024]{1,0:T(8,128)(2,1)}, bf16[256,1024]{1,0:T(8,128)(2,1)}, u32[]{:S(2)}, u32[]{:S(2)}) %collective-permute-start.34) | collective-permute-done | bytes 524320 | tf_op jit(solution)/shard_map/ppermute | solution.py:578
  120.9 1.0 collective-permute-start.6
  122.0 1.4 collective-permute-start.33
  125.1 1.0 copy-done.15
  126.1 1.0 copy-done.18
  127.1 1.0 copy-done.20
  128.2 1.0 copy-done.22
  129.3 12.5 %project.1 = (bf16[512,512]{1,0:T(8,128)(2,1)S(1)}, bf16[512,512]{1,0:T(8,128)(2,1)S(1)}, bf16[1536,512]{1,0:T(8,128)(2,1)}, bf16[512,1536]{1,0:T(8,128)(2,1)}, ...) custom-call(s32[11]{0:T(128)S(1)} %stack.56.info, ...), custom_call_target="tpu_custom_call" | custom-call | tf_op jit(solution)/shard_map/project/pallas_call | solution.py:136
  141.8 1.8 copy-done
  143.6 1.4 copy-done.13
  145.0 12.8 %attend.1 = (bf16[256,512]{1,0:T(8,128)(2,1)S(1)}, bf16[256,512]{1,0:T(8,128)(2,1)S(1)}, f32[512,512]{1,0:T(8,128)S(1)}, f32[8,512]{1,0:T(8,128)S(1)}) custom-call(s32[5]{0:T(128)S(1)} %pad_add_fusion.1.info, s32[1,512]{1,0:T(1,128)S(1)} %bitcast.24, s32[1,512]{1,0:T(1,128)S(1)} %bitcast.27, bf16[512,512]{1,0:T(8,128)(2,1)S(1)} %get-tuple-element.38.qt_ref, ...), custom_call_target="tpu_custom_call" | custom-call | tf_op jit(solution)/shard_map/attend/pallas_call | solution.py:234
  162.9 12.5 %up.1 = (f32[256,1024]{1,0:T(8,128)}, f32[256,1024]{1,0:T(8,128)}, f32[256,128]{1,0:T(8,128)S(1)}, bf16[256,4096]{1,0:T(8,128)(2,1)}, bf16[256,4096]{1,0:T(8,128)(2,1)}) custom-call(s32[11]{0:T(128)S(1)} %stack.56.info, bf16[256,512]{1,0:T(8,128)(2,1)S(1)} %get-tuple-element.43.own_att, bf16[256,512]{1,0:T(8,128)(2,1)S(1)} %collective-permute-done.18.got_att, ...), custom_call_target="tpu_custom_call" | custom-call | tf_op jit(solution)/shard_map/up/pallas_call | solution.py:484
  177.8 19.6 %down.1 = (bf16[256,1024]{1,0:T(8,128)(2,1)}, f32[256,1024]{1,0:T(8,128)}, bf16[256,512]{1,0:T(8,128)(2,1)}, bf16[256,512]{1,0:T(8,128)(2,1)}) custom-call(s32[11]{0:T(128)} %copy-done.29, f32[256,1024]{1,0:T(8,128)} %get-tuple-element.45.nrm_ref, f32[256,1024]{1,0:T(8,128)} %get-tuple-element.46.hat_ref, f32[256,128]{1,0:T(8,128)} %copy-done.27, ...), custom_call_target="tpu_custom_call" | custom-call | tf_op jit(solution)/shard_map/down/pallas_call | solution.py:539
  197.6 1.6 collective-permute-done.40.recv_in
  200.1 11.8 %remote_grads.1 = (bf16[512,1024]{1,0:T(8,128)(2,1)}, f32[256,1024]{1,0:T(8,128)}, f32[256,1024]{1,0:T(8,128)}, f32[128,512]{1,0:T(8,128)S(1)}, f32[512,512]{1,0...) custom-call(s32[5]{0:T(128)S(1)} %pad_add_fusion.1.info, ...), custom_call_target="tpu_custom_call" | custom-call | tf_op jit(solution)/shard_map/remote_grads/pallas_call | solution.py:345
  212.0 5.6 %collective-permute-start.46 = (bf16[128,512]{1,0:T(8,128)(2,1)S(1)}, bf16[128,512]{1,0:T(8,128)(2,1)S(1)}, u32[]{:S(2)}, u32[]{:S(2)}) collective-permute-start(bf16[128,512]{1,0:T(8,128)(2,1)S(1)} %convert_element_type.76), channel_id=1, source_target_pairs={{0,16},{8,24},{16,0},{24,8},{1,17},{9,25},{17,1},{25,9},{2,18},{10... | collective-permute-start | bytes 393224 | tf_op jit(solution)/shard_map/ppermute | solution.py:575
  217.6 3.7 %collective-permute-done.46 = bf16[128,512]{1,0:T(8,128)(2,1)S(1)} collective-permute-done((bf16[128,512]{1,0:T(8,128)(2,1)S(1)}, bf16[128,512]{1,0:T(8,128)(2,1)S(1)}, u32[]{:S(2)}, u32[]{:S(2)}) %collective-permute-start.46) | collective-permute-done | bytes 131104 | tf_op jit(solution)/shard_map/ppermute | solution.py:575
  221.4 1.3 collective-permute-start.47
  222.8 14.4 %local_grads.1 = (f32[256,1024]{1,0:T(8,128)}, bf16[256,1024]{1,0:T(8,128)(2,1)S(1)}) custom-call(s32[5]{0:T(128)S(1)} %pad_add_fusion.1.info, s32[1,512]{1,0:T(1,128)S(1)} %bitcast.26, s32[1,512]{1,0:T(1,128)S(1)} %bitcast.29, bf16[512,512]{1,0:T(8,128)(2,1)S(1)} %copy-done.12, bf16[512,512]{1,0:T(8,128)(2,1)S(1)} %copy-done.8, ...), custom_call_target="tpu_custom_call" | custom-call | tf_op jit(solution)/shard_map/local_grads/pallas_call | solution.py:414
  237.2 1.3 collective-permute-start.41
  238.6 6.3 %collective-permute-start.48 = (bf16[128,512]{1,0:T(8,128)(2,1)S(1)}, bf16[128,512]{1,0:T(8,128)(2,1)S(1)}, u32[]{:S(2)}, u32[]{:S(2)}) collective-permute-start(bf16[128,512]{1,0:T(8,128)(2,1)S(1)} %add_convert_fusion.5), channel_id=1, source_target_pairs={{0,2},{1,3},{2,0},{3,1},{4,6},{5,7},{6,4},{7,5},{8,10},{9,11},{10,... | collective-permute-start | bytes 393224 | tf_op jit(solution)/shard_map/ppermute | solution.py:578
  245.0 2.6 collective-permute-start.39
  248.5 4.0 %collective-permute-start.49 = (bf16[128,512]{1,0:T(8,128)(2,1)S(1)}, bf16[128,512]{1,0:T(8,128)(2,1)S(1)}, u32[]{:S(2)}, u32[]{:S(2)}) collective-permute-start(bf16[128,512]{1,0:T(8,128)(2,1)S(1)} %add_convert_fusion.4), channel_id=1, source_target_pairs={{0,4},{1,5},{2,6},{3,7},{4,0},{5,1},{6,2},{7,3},{8,12},{9,13},{10,... | collective-permute-start | bytes 393224 | tf_op jit(solution)/shard_map/ppermute | solution.py:578
  252.5 1.4 add_convert_fusion.3
  253.9 5.0 %collective-permute-start.42 = (bf16[256,1024]{1,0:T(8,128)(2,1)S(1)}, bf16[256,1024]{1,0:T(8,128)(2,1)S(1)}, u32[]{:S(2)}, u32[]{:S(2)}) collective-permute-start(bf16[256,1024]{1,0:T(8,128)(2,1)S(1)} %add_convert_fusion.3), channel_id=1, source_target_pairs={{0,0},{1,8},{2,2},{3,10},{4,4},{5,12},{6,6},{7,14},{8,1},{9,9},{10... | collective-permute-start | bytes 1572872 | tf_op jit(solution)/shard_map/ppermute | solution.py:587
  259.9 1.3 add_convert_fusion.2
  261.2 1.3 collective-permute-start.44
  262.5 6.0 %collective-permute-start.45 = (bf16[256,1024]{1,0:T(8,128)(2,1)}, bf16[256,1024]{1,0:T(8,128)(2,1)}, u32[]{:S(2)}, u32[]{:S(2)}) collective-permute-start(bf16[256,1024]{1,0:T(8,128)(2,1)} %get-tuple-element.79), channel_id=1, source_target_pairs={{0,2},{1,10},{2,4},{3,12},{4,6},{5,14},{8,3},{9,11},{10,5},{11,13}... | collective-permute-start | bytes 1572872 | tf_op jit(solution)/shard_map/ppermute | solution.py:587
  269.4 9.0 %collective-permute-done.44 = bf16[256,1024]{1,0:T(8,128)(2,1)S(1)} collective-permute-done((bf16[256,1024]{1,0:T(8,128)(2,1)}, bf16[256,1024]{1,0:T(8,128)(2,1)S(1)}, u32[]{:S(2)}, u32[]{:S(2)}) %collective-permute-start.44) | collective-permute-done | bytes 524320 | tf_op jit(solution)/shard_map/ppermute | solution.py:587
  279.3 2.1 fusion
  (190 shorter events, 19.2 us)
Async XLA Ops:
  4.9 13.8 %collective-permute-start.10 = (bf16[64,4096]{1,0:T(8,128)(2,1)S(1)}, bf16[64,4096]{1,0:T(8,128)(2,1)S(1)}, u32[]{:S(2)}, u32[]{:S(2)}) collective-permute-start(bf16[64,4096]{1,0:T(8,128)(2,1)S(1)} %pad_maximum_fusion), channel_id=1, source_target_pairs={{0,16},{8,24},{16,0},{24,8},{1,17},{9,25},{17,1},{25,9},{2,18},{10... | collective-permute-start | bytes 1572872 | tf_op jit(solution)/shard_map/ppermute | solution.py:575
  7.1 22.8 %collective-permute-start.11 = (bf16[64,4096]{1,0:T(8,128)(2,1)S(1)}, bf16[64,4096]{1,0:T(8,128)(2,1)S(1)}, u32[]{:S(2)}, u32[]{:S(2)}) collective-permute-start(bf16[64,4096]{1,0:T(8,128)(2,1)S(1)} %pad_maximum_fusion.1), channel_id=1, source_target_pairs={{0,16},{8,24},{16,0},{24,8},{1,17},{9,25},{17,1},{25,9},{2,18},{10... | collective-permute-start | bytes 1572872 | tf_op jit(solution)/shard_map/ppermute | solution.py:575
  7.1 24.0 %collective-permute-start.1 = (bf16[256,1024]{1,0:T(8,128)(2,1)S(1)}, bf16[256,1024]{1,0:T(8,128)(2,1)S(1)}, u32[]{:S(2)}, u32[]{:S(2)}) collective-permute-start(bf16[256,1024]{1,0:T(8,128)(2,1)S(1)} %bitcast.31), channel_id=1, source_target_pairs={{0,0},{1,8},{2,2},{3,10},{4,4},{5,12},{6,6},{7,14},{8,1},{9,9},{10... | collective-permute-start | bytes 1572872 | tf_op jit(solution)/shard_map/ppermute | solution.py:587
  11.6 91.7 %copy-start.40 = (bf16[1024]{0:T(1024)(128)(2,1)S(1)}, bf16[1024]{0:T(1024)(128)(2,1)}, u32[]{:S(2)}) copy-start(bf16[1024]{0:T(1024)(128)(2,1)} %param.26) | copy-start | bytes 6148
  11.6 91.7 %copy-start.41 = (bf16[1024]{0:T(1024)(128)(2,1)S(1)}, bf16[1024]{0:T(1024)(128)(2,1)}, u32[]{:S(2)}) copy-start(bf16[1024]{0:T(1024)(128)(2,1)} %param.29) | copy-start | bytes 6148
  11.6 113.4 %copy-start.25 = (bf16[64,1024]{1,0:T(8,128)(2,1)S(1)}, bf16[64,1024]{1,0:T(8,128)(2,1)}, u32[]{:S(2)}) copy-start(bf16[64,1024]{1,0:T(8,128)(2,1)} %pk.1) | copy-start | bytes 393220
  11.6 113.4 %copy-start.26 = (bf16[64,1024]{1,0:T(8,128)(2,1)S(1)}, bf16[64,1024]{1,0:T(8,128)(2,1)}, u32[]{:S(2)}) copy-start(bf16[64,1024]{1,0:T(8,128)(2,1)} %pv.1) | copy-start | bytes 393220
  11.6 21.8 %collective-permute-start.29 = (bf16[256,1024]{1,0:T(8,128)(2,1)S(1)}, bf16[256,1024]{1,0:T(8,128)(2,1)}, u32[]{:S(2)}, u32[]{:S(2)}) collective-permute-start(bf16[256,1024]{1,0:T(8,128)(2,1)S(1)} %bitcast.32), channel_id=1, source_target_pairs={{0,0},{1,8},{2,2},{3,10},{4,4},{5,12},{6,6},{7,14},{8,1},{9,9},{10... | collective-permute-start | bytes 1572872 | tf_op jit(solution)/shard_map/ppermute | solution.py:587
  13.7 1.2 collective-permute-start
  14.9 21.4 %collective-permute-start.7 = (bf16[256,1024]{1,0:T(8,128)(2,1)S(1)}, bf16[256,1024]{1,0:T(8,128)(2,1)}, u32[]{:S(2)}, u32[]{:S(2)}) collective-permute-start(bf16[256,1024]{1,0:T(8,128)(2,1)S(1)} %copy-done.14), channel_id=1, source_target_pairs={{0,8},{8,0},{16,24},{24,16},{1,9},{9,1},{17,25},{25,17},{2,10},{10... | collective-permute-start | bytes 1572872 | tf_op jit(solution)/shard_map/ppermute | solution.py:572
  18.7 39.4 %copy-start.1 = (bf16[64,4096]{1,0:T(8,128)(2,1)}, bf16[64,4096]{1,0:T(8,128)(2,1)S(1)}, u32[]{:S(2)}) copy-start(bf16[64,4096]{1,0:T(8,128)(2,1)S(1)} %collective-permute-done.10.rest_12_.rest_2_) | copy-start | bytes 1572868
  18.7 17.7 %collective-permute-start.8 = (bf16[256,1024]{1,0:T(8,128)(2,1)}, bf16[256,1024]{1,0:T(8,128)(2,1)}, u32[]{:S(2)}, u32[]{:S(2)}) collective-permute-start(bf16[256,1024]{1,0:T(8,128)(2,1)} %rest_7_.1), channel_id=1, source_target_pairs={{0,8},{8,0},{16,24},{24,16},{1,9},{9,1},{17,25},{25,17},{2,10},{10... | collective-permute-start | bytes 1572872 | tf_op jit(solution)/shard_map/ppermute | solution.py:572
  29.9 39.4 %copy-start.3 = (bf16[64,4096]{1,0:T(8,128)(2,1)}, bf16[64,4096]{1,0:T(8,128)(2,1)S(1)}, u32[]{:S(2)}) copy-start(bf16[64,4096]{1,0:T(8,128)(2,1)S(1)} %collective-permute-done.11.rest_13_.rest_3_) | copy-start | bytes 1572868
  29.9 7.9 %collective-permute-start.9 = (bf16[256,1024]{1,0:T(8,128)(2,1)}, bf16[256,1024]{1,0:T(8,128)(2,1)}, u32[]{:S(2)}, u32[]{:S(2)}) collective-permute-start(bf16[256,1024]{1,0:T(8,128)(2,1)} %rest_8_.1), channel_id=1, source_target_pairs={{0,8},{8,0},{16,24},{24,16},{1,9},{9,1},{17,25},{25,17},{2,10},{10... | collective-permute-start | bytes 1572872 | tf_op jit(solution)/shard_map/ppermute | solution.py:572
  31.1 6.8 %collective-permute-start.19 = (bf16[256,1024]{1,0:T(8,128)(2,1)S(1)}, bf16[256,1024]{1,0:T(8,128)(2,1)S(1)}, u32[]{:S(2)}, u32[]{:S(2)}) collective-permute-start(bf16[256,1024]{1,0:T(8,128)(2,1)S(1)} %copy-done.9), channel_id=1, source_target_pairs={{0,8},{8,0},{16,24},{24,16},{1,9},{9,1},{17,25},{25,17},{2,10},{10... | collective-permute-start | bytes 1572872 | tf_op jit(solution)/shard_map/ppermute | solution.py:572
  33.5 13.4 %collective-permute-start.22 = (bf16[64,4096]{1,0:T(8,128)(2,1)}, bf16[64,4096]{1,0:T(8,128)(2,1)}, u32[]{:S(2)}, u32[]{:S(2)}) collective-permute-start(bf16[64,4096]{1,0:T(8,128)(2,1)} %get-tuple-element.76), channel_id=1, source_target_pairs={{0,16},{8,24},{16,0},{24,8},{1,17},{9,25},{17,1},{25,9},{2,18},{10... | collective-permute-start | bytes 1572872 | tf_op jit(solution)/shard_map/ppermute | solution.py:575
  36.3 21.8 %collective-permute-start.21 = (bf16[64,4096]{1,0:T(8,128)(2,1)S(1)}, bf16[64,4096]{1,0:T(8,128)(2,1)}, u32[]{:S(2)}, u32[]{:S(2)}) collective-permute-start(bf16[64,4096]{1,0:T(8,128)(2,1)S(1)} %copy-done.38), channel_id=1, source_target_pairs={{0,16},{8,24},{16,0},{24,8},{1,17},{9,25},{17,1},{25,9},{2,18},{10... | collective-permute-start | bytes 1572872 | tf_op jit(solution)/shard_map/ppermute | solution.py:575
  36.4 32.9 %collective-permute-start.32 = (bf16[256,1024]{1,0:T(8,128)(2,1)S(1)}, bf16[256,1024]{1,0:T(8,128)(2,1)}, u32[]{:S(2)}, u32[]{:S(2)}) collective-permute-start(bf16[256,1024]{1,0:T(8,128)(2,1)S(1)} %get-tuple-element.74), channel_id=1, source_target_pairs={{0,16},{8,24},{16,0},{24,8},{1,17},{9,25},{17,1},{25,9},{2,18},{10... | collective-permute-start | bytes 1572872 | tf_op jit(solution)/shard_map/ppermute | solution.py:575
  37.8 42.7 %collective-permute-start.31 = (bf16[256,1024]{1,0:T(8,128)(2,1)S(1)}, bf16[256,1024]{1,0:T(8,128)(2,1)}, u32[]{:S(2)}, u32[]{:S(2)}) collective-permute-start(bf16[256,1024]{1,0:T(8,128)(2,1)S(1)} %get-tuple-element.75), channel_id=1, source_target_pairs={{0,16},{8,24},{16,0},{24,8},{1,17},{9,25},{17,1},{25,9},{2,18},{10... | collective-permute-start | bytes 1572872 | tf_op jit(solution)/shard_map/ppermute | solution.py:575
  37.9 43.9 %collective-permute-start.14 = (bf16[64,4096]{1,0:T(8,128)(2,1)S(1)}, bf16[64,4096]{1,0:T(8,128)(2,1)}, u32[]{:S(2)}, u32[]{:S(2)}) collective-permute-start(bf16[64,4096]{1,0:T(8,128)(2,1)S(1)} %collective-permute-done.10.rest_12_.rest_2_), channel_id=1, source_target_pairs={{0,8},{8,0},{16,24},{24,16},{1,9},{9,1},{17,25},{25,17},{2,10},{10... | collective-permute-start | bytes 1572872 | tf_op jit(solution)/shard_map/ppermute | solution.py:572
  46.9 36.3 %collective-permute-start.13 = (bf16[64,4096]{1,0:T(8,128)(2,1)S(1)}, bf16[64,4096]{1,0:T(8,128)(2,1)}, u32[]{:S(2)}, u32[]{:S(2)}) collective-permute-start(bf16[64,4096]{1,0:T(8,128)(2,1)S(1)} %collective-permute-done.10.rest_12_.rest_2_), channel_id=1, source_target_pairs={{0,2},{1,3},{2,0},{3,1},{4,6},{5,7},{6,4},{7,5},{8,10},{9,11},{10,... | collective-permute-start | bytes 1572872 | tf_op jit(solution)/shard_map/ppermute | solution.py:578
  58.1 29.1 %collective-permute-start.12 = (bf16[64,4096]{1,0:T(8,128)(2,1)S(1)}, bf16[64,4096]{1,0:T(8,128)(2,1)S(1)}, u32[]{:S(2)}, u32[]{:S(2)}) collective-permute-start(bf16[64,4096]{1,0:T(8,128)(2,1)S(1)} %collective-permute-done.10.rest_12_.rest_2_), channel_id=1, source_target_pairs={{0,1},{1,0},{2,3},{3,2},{4,5},{5,4},{6,7},{7,6},{8,9},{9,8},{10,11... | collective-permute-start | bytes 1572872 | tf_op jit(solution)/shard_map/ppermute | solution.py:578
  69.3 18.5 %collective-permute-start.15 = (bf16[64,4096]{1,0:T(8,128)(2,1)S(1)}, bf16[64,4096]{1,0:T(8,128)(2,1)S(1)}, u32[]{:S(2)}, u32[]{:S(2)}) collective-permute-start(bf16[64,4096]{1,0:T(8,128)(2,1)S(1)} %collective-permute-done.11.rest_13_.rest_3_), channel_id=1, source_target_pairs={{0,8},{8,0},{16,24},{24,16},{1,9},{9,1},{17,25},{25,17},{2,10},{10... | collective-permute-start | bytes 1572872 | tf_op jit(solution)/shard_map/ppermute | solution.py:572
  80.6 7.4 %collective-permute-start.5 = (bf16[256,1024]{1,0:T(8,128)(2,1)S(1)}, bf16[256,1024]{1,0:T(8,128)(2,1)S(1)}, u32[]{:S(2)}, u32[]{:S(2)}) collective-permute-start(bf16[256,1024]{1,0:T(8,128)(2,1)S(1)} %collective-permute-done.1.rest_1_.tok), channel_id=1, source_target_pairs={{0,8},{8,0},{16,24},{24,16},{1,9},{9,1},{17,25},{25,17},{2,10},{10... | collective-permute-start | bytes 1572872 | tf_op jit(solution)/shard_map/ppermute | solution.py:572
  81.8 15.6 %collective-permute-start.3 = (bf16[256,1024]{1,0:T(8,128)(2,1)S(1)}, bf16[256,1024]{1,0:T(8,128)(2,1)S(1)}, u32[]{:S(2)}, u32[]{:S(2)}) collective-permute-start(bf16[256,1024]{1,0:T(8,128)(2,1)S(1)} %collective-permute-done.1.rest_1_.tok), channel_id=1, source_target_pairs={{2,0},{3,1},{4,2},{5,3},{6,4},{7,5},{10,8},{11,9},{12,10},{13,11},... | collective-permute-start | bytes 1572872 | tf_op jit(solution)/shard_map/ppermute | solution.py:591
  83.1 15.6 %collective-permute-start.2 = (bf16[256,1024]{1,0:T(8,128)(2,1)S(1)}, bf16[256,1024]{1,0:T(8,128)(2,1)S(1)}, u32[]{:S(2)}, u32[]{:S(2)}) collective-permute-start(bf16[256,1024]{1,0:T(8,128)(2,1)S(1)} %collective-permute-done.1.rest_1_.tok), channel_id=1, source_target_pairs={{0,2},{1,3},{2,4},{3,5},{4,6},{5,7},{8,10},{9,11},{10,12},{11,13},... | collective-permute-start | bytes 1572872 | tf_op jit(solution)/shard_map/ppermute | solution.py:590
  87.2 37.8 %copy-start.5 = (bf16[64,4096]{1,0:T(8,128)(2,1)}, bf16[64,4096]{1,0:T(8,128)(2,1)S(1)}, u32[]{:S(2)}) copy-start(bf16[64,4096]{1,0:T(8,128)(2,1)S(1)} %collective-permute-done.12.rest_14_.rest_4_) | copy-start | bytes 1572868
  87.3 13.0 %collective-permute-start.26 = (bf16[64,4096]{1,0:T(8,128)(2,1)}, bf16[64,4096]{1,0:T(8,128)(2,1)S(1)}, u32[]{:S(2)}, u32[]{:S(2)}) collective-permute-start(bf16[64,4096]{1,0:T(8,128)(2,1)} %collective-permute-done.22.rest_13_), channel_id=1, source_target_pairs={{0,8},{8,0},{16,24},{24,16},{1,9},{9,1},{17,25},{25,17},{2,10},{10... | collective-permute-start | bytes 1572872 | tf_op jit(solution)/shard_map/ppermute | solution.py:572
  87.8 14.4 %collective-permute-start.25 = (bf16[64,4096]{1,0:T(8,128)(2,1)}, bf16[64,4096]{1,0:T(8,128)(2,1)}, u32[]{:S(2)}, u32[]{:S(2)}) collective-permute-start(bf16[64,4096]{1,0:T(8,128)(2,1)} %collective-permute-done.21.rest_12_), channel_id=1, source_target_pairs={{0,8},{8,0},{16,24},{24,16},{1,9},{9,1},{17,25},{25,17},{2,10},{10... | collective-permute-start | bytes 1572872 | tf_op jit(solution)/shard_map/ppermute | solution.py:572
  88.8 20.8 %collective-permute-start.24 = (bf16[64,4096]{1,0:T(8,128)(2,1)}, bf16[64,4096]{1,0:T(8,128)(2,1)S(1)}, u32[]{:S(2)}, u32[]{:S(2)}) collective-permute-start(bf16[64,4096]{1,0:T(8,128)(2,1)} %collective-permute-done.21.rest_12_), channel_id=1, source_target_pairs={{0,2},{1,3},{2,0},{3,1},{4,6},{5,7},{6,4},{7,5},{8,10},{9,11},{10,... | collective-permute-start | bytes 1572872 | tf_op jit(solution)/shard_map/ppermute | solution.py:578
  97.4 13.9 %collective-permute-start.23 = (bf16[64,4096]{1,0:T(8,128)(2,1)}, bf16[64,4096]{1,0:T(8,128)(2,1)}, u32[]{:S(2)}, u32[]{:S(2)}) collective-permute-start(bf16[64,4096]{1,0:T(8,128)(2,1)} %collective-permute-done.21.rest_12_), channel_id=1, source_target_pairs={{0,1},{1,0},{2,3},{3,2},{4,5},{5,4},{6,7},{7,6},{8,9},{9,8},{10,11... | collective-permute-start | bytes 1572872 | tf_op jit(solution)/shard_map/ppermute | solution.py:578
  98.7 61.9 %collective-permute-start.20 = (bf16[256,4096]{1,0:T(8,128)(2,1)}, bf16[256,4096]{1,0:T(8,128)(2,1)}, u32[]{:S(2)}, u32[]{:S(2)}) collective-permute-start(bf16[256,4096]{1,0:T(8,128)(2,1)} %rest_10_.3), channel_id=1, source_target_pairs={{0,8},{8,0},{16,24},{24,16},{1,9},{9,1},{17,25},{25,17},{2,10},{10... | collective-permute-start | bytes 6291464 | tf_op jit(solution)/shard_map/ppermute | solution.py:572
  100.3 20.6 %collective-permute-start.34 = (bf16[256,1024]{1,0:T(8,128)(2,1)}, bf16[256,1024]{1,0:T(8,128)(2,1)}, u32[]{:S(2)}, u32[]{:S(2)}) collective-permute-start(bf16[256,1024]{1,0:T(8,128)(2,1)} %collective-permute-done.31.rest_22_), channel_id=1, source_target_pairs={{0,2},{1,3},{2,0},{3,1},{4,6},{5,7},{6,4},{7,5},{8,10},{9,11},{10,... | collective-permute-start | bytes 1572872 | tf_op jit(solution)/shard_map/ppermute | solution.py:578
  102.2 19.7 %collective-permute-start.17 = (bf16[64,4096]{1,0:T(8,128)(2,1)}, bf16[64,4096]{1,0:T(8,128)(2,1)}, u32[]{:S(2)}, u32[]{:S(2)}) collective-permute-start(bf16[64,4096]{1,0:T(8,128)(2,1)} %collective-permute-done.13.rest_15_.rest_5_), channel_id=1, source_target_pairs={{0,8},{8,0},{16,24},{24,16},{1,9},{9,1},{17,25},{25,17},{2,10},{10... | collective-permute-start | bytes 1572872 | tf_op jit(solution)/shard_map/ppermute | solution.py:572
  103.4 59.4 %copy-start.29 = (s32[11]{0:T(128)}, s32[11]{0:T(128)S(1)}, u32[]{:S(2)}) copy-start(s32[11]{0:T(128)S(1)} %stack.56.info) | copy-start | bytes 136
  109.6 67.2 %collective-permute-start.30 = (bf16[1024,1024]{1,0:T(8,128)(2,1)}, bf16[1024,1024]{1,0:T(8,128)(2,1)}, u32[]{:S(2)}, u32[]{:S(2)}) collective-permute-start(bf16[1024,1024]{1,0:T(8,128)(2,1)} %rest_20_.1), channel_id=1, source_target_pairs={{0,8},{8,0},{16,24},{24,16},{1,9},{9,1},{17,25},{25,17},{2,10},{10... | collective-permute-start | bytes 6291464 | tf_op jit(solution)/shard_map/ppermute | solution.py:572
  111.3 10.7 %collective-permute-start.16 = (bf16[64,4096]{1,0:T(8,128)(2,1)S(1)}, bf16[64,4096]{1,0:T(8,128)(2,1)S(1)}, u32[]{:S(2)}, u32[]{:S(2)}) collective-permute-start(bf16[64,4096]{1,0:T(8,128)(2,1)S(1)} %collective-permute-done.12.rest_14_.rest_4_), channel_id=1, source_target_pairs={{0,8},{8,0},{16,24},{24,16},{1,9},{9,1},{17,25},{25,17},{2,10},{10... | collective-permute-start | bytes 1572872 | tf_op jit(solution)/shard_map/ppermute | solution.py:572
  120.9 2.8 collective-permute-start.6
  121.9 2.6 collective-permute-start.4
  122.0 36.9 %collective-permute-start.33 = (bf16[256,1024]{1,0:T(8,128)(2,1)}, bf16[256,1024]{1,0:T(8,128)(2,1)}, u32[]{:S(2)}, u32[]{:S(2)}) collective-permute-start(bf16[256,1024]{1,0:T(8,128)(2,1)} %collective-permute-done.31.rest_22_), channel_id=1, source_target_pairs={{0,1},{1,0},{2,3},{3,2},{4,5},{5,4},{6,7},{7,6},{8,9},{9,8},{10,11... | collective-permute-start | bytes 1572872 | tf_op jit(solution)/shard_map/ppermute | solution.py:578
  123.7 35.4 %collective-permute-start.28 = (bf16[64,4096]{1,0:T(8,128)(2,1)}, bf16[64,4096]{1,0:T(8,128)(2,1)}, u32[]{:S(2)}, u32[]{:S(2)}) collective-permute-start(bf16[64,4096]{1,0:T(8,128)(2,1)} %copy-done.33), channel_id=1, source_target_pairs={{0,8},{8,0},{16,24},{24,16},{1,9},{9,1},{17,25},{25,17},{2,10},{10... | collective-permute-start | bytes 1572872 | tf_op jit(solution)/shard_map/ppermute | solution.py:572
  124.4 35.0 %collective-permute-start.27 = (bf16[64,4096]{1,0:T(8,128)(2,1)}, bf16[64,4096]{1,0:T(8,128)(2,1)}, u32[]{:S(2)}, u32[]{:S(2)}) collective-permute-start(bf16[64,4096]{1,0:T(8,128)(2,1)} %collective-permute-done.23.rest_14_), channel_id=1, source_target_pairs={{0,8},{8,0},{16,24},{24,16},{1,9},{9,1},{17,25},{25,17},{2,10},{10... | collective-permute-start | bytes 1572872 | tf_op jit(solution)/shard_map/ppermute | solution.py:572
  129.2 32.4 %copy-start.46 = (bf16[1024]{0:T(1024)(128)(2,1)S(1)}, bf16[1024]{0:T(1024)(128)(2,1)}, u32[]{:S(2)}) copy-start(bf16[1024]{0:T(1024)(128)(2,1)} %param.38) | copy-start | bytes 6148
  129.2 33.0 %copy-start.47 = (bf16[1024]{0:T(1024)(128)(2,1)S(1)}, bf16[1024]{0:T(1024)(128)(2,1)}, u32[]{:S(2)}) copy-start(bf16[1024]{0:T(1024)(128)(2,1)} %param.39) | copy-start | bytes 6148
  129.2 33.6 %copy-start.2 = (bf16[64,4096]{1,0:T(8,128)(2,1)S(1)}, bf16[64,4096]{1,0:T(8,128)(2,1)}, u32[]{:S(2)}) copy-start(bf16[64,4096]{1,0:T(8,128)(2,1)} %copy-done.1) | copy-start | bytes 1572868
  129.3 33.6 %copy-start.4 = (bf16[64,4096]{1,0:T(8,128)(2,1)S(1)}, bf16[64,4096]{1,0:T(8,128)(2,1)}, u32[]{:S(2)}) copy-start(bf16[64,4096]{1,0:T(8,128)(2,1)} %copy-done.3) | copy-start | bytes 1572868
  141.8 33.5 %copy-start.7 = (bf16[512,512]{1,0:T(8,128)(2,1)}, bf16[512,512]{1,0:T(8,128)(2,1)S(1)}, u32[]{:S(2)}) copy-start(bf16[512,512]{1,0:T(8,128)(2,1)S(1)} %get-tuple-element.38.qt_ref) | copy-start | bytes 1572868
  158.9 1.5 collective-permute-start.18
  159.1 17.7 %collective-permute-start.35 = (bf16[256,1024]{1,0:T(8,128)(2,1)}, bf16[256,1024]{1,0:T(8,128)(2,1)S(1)}, u32[]{:S(2)}, u32[]{:S(2)}) collective-permute-start(bf16[256,1024]{1,0:T(8,128)(2,1)} %collective-permute-done.31.rest_22_), channel_id=1, source_target_pairs={{0,8},{8,0},{16,24},{24,16},{1,9},{9,1},{17,25},{25,17},{2,10},{10... | collective-permute-start | bytes 1572872 | tf_op jit(solution)/shard_map/ppermute | solution.py:572
  159.4 17.4 %collective-permute-start.36 = (bf16[256,1024]{1,0:T(8,128)(2,1)}, bf16[256,1024]{1,0:T(8,128)(2,1)S(1)}, u32[]{:S(2)}, u32[]{:S(2)}) collective-permute-start(bf16[256,1024]{1,0:T(8,128)(2,1)} %collective-permute-done.32.rest_23_), channel_id=1, source_target_pairs={{0,8},{8,0},{16,24},{24,16},{1,9},{9,1},{17,25},{25,17},{2,10},{10... | collective-permute-start | bytes 1572872 | tf_op jit(solution)/shard_map/ppermute | solution.py:572
  160.4 16.4 %collective-permute-start.38 = (bf16[256,1024]{1,0:T(8,128)(2,1)}, bf16[256,1024]{1,0:T(8,128)(2,1)}, u32[]{:S(2)}, u32[]{:S(2)}) collective-permute-start(bf16[256,1024]{1,0:T(8,128)(2,1)} %collective-permute-done.34.rest_25_), channel_id=1, source_target_pairs={{0,8},{8,0},{16,24},{24,16},{1,9},{9,1},{17,25},{25,17},{2,10},{10... | collective-permute-start | bytes 1572872 | tf_op jit(solution)/shard_map/ppermute | solution.py:572
  160.6 16.2 %collective-permute-start.37 = (bf16[256,1024]{1,0:T(8,128)(2,1)}, bf16[256,1024]{1,0:T(8,128)(2,1)}, u32[]{:S(2)}, u32[]{:S(2)}) collective-permute-start(bf16[256,1024]{1,0:T(8,128)(2,1)} %collective-permute-done.33.rest_24_), channel_id=1, source_target_pairs={{0,8},{8,0},{16,24},{24,16},{1,9},{9,1},{17,25},{25,17},{2,10},{10... | collective-permute-start | bytes 1572872 | tf_op jit(solution)/shard_map/ppermute | solution.py:572
  197.4 1.8 collective-permute-start.40
  212.0 9.4 %collective-permute-start.46 = (bf16[128,512]{1,0:T(8,128)(2,1)S(1)}, bf16[128,512]{1,0:T(8,128)(2,1)S(1)}, u32[]{:S(2)}, u32[]{:S(2)}) collective-permute-start(bf16[128,512]{1,0:T(8,128)(2,1)S(1)} %convert_element_type.76), channel_id=1, source_target_pairs={{0,16},{8,24},{16,0},{24,8},{1,17},{9,25},{17,1},{25,9},{2,18},{10... | collective-permute-start | bytes 393224 | tf_op jit(solution)/shard_map/ppermute | solution.py:575
  221.4 17.1 %collective-permute-start.47 = (bf16[128,512]{1,0:T(8,128)(2,1)S(1)}, bf16[128,512]{1,0:T(8,128)(2,1)S(1)}, u32[]{:S(2)}, u32[]{:S(2)}) collective-permute-start(bf16[128,512]{1,0:T(8,128)(2,1)S(1)} %add_convert_fusion.6), channel_id=1, source_target_pairs={{0,1},{1,0},{2,3},{3,2},{4,5},{5,4},{6,7},{7,6},{8,9},{9,8},{10,11... | collective-permute-start | bytes 393224 | tf_op jit(solution)/shard_map/ppermute | solution.py:578
  237.2 15.3 %collective-permute-start.41 = (bf16[256,1024]{1,0:T(8,128)(2,1)S(1)}, bf16[256,1024]{1,0:T(8,128)(2,1)S(1)}, u32[]{:S(2)}, u32[]{:S(2)}) collective-permute-start(bf16[256,1024]{1,0:T(8,128)(2,1)S(1)} %get-tuple-element.67), channel_id=1, source_target_pairs={{0,8},{8,0},{16,24},{24,16},{1,9},{9,1},{17,25},{25,17},{2,10},{10... | collective-permute-start | bytes 1572872 | tf_op jit(solution)/shard_map/ppermute | solution.py:572
  238.5 21.4 %collective-permute-start.43 = (bf16[512,1024]{1,0:T(8,128)(2,1)S(1)}, bf16[512,1024]{1,0:T(8,128)(2,1)S(1)}, u32[]{:S(2)}, u32[]{:S(2)}) collective-permute-start(bf16[512,1024]{1,0:T(8,128)(2,1)S(1)} %copy-done.49), channel_id=1, source_target_pairs={{0,8},{8,0},{16,24},{24,16},{1,9},{9,1},{17,25},{25,17},{2,10},{10... | collective-permute-start | bytes 3145736 | tf_op jit(solution)/shard_map/ppermute | solution.py:572
  238.6 9.9 %collective-permute-start.48 = (bf16[128,512]{1,0:T(8,128)(2,1)S(1)}, bf16[128,512]{1,0:T(8,128)(2,1)S(1)}, u32[]{:S(2)}, u32[]{:S(2)}) collective-permute-start(bf16[128,512]{1,0:T(8,128)(2,1)S(1)} %add_convert_fusion.5), channel_id=1, source_target_pairs={{0,2},{1,3},{2,0},{3,1},{4,6},{5,7},{6,4},{7,5},{8,10},{9,11},{10,... | collective-permute-start | bytes 393224 | tf_op jit(solution)/shard_map/ppermute | solution.py:578
  245.0 23.6 %collective-permute-start.39 = (bf16[256,1024]{1,0:T(8,128)(2,1)}, bf16[256,1024]{1,0:T(8,128)(2,1)S(1)}, u32[]{:S(2)}, u32[]{:S(2)}) collective-permute-start(bf16[256,1024]{1,0:T(8,128)(2,1)} %get-tuple-element.50), channel_id=1, source_target_pairs={{0,0},{1,8},{2,2},{3,10},{4,4},{5,12},{6,6},{7,14},{8,1},{9,9},{10... | collective-permute-start | bytes 1572872 | tf_op jit(solution)/shard_map/ppermute | solution.py:587
  248.5 10.5 %collective-permute-start.49 = (bf16[128,512]{1,0:T(8,128)(2,1)S(1)}, bf16[128,512]{1,0:T(8,128)(2,1)S(1)}, u32[]{:S(2)}, u32[]{:S(2)}) collective-permute-start(bf16[128,512]{1,0:T(8,128)(2,1)S(1)} %add_convert_fusion.4), channel_id=1, source_target_pairs={{0,4},{1,5},{2,6},{3,7},{4,0},{5,1},{6,2},{7,3},{8,12},{9,13},{10,... | collective-permute-start | bytes 393224 | tf_op jit(solution)/shard_map/ppermute | solution.py:578
  253.9 15.5 %collective-permute-start.42 = (bf16[256,1024]{1,0:T(8,128)(2,1)S(1)}, bf16[256,1024]{1,0:T(8,128)(2,1)S(1)}, u32[]{:S(2)}, u32[]{:S(2)}) collective-permute-start(bf16[256,1024]{1,0:T(8,128)(2,1)S(1)} %add_convert_fusion.3), channel_id=1, source_target_pairs={{0,0},{1,8},{2,2},{3,10},{4,4},{5,12},{6,6},{7,14},{8,1},{9,9},{10... | collective-permute-start | bytes 1572872 | tf_op jit(solution)/shard_map/ppermute | solution.py:587
  259.0 9.5 %collective-permute-start.50 = (f32[128,512]{1,0:T(8,128)S(1)}, f32[128,512]{1,0:T(8,128)S(1)}, u32[]{:S(2)}, u32[]{:S(2)}) collective-permute-start(f32[128,512]{1,0:T(8,128)S(1)} %convert_add_fusion), channel_id=1, source_target_pairs={{0,8},{8,0},{16,24},{24,16},{1,9},{9,1},{17,25},{25,17},{2,10},{10... | collective-permute-start | bytes 786440 | tf_op jit(solution)/shard_map/ppermute | solution.py:572
  261.2 17.2 %collective-permute-start.44 = (bf16[256,1024]{1,0:T(8,128)(2,1)}, bf16[256,1024]{1,0:T(8,128)(2,1)S(1)}, u32[]{:S(2)}, u32[]{:S(2)}) collective-permute-start(bf16[256,1024]{1,0:T(8,128)(2,1)} %get-tuple-element.78), channel_id=1, source_target_pairs={{2,0},{3,8},{4,2},{5,10},{6,4},{7,12},{10,1},{11,9},{12,3},{13,11}... | collective-permute-start | bytes 1572872 | tf_op jit(solution)/shard_map/ppermute | solution.py:587
  262.5 16.8 %collective-permute-start.45 = (bf16[256,1024]{1,0:T(8,128)(2,1)}, bf16[256,1024]{1,0:T(8,128)(2,1)}, u32[]{:S(2)}, u32[]{:S(2)}) collective-permute-start(bf16[256,1024]{1,0:T(8,128)(2,1)} %get-tuple-element.79), channel_id=1, source_target_pairs={{0,2},{1,10},{2,4},{3,12},{4,6},{5,14},{8,3},{9,11},{10,5},{11,13}... | collective-permute-start | bytes 1572872 | tf_op jit(solution)/shard_map/ppermute | solution.py:587
  (39 other events, 399.0 us)

commit v2 on v1

--- a/solution.py
+++ b/solution.py
@@ -13,6 +13,7 @@
 MASKED = -1e30
 TILE = 256
 CHUNK = 512
+GRAD_LAGS = (0, 1, 2)
 
 f32 = jnp.float32
 bf16 = jnp.bfloat16
@@ -21,6 +22,10 @@
 HB = pl.BlockSpec(memory_space=pl.ANY)
 
 
+def cost(us):
+    return pl.CostEstimate(flops=int(us * 1e9), bytes_accessed=0, transcendentals=0)
+
+
 def shape_of(shape, kind):
     return jax.ShapeDtypeStruct(shape, kind)
 
@@ -55,14 +60,68 @@
     return (g - jnp.mean(g, -1, keepdims=True) - n * jnp.mean(g * n, -1, keepdims=True)) * inv
 
 
-def project_kernel(info, bq, bv, pk, pv, *rest, count, half):
+def pack_kernel(info, *rest, plan, n_in):
+    srcs, outs, sem = rest[:n_in], rest[n_in:-1], rest[-1]
+    pairs = []
+    for i, which, o, col in plan:
+        rows, cols = outs[o].shape[0], srcs[i].shape[1]
+        pairs.append((srcs[i].at[row_at(info[which] * rows, rows), :], outs[o].at[:, pl.ds(col, cols)]))
+    wait_all(start_all(pairs, sem))
+
+
+def pack(info, srcs, shapes, plan):
+    return pl.pallas_call(
+        functools.partial(pack_kernel, plan=plan, n_in=len(srcs)),
+        out_shape=tuple(shape_of(a, bf16) for a in shapes),
+        in_specs=[SM] + [HB] * len(srcs),
+        out_specs=(VM,) * len(shapes),
+        scratch_shapes=[pltpu.SemaphoreType.DMA((len(plan),))],
+        name="pack",
+        cost_estimate=cost(2),
+    )(info, *srcs)
+
+
+def head_rows(ref, h, at):
+    own = ref[pl.ds(h * HEAD, HEAD), at]
+    zero = jnp.zeros_like(own)
+    return jnp.concatenate([own, zero] if h % 2 == 0 else [zero, own], 0)
+
+
+def head_cols(ref, h, at):
+    block = ref[at, pl.ds((h // 2) * 2 * HEAD, 2 * HEAD)]
+    lane = lax.broadcasted_iota(jnp.int32, block.shape, 1)
+    return jnp.where((lane < HEAD) == (h % 2 == 0), block, jnp.zeros_like(block))
+
+
+def pair_cols(h):
+    return pl.ds((h // 2) * 2 * HEAD, 2 * HEAD)
+
+
+def allowed_bias(k0, first, last):
+    place = k0 + lax.broadcasted_iota(jnp.int32, (TILE, TILE), 0)
+    return jnp.where((place >= first) & (place < last), 0.0, MASKED).astype(f32)
+
+
+def staged(heads, stages, lags):
+    held = [{} for _ in stages]
+    for step in range(heads + sum(lags)):
+        behind = 0
+        for i, stage in enumerate(stages):
+            behind += lags[i]
+            h = step - behind
+            if 0 <= h < heads:
+                held[i][h] = stage(h, held[i - 1].pop(h) if i else None)
+
+
+def front_kernel(info, tiles, first, last, bq, bv, pk, pv, *rest, count, half):
     tok_in = rest[:6]
     own, mate = rest[6:9], rest[9:12]
     pieces = rest[12 : 12 + count]
-    (q_ref, qt_ref, k_ref, kt_ref, v_ref, vt_ref, pk_ref, pkt_ref, pv_ref, pvt_ref, w_ref) = rest[
-        12 + count : 23 + count
-    ]
-    tok, sem_x, sem_w = rest[23 + count :]
+    outs = rest[12 + count : 26 + count]
+    (keep_ref, send_ref, ot_ref, lse_ref, pk_ref, pkt_ref, pv_ref, q_out, qt_out, k_out, kt_out, v_out,
+     w_out, pvt_ref) = outs
+    (tok, w_ref, q_ref, qt_ref, k_ref, kt_ref, v_ref, vt_ref, stat, acc, bias, sem_x, sem_w,
+     sem_o) = rest[26 + count :]
     core = info[0]
     tokens = tok_in[0].shape[0]
     width = tok.shape[1]
@@ -88,10 +147,10 @@
     pk_half, pv_half = pk[:, pl.ds(cols, half)], pv[:, pl.ds(cols, half)]
     pk_ref[...], pkt_ref[...] = pk_half, pk_half.astype(f32).T.astype(bf16)
     pv_ref[...], pvt_ref[...] = pv_half, pv_half.astype(f32).T.astype(bf16)
-    wait_all(got_tok)
     bias_v = bv[:, pl.ds(cols, half)].astype(f32)
     bias_q = bq[:, pl.ds(cols, half)].astype(f32)
     blocks = k_ref.shape[0] // TILE
+    wait_all(got_tok)
     wait_all(got_w[0])
 
     def key_block(b, carry):
@@ -123,89 +182,58 @@
         return carry
 
     lax.fori_loop(0, 2 * tokens // TILE, query_block, 0)
-
-
-def project(info, bq, bv, pk, pv, toks, own, mate, pieces):
-    tokens, width = toks[0].shape
-    half = width // 2
-    pre = pk.shape[0]
-    n_q, n_k = 2 * tokens, 6 * tokens
-    count = len(pieces)
-    outs = [(n_q, half), (half, n_q), (n_k, half), (half, n_k), (n_k, half), (half, n_k)]
-    outs += [(pre, half), (half, pre), (pre, half), (half, pre), (3, width, half)]
-    return pl.pallas_call(
-        functools.partial(project_kernel, count=count, half=half),
-        out_shape=tuple(shape_of(s, bf16) for s in outs),
-        in_specs=[SM] + [VM] * 4 + [HB] * (12 + count),
-        out_specs=(VM,) * len(outs),
-        scratch_shapes=[
-            pltpu.VMEM((n_k, width), bf16),
-            pltpu.SemaphoreType.DMA((6,)),
-            pltpu.SemaphoreType.DMA((3, 2 + count)),
-        ],
-        compiler_params=pltpu.CompilerParams(vmem_limit_bytes=48 << 20),
-        name="project",
-    )(info, bq, bv, pk, pv, *toks, *own, *mate, *pieces)
-
-
-def head_rows(ref, h, at):
-    own = ref[pl.ds(h * HEAD, HEAD), at]
-    zero = jnp.zeros_like(own)
-    return jnp.concatenate([own, zero] if h % 2 == 0 else [zero, own], 0)
-
-
-def head_cols(ref, h, at):
-    block = ref[at, pl.ds((h // 2) * 2 * HEAD, 2 * HEAD)]
-    lane = lax.broadcasted_iota(jnp.int32, block.shape, 1)
-    return jnp.where((lane < HEAD) == (h % 2 == 0), block, jnp.zeros_like(block))
-
-
-def pair_cols(h):
-    return pl.ds((h // 2) * 2 * HEAD, 2 * HEAD)
-
-
-def allowed_bias(k0, first, last):
-    place = k0 + lax.broadcasted_iota(jnp.int32, (TILE, TILE), 0)
-    return jnp.where((place >= first) & (place < last), 0.0, MASKED).astype(f32)
-
-
-def forward_kernel(
-    info, first, last, qt_ref, k_ref, vt_ref, pk_ref, pvt_ref, keep_ref, send_ref, ot_ref, lse_ref,
-    stat, acc, bias, *, heads,
-):
-    tokens = keep_ref.shape[0]
+    saved = start_all(
+        [(w_ref, w_out), (k_ref, k_out), (kt_ref, kt_out), (v_ref, v_out), (q_ref, q_out), (qt_ref, qt_out)],
+        sem_o,
+    )
+    heads = half // HEAD
 
     def one_query_tile(t, carry):
         at = pl.ds(pl.multiple_of(t * TILE, TILE), TILE)
         qs, qe = first[:, at], last[:, at]
-        for h in range(heads):
-            s = dot(pk_ref[:, pair_cols(h)], head_rows(qt_ref, h, at))
+
+        def prefix_score(h, _):
+            return dot(pk_ref[:, pair_cols(h)], head_rows(qt_ref, h, at))
+
+        def prefix_soft(h, s):
             top = jnp.max(s, axis=0, keepdims=True)
             p = jnp.exp(s - top)
             stat[pl.ds(h, 1), :] = top
             stat[pl.ds(heads + h, 1), :] = jnp.sum(p, axis=0, keepdims=True)
-            acc[pl.ds(h * HEAD, HEAD), :] = dot(pvt_ref[pl.ds(h * HEAD, HEAD), :], p.astype(bf16))
+            return p.astype(bf16)
+
+        def prefix_mix(h, p):
+            acc[pl.ds(h * HEAD, HEAD), :] = dot(pvt_ref[pl.ds(h * HEAD, HEAD), :], p)
+
+        staged(heads, (prefix_score, prefix_soft, prefix_mix), (0, 1, 3))
 
         def one_key_tile(j, inner):
             k0 = pl.multiple_of(j * TILE, TILE)
             bias[...] = allowed_bias(k0, qs, qe)
-            for h in range(heads):
-                s = dot(k_ref[pl.ds(k0, TILE), pair_cols(h)], head_rows(qt_ref, h, at)) + bias[...]
+
+            def score(h, _):
+                return dot(k_ref[pl.ds(k0, TILE), pair_cols(h)], head_rows(qt_ref, h, at))
+
+            def soft(h, s):
+                s = s + bias[...]
                 old = stat[pl.ds(h, 1), :]
                 top = jnp.maximum(old, jnp.max(s, axis=0, keepdims=True))
                 factor = jnp.exp(old - top)
                 p = jnp.exp(s - top)
                 stat[pl.ds(h, 1), :] = top
-                stat[pl.ds(heads + h, 1), :] = stat[pl.ds(heads + h, 1), :] * factor + jnp.sum(
-                    p, axis=0, keepdims=True
-                )
+                total = jnp.sum(p, axis=0, keepdims=True)
+                stat[pl.ds(heads + h, 1), :] = stat[pl.ds(heads + h, 1), :] * factor + total
+                return p.astype(bf16), factor
+
+            def mix(h, held):
+                p, factor = held
                 rows = pl.ds(h * HEAD, HEAD)
-                acc[rows, :] = acc[rows, :] * factor + dot(
-                    vt_ref[rows, pl.ds(k0, TILE)], p.astype(bf16)
-                )
+                acc[rows, :] = acc[rows, :] * factor + dot(vt_ref[rows, pl.ds(k0, TILE)], p)
+
+            staged(heads, (score, soft, mix), (0, 1, 3))
             return inner
 
-        lax.fori_loop(info[1 + 2 * t], info[2 + 2 * t], one_key_tile, 0)
+        lax.fori_loop(tiles[1 + 2 * t], tiles[2 + 2 * t], one_key_tile, 0)
         for h in range(heads):
             rows = pl.ds(h * HEAD, HEAD)
             acc[rows, :] = acc[rows, :] / stat[pl.ds(heads + h, 1), :]
@@ -215,49 +243,68 @@
         side = (t * TILE) // tokens
         rows = pl.ds(pl.multiple_of(t * TILE - side * tokens, TILE), TILE)
 
-        @pl.when(side == info[0])
+        @pl.when(side == core)
         def _():
             keep_ref[rows, :] = low
 
-        @pl.when(side != info[0])
+        @pl.when(side != core)
         def _():
             send_ref[rows, :] = low
 
         return carry
 
     lax.fori_loop(0, 2 * tokens // TILE, one_query_tile, 0)
-
-
-def attend(info, first, last, qt, k, vt, pk, pvt):
-    half, n_q = qt.shape
-    heads = half // HEAD
+    wait_all(saved)
+
+
+def front(info, tiles, first, last, bq, bv, pk, pv, toks, own, mate, pieces):
+    tokens, width = toks[0].shape
+    half = width // 2
+    heads, pre = half // HEAD, pk.shape[0]
+    n_q, n_k = 2 * tokens, 6 * tokens
+    count = len(pieces)
+    outs = [((tokens, half), bf16), ((tokens, half), bf16), ((half, n_q), f32), ((heads, n_q), f32)]
+    outs += [((pre, half), bf16), ((half, pre), bf16), ((pre, half), bf16)]
+    kept = [(n_q, half), (half, n_q), (n_k, half), (half, n_k), (n_k, half)]
+    outs += [(a, bf16) for a in kept] + [((3, width, half), bf16)]
+    vmem = [pltpu.VMEM((n_k, width), bf16), pltpu.VMEM((3, width, half), bf16)]
+    vmem += [pltpu.VMEM(a, bf16) for a in kept + [(half, n_k)]]
     return pl.pallas_call(
-        functools.partial(forward_kernel, heads=heads),
-        out_shape=(
-            shape_of((n_q // 2, half), bf16),
-            shape_of((n_q // 2, half), bf16),
-            shape_of((half, n_q), f32),
-            shape_of((heads, n_q), f32),
-        ),
-        in_specs=[SM] + [VM] * 7,
-        out_specs=(VM,) * 4,
-        scratch_shapes=[
+        functools.partial(front_kernel, count=count, half=half),
+        out_shape=tuple(shape_of(*a) for a in outs) + (shape_of((half, pre), bf16),),
+        in_specs=[SM, SM] + [VM] * 6 + [HB] * (12 + count),
+        out_specs=(VM,) * 7 + (HB,) * 6 + (VM,),
+        scratch_shapes=vmem
+        + [
             pltpu.VMEM((2 * heads, TILE), f32),
             pltpu.VMEM((half, TILE), f32),
             pltpu.VMEM((TILE, TILE), f32),
+            pltpu.SemaphoreType.DMA((6,)),
+            pltpu.SemaphoreType.DMA((3, 2 + count)),
+            pltpu.SemaphoreType.DMA((6,)),
         ],
-        compiler_params=pltpu.CompilerParams(vmem_limit_bytes=40 << 20),
-        name="attend",
-    )(info, first, last, qt, k, vt, pk, pvt)
-
-
-def tile_grads(h, k_b, v_b, kt_b, bias, qt_m, dot_m, q_m, do_m, lse, inner):
-    s = dot(k_b, qt_m)
-    if bias is not None:
-        s = s + bias
-    p = jnp.exp(s - lse)
-    ds = (p * (dot(v_b, dot_m) - inner)).astype(bf16)
-    return dot(p.astype(bf16), do_m), dot(ds, q_m), dot(kt_b, ds)
+        compiler_params=pltpu.CompilerParams(vmem_limit_bytes=48 << 20),
+        name="front",
+        cost_estimate=cost(20),
+    )(info, tiles, first, last, bq, bv, pk, pv, *toks, *own, *mate, *pieces)
+
+
+def grad_stages(q, qt, kb, vb, ktb, do, do_t, lse, inner, bias, put):
+    def products(h, _):
+        return dot(kb(h), qt(h)), dot(vb(h), do_t(h))
+
+    def scores(h, held):
+        s, dp = held
+        if bias is not None:
+            s = s + bias[...]
+        p = jnp.exp(s - lse(h))
+        return p.astype(bf16), (p * (dp - inner(h))).astype(bf16)
+
+    def sums(h, held):
+        p, ds = held
+        put(h, dot(p, do(h)), dot(ds, q(h)), dot(ktb(h), ds))
+
+    return products, scores, sums
 
 
 def sweep(ranges, at, first, last, refs, acc, heads):
@@ -269,16 +316,21 @@
         k0 = pl.multiple_of(j * TILE, TILE)
         r = pl.ds(k0, TILE)
         bias[...] = allowed_bias(k0, qs, qe)
-        for h in range(heads):
+
+        def put(h, gv, gk, gq):
             c, rows = pair_cols(h), pl.ds(h * HEAD, HEAD)
-            gv, gk, gq = tile_grads(
-                h, k_ref[r, c], v_ref[r, c], kt_ref[rows, r], bias[...], head_rows(qt_ref, h, at),
-                head_rows(dot_ref, h, at), head_cols(q_ref, h, at), head_cols(do_ref, h, at),
-                lse_ref[pl.ds(h, 1), at], inner_ref[pl.ds(h, 1), at],
-            )
             dv[r, c] += gv
             dk[r, c] += gk
             dqt[rows, at] += gq
+
+        stages = grad_stages(
+            lambda h: head_cols(q_ref, h, at), lambda h: head_rows(qt_ref, h, at),
+            lambda h: k_ref[r, pair_cols(h)], lambda h: v_ref[r, pair_cols(h)],
+            lambda h: kt_ref[pl.ds(h * HEAD, HEAD), r], lambda h: head_cols(do_ref, h, at),
+            lambda h: head_rows(dot_ref, h, at), lambda h: lse_ref[pl.ds(h, 1), at],
+            lambda h: inner_ref[pl.ds(h, 1), at], bias, put,
+        )
+        staged(heads, stages, GRAD_LAGS)
         return carry
 
     for lo, hi in ranges:
@@ -308,16 +360,21 @@
             inner_s[pl.ds(h, 1), at] = jnp.sum(
                 dot_s[rows, at].astype(f32) * ot_ref[rows, at], axis=0, keepdims=True
             )
-        for h in range(heads):
-            c, rows = pair_cols(h), pl.ds(h * HEAD, HEAD)
-            gv, gk, gq = tile_grads(
-                h, pk_ref[:, c], pv_ref[:, c], pkt_ref[rows, :], None, head_rows(qt_ref, h, at),
-                head_rows(dot_s, h, at), head_cols(q_ref, h, at), head_cols(do_s, h, at),
-                lse_ref[pl.ds(h, 1), at], inner_s[pl.ds(h, 1), at],
-            )
+
+        def put(h, gv, gk, gq):
+            c = pair_cols(h)
             pre_ref[pl.ds(0, pre), c] += gk
             pre_ref[pl.ds(pre, pre), c] += gv
-            dqt[rows, at] = gq
+            dqt[pl.ds(h * HEAD, HEAD), at] = gq
+
+        stages = grad_stages(
+            lambda h: head_cols(q_ref, h, at), lambda h: head_rows(qt_ref, h, at),
+            lambda h: pk_ref[:, pair_cols(h)], lambda h: pv_ref[:, pair_cols(h)],
+            lambda h: pkt_ref[pl.ds(h * HEAD, HEAD), :], lambda h: head_cols(do_s, h, at),
+            lambda h: head_rows(dot_s, h, at), lambda h: lse_ref[pl.ds(h, 1), at],
+            lambda h: inner_s[pl.ds(h, 1), at], None, put,
+        )
+        staged(heads, stages, GRAD_LAGS)
         lo, hi = info[1 + 2 * t], info[2 + 2 * t]
         side = 2 * tokens // TILE
         refs = (q_ref, qt_ref, k_ref, kt_ref, v_ref, do_s, dot_s, lse_ref, inner_s, bias)
@@ -365,6 +422,7 @@
         ],
         compiler_params=pltpu.CompilerParams(vmem_limit_bytes=52 << 20),
         name="remote_grads",
+        cost_estimate=cost(14),
     )(info, first, last, q, qt, k, kt, v, pk, pkt, pv, keep, recv, ot, lse, w)
 
 
@@ -426,6 +484,7 @@
         ],
         compiler_params=pltpu.CompilerParams(vmem_limit_bytes=52 << 20),
         name="local_grads",
+        cost_estimate=cost(14),
     )(info, first, last, q, qt, k, kt, v, do, dot_, lse, inner, dqt, gh, w)
 
 
@@ -440,13 +499,13 @@
 
 def out_pairs(parts, info, width, dst):
     return placed(parts[:2], info, 1, 1, dst) + placed(
-        parts[2:], info, 3, 1, dst, pl.ds(3 * width, width)
-    )
-
-
-def up_kernel(info, own_att, got_att, tok, bo, ga, sa, bu, *rest, count):
-    wo, wu = rest[:count], rest[count : 2 * count]
-    nrm_ref, hat_ref, inv_ref, act_ref, slope_ref, wo_s, wu_s, sem_o, sem_u = rest[2 * count :]
+        parts[2:], info, 11, 1, dst, pl.ds(3 * width, width)
+    )
+
+
+def up_kernel(info, own_att, got_att, tok, bo, ga, sa, bu, *rest, n_o, count):
+    wo, wu = rest[:n_o], rest[n_o : n_o + count]
+    nrm_ref, hat_ref, inv_ref, act_ref, slope_ref, wo_s, wu_s, sem_o, sem_u = rest[n_o + count :]
     width, ff = wu_s.shape
     half = own_att.shape[1]
     got_o = start_all(out_pairs(wo, info, width, wo_s), sem_o)
@@ -480,9 +539,9 @@
 
 def up(info, own_att, got_att, tok, bo, ga, sa, bu, wo, wu):
     tokens, width = tok.shape
-    ff, count = bu.shape[1], len(wo)
+    ff, count = bu.shape[1], len(wu)
     return pl.pallas_call(
-        functools.partial(up_kernel, count=count),
+        functools.partial(up_kernel, n_o=len(wo), count=count),
         out_shape=(
             shape_of((tokens, width), f32),
             shape_of((tokens, width), f32),
@@ -490,7 +549,7 @@
             shape_of((tokens, ff), bf16),
             shape_of((tokens, ff), bf16),
         ),
-        in_specs=[SM] + [VM] * 7 + [HB] * (2 * count),
+        in_specs=[SM] + [VM] * 7 + [HB] * (len(wo) + count),
         out_specs=(VM,) * 5,
         scratch_shapes=[
             pltpu.VMEM((width, width), bf16),
@@ -500,20 +559,26 @@
         ],
         compiler_params=pltpu.CompilerParams(vmem_limit_bytes=50 << 20),
         name="up",
+        cost_estimate=cost(10),
     )(info, own_att, got_att, tok, bo, ga, sa, bu, *wo, *wu)
 
 
-def down_kernel(info, nrm_ref, hat_ref, inv_ref, act_ref, slope_ref, cot, bd, gf, sf, ga, *rest, count):
-    wo, wu, wd = rest[:count], rest[count : 2 * count], rest[2 * count : 3 * count]
-    out_ref, gh_ref, keep_ref, send_ref, wo_s, wu_s, wd_s, sem_o, sem_u, sem_d = rest[3 * count :]
+def down_kernel(info, nrm_ref, hat_ref, inv_ref, act_ref, slope_ref, cot, bd, gf, sf, ga, *rest, n_o, count):
+    wo, wu, wd = rest[:n_o], rest[n_o : n_o + count], rest[n_o + count : n_o + 2 * count]
+    out_ref, gh_ref, keep_ref, send_ref, wo_s, wu_s, wd_s, sem_o, sem_u, sem_d = rest[n_o + 2 * count :]
     width, ff = wu_s.shape
     half = keep_ref.shape[1]
     got_d = start_all(placed(wd, info, 1, ff // width, wd_s), sem_d)
     got_u = start_all(placed(wu, info, 1, 1, wu_s), sem_u)
     got_o = start_all(out_pairs(wo, info, width, wo_s), sem_o)
     core = info[0]
-    wait_all(got_d)
-    summed = nrm_ref[...] + dot(act_ref[...], wd_s[...]) + bd[...].astype(f32)
+    summed = nrm_ref[...] + bd[...].astype(f32)
+    for i, one in enumerate(got_d):
+        one.wait()
+        size = wd[i].shape[0]
+        at = row_at(info[1 + i] * (ff // width), size)
+        cols = pl.ds(pl.multiple_of(info[1 + i] * (ff // width), 128), size)
+        summed = summed + dot(act_ref[:, cols], wd_s[at, :])
     n, inv = normalised(summed)
     gain = gf[...].astype(f32)
     out_ref[...] = (n * gain + sf[...].astype(f32)).astype(bf16)
@@ -535,16 +600,16 @@
 
 def down(info, nrm, hat, inv, act, slope, cot, bd, gf, sf, ga, wo, wu, wd):
     tokens, width = nrm.shape
-    ff, count = act.shape[1], len(wo)
+    ff, count = act.shape[1], len(wu)
     return pl.pallas_call(
-        functools.partial(down_kernel, count=count),
+        functools.partial(down_kernel, n_o=len(wo), count=count),
         out_shape=(
             shape_of((tokens, width), bf16),
             shape_of((tokens, width), f32),
             shape_of((tokens, width // 2), bf16),
             shape_of((tokens, width // 2), bf16),
         ),
-        in_specs=[SM] + [VM] * 10 + [HB] * (3 * count),
+        in_specs=[SM] + [VM] * 10 + [HB] * (len(wo) + 2 * count),
         out_specs=(VM,) * 4,
         scratch_shapes=[
             pltpu.VMEM((width, width), bf16),
@@ -556,6 +621,7 @@
         ],
         compiler_params=pltpu.CompilerParams(vmem_limit_bytes=58 << 20),
         name="down",
+        cost_estimate=cost(16),
     )(info, nrm, hat, inv, act, slope, cot, bd, gf, sf, ga, *wo, *wu, *wd)
 
 
@@ -577,6 +643,10 @@
     def by_seq(a, bit):
         return lax.ppermute(a, "seq", [(i, i ^ bit) for i in range(n_seq)])
 
+    def by_both(a, row_bit, bit):
+        route = [(i * n_seq + j, (i ^ row_bit) * n_seq + (j ^ bit)) for i in range(n_row) for j in range(n_seq)]
+        return lax.ppermute(a, ("row", "seq"), route)
+
     def swapped(a, shift):
         route = []
         for i in range(n_row):
@@ -586,36 +656,39 @@
                     route.append((i * n_seq + j, ((i & ~1) | (j & 1)) * n_seq + to + (i & 1)))
         return lax.ppermute(a, ("row", "seq"), route)
 
-    own = swapped(tokens[0], 0)
-    below = lax.ppermute(own, "seq", [(j, j + 2) for j in range(n_seq - 2)])
-    above = lax.ppermute(own, "seq", [(j + 2, j) for j in range(n_seq - 2)])
+    def after(a, *others):
+        return lax.optimization_barrier((a,) + others)[0]
+
+    h = x ^ zbit
+    first_q, second_q = 2 * h + x, 2 * h + 1 - x
+    which = jnp.stack([first_q, second_q]).astype(jnp.int32)
+    attn = (w_query, w_key, w_value, w_out)
+    short, ff = w_query.shape[0] // 4, w_up.shape[1]
+    (a_half,) = pack(h[None].astype(jnp.int32), attn, [(2 * short, 4 * width)], [(i, 0, 0, i * width) for i in range(4)])
+    plan = [(0, 0, 0, 0), (1, 0, 1, 0), (0, 1, 2, 0), (1, 1, 3, 0)]
+    shapes = [(short, ff), (w_down.shape[0] // 4, width)] * 2
+    a_half = by_y(a_half)
+    own, below, above = (swapped(tokens[0], k) for k in (0, 1, -1))
+    a_own = [by_core(a) for a in attn]
+    mates = a_own
+    u_one, d_one, u_two, d_two = pack(after(which, below), (w_up, w_down), shapes, plan)
+    a_part = lax.dynamic_slice_in_dim(a_half, x * short, short, 0)
+    a_x, a_z = by_seq(a_part, 1), by_seq(a_part, 2)
+    u_one = by_y(after(u_one, a_half))
+    d_one = by_y(after(d_one, a_x))
+    u_two = by_y(after(u_two, a_z))
     toks = [below, own, above]
     toks = toks + [by_core(a) for a in toks]
-    cot = swapped(cotangent[0], 0)
-
-    h = x ^ zbit
-    first_q, second_q = 2 * h + x, 2 * h + 1 - x
-
-    def quarter(shards, which):
-        rows = shards[0].shape[0] // 4
-        cut = [lax.dynamic_slice_in_dim(a, which * rows, rows, 0) for a in shards]
-        return cut[0] if len(cut) == 1 else jnp.concatenate(cut, 1)
-
-    groups = ((w_query, w_key, w_value, w_out), (w_up,), (w_down,))
-    gathered = []
-    for shards in groups:
-        one = by_y(quarter(shards, first_q))
-        two = by_y(quarter(shards, second_q))
-        got = [one, two, by_seq(one, 1), by_seq(one, 2)]
-        gathered.append(got + [by_core(a) for a in got])
-    mates = [by_core(a) for a in (w_query, w_key, w_value, w_out, w_up, w_down)]
+    a_got = [a_half, a_x, a_z]
+    a_got = a_got + [by_core(a_half), by_core(a_x), by_core(a_z)]
+    u_own = by_core(after(w_up, a_z))
     m = w_query.shape[0]
-    offsets = [r * m, (r ^ 1) * m]
-    for base in ((r ^ 2) * m, (r ^ 3) * m):
-        for which in (first_q, second_q, 2 * (1 - h) + 1 - x, 2 * (1 - h) + x):
-            offsets.append(base + which * (m // 4))
-
-    theirs = by_core(pair_lengths)
+    far = [2 * (1 - h) + 1 - x, 2 * (1 - h) + x]
+    places = [r * m, (r ^ 1) * m]
+    halves = [(r ^ k) * m + j * (m // 4) for k in (2, 3) for j in [2 * h] + far]
+    quarters = [(r ^ k) * m + j * (m // 4) for k in (2, 3) for j in [first_q, second_q] + far]
+
+    theirs = by_core(after(pair_lengths, a_half))
     lengths = jnp.where(x == core, pair_lengths, theirs)[0]
     pairs = lengths.shape[0]
     later = jnp.arange(pairs)[:, None] >= jnp.arange(pairs)[None, :]
@@ -628,24 +701,34 @@
     last = jnp.min(jnp.where(passed, n_seq * tok_count, ends[:, None]), axis=0) - origin
     bounds = jnp.stack([first[::TILE] // TILE, (last[TILE - 1 :: TILE] + TILE - 1) // TILE], 1)
     tile_info = jnp.concatenate([core[None], bounds.reshape(-1)]).astype(jnp.int32)
-    info = jnp.stack([core] + offsets).astype(jnp.int32)
+    info_a = jnp.stack([core] + places + halves).astype(jnp.int32)
+    info = jnp.stack([core] + places + quarters + halves).astype(jnp.int32)
     first, last = first[None], last[None]
 
     def row(a):
         return a.reshape(1, -1)
 
-    q, qt, k, kt, v, vt, pk, pkt, pv, pvt, w_half = project(
-        info, row(b_query), row(b_value), prefix_key, prefix_value, toks,
-        (w_query, w_key, w_value), mates[:3], gathered[0],
-    )
-    att_keep, att_send, ot, lse = attend(tile_info, first, last, qt, k, vt, pk, pvt)
-    parts_o = [w_out, mates[3]] + gathered[0]
-    parts_u = [w_up, mates[4]] + gathered[1]
-    parts_d = [w_down, mates[5]] + gathered[2]
+    (att_keep, att_send, ot, lse, pk, pkt, pv, q, qt, k, kt, v, w_half, _) = front(
+        info_a, tile_info, first, last, row(b_query), row(b_value), prefix_key, prefix_value, toks,
+        (w_query, w_key, w_value), mates[:3], a_got,
+    )
+    u_x, u_z = by_seq(u_one, 1), by_seq(u_one, 2)
+    d_own = by_core(after(w_down, lse))
+    cot = swapped(after(cotangent[0], lse), 0)
+    d_two = by_y(after(d_two, lse))
+    d_one, lse = lax.optimization_barrier((d_one, lse))
+    d_x, d_z = by_seq(d_one, 1), by_seq(d_one, 2)
+    u_got = [u_one, u_two, u_x, u_z]
+    u_got = u_got + [by_core(after(a, lse)) for a in u_got]
+    parts_o = [w_out, mates[3]] + a_got
+    parts_u = [w_up, u_own] + u_got
     nrm, hat, inv, act, slope = up(
         info, att_keep, by_core(att_send), own, row(b_out), row(gain_attn), row(shift_attn), row(b_up),
         parts_o, parts_u,
     )
+    d_got = [d_one, d_two, d_x, d_z]
+    d_got = d_got + [by_core(a if a is d_one else after(a, inv, cot)) for a in d_got]
+    parts_d = [w_down, d_own] + d_got
     result, gh, ga_keep, ga_send = down(
         info, nrm, hat, inv, act, slope, cot, row(b_down), row(gain_ffn), row(shift_ffn), row(gain_attn),
         parts_o, parts_u, parts_d,
@@ -654,29 +737,38 @@
     give, keep_lo, keep_hi, pre, dqt, do, dot_, inner = remote_grads(
         tile_info, first, last, q, qt, k, kt, v, pk, pkt, pv, ga_keep, by_core(ga_send), ot, lse, w_half
     )
-    got = by_core(give)
-    low_part = swapped((keep_lo + got[:tok_count].astype(f32)).astype(bf16), -1)
-    high_part = swapped((keep_hi + got[tok_count:].astype(f32)).astype(bf16), 1)
-
-    def added(a, exchange):
+    got = by_core(after(give, out_tokens))
+    low_part = (keep_lo + got[:tok_count].astype(f32)).astype(bf16)
+    high_part = (keep_hi + got[tok_count:].astype(f32)).astype(bf16)
+    tile_info = after(tile_info, low_part, high_part)
+    pre = after(pre, low_part)
+    low_part = lax.ppermute(low_part, "seq", [(j + 2, j) for j in range(n_seq - 2)])
+    high_part = lax.ppermute(high_part, "seq", [(j, j + 2) for j in range(n_seq - 2)])
+
+    def summed(a, one, two):
         low = a.astype(bf16)
-        return low.astype(f32) + exchange(low).astype(f32)
-
-    pre = added(pre, by_y)
-    bit = 1
-    while bit < n_seq:
-        pre = added(pre, functools.partial(by_seq, bit=bit))
-        bit *= 2
+        sides = [by_both(low, *one), by_both(low, *two), by_both(low, one[0] | two[0], one[1] | two[1])]
+        low, p, q, r = (v.astype(f32) for v in [low] + sides)
+        return (low + p) + (q + r)
+
+    bits = [(2, 0)] + [(0, 1 << i) for i in range(n_seq.bit_length() - 1)]
+    if len(bits) % 2:
+        low = pre.astype(bf16)
+        pre = low.astype(f32) + by_both(low, *bits[0]).astype(f32)
+        bits = bits[1:]
+    pre = summed(pre, bits[0], bits[1])
+    keep, give = local_grads(
+        tile_info, first, last, q, qt, k, kt, v, do, dot_, lse, inner, dqt, gh, w_half
+    )
+    pre, give, low_part, high_part = lax.optimization_barrier((pre, give, low_part, high_part))
+    mine = (keep + low_part.astype(f32)) + (by_core(give).astype(f32) + high_part.astype(f32))
+    grad_tokens = swapped(mine.astype(bf16), 0)
+    for i in range(2, len(bits), 2):
+        pre = summed(pre, bits[i], bits[i + 1])
     other = by_core(pre)
     pre = jnp.concatenate(
         [jnp.where(core == 0, pre, other), jnp.where(core == 0, other, pre)], axis=1
     )
-
-    keep, give = local_grads(
-        tile_info, first, last, q, qt, k, kt, v, do, dot_, lse, inner, dqt, gh, w_half
-    )
-    mine = swapped((keep + by_core(give).astype(f32)).astype(bf16), 0)
-    grad_tokens = (mine.astype(f32) + low_part.astype(f32) + high_part.astype(f32)).astype(bf16)
     n_pre = prefix_key.shape[0]
     return out_tokens[None], grad_tokens[None], pre[:n_pre], pre[n_pre:]
 

time: 284 us -> 200 us (0.70)
  waiting for transfers between devices: 88.9 us -> 44.2 us
  starting transfers between devices: 78.5 us -> 57.4 us
  Pallas kernels: 83.6 us -> 75.3 us
  local copies, waits for them, and re-layouts: 23.5 us -> 16 us
    ppermute x7 -> x5, waiting for transfers between devices: 52.5 us -> 1.64 us  [by_y(): return lax.ppermute(a, 'row', [(i, i ^ 2) for i in range(n_row)])]
    ppermute x9 -> x6, starting transfers between devices: 20.9 us -> 8.14 us  [by_seq(): return lax.ppermute(a, 'seq', [(i, i ^ bit) for i in range(n_seq)])]
    ppermute x2 -> x8, starting transfers between devices: 5.36 us -> 13.6 us  [the longest x6 6.58 us: by_both(): return lax.ppermute(a, ('row', 'seq'), route)]
    ppermute x9 -> x6, waiting for transfers between devices: 15.8 us -> 8.89 us  [by_seq(): return lax.ppermute(a, 'seq', [(i, i ^ bit) for i in range(n_seq)])]
    ppermute x27 -> x26, starting transfers between devices: 20 us -> 13.7 us  [by_core(): return lax.ppermute(a, 'row', [(i, i ^ 1) for i in range(n_row)])]
    dynamic_slice x6 -> x1, local copies, waits for them, and re-layouts: 7.69 us -> 1.86 us  [per_device(): a_part = lax.dynamic_slice_in_dim(a_half, x * short, short, 0)]
    ppermute x6, waiting for transfers between devices: 9.93 us -> 15.6 us  [swapped(): return lax.ppermute(a, ('row', 'seq'), route)]
    ppermute x6, starting transfers between devices: 21.4 us -> 16.1 us  [swapped(): return lax.ppermute(a, ('row', 'seq'), route)]
  transfers between devices with their start and end apart: 51 -> 51, of which waited for: 16 -> 17; matrix products, arithmetic and copies ran while one was open for 4% -> 3% of each run, Pallas kernels for 19% -> 28%
where the time goes in v2:
time: 200 us; the launch traced here: 199 us
  Pallas kernels  75.3 us (38%)
  starting transfers between devices  57.4 us (29%)
  waiting for transfers between devices  44.2 us (22%)
  local copies, waits for them, and re-layouts  16 us (8%)
  other arithmetic  4.29 us (2%)
    pallas_call x1, Pallas kernels, down(): pl.pallas_call(functools.partial(down_kernel, n_o=len(wo), count=count),...  17.7 us
    pallas_call x1, Pallas kernels, front(): pl.pallas_call(functools.partial(front_kernel, count=count, half=half), o...  17.5 us
    ppermute x6, starting transfers between devices, swapped(): return lax.ppermute(a, ('row', 'seq'), route)  16.1 us
    ppermute x6, waiting for transfers between devices, swapped(): return lax.ppermute(a, ('row', 'seq'), route)  15.6 us
    ppermute x26, starting transfers between devices, by_core(): return lax.ppermute(a, 'row', [(i, i ^ 1) for i in range(n_row)])  13.7 us
    pallas_call x1, Pallas kernels, up(): pl.pallas_call(functools.partial(up_kernel, n_o=len(wo), count=count), ou...  12.3 us
    pallas_call x1, Pallas kernels, local_grads(): pl.pallas_call(functools.partial(local_grads_kernel, heads=heads), out_sh...  12.3 us
    unnamed x106, local copies, waits for them, and re-layouts  11.8 us
  transfers between devices with their start and end apart: 51, of which 17 were waited for; matrix products, arithmetic and copies ran while one was open for 3% of the time, Pallas kernels for 28%

profile of v2, /device:TPU:1, one launch (start us, length us, event | category | flops | bytes accessed | tf_op | source)
XLA Modules:
  0.0 198.7 jit_solution(2448643456370947466)
XLA Ops:
  0.7 2.3 %pack.2 = bf16[128,4096]{1,0:T(8,128)(2,1)} custom-call(s32[1]{0:T(128)} %bitcast.13.info, bf16[256,1024]{1,0:T(8,128)(2,1)} %rest_6_.1, bf16[256,1024]{1,0:T(8,128)(2,1)} %rest_7_.1, bf16[256,1024]{1,0:T(8,128)(2,1)} %rest_8_.3, bf16[256,1024]{1,0:T(8,128)(2,1)} %rest_0_.7), custom_call_target="tpu_custom_call" | custom-call | flops 2000000000 | tf_op jit(solution)/shard_map/pack/pallas_call | solution.py:73
  3.0 2.1 %collective-permute-start = (bf16[128,4096]{1,0:T(8,128)(2,1)}, bf16[128,4096]{1,0:T(8,128)(2,1)}, u32[]{:S(2)}, u32[]{:S(2)}) collective-permute-start(bf16[128,4096]{1,0:T(8,128)(2,1)} %pack.2), channel_id=1, source_target_pairs={{0,16},{8,24},{16,0},{24,8},{1,17},{9,25},{17,1},{25,9},{2,18},{10... | collective-permute-start | bytes 3145736 | tf_op jit(solution)/shard_map/ppermute | solution.py:641
  5.1 5.0 %collective-permute-start.2 = (bf16[256,1024]{1,0:T(8,128)(2,1)S(1)}, bf16[256,1024]{1,0:T(8,128)(2,1)S(1)}, u32[]{:S(2)}, u32[]{:S(2)}) collective-permute-start(bf16[256,1024]{1,0:T(8,128)(2,1)S(1)} %bitcast.36), channel_id=1, source_target_pairs={{0,2},{1,10},{2,4},{3,12},{4,6},{5,14},{8,3},{9,11},{10,5},{11,13}... | collective-permute-start | bytes 1572872 | tf_op jit(solution)/shard_map/ppermute | solution.py:657
  10.1 1.3 collective-permute-start.4
  11.4 1.9 collective-permute-start.3
  14.3 7.2 %collective-permute-done.2.rest_0_ = bf16[256,1024]{1,0:T(8,128)(2,1)S(1)} collective-permute-done((bf16[256,1024]{1,0:T(8,128)(2,1)S(1)}, bf16[256,1024]{1,0:T(8,128)(2,1)S(1)}, u32[]{:S(2)}, u32[]{:S(2)}) %collective-permute-start.2) | collective-permute-done | bytes 524320 | tf_op jit(solution)/shard_map/ppermute | solution.py:657
  21.6 3.6 %pack.3 = (bf16[64,4096]{1,0:T(8,128)(2,1)}, bf16[256,1024]{1,0:T(8,128)(2,1)}, bf16[64,4096]{1,0:T(8,128)(2,1)}, bf16[256,1024]{1,0:T(8,128)(2,1)}) custom-call(s32[2]{0:T(128)} %pad_add_fusion.2.info, bf16[256,4096]{1,0:T(8,128)(2,1)} %rest_8_.5, bf16[1024,1024]{1,0:T(8,128)(2,1)} %rest_18_.1), custom_call_target="tpu_custom_call" | custom-call | flops 2000000000 | tf_op jit(solution)/shard_map/pack/pallas_call | solution.py:73
  25.2 1.0 collective-permute-start.10
  26.2 1.6 collective-permute-done.3.rest_1_.tok
  28.3 1.2 collective-permute-start.6
  29.6 1.9 constant_dynamic-slice_fusion
  31.5 2.6 %collective-permute-start.12 = (bf16[64,4096]{1,0:T(8,128)(2,1)}, bf16[64,4096]{1,0:T(8,128)(2,1)S(1)}, u32[]{:S(2)}, u32[]{:S(2)}) collective-permute-start(bf16[64,4096]{1,0:T(8,128)(2,1)} %constant_dynamic-slice_fusion), channel_id=1, source_target_pairs={{0,2},{1,3},{2,0},{3,1},{4,6},{5,7},{6,4},{7,5},{8,10},{9,11},{10,... | collective-permute-start | bytes 1572872 | tf_op jit(solution)/shard_map/ppermute | solution.py:644
  34.0 1.1 collective-permute-start.11
  35.1 0.7 collective-permute-start.13
  36.6 0.7 collective-permute-start.19
  37.4 8.9 %collective-permute-done.12.rest_14_.rest_4_ = bf16[64,4096]{1,0:T(8,128)(2,1)S(1)} collective-permute-done((bf16[64,4096]{1,0:T(8,128)(2,1)}, bf16[64,4096]{1,0:T(8,128)(2,1)S(1)}, u32[]{:S(2)}, u32[]{:S(2)}) %collective-permute-start.12) | collective-permute-done | bytes 524320 | tf_op jit(solution)/shard_map/ppermute | solution.py:644
  46.3 0.8 collective-permute-start.15
  47.1 1.5 collective-permute-start.14
  49.3 1.1 collective-permute-done.19.rest_10_
  50.4 0.7 collective-permute-start.20
  51.2 1.1 collective-permute-start.18
  53.3 1.0 copy-done.9
  54.3 17.5 %front.1 = (bf16[256,512]{1,0:T(8,128)(2,1)S(1)}, bf16[256,512]{1,0:T(8,128)(2,1)S(1)}, f32[512,512]{1,0:T(8,128)}, f32[8,512]{1,0:T(8,128)S(1)}, bf16[64,512]{1...) custom-call(s32[9]{0:T(128)S(1)} %stack.90.info, ...), custom_call_target="tpu_custom_call" | custom-call | flops 20000000000 | tf_op jit(solution)/shard_map/front/pallas_call | solution.py:272
  71.9 0.7 copy-done.13
  72.6 0.8 copy-done.15
  73.3 0.8 copy-done.17
  75.5 0.7 collective-permute-start.17
  76.7 0.9 collective-permute-done.17.rest_1_
  78.1 0.7 collective-permute-done.16.got_att
  80.3 0.9 collective-permute-done.25.rest_15_
  81.3 1.9 collective-permute-start.32
  83.6 1.6 collective-permute-start.31
  85.3 2.5 %collective-permute-start.28 = (bf16[256,1024]{1,0:T(8,128)(2,1)}, bf16[256,1024]{1,0:T(8,128)(2,1)S(1)}, u32[]{:S(2)}, u32[]{:S(2)}) collective-permute-start(bf16[256,1024]{1,0:T(8,128)(2,1)} %bitcast.39), channel_id=1, source_target_pairs={{0,0},{1,8},{2,2},{3,10},{4,4},{5,12},{6,6},{7,14},{8,1},{9,9},{10... | collective-permute-start | bytes 1572872 | tf_op jit(solution)/shard_map/ppermute | solution.py:657
  87.7 2.0 collective-permute-start.30
  89.7 1.0 copy-done.5
  90.8 1.0 copy-done.7
  91.8 0.9 copy-done.14
  92.8 12.3 %up.1 = (f32[256,1024]{1,0:T(8,128)}, f32[256,1024]{1,0:T(8,128)}, f32[256,128]{1,0:T(8,128)S(1)}, bf16[256,4096]{1,0:T(8,128)(2,1)}, bf16[256,4096]{1,0:T(8,128)(2,1)}) custom-call(s32[17]{0:T(128)S(1)} %stack.89.info, bf16[256,512]{1,0:T(8,128)(2,1)S(1)} %copy-done.14, bf16[256,512]{1,0:T(8,128)(2,1)S(1)} %collective-permute-done.16.got_att, ...), custom_call_target="tpu_custom_call" | custom-call | flops 10000000000 | tf_op jit(solution)/shard_map/up/pallas_call | solution.py:543
  109.3 0.7 collective-permute-done.36.rest_27_
  110.1 0.8 copy-done.51
  110.8 17.7 %down.1 = (bf16[256,1024]{1,0:T(8,128)(2,1)}, f32[256,1024]{1,0:T(8,128)}, bf16[256,512]{1,0:T(8,128)(2,1)}, bf16[256,512]{1,0:T(8,128)(2,1)}) custom-call(s32[17]{0:T(128)} %copy-done.1, f32[256,1024]{1,0:T(8,128)} %get-tuple-element.82.nrm_ref, f32[256,1024]{1,0:T(8,128)} %get-tuple-element.83.hat_ref, f32[256,128]{1,0:T(8,128)} %copy-done.21, ...), custom_call_target="tpu_custom_call" | custom-call | flops 16000000000 | tf_op jit(solution)/shard_map/down/pallas_call | solution.py:604
  128.7 2.7 %collective-permute-start.37 = (bf16[256,1024]{1,0:T(8,128)(2,1)}, bf16[256,1024]{1,0:T(8,128)(2,1)S(1)}, u32[]{:S(2)}, u32[]{:S(2)}) collective-permute-start(bf16[256,1024]{1,0:T(8,128)(2,1)} %get-tuple-element.95), channel_id=1, source_target_pairs={{0,0},{1,8},{2,2},{3,10},{4,4},{5,12},{6,6},{7,14},{8,1},{9,9},{10... | collective-permute-start | bytes 1572872 | tf_op jit(solution)/shard_map/ppermute | solution.py:657
  131.4 0.9 copy-done.20
  132.4 9.6 %remote_grads.1 = (bf16[512,1024]{1,0:T(8,128)(2,1)}, f32[256,1024]{1,0:T(8,128)}, f32[256,1024]{1,0:T(8,128)}, f32[128,512]{1,0:T(8,128)S(1)}, f32[512,512]{1,0...) custom-call(s32[5]{0:T(128)S(1)} %pad_add_fusion.1.tiles.info, ...), custom_call_target="tpu_custom_call" | custom-call | flops 14000000000 | tf_op jit(solution)/shard_map/remote_grads/pallas_call | solution.py:402
  142.1 2.9 %collective-permute-done.39 = bf16[512,1024]{1,0:T(8,128)(2,1)S(1)} collective-permute-done((bf16[512,1024]{1,0:T(8,128)(2,1)}, bf16[512,1024]{1,0:T(8,128)(2,1)S(1)}, u32[]{:S(2)}, u32[]{:S(2)}) %collective-permute-start.39) | collective-permute-done | bytes 1048608 | tf_op jit(solution)/shard_map/ppermute | solution.py:638
  144.9 2.0 %add_convert_fusion.1 = (bf16[256,1024]{1,0:T(8,128)(2,1)S(1)}, bf16[256,1024]{1,0:T(8,128)(2,1)S(1)}) fusion(f32[256,1024]{1,0:T(8,128)} %get-tuple-element.111, bf16[512,1024]{1,0:T(8,128)(2,1)S(1)} %collective-permute-done.39, f32[256,1024]{1,0:T(8,128)} %get-tuple-element.108), kind=kLoop, calls=%fused_computation.1 | loop fusion | flops 1572864 | bytes 4194304 | tf_op jit(solution)/shard_map/convert_element_type | solution.py:742
  147.0 0.8 collective-permute-start.41
  147.8 1.1 collective-permute-start.40
  148.8 1.1 collective-permute-start.42
  149.9 5.8 %collective-permute-start.44 = (bf16[256,1024]{1,0:T(8,128)(2,1)S(1)}, bf16[256,1024]{1,0:T(8,128)(2,1)S(1)}, u32[]{:S(2)}, u32[]{:S(2)}) collective-permute-start(bf16[256,1024]{1,0:T(8,128)(2,1)S(1)} %get-tuple-element.128), channel_id=1, source_target_pairs={{0,2},{1,3},{2,4},{3,5},{4,6},{5,7},{8,10},{9,11},{10,12},{11,13},... | collective-permute-start | bytes 1572872 | tf_op jit(solution)/shard_map/ppermute | solution.py:746
  155.7 1.3 collective-permute-start.43
  157.0 12.3 %local_grads.1 = (f32[256,1024]{1,0:T(8,128)}, bf16[256,1024]{1,0:T(8,128)(2,1)S(1)}) custom-call(s32[5]{0:T(128)S(1)} %pad_add_fusion.1.tiles.info, s32[1,512]{1,0:T(1,128)S(1)} %bitcast.33, s32[1,512]{1,0:T(1,128)S(1)} %bitcast.30, bf16[512,512]{1,0:T(8,128)(2,1)S(1)} %copy-done.16, bf16[512,512]{1,0:T(8,128)(2,1)S(1)} %copy-done.18, ...), custom_call_target="tpu_custom_call" | custom-call | flops 14000000000 | tf_op jit(solution)/shard_map/local_grads/pallas_call | solution.py:472
  169.5 1.0 collective-permute-done.43
  170.5 1.9 collective-permute-start.45
  172.4 2.4 %collective-permute-start.48 = (bf16[128,512]{1,0:T(8,128)(2,1)S(1)}, bf16[128,512]{1,0:T(8,128)(2,1)S(1)}, u32[]{:S(2)}, u32[]{:S(2)}) collective-permute-start(bf16[128,512]{1,0:T(8,128)(2,1)S(1)} %add_add_fusion.1), channel_id=1, source_target_pairs={{0,4},{1,5},{2,6},{3,7},{4,0},{5,1},{6,2},{7,3},{8,12},{9,13},{10,... | collective-permute-start | bytes 393224 | tf_op jit(solution)/shard_map/ppermute | solution.py:648
  174.8 1.2 collective-permute-start.49
  176.0 5.4 %collective-permute-done.48 = bf16[128,512]{1,0:T(8,128)(2,1)S(1)} collective-permute-done((bf16[128,512]{1,0:T(8,128)(2,1)S(1)}, bf16[128,512]{1,0:T(8,128)(2,1)S(1)}, u32[]{:S(2)}, u32[]{:S(2)}) %collective-permute-start.48) | collective-permute-done | bytes 131104 | tf_op jit(solution)/shard_map/ppermute | solution.py:648
  181.4 3.9 %collective-permute-done.49 = bf16[128,512]{1,0:T(8,128)(2,1)S(1)} collective-permute-done((bf16[128,512]{1,0:T(8,128)(2,1)S(1)}, bf16[128,512]{1,0:T(8,128)(2,1)S(1)}, u32[]{:S(2)}, u32[]{:S(2)}) %collective-permute-start.49) | collective-permute-done | bytes 131104 | tf_op jit(solution)/shard_map/ppermute | solution.py:648
  185.4 0.9 collective-permute-start.50
  186.6 2.8 %collective-permute-start.46 = (bf16[256,1024]{1,0:T(8,128)(2,1)S(1)}, bf16[256,1024]{1,0:T(8,128)(2,1)S(1)}, u32[]{:S(2)}, u32[]{:S(2)}) collective-permute-start(bf16[256,1024]{1,0:T(8,128)(2,1)S(1)} %add_convert_fusion), channel_id=1, source_target_pairs={{0,0},{1,8},{2,2},{3,10},{4,4},{5,12},{6,6},{7,14},{8,1},{9,9},{10... | collective-permute-start | bytes 1572872 | tf_op jit(solution)/shard_map/ppermute | solution.py:657
  189.5 0.8 pad_maximum_fusion
  190.3 6.8 %collective-permute-done.46 = bf16[256,1024]{1,0:T(8,128)(2,1)S(1)} collective-permute-done((bf16[256,1024]{1,0:T(8,128)(2,1)S(1)}, bf16[256,1024]{1,0:T(8,128)(2,1)S(1)}, u32[]{:S(2)}, u32[]{:S(2)}) %collective-permute-start.46) | collective-permute-done | bytes 524320 | tf_op jit(solution)/shard_map/ppermute | solution.py:657
  197.1 0.8 copy.28
  197.9 0.8 copy.29
  (184 shorter events, 13.1 us)
Async XLA Ops:
  0.7 20.8 %copy-start.38 = (bf16[256,1024]{1,0:T(8,128)(2,1)S(1)}, bf16[256,1024]{1,0:T(8,128)(2,1)}, u32[]{:S(2)}) copy-start(bf16[256,1024]{1,0:T(8,128)(2,1)} %rest_7_.1) | copy-start | bytes 1572868
  3.0 25.3 %collective-permute-start = (bf16[128,4096]{1,0:T(8,128)(2,1)}, bf16[128,4096]{1,0:T(8,128)(2,1)}, u32[]{:S(2)}, u32[]{:S(2)}) collective-permute-start(bf16[128,4096]{1,0:T(8,128)(2,1)} %pack.2), channel_id=1, source_target_pairs={{0,16},{8,24},{16,0},{24,8},{1,17},{9,25},{17,1},{25,9},{2,18},{10... | collective-permute-start | bytes 3145736 | tf_op jit(solution)/shard_map/ppermute | solution.py:641
  5.1 16.3 %collective-permute-start.2 = (bf16[256,1024]{1,0:T(8,128)(2,1)S(1)}, bf16[256,1024]{1,0:T(8,128)(2,1)S(1)}, u32[]{:S(2)}, u32[]{:S(2)}) collective-permute-start(bf16[256,1024]{1,0:T(8,128)(2,1)S(1)} %bitcast.36), channel_id=1, source_target_pairs={{0,2},{1,10},{2,4},{3,12},{4,6},{5,14},{8,3},{9,11},{10,5},{11,13}... | collective-permute-start | bytes 1572872 | tf_op jit(solution)/shard_map/ppermute | solution.py:657
  10.1 15.1 %collective-permute-start.4 = (bf16[256,1024]{1,0:T(8,128)(2,1)S(1)}, bf16[256,1024]{1,0:T(8,128)(2,1)S(1)}, u32[]{:S(2)}, u32[]{:S(2)}) collective-permute-start(bf16[256,1024]{1,0:T(8,128)(2,1)S(1)} %bitcast.37), channel_id=1, source_target_pairs={{2,0},{3,8},{4,2},{5,10},{6,4},{7,12},{10,1},{11,9},{12,3},{13,11}... | collective-permute-start | bytes 1572872 | tf_op jit(solution)/shard_map/ppermute | solution.py:657
  11.4 16.3 %collective-permute-start.3 = (bf16[256,1024]{1,0:T(8,128)(2,1)S(1)}, bf16[256,1024]{1,0:T(8,128)(2,1)S(1)}, u32[]{:S(2)}, u32[]{:S(2)}) collective-permute-start(bf16[256,1024]{1,0:T(8,128)(2,1)S(1)} %bitcast.38), channel_id=1, source_target_pairs={{0,0},{1,8},{2,2},{3,10},{4,4},{5,12},{6,6},{7,14},{8,1},{9,9},{10... | collective-permute-start | bytes 1572872 | tf_op jit(solution)/shard_map/ppermute | solution.py:657
  13.4 18.1 %collective-permute-start.8 = (bf16[256,1024]{1,0:T(8,128)(2,1)S(1)}, bf16[256,1024]{1,0:T(8,128)(2,1)}, u32[]{:S(2)}, u32[]{:S(2)}) collective-permute-start(bf16[256,1024]{1,0:T(8,128)(2,1)S(1)} %copy-done.2), channel_id=1, source_target_pairs={{0,8},{8,0},{16,24},{24,16},{1,9},{9,1},{17,25},{25,17},{2,10},{10... | collective-permute-start | bytes 1572872 | tf_op jit(solution)/shard_map/ppermute | solution.py:638
  14.2 39.0 %copy-start.11 = (bf16[64,1024]{1,0:T(8,128)(2,1)S(1)}, bf16[64,1024]{1,0:T(8,128)(2,1)}, u32[]{:S(2)}) copy-start(bf16[64,1024]{1,0:T(8,128)(2,1)} %pk.1) | copy-start | bytes 393220
  14.3 39.0 %copy-start.12 = (bf16[64,1024]{1,0:T(8,128)(2,1)S(1)}, bf16[64,1024]{1,0:T(8,128)(2,1)}, u32[]{:S(2)}) copy-start(bf16[64,1024]{1,0:T(8,128)(2,1)} %pv.1) | copy-start | bytes 393220
  21.5 10.0 %collective-permute-start.9 = (bf16[256,1024]{1,0:T(8,128)(2,1)S(1)}, bf16[256,1024]{1,0:T(8,128)(2,1)}, u32[]{:S(2)}, u32[]{:S(2)}) collective-permute-start(bf16[256,1024]{1,0:T(8,128)(2,1)S(1)} %copy-done.38), channel_id=1, source_target_pairs={{0,8},{8,0},{16,24},{24,16},{1,9},{9,1},{17,25},{25,17},{2,10},{10... | collective-permute-start | bytes 1572872 | tf_op jit(solution)/shard_map/ppermute | solution.py:638
  25.2 28.0 %copy-start.8 = (bf16[256,1024]{1,0:T(8,128)(2,1)}, bf16[256,1024]{1,0:T(8,128)(2,1)S(1)}, u32[]{:S(2)}) copy-start(bf16[256,1024]{1,0:T(8,128)(2,1)S(1)} %collective-permute-done.4.rest_2_) | copy-start | bytes 1572868
  25.2 9.9 %collective-permute-start.10 = (bf16[256,1024]{1,0:T(8,128)(2,1)}, bf16[256,1024]{1,0:T(8,128)(2,1)S(1)}, u32[]{:S(2)}, u32[]{:S(2)}) collective-permute-start(bf16[256,1024]{1,0:T(8,128)(2,1)} %rest_8_.3), channel_id=1, source_target_pairs={{0,8},{8,0},{16,24},{24,16},{1,9},{9,1},{17,25},{25,17},{2,10},{10... | collective-permute-start | bytes 1572872 | tf_op jit(solution)/shard_map/ppermute | solution.py:638
  27.8 8.4 %collective-permute-start.7 = (bf16[256,1024]{1,0:T(8,128)(2,1)S(1)}, bf16[256,1024]{1,0:T(8,128)(2,1)}, u32[]{:S(2)}, u32[]{:S(2)}) collective-permute-start(bf16[256,1024]{1,0:T(8,128)(2,1)S(1)} %collective-permute-done.4.rest_2_), channel_id=1, source_target_pairs={{0,8},{8,0},{16,24},{24,16},{1,9},{9,1},{17,25},{25,17},{2,10},{10... | collective-permute-start | bytes 1572872 | tf_op jit(solution)/shard_map/ppermute | solution.py:638
  28.3 8.3 %collective-permute-start.6 = (bf16[256,1024]{1,0:T(8,128)(2,1)S(1)}, bf16[256,1024]{1,0:T(8,128)(2,1)}, u32[]{:S(2)}, u32[]{:S(2)}) collective-permute-start(bf16[256,1024]{1,0:T(8,128)(2,1)S(1)} %collective-permute-done.3.rest_1_.tok), channel_id=1, source_target_pairs={{0,8},{8,0},{16,24},{24,16},{1,9},{9,1},{17,25},{25,17},{2,10},{10... | collective-permute-start | bytes 1572872 | tf_op jit(solution)/shard_map/ppermute | solution.py:638
  31.4 2.6 %collective-permute-start.1 = (s32[1,8]{1,0:T(1,128)S(1)}, s32[1,8]{1,0:T(1,128)S(1)}, u32[]{:S(2)}, u32[]{:S(2)}) collective-permute-start(s32[1,8]{1,0:T(1,128)S(1)} %copy-done.36), channel_id=1, source_target_pairs={{0,8},{8,0},{16,24},{24,16},{1,9},{9,1},{17,25},{25,17},{2,10},{10... | collective-permute-start | bytes 104 | tf_op jit(solution)/shard_map/ppermute | solution.py:638
  31.5 14.8 %collective-permute-start.12 = (bf16[64,4096]{1,0:T(8,128)(2,1)}, bf16[64,4096]{1,0:T(8,128)(2,1)S(1)}, u32[]{:S(2)}, u32[]{:S(2)}) collective-permute-start(bf16[64,4096]{1,0:T(8,128)(2,1)} %constant_dynamic-slice_fusion), channel_id=1, source_target_pairs={{0,2},{1,3},{2,0},{3,1},{4,6},{5,7},{6,4},{7,5},{8,10},{9,11},{10,... | collective-permute-start | bytes 1572872 | tf_op jit(solution)/shard_map/ppermute | solution.py:644
  34.0 13.1 %collective-permute-start.11 = (bf16[64,4096]{1,0:T(8,128)(2,1)}, bf16[64,4096]{1,0:T(8,128)(2,1)S(1)}, u32[]{:S(2)}, u32[]{:S(2)}) collective-permute-start(bf16[64,4096]{1,0:T(8,128)(2,1)} %constant_dynamic-slice_fusion), channel_id=1, source_target_pairs={{0,1},{1,0},{2,3},{3,2},{4,5},{5,4},{6,7},{7,6},{8,9},{9,8},{10,11... | collective-permute-start | bytes 1572872 | tf_op jit(solution)/shard_map/ppermute | solution.py:644
  35.1 17.7 %collective-permute-start.13 = (bf16[128,4096]{1,0:T(8,128)(2,1)}, bf16[128,4096]{1,0:T(8,128)(2,1)}, u32[]{:S(2)}, u32[]{:S(2)}) collective-permute-start(bf16[128,4096]{1,0:T(8,128)(2,1)} %collective-permute-done.rest_12_.rest_2_), channel_id=1, source_target_pairs={{0,8},{8,0},{16,24},{24,16},{1,9},{9,1},{17,25},{25,17},{2,10},{10... | collective-permute-start | bytes 3145736 | tf_op jit(solution)/shard_map/ppermute | solution.py:638
  36.1 12.8 %collective-permute-start.5 = (bf16[256,1024]{1,0:T(8,128)(2,1)S(1)}, bf16[256,1024]{1,0:T(8,128)(2,1)}, u32[]{:S(2)}, u32[]{:S(2)}) collective-permute-start(bf16[256,1024]{1,0:T(8,128)(2,1)S(1)} %collective-permute-done.2.rest_0_), channel_id=1, source_target_pairs={{0,8},{8,0},{16,24},{24,16},{1,9},{9,1},{17,25},{25,17},{2,10},{10... | collective-permute-start | bytes 1572872 | tf_op jit(solution)/shard_map/ppermute | solution.py:638
  36.6 13.8 %collective-permute-start.19 = (bf16[64,4096]{1,0:T(8,128)(2,1)}, bf16[64,4096]{1,0:T(8,128)(2,1)}, u32[]{:S(2)}, u32[]{:S(2)}) collective-permute-start(bf16[64,4096]{1,0:T(8,128)(2,1)} %get-tuple-element.71), channel_id=1, source_target_pairs={{0,16},{8,24},{16,0},{24,8},{1,17},{9,25},{17,1},{25,9},{2,18},{10... | collective-permute-start | bytes 1572872 | tf_op jit(solution)/shard_map/ppermute | solution.py:641
  46.3 4.9 %collective-permute-start.15 = (bf16[64,4096]{1,0:T(8,128)(2,1)S(1)}, bf16[64,4096]{1,0:T(8,128)(2,1)}, u32[]{:S(2)}, u32[]{:S(2)}) collective-permute-start(bf16[64,4096]{1,0:T(8,128)(2,1)S(1)} %collective-permute-done.12.rest_14_.rest_4_), channel_id=1, source_target_pairs={{0,8},{8,0},{16,24},{24,16},{1,9},{9,1},{17,25},{25,17},{2,10},{10... | collective-permute-start | bytes 1572872 | tf_op jit(solution)/shard_map/ppermute | solution.py:638
  47.1 5.2 %collective-permute-start.14 = (bf16[64,4096]{1,0:T(8,128)(2,1)S(1)}, bf16[64,4096]{1,0:T(8,128)(2,1)}, u32[]{:S(2)}, u32[]{:S(2)}) collective-permute-start(bf16[64,4096]{1,0:T(8,128)(2,1)S(1)} %collective-permute-done.11.rest_13_.rest_3_), channel_id=1, source_target_pairs={{0,8},{8,0},{16,24},{24,16},{1,9},{9,1},{17,25},{25,17},{2,10},{10... | collective-permute-start | bytes 1572872 | tf_op jit(solution)/shard_map/ppermute | solution.py:638
  49.0 26.5 %collective-permute-start.23 = (bf16[256,1024]{1,0:T(8,128)(2,1)}, bf16[256,1024]{1,0:T(8,128)(2,1)S(1)}, u32[]{:S(2)}, u32[]{:S(2)}) collective-permute-start(bf16[256,1024]{1,0:T(8,128)(2,1)} %get-tuple-element.75), channel_id=1, source_target_pairs={{0,16},{8,24},{16,0},{24,8},{1,17},{9,25},{17,1},{25,9},{2,18},{10... | collective-permute-start | bytes 1572872 | tf_op jit(solution)/shard_map/ppermute | solution.py:641
  50.4 25.7 %collective-permute-start.20 = (bf16[64,4096]{1,0:T(8,128)(2,1)}, bf16[64,4096]{1,0:T(8,128)(2,1)}, u32[]{:S(2)}, u32[]{:S(2)}) collective-permute-start(bf16[64,4096]{1,0:T(8,128)(2,1)} %get-tuple-element.73), channel_id=1, source_target_pairs={{0,16},{8,24},{16,0},{24,8},{1,17},{9,25},{17,1},{25,9},{2,18},{10... | collective-permute-start | bytes 1572872 | tf_op jit(solution)/shard_map/ppermute | solution.py:641
  51.2 36.6 %collective-permute-start.18 = (bf16[256,4096]{1,0:T(8,128)(2,1)}, bf16[256,4096]{1,0:T(8,128)(2,1)}, u32[]{:S(2)}, u32[]{:S(2)}) collective-permute-start(bf16[256,4096]{1,0:T(8,128)(2,1)} %rest_8_.5), channel_id=1, source_target_pairs={{0,8},{8,0},{16,24},{24,16},{1,9},{9,1},{17,25},{25,17},{2,10},{10... | collective-permute-start | bytes 6291464 | tf_op jit(solution)/shard_map/ppermute | solution.py:638
  52.3 23.9 %collective-permute-start.22 = (bf16[64,4096]{1,0:T(8,128)(2,1)}, bf16[64,4096]{1,0:T(8,128)(2,1)}, u32[]{:S(2)}, u32[]{:S(2)}) collective-permute-start(bf16[64,4096]{1,0:T(8,128)(2,1)} %collective-permute-done.19.rest_10_), channel_id=1, source_target_pairs={{0,2},{1,3},{2,0},{3,1},{4,6},{5,7},{6,4},{7,5},{8,10},{9,11},{10,... | collective-permute-start | bytes 1572872 | tf_op jit(solution)/shard_map/ppermute | solution.py:644
  52.9 23.8 %collective-permute-start.21 = (bf16[64,4096]{1,0:T(8,128)(2,1)}, bf16[64,4096]{1,0:T(8,128)(2,1)}, u32[]{:S(2)}, u32[]{:S(2)}) collective-permute-start(bf16[64,4096]{1,0:T(8,128)(2,1)} %collective-permute-done.19.rest_10_), channel_id=1, source_target_pairs={{0,1},{1,0},{2,3},{3,2},{4,5},{5,4},{6,7},{7,6},{8,9},{9,8},{10,11... | collective-permute-start | bytes 1572872 | tf_op jit(solution)/shard_map/ppermute | solution.py:644
  54.3 21.1 %copy-start.3 = (bf16[256,1024]{1,0:T(8,128)(2,1)S(1)}, bf16[256,1024]{1,0:T(8,128)(2,1)}, u32[]{:S(2)}) copy-start(bf16[256,1024]{1,0:T(8,128)(2,1)} %rest_0_.7) | copy-start | bytes 1572868
  54.3 25.8 %copy-start.30 = (bf16[1024]{0:T(1024)(128)(2,1)S(1)}, bf16[1024]{0:T(1024)(128)(2,1)}, u32[]{:S(2)}) copy-start(bf16[1024]{0:T(1024)(128)(2,1)} %param.32) | copy-start | bytes 6148
  54.3 25.8 %copy-start.31 = (bf16[1024]{0:T(1024)(128)(2,1)S(1)}, bf16[1024]{0:T(1024)(128)(2,1)}, u32[]{:S(2)}) copy-start(bf16[1024]{0:T(1024)(128)(2,1)} %param.31) | copy-start | bytes 6148
  54.3 25.9 %copy-start.32 = (bf16[1024]{0:T(1024)(128)(2,1)S(1)}, bf16[1024]{0:T(1024)(128)(2,1)}, u32[]{:S(2)}) copy-start(bf16[1024]{0:T(1024)(128)(2,1)} %param.33) | copy-start | bytes 6148
  54.3 25.9 %copy-start.27 = (bf16[4096]{0:T(1024)(128)(2,1)S(1)}, bf16[4096]{0:T(1024)(128)(2,1)}, u32[]{:S(2)}) copy-start(bf16[4096]{0:T(1024)(128)(2,1)} %param.35) | copy-start | bytes 24580
  75.5 2.2 %collective-permute-start.17 = (bf16[256,1024]{1,0:T(8,128)(2,1)S(1)}, bf16[256,1024]{1,0:T(8,128)(2,1)S(1)}, u32[]{:S(2)}, u32[]{:S(2)}) collective-permute-start(bf16[256,1024]{1,0:T(8,128)(2,1)S(1)} %copy-done.3), channel_id=1, source_target_pairs={{0,8},{8,0},{16,24},{24,16},{1,9},{9,1},{17,25},{25,17},{2,10},{10... | collective-permute-start | bytes 1572872 | tf_op jit(solution)/shard_map/ppermute | solution.py:638
  76.1 3.6 %collective-permute-start.24 = (bf16[64,4096]{1,0:T(8,128)(2,1)}, bf16[64,4096]{1,0:T(8,128)(2,1)S(1)}, u32[]{:S(2)}, u32[]{:S(2)}) collective-permute-start(bf16[64,4096]{1,0:T(8,128)(2,1)} %collective-permute-done.19.rest_10_), channel_id=1, source_target_pairs={{0,8},{8,0},{16,24},{24,16},{1,9},{9,1},{17,25},{25,17},{2,10},{10... | collective-permute-start | bytes 1572872 | tf_op jit(solution)/shard_map/ppermute | solution.py:638
  76.2 2.6 %collective-permute-start.16 = (bf16[256,512]{1,0:T(8,128)(2,1)S(1)}, bf16[256,512]{1,0:T(8,128)(2,1)S(1)}, u32[]{:S(2)}, u32[]{:S(2)}) collective-permute-start(bf16[256,512]{1,0:T(8,128)(2,1)S(1)} %get-tuple-element.67), channel_id=1, source_target_pairs={{0,8},{8,0},{16,24},{24,16},{1,9},{9,1},{17,25},{25,17},{2,10},{10... | collective-permute-start | bytes 786440 | tf_op jit(solution)/shard_map/ppermute | solution.py:638
  76.7 32.1 %collective-permute-start.29 = (bf16[1024,1024]{1,0:T(8,128)(2,1)}, bf16[1024,1024]{1,0:T(8,128)(2,1)}, u32[]{:S(2)}, u32[]{:S(2)}) collective-permute-start(bf16[1024,1024]{1,0:T(8,128)(2,1)} %rest_18_.1), channel_id=1, source_target_pairs={{0,8},{8,0},{16,24},{24,16},{1,9},{9,1},{17,25},{25,17},{2,10},{10... | collective-permute-start | bytes 6291464 | tf_op jit(solution)/shard_map/ppermute | solution.py:638
  77.7 27.4 %copy-start.10 = (bf16[256,1024]{1,0:T(8,128)(2,1)}, bf16[256,1024]{1,0:T(8,128)(2,1)S(1)}, u32[]{:S(2)}) copy-start(bf16[256,1024]{1,0:T(8,128)(2,1)S(1)} %collective-permute-done.17.rest_1_) | copy-start | bytes 1572868
  77.7 3.6 %collective-permute-start.25 = (bf16[64,4096]{1,0:T(8,128)(2,1)}, bf16[64,4096]{1,0:T(8,128)(2,1)S(1)}, u32[]{:S(2)}, u32[]{:S(2)}) collective-permute-start(bf16[64,4096]{1,0:T(8,128)(2,1)} %collective-permute-done.20.rest_11_), channel_id=1, source_target_pairs={{0,8},{8,0},{16,24},{24,16},{1,9},{9,1},{17,25},{25,17},{2,10},{10... | collective-permute-start | bytes 1572872 | tf_op jit(solution)/shard_map/ppermute | solution.py:638
  78.8 4.8 %collective-permute-start.26 = (bf16[64,4096]{1,0:T(8,128)(2,1)}, bf16[64,4096]{1,0:T(8,128)(2,1)}, u32[]{:S(2)}, u32[]{:S(2)}) collective-permute-start(bf16[64,4096]{1,0:T(8,128)(2,1)} %collective-permute-done.21.rest_12_), channel_id=1, source_target_pairs={{0,8},{8,0},{16,24},{24,16},{1,9},{9,1},{17,25},{25,17},{2,10},{10... | collective-permute-start | bytes 1572872 | tf_op jit(solution)/shard_map/ppermute | solution.py:638
  79.8 5.5 %collective-permute-start.27 = (bf16[64,4096]{1,0:T(8,128)(2,1)}, bf16[64,4096]{1,0:T(8,128)(2,1)}, u32[]{:S(2)}, u32[]{:S(2)}) collective-permute-start(bf16[64,4096]{1,0:T(8,128)(2,1)} %collective-permute-done.22.rest_13_), channel_id=1, source_target_pairs={{0,8},{8,0},{16,24},{24,16},{1,9},{9,1},{17,25},{25,17},{2,10},{10... | collective-permute-start | bytes 1572872 | tf_op jit(solution)/shard_map/ppermute | solution.py:638
  80.2 25.0 %copy-start = (bf16[1,1024]{1,0:T(2,128)(2,1)}, bf16[1,1024]{1,0:T(2,128)(2,1)S(1)}, u32[]{:S(2)}) copy-start(bf16[1,1024]{1,0:T(2,128)(2,1)S(1)} %reshape.66.ga) | copy-start | bytes 6148
  80.3 24.8 %copy-start.1 = (s32[17]{0:T(128)}, s32[17]{0:T(128)S(1)}, u32[]{:S(2)}) copy-start(s32[17]{0:T(128)S(1)} %stack.89.info) | copy-start | bytes 208
  81.3 24.5 %collective-permute-start.32 = (bf16[256,1024]{1,0:T(8,128)(2,1)}, bf16[256,1024]{1,0:T(8,128)(2,1)S(1)}, u32[]{:S(2)}, u32[]{:S(2)}) collective-permute-start(bf16[256,1024]{1,0:T(8,128)(2,1)} %copy-done.39), channel_id=1, source_target_pairs={{0,2},{1,3},{2,0},{3,1},{4,6},{5,7},{6,4},{7,5},{8,10},{9,11},{10,... | collective-permute-start | bytes 1572872 | tf_op jit(solution)/shard_map/ppermute | solution.py:644
  83.6 22.2 %collective-permute-start.31 = (bf16[256,1024]{1,0:T(8,128)(2,1)}, bf16[256,1024]{1,0:T(8,128)(2,1)S(1)}, u32[]{:S(2)}, u32[]{:S(2)}) collective-permute-start(bf16[256,1024]{1,0:T(8,128)(2,1)} %copy-done.39), channel_id=1, source_target_pairs={{0,1},{1,0},{2,3},{3,2},{4,5},{5,4},{6,7},{7,6},{8,9},{9,8},{10,11... | collective-permute-start | bytes 1572872 | tf_op jit(solution)/shard_map/ppermute | solution.py:644
  85.3 20.6 %collective-permute-start.28 = (bf16[256,1024]{1,0:T(8,128)(2,1)}, bf16[256,1024]{1,0:T(8,128)(2,1)S(1)}, u32[]{:S(2)}, u32[]{:S(2)}) collective-permute-start(bf16[256,1024]{1,0:T(8,128)(2,1)} %bitcast.39), channel_id=1, source_target_pairs={{0,0},{1,8},{2,2},{3,10},{4,4},{5,12},{6,6},{7,14},{8,1},{9,9},{10... | collective-permute-start | bytes 1572872 | tf_op jit(solution)/shard_map/ppermute | solution.py:657
  87.7 18.2 %collective-permute-start.30 = (bf16[256,1024]{1,0:T(8,128)(2,1)}, bf16[256,1024]{1,0:T(8,128)(2,1)S(1)}, u32[]{:S(2)}, u32[]{:S(2)}) collective-permute-start(bf16[256,1024]{1,0:T(8,128)(2,1)} %get-tuple-element.91), channel_id=1, source_target_pairs={{0,16},{8,24},{16,0},{24,8},{1,17},{9,25},{17,1},{25,9},{2,18},{10... | collective-permute-start | bytes 1572872 | tf_op jit(solution)/shard_map/ppermute | solution.py:641
  105.8 3.0 %collective-permute-start.33 = (bf16[256,1024]{1,0:T(8,128)(2,1)S(1)}, bf16[256,1024]{1,0:T(8,128)(2,1)S(1)}, u32[]{:S(2)}, u32[]{:S(2)}) collective-permute-start(bf16[256,1024]{1,0:T(8,128)(2,1)S(1)} %copy-done.40), channel_id=1, source_target_pairs={{0,8},{8,0},{16,24},{24,16},{1,9},{9,1},{17,25},{25,17},{2,10},{10... | collective-permute-start | bytes 1572872 | tf_op jit(solution)/shard_map/ppermute | solution.py:638
  105.9 2.9 %collective-permute-start.34 = (bf16[256,1024]{1,0:T(8,128)(2,1)S(1)}, bf16[256,1024]{1,0:T(8,128)(2,1)S(1)}, u32[]{:S(2)}, u32[]{:S(2)}) collective-permute-start(bf16[256,1024]{1,0:T(8,128)(2,1)S(1)} %collective-permute-done.30.rest_21_), channel_id=1, source_target_pairs={{0,8},{8,0},{16,24},{24,16},{1,9},{9,1},{17,25},{25,17},{2,10},{10... | collective-permute-start | bytes 1572872 | tf_op jit(solution)/shard_map/ppermute | solution.py:638
  106.5 2.8 %collective-permute-start.35 = (bf16[256,1024]{1,0:T(8,128)(2,1)S(1)}, bf16[256,1024]{1,0:T(8,128)(2,1)S(1)}, u32[]{:S(2)}, u32[]{:S(2)}) collective-permute-start(bf16[256,1024]{1,0:T(8,128)(2,1)S(1)} %collective-permute-done.31.rest_22_), channel_id=1, source_target_pairs={{0,8},{8,0},{16,24},{24,16},{1,9},{9,1},{17,25},{25,17},{2,10},{10... | collective-permute-start | bytes 1572872 | tf_op jit(solution)/shard_map/ppermute | solution.py:638
  106.6 3.5 %collective-permute-start.36 = (bf16[256,1024]{1,0:T(8,128)(2,1)S(1)}, bf16[256,1024]{1,0:T(8,128)(2,1)S(1)}, u32[]{:S(2)}, u32[]{:S(2)}) collective-permute-start(bf16[256,1024]{1,0:T(8,128)(2,1)S(1)} %collective-permute-done.32.rest_23_), channel_id=1, source_target_pairs={{0,8},{8,0},{16,24},{24,16},{1,9},{9,1},{17,25},{25,17},{2,10},{10... | collective-permute-start | bytes 1572872 | tf_op jit(solution)/shard_map/ppermute | solution.py:638
  110.8 20.6 %copy-start.25 = (bf16[64,512]{1,0:T(8,128)(2,1)S(1)}, bf16[64,512]{1,0:T(8,128)(2,1)}, u32[]{:S(2)}) copy-start(bf16[64,512]{1,0:T(8,128)(2,1)} %copy-done.24) | copy-start | bytes 196612
  128.5 2.9 %collective-permute-start.38 = (bf16[256,512]{1,0:T(8,128)(2,1)}, bf16[256,512]{1,0:T(8,128)(2,1)S(1)}, u32[]{:S(2)}, u32[]{:S(2)}) collective-permute-start(bf16[256,512]{1,0:T(8,128)(2,1)} %get-tuple-element.105), channel_id=1, source_target_pairs={{0,8},{8,0},{16,24},{24,16},{1,9},{9,1},{17,25},{25,17},{2,10},{10... | collective-permute-start | bytes 786440 | tf_op jit(solution)/shard_map/ppermute | solution.py:638
  128.7 13.3 %collective-permute-start.37 = (bf16[256,1024]{1,0:T(8,128)(2,1)}, bf16[256,1024]{1,0:T(8,128)(2,1)S(1)}, u32[]{:S(2)}, u32[]{:S(2)}) collective-permute-start(bf16[256,1024]{1,0:T(8,128)(2,1)} %get-tuple-element.95), channel_id=1, source_target_pairs={{0,0},{1,8},{2,2},{3,10},{4,4},{5,12},{6,6},{7,14},{8,1},{9,9},{10... | collective-permute-start | bytes 1572872 | tf_op jit(solution)/shard_map/ppermute | solution.py:657
  142.0 2.9 %collective-permute-start.39 = (bf16[512,1024]{1,0:T(8,128)(2,1)}, bf16[512,1024]{1,0:T(8,128)(2,1)S(1)}, u32[]{:S(2)}, u32[]{:S(2)}) collective-permute-start(bf16[512,1024]{1,0:T(8,128)(2,1)} %get-tuple-element.110), channel_id=1, source_target_pairs={{0,8},{8,0},{16,24},{24,16},{1,9},{9,1},{17,25},{25,17},{2,10},{10... | collective-permute-start | bytes 3145736 | tf_op jit(solution)/shard_map/ppermute | solution.py:638
  147.0 22.4 %collective-permute-start.41 = (bf16[128,512]{1,0:T(8,128)(2,1)S(1)}, bf16[128,512]{1,0:T(8,128)(2,1)S(1)}, u32[]{:S(2)}, u32[]{:S(2)}) collective-permute-start(bf16[128,512]{1,0:T(8,128)(2,1)S(1)} %convert_element_type.58), channel_id=1, source_target_pairs={{0,1},{1,0},{2,3},{3,2},{4,5},{5,4},{6,7},{7,6},{8,9},{9,8},{10,11... | collective-permute-start | bytes 393224 | tf_op jit(solution)/shard_map/ppermute | solution.py:648
  147.8 21.6 %collective-permute-start.40 = (bf16[128,512]{1,0:T(8,128)(2,1)S(1)}, bf16[128,512]{1,0:T(8,128)(2,1)S(1)}, u32[]{:S(2)}, u32[]{:S(2)}) collective-permute-start(bf16[128,512]{1,0:T(8,128)(2,1)S(1)} %convert_element_type.58), channel_id=1, source_target_pairs={{0,16},{1,17},{2,18},{3,19},{4,20},{5,21},{6,22},{7,23},{8,24},{9,... | collective-permute-start | bytes 393224 | tf_op jit(solution)/shard_map/ppermute | solution.py:648
  148.8 20.5 %collective-permute-start.42 = (bf16[128,512]{1,0:T(8,128)(2,1)S(1)}, bf16[128,512]{1,0:T(8,128)(2,1)S(1)}, u32[]{:S(2)}, u32[]{:S(2)}) collective-permute-start(bf16[128,512]{1,0:T(8,128)(2,1)S(1)} %convert_element_type.58), channel_id=1, source_target_pairs={{0,17},{1,16},{2,19},{3,18},{4,21},{5,20},{6,23},{7,22},{8,25},{9,... | collective-permute-start | bytes 393224 | tf_op jit(solution)/shard_map/ppermute | solution.py:648
  149.9 19.5 %collective-permute-start.44 = (bf16[256,1024]{1,0:T(8,128)(2,1)S(1)}, bf16[256,1024]{1,0:T(8,128)(2,1)S(1)}, u32[]{:S(2)}, u32[]{:S(2)}) collective-permute-start(bf16[256,1024]{1,0:T(8,128)(2,1)S(1)} %get-tuple-element.128), channel_id=1, source_target_pairs={{0,2},{1,3},{2,4},{3,5},{4,6},{5,7},{8,10},{9,11},{10,12},{11,13},... | collective-permute-start | bytes 1572872 | tf_op jit(solution)/shard_map/ppermute | solution.py:746
  155.7 14.8 %collective-permute-start.43 = (bf16[256,1024]{1,0:T(8,128)(2,1)S(1)}, bf16[256,1024]{1,0:T(8,128)(2,1)S(1)}, u32[]{:S(2)}, u32[]{:S(2)}) collective-permute-start(bf16[256,1024]{1,0:T(8,128)(2,1)S(1)} %get-tuple-element.129), channel_id=1, source_target_pairs={{2,0},{3,1},{4,2},{5,3},{6,4},{7,5},{10,8},{11,9},{12,10},{13,11},... | collective-permute-start | bytes 1572872 | tf_op jit(solution)/shard_map/ppermute | solution.py:745
  170.5 15.8 %collective-permute-start.45 = (bf16[256,1024]{1,0:T(8,128)(2,1)S(1)}, bf16[256,1024]{1,0:T(8,128)(2,1)S(1)}, u32[]{:S(2)}, u32[]{:S(2)}) collective-permute-start(bf16[256,1024]{1,0:T(8,128)(2,1)S(1)} %get-tuple-element.123), channel_id=1, source_target_pairs={{0,8},{8,0},{16,24},{24,16},{1,9},{9,1},{17,25},{25,17},{2,10},{10... | collective-permute-start | bytes 1572872 | tf_op jit(solution)/shard_map/ppermute | solution.py:638
  172.4 9.0 %collective-permute-start.48 = (bf16[128,512]{1,0:T(8,128)(2,1)S(1)}, bf16[128,512]{1,0:T(8,128)(2,1)S(1)}, u32[]{:S(2)}, u32[]{:S(2)}) collective-permute-start(bf16[128,512]{1,0:T(8,128)(2,1)S(1)} %add_add_fusion.1), channel_id=1, source_target_pairs={{0,4},{1,5},{2,6},{3,7},{4,0},{5,1},{6,2},{7,3},{8,12},{9,13},{10,... | collective-permute-start | bytes 393224 | tf_op jit(solution)/shard_map/ppermute | solution.py:648
  174.8 6.5 %collective-permute-start.47 = (bf16[128,512]{1,0:T(8,128)(2,1)S(1)}, bf16[128,512]{1,0:T(8,128)(2,1)S(1)}, u32[]{:S(2)}, u32[]{:S(2)}) collective-permute-start(bf16[128,512]{1,0:T(8,128)(2,1)S(1)} %add_add_fusion.1), channel_id=1, source_target_pairs={{0,2},{1,3},{2,0},{3,1},{4,6},{5,7},{6,4},{7,5},{8,10},{9,11},{10,... | collective-permute-start | bytes 393224 | tf_op jit(solution)/shard_map/ppermute | solution.py:648
  174.8 10.5 %collective-permute-start.49 = (bf16[128,512]{1,0:T(8,128)(2,1)S(1)}, bf16[128,512]{1,0:T(8,128)(2,1)S(1)}, u32[]{:S(2)}, u32[]{:S(2)}) collective-permute-start(bf16[128,512]{1,0:T(8,128)(2,1)S(1)} %add_add_fusion.1), channel_id=1, source_target_pairs={{0,6},{1,7},{2,4},{3,5},{4,2},{5,3},{6,0},{7,1},{8,14},{9,15},{10,... | collective-permute-start | bytes 393224 | tf_op jit(solution)/shard_map/ppermute | solution.py:648
  185.4 4.1 %collective-permute-start.50 = (f32[128,512]{1,0:T(8,128)S(1)}, f32[128,512]{1,0:T(8,128)S(1)}, u32[]{:S(2)}, u32[]{:S(2)}) collective-permute-start(f32[128,512]{1,0:T(8,128)S(1)} %add_add_fusion), channel_id=1, source_target_pairs={{0,8},{8,0},{16,24},{24,16},{1,9},{9,1},{17,25},{25,17},{2,10},{10... | collective-permute-start | bytes 786440 | tf_op jit(solution)/shard_map/ppermute | solution.py:638
  186.6 10.5 %collective-permute-start.46 = (bf16[256,1024]{1,0:T(8,128)(2,1)S(1)}, bf16[256,1024]{1,0:T(8,128)(2,1)S(1)}, u32[]{:S(2)}, u32[]{:S(2)}) collective-permute-start(bf16[256,1024]{1,0:T(8,128)(2,1)S(1)} %add_convert_fusion), channel_id=1, source_target_pairs={{0,0},{1,8},{2,2},{3,10},{4,4},{5,12},{6,6},{7,14},{8,1},{9,9},{10... | collective-permute-start | bytes 1572872 | tf_op jit(solution)/shard_map/ppermute | solution.py:657
  (39 other events, 250.1 us)

commit v3 on v2

--- a/solution.py
+++ b/solution.py
@@ -13,13 +13,15 @@
 MASKED = -1e30
 TILE = 256
 CHUNK = 512
+UP_PARTS = 4
+HALF_AT, Q_AT, H_AT = 11, 17, 19
 GRAD_LAGS = (0, 1, 2)
 
 f32 = jnp.float32
 bf16 = jnp.bfloat16
 VM = pl.BlockSpec(memory_space=pltpu.VMEM)
 SM = pl.BlockSpec(memory_space=pltpu.SMEM)
-HB = pl.BlockSpec(memory_space=pl.ANY)
+HB = pl.BlockSpec(memory_space=pltpu.HBM)
 
 
 def cost(us):
@@ -60,22 +62,26 @@
     return (g - jnp.mean(g, -1, keepdims=True) - n * jnp.mean(g * n, -1, keepdims=True)) * inv
 
 
-def pack_kernel(info, *rest, plan, n_in):
-    srcs, outs, sem = rest[:n_in], rest[n_in:-1], rest[-1]
+def pack_kernel(info, *rest, plan, n_in, n_out):
+    srcs, outs, bufs = rest[:n_in], rest[n_in : n_in + n_out], rest[n_in + n_out : n_in + 2 * n_out]
+    sem_in, sem_out = rest[n_in + 2 * n_out :]
     pairs = []
     for i, which, o, col in plan:
         rows, cols = outs[o].shape[0], srcs[i].shape[1]
-        pairs.append((srcs[i].at[row_at(info[which] * rows, rows), :], outs[o].at[:, pl.ds(col, cols)]))
-    wait_all(start_all(pairs, sem))
+        pairs.append((srcs[i].at[row_at(info[which] * rows, rows), :], bufs[o].at[:, pl.ds(col, cols)]))
+    wait_all(start_all(pairs, sem_in))
+    wait_all(start_all(list(zip(bufs, outs)), sem_out))
 
 
 def pack(info, srcs, shapes, plan):
     return pl.pallas_call(
-        functools.partial(pack_kernel, plan=plan, n_in=len(srcs)),
+        functools.partial(pack_kernel, plan=plan, n_in=len(srcs), n_out=len(shapes)),
         out_shape=tuple(shape_of(a, bf16) for a in shapes),
         in_specs=[SM] + [HB] * len(srcs),
-        out_specs=(VM,) * len(shapes),
-        scratch_shapes=[pltpu.SemaphoreType.DMA((len(plan),))],
+        out_specs=(HB,) * len(shapes),
+        scratch_shapes=[pltpu.VMEM(a, bf16) for a in shapes]
+        + [pltpu.SemaphoreType.DMA((len(plan),)), pltpu.SemaphoreType.DMA((len(shapes),))],
+        compiler_params=pltpu.CompilerParams(vmem_limit_bytes=58 << 20),
         name="pack",
         cost_estimate=cost(2),
     )(info, *srcs)
@@ -117,17 +123,18 @@
     tok_in = rest[:6]
     own, mate = rest[6:9], rest[9:12]
     pieces = rest[12 : 12 + count]
-    outs = rest[12 + count : 26 + count]
-    (keep_ref, send_ref, ot_ref, lse_ref, pk_ref, pkt_ref, pv_ref, q_out, qt_out, k_out, kt_out, v_out,
-     w_out, pvt_ref) = outs
-    (tok, w_ref, q_ref, qt_ref, k_ref, kt_ref, v_ref, vt_ref, stat, acc, bias, sem_x, sem_w,
-     sem_o) = rest[26 + count :]
+    outs = rest[12 + count : 25 + count]
+    keep_ref, send_ref, ot_out, lse_out, pk_out, pkt_out, pv_out = outs[:7]
+    q_out, qt_out, k_out, kt_out, v_out, w_out = outs[7:]
+    (tok, w_ref, q_ref, qt_ref, k_ref, kt_ref, v_ref, vt_ref, pk_ref, pkt_ref, pv_ref, pvt_ref, ot_ref, lse_ref,
+     att, stat, acc, bias, sem_x, sem_w, sem_o, sem_a) = rest[25 + count :]
     core = info[0]
     tokens = tok_in[0].shape[0]
     width = tok.shape[1]
     pairs = []
     for i in range(6):
-        slot = 2 * (i % 3) + (core if i < 3 else 1 - core)
+        place = (1, 2 - 2 * tiles[0], 2 * tiles[0])[i % 3]
+        slot = 2 * place + (core if i < 3 else 1 - core)
         pairs.append((tok_in[i], tok.at[row_at(slot * tokens, tokens), :]))
     got_tok = start_all(pairs, sem_x)
     cols = pl.multiple_of(core * half, 128)
@@ -140,15 +147,15 @@
             pairs.append(
                 (
                     ref.at[:, pl.ds(i * width + cols, half)],
-                    w_ref.at[i, row_at(info[3 + j], ref.shape[0]), :],
+                    w_ref.at[i, row_at(info[HALF_AT + j], ref.shape[0]), :],
                 )
             )
         got_w.append(start_all(pairs, sem_w.at[i]))
     pk_half, pv_half = pk[:, pl.ds(cols, half)], pv[:, pl.ds(cols, half)]
     pk_ref[...], pkt_ref[...] = pk_half, pk_half.astype(f32).T.astype(bf16)
     pv_ref[...], pvt_ref[...] = pv_half, pv_half.astype(f32).T.astype(bf16)
-    bias_v = bv[:, pl.ds(cols, half)].astype(f32)
-    bias_q = bq[:, pl.ds(cols, half)].astype(f32)
+    bias_v = bv[pl.ds(cols, half)].astype(f32)[None, :]
+    bias_q = bq[pl.ds(cols, half)].astype(f32)[None, :]
     blocks = k_ref.shape[0] // TILE
     wait_all(got_tok)
     wait_all(got_w[0])
@@ -160,7 +167,7 @@
         kt_ref[:, at] = full.T.astype(bf16)
         return carry
 
-    lax.fori_loop(0, blocks, key_block, 0)
+    lax.fori_loop(0, blocks, key_block, 0, unroll=2)
     wait_all(got_w[1])
 
     def value_block(b, carry):
@@ -170,7 +177,7 @@
         vt_ref[:, at] = full.T.astype(bf16)
         return carry
 
-    lax.fori_loop(0, blocks, value_block, 0)
+    lax.fori_loop(0, blocks, value_block, 0, unroll=2)
     wait_all(got_w[2])
 
     def query_block(b, carry):
@@ -181,11 +188,10 @@
         qt_ref[:, at] = full.T.astype(bf16)
         return carry
 
-    lax.fori_loop(0, 2 * tokens // TILE, query_block, 0)
-    saved = start_all(
-        [(w_ref, w_out), (k_ref, k_out), (kt_ref, kt_out), (v_ref, v_out), (q_ref, q_out), (qt_ref, qt_out)],
-        sem_o,
-    )
+    lax.fori_loop(0, 2 * tokens // TILE, query_block, 0, unroll=2)
+    pairs = [(w_ref, w_out), (k_ref, k_out), (kt_ref, kt_out), (v_ref, v_out), (q_ref, q_out), (qt_ref, qt_out)]
+    pairs += [(pk_ref, pk_out), (pkt_ref, pkt_out), (pv_ref, pv_out)]
+    saved = start_all(pairs, sem_o)
     heads = half // HEAD
 
     def one_query_tile(t, carry):
@@ -239,21 +245,13 @@
             acc[rows, :] = acc[rows, :] / stat[pl.ds(heads + h, 1), :]
         ot_ref[:, at] = acc[...]
         lse_ref[:, at] = stat[pl.ds(0, heads), :] + jnp.log(stat[pl.ds(heads, heads), :])
-        low = acc[...].T.astype(bf16)
-        side = (t * TILE) // tokens
-        rows = pl.ds(pl.multiple_of(t * TILE - side * tokens, TILE), TILE)
-
-        @pl.when(side == core)
-        def _():
-            keep_ref[rows, :] = low
-
-        @pl.when(side != core)
-        def _():
-            send_ref[rows, :] = low
-
+        att[at, :] = acc[...].T.astype(bf16)
         return carry
 
     lax.fori_loop(0, 2 * tokens // TILE, one_query_tile, 0)
+    mine, theirs = row_at(core * tokens, tokens), row_at((1 - core) * tokens, tokens)
+    pairs = [(att.at[theirs, :], send_ref), (att.at[mine, :], keep_ref), (ot_ref, ot_out), (lse_ref, lse_out)]
+    wait_all(start_all(pairs, sem_a))
     wait_all(saved)
 
 
@@ -263,27 +261,30 @@
     heads, pre = half // HEAD, pk.shape[0]
     n_q, n_k = 2 * tokens, 6 * tokens
     count = len(pieces)
-    outs = [((tokens, half), bf16), ((tokens, half), bf16), ((half, n_q), f32), ((heads, n_q), f32)]
-    outs += [((pre, half), bf16), ((half, pre), bf16), ((pre, half), bf16)]
     kept = [(n_q, half), (half, n_q), (n_k, half), (half, n_k), (n_k, half)]
-    outs += [(a, bf16) for a in kept] + [((3, width, half), bf16)]
-    vmem = [pltpu.VMEM((n_k, width), bf16), pltpu.VMEM((3, width, half), bf16)]
-    vmem += [pltpu.VMEM(a, bf16) for a in kept + [(half, n_k)]]
+    pres = [(pre, half), (half, pre), (pre, half)]
+    stats = [(half, n_q), (heads, n_q)]
+    outs = [shape_of((tokens, half), bf16)] * 2 + [shape_of(a, f32) for a in stats]
+    outs += [shape_of(a, bf16) for a in pres + kept + [(3, width, half)]]
+    vmem = [(n_k, width), (3, width, half)] + kept + [(half, n_k)] + pres + [(half, pre)]
     return pl.pallas_call(
         functools.partial(front_kernel, count=count, half=half),
-        out_shape=tuple(shape_of(*a) for a in outs) + (shape_of((half, pre), bf16),),
+        out_shape=tuple(outs),
         in_specs=[SM, SM] + [VM] * 6 + [HB] * (12 + count),
-        out_specs=(VM,) * 7 + (HB,) * 6 + (VM,),
-        scratch_shapes=vmem
+        out_specs=(HB,) * len(outs),
+        scratch_shapes=[pltpu.VMEM(a, bf16) for a in vmem]
+        + [pltpu.VMEM(a, f32) for a in stats]
         + [
+            pltpu.VMEM((n_q, half), bf16),
             pltpu.VMEM((2 * heads, TILE), f32),
             pltpu.VMEM((half, TILE), f32),
             pltpu.VMEM((TILE, TILE), f32),
             pltpu.SemaphoreType.DMA((6,)),
             pltpu.SemaphoreType.DMA((3, 2 + count)),
-            pltpu.SemaphoreType.DMA((6,)),
+            pltpu.SemaphoreType.DMA((9,)),
+            pltpu.SemaphoreType.DMA((4,)),
         ],
-        compiler_params=pltpu.CompilerParams(vmem_limit_bytes=48 << 20),
+        compiler_params=pltpu.CompilerParams(vmem_limit_bytes=60 << 20),
         name="front",
         cost_estimate=cost(20),
     )(info, tiles, first, last, bq, bv, pk, pv, *toks, *own, *mate, *pieces)
@@ -337,19 +338,15 @@
         lax.fori_loop(lo, hi, one_key_tile, 0)
 
 
-def remote_grads_kernel(
-    info, first, last, q_ref, qt_ref, k_ref, kt_ref, v_ref, pk_ref, pkt_ref, pv_ref, keep_in, recv_in,
-    ot_ref, lse_ref, w_in, give_ref, keep_lo, keep_hi, pre_ref, dqt, do_s, dot_s, inner_s, dk, dv, bias,
-    wsc, wsem, *, heads,
+def prefix_grads_kernel(
+    info, q_ref, qt_ref, pk_ref, pkt_ref, pv_ref, keep_in, recv_in, ot_ref, lse_ref,
+    pre_ref, dqt, do_s, dot_s, inner_s, *, heads,
 ):
-    copies = start_all([(w_in.at[1], wsc.at[0]), (w_in.at[2], wsc.at[1])], wsem)
     core = info[0]
     tokens = keep_in.shape[0]
     n_q, pre = q_ref.shape[0], pk_ref.shape[0]
     do_s[row_at(core * tokens, tokens), :] = keep_in[...]
     do_s[row_at((1 - core) * tokens, tokens), :] = recv_in[...]
-    dk[...] = jnp.zeros_like(dk)
-    dv[...] = jnp.zeros_like(dv)
     pre_ref[...] = jnp.zeros_like(pre_ref)
 
     def one_query_tile(t, carry):
@@ -375,44 +372,80 @@
             lambda h: inner_s[pl.ds(h, 1), at], None, put,
         )
         staged(heads, stages, GRAD_LAGS)
-        lo, hi = info[1 + 2 * t], info[2 + 2 * t]
-        side = 2 * tokens // TILE
-        refs = (q_ref, qt_ref, k_ref, kt_ref, v_ref, do_s, dot_s, lse_ref, inner_s, bias)
-        ranges = ((lo, jnp.minimum(hi, side)), (jnp.maximum(lo, 2 * side), hi))
-        sweep(ranges, at, first, last, refs, (dqt, dk, dv), heads)
         return carry
 
     lax.fori_loop(0, n_q // TILE, one_query_tile, 0)
-    wait_all(copies)
-    for i, keep in ((0, keep_lo), (1, keep_hi)):
-        for mine in (True, False):
-            block = core if mine else 1 - core
-            r = row_at(i * 4 * tokens + block * tokens, tokens)
-            out = dot(dk[r, :].astype(bf16), wsc[0], 1, 1) + dot(dv[r, :].astype(bf16), wsc[1], 1, 1)
-            if mine:
-                keep[...] = out
-            else:
-                give_ref[pl.ds(i * tokens, tokens), :] = out.astype(bf16)
-
-
-def remote_grads(info, first, last, q, qt, k, kt, v, pk, pkt, pv, keep, recv, ot, lse, w):
+
+
+def prefix_grads(info, q, qt, pk, pkt, pv, keep, recv, ot, lse):
     n_q, half = q.shape
-    heads, tokens, width = half // HEAD, n_q // 2, w.shape[1]
-    n_k, pre = k.shape[0], pk.shape[0]
+    heads, pre = half // HEAD, pk.shape[0]
     return pl.pallas_call(
-        functools.partial(remote_grads_kernel, heads=heads),
+        functools.partial(prefix_grads_kernel, heads=heads),
         out_shape=(
-            shape_of((2 * tokens, width), bf16),
-            shape_of((tokens, width), f32),
-            shape_of((tokens, width), f32),
             shape_of((2 * pre, half), f32),
             shape_of((half, n_q), f32),
             shape_of((n_q, half), bf16),
             shape_of((half, n_q), bf16),
             shape_of((heads, n_q), f32),
         ),
-        in_specs=[SM] + [VM] * 14 + [HB],
-        out_specs=(VM,) * 8,
+        in_specs=[SM] + [VM] * 9,
+        out_specs=(VM,) * 5,
+        compiler_params=pltpu.CompilerParams(vmem_limit_bytes=10 << 20),
+        name="prefix_grads",
+        cost_estimate=cost(5),
+    )(info, q, qt, pk, pkt, pv, keep, recv, ot, lse)
+
+
+def remote_grads_kernel(
+    info, first, last, q_ref, qt_ref, k_ref, kt_ref, v_ref, do_ref, dot_ref, lse_ref, inner_ref, dqt_in,
+    w_in, give_ref, keep_near, keep_far, dqt, dk, dv, bias, wsc, wsem, *, heads,
+):
+    copies = start_all([(w_in.at[1], wsc.at[0]), (w_in.at[2], wsc.at[1])], wsem)
+    n_q = q_ref.shape[0]
+    tokens = n_q // 2
+    core = info[1 + 2 * (n_q // TILE)]
+    dk[...] = jnp.zeros_like(dk)
+    dv[...] = jnp.zeros_like(dv)
+    dqt[...] = dqt_in[...]
+
+    def one_query_tile(t, carry):
+        at = pl.ds(pl.multiple_of(t * TILE, TILE), TILE)
+        lo, hi = info[1 + 2 * t], info[2 + 2 * t]
+        side = 2 * tokens // TILE
+        refs = (q_ref, qt_ref, k_ref, kt_ref, v_ref, do_ref, dot_ref, lse_ref, inner_ref, bias)
+        ranges = ((lo, jnp.minimum(hi, side)), (jnp.maximum(lo, 2 * side), hi))
+        sweep(ranges, at, first, last, refs, (dqt, dk, dv), heads)
+        return carry
+
+    lax.fori_loop(0, n_q // TILE, one_query_tile, 0)
+    wait_all(copies)
+    for i, keep in ((0, keep_near), (1, keep_far)):
+        for mine in (True, False):
+            block = core if mine else 1 - core
+            side = info[0] if i else 1 - info[0]
+            r = row_at(side * 4 * tokens + block * tokens, tokens)
+            out = dot(dk[r, :].astype(bf16), wsc[0], 1, 1) + dot(dv[r, :].astype(bf16), wsc[1], 1, 1)
+            if mine:
+                keep[...] = out.astype(bf16)
+            else:
+                give_ref[pl.ds(i * tokens, tokens), :] = out.astype(bf16)
+
+
+def remote_grads(info, first, last, q, qt, k, kt, v, do, dot_, lse, inner, dqt, w):
+    n_q, half = q.shape
+    heads, tokens, width = half // HEAD, n_q // 2, w.shape[1]
+    n_k = k.shape[0]
+    return pl.pallas_call(
+        functools.partial(remote_grads_kernel, heads=heads),
+        out_shape=(
+            shape_of((2 * tokens, width), bf16),
+            shape_of((tokens, width), bf16),
+            shape_of((tokens, width), bf16),
+            shape_of((half, n_q), f32),
+        ),
+        in_specs=[SM] + [VM] * 12 + [HB],
+        out_specs=(VM,) * 4,
         scratch_shapes=[
             pltpu.VMEM((n_k, half), f32),
             pltpu.VMEM((n_k, half), f32),
@@ -420,10 +453,10 @@
             pltpu.VMEM((2, width, half), bf16),
             pltpu.SemaphoreType.DMA((2,)),
         ],
-        compiler_params=pltpu.CompilerParams(vmem_limit_bytes=52 << 20),
+        compiler_params=pltpu.CompilerParams(vmem_limit_bytes=24 << 20),
         name="remote_grads",
         cost_estimate=cost(14),
-    )(info, first, last, q, qt, k, kt, v, pk, pkt, pv, keep, recv, ot, lse, w)
+    )(info, first, last, q, qt, k, kt, v, do, dot_, lse, inner, dqt, w)
 
 
 def local_grads_kernel(
@@ -431,7 +464,7 @@
     gh_ref, w_in, keep_ref, give_ref, dqt, dk, dv, bias, wsc, wsem, *, heads,
 ):
     copies = start_all([(w_in, wsc)], wsem)
-    core = info[0]
+    core = info[1 + 2 * (q_ref.shape[0] // TILE)]
     n_q = q_ref.shape[0]
     tokens = n_q // 2
     dqt[...] = dqt_in[...]
@@ -482,66 +515,73 @@
             pltpu.VMEM((3, width, half), bf16),
             pltpu.SemaphoreType.DMA((1,)),
         ],
-        compiler_params=pltpu.CompilerParams(vmem_limit_bytes=52 << 20),
+        compiler_params=pltpu.CompilerParams(vmem_limit_bytes=23 << 20),
         name="local_grads",
         cost_estimate=cost(14),
     )(info, first, last, q, qt, k, kt, v, do, dot_, lse, inner, dqt, gh, w)
 
 
-def placed(refs, info, at, scale, dst, src_cols=None, dst_cols=None):
+def placed(refs, info, at, scale, dst, cols=None):
     pairs = []
     for i, ref in enumerate(refs):
-        src = ref if src_cols is None else ref.at[:, src_cols]
+        src = ref if cols is None else ref.at[:, cols[0]]
         rows = row_at(info[at + i] * scale, ref.shape[0])
-        pairs.append((src, dst.at[rows, :] if dst_cols is None else dst.at[rows, dst_cols]))
+        pairs.append((src, dst.at[rows, :] if cols is None else dst.at[rows, cols[1]]))
     return pairs
 
 
-def out_pairs(parts, info, width, dst):
-    return placed(parts[:2], info, 1, 1, dst) + placed(
-        parts[2:], info, 11, 1, dst, pl.ds(3 * width, width)
+def up_pairs(parts, info, dst, cols):
+    return placed((parts[0], parts[2]) + tuple(parts[4:]), info, 1, 1, dst, (cols, cols))
+
+
+def out_pairs(parts, info, ff, dst):
+    whole = pl.ds(0, dst.shape[1])
+    return placed((parts[1], parts[3]), info, 1, 1, dst) + placed(
+        parts[4:], info, 3, 1, dst, (pl.ds(ff, dst.shape[1]), whole)
     )
 
 
-def up_kernel(info, own_att, got_att, tok, bo, ga, sa, bu, *rest, n_o, count):
-    wo, wu = rest[:n_o], rest[n_o : n_o + count]
-    nrm_ref, hat_ref, inv_ref, act_ref, slope_ref, wo_s, wu_s, sem_o, sem_u = rest[n_o + count :]
+def up_kernel(info, own_att, got_att, tok, bo, ga, sa, bu, *rest, count):
+    wu = rest[:count]
+    nrm_ref, hat_ref, inv_ref, act_ref, slope_ref, wo_s, wu_s, own_s, got_s, tok_s, sem_a, sem_o, sem_u = rest[count:]
+    acts = start_all([(own_att, own_s), (got_att, got_s), (tok, tok_s)], sem_a)
     width, ff = wu_s.shape
     half = own_att.shape[1]
-    got_o = start_all(out_pairs(wo, info, width, wo_s), sem_o)
+    got_o = start_all(out_pairs(wu, info, ff, wo_s), sem_o)
+    part = ff // UP_PARTS
     got_u = []
-    for j in range(ff // width):
-        cs = pl.ds(j * width, width)
-        got_u.append(start_all(placed(wu, info, 1, 1, wu_s, cs, cs), sem_u.at[j]))
+    for j in range(UP_PARTS):
+        got_u.append(start_all(up_pairs(wu, info, wu_s, pl.ds(j * part, part)), sem_u.at[j]))
     core = info[0]
+    wait_all(acts)
     wait_all(got_o)
     hidden = (
-        tok[...].astype(f32)
-        + dot(own_att[...], wo_s[row_at(core * half, half), :])
-        + dot(got_att[...], wo_s[row_at((1 - core) * half, half), :])
-        + bo[...].astype(f32)
+        tok_s[...].astype(f32)
+        + dot(own_s[...], wo_s[row_at(core * half, half), :])
+        + dot(got_s[...], wo_s[row_at((1 - core) * half, half), :])
+        + bo[...].astype(f32)[None, :]
     )
     hat, inv = normalised(hidden)
     hat_ref[...] = hat
     inv_ref[...] = jnp.broadcast_to(inv, inv_ref.shape)
-    nrm = hat * ga[...].astype(f32) + sa[...].astype(f32)
+    nrm = hat * ga[...].astype(f32)[None, :] + sa[...].astype(f32)[None, :]
     nrm_ref[...] = nrm
     low = nrm.astype(bf16)
     for j in range(ff // CHUNK):
-        if (j * CHUNK) % width == 0:
-            wait_all(got_u[j * CHUNK // width])
+        if (j * CHUNK) % part == 0:
+            wait_all(got_u[j * CHUNK // part])
         cs = pl.ds(j * CHUNK, CHUNK)
-        v = dot(low, wu_s[:, cs]) + bu[:, cs].astype(f32)
+        v = dot(low, wu_s[:, cs]) + bu[cs].astype(f32)[None, :]
         phi = 0.5 + 0.5 * lax.erf(v * (0.5**0.5))
         act_ref[:, cs] = (v * phi).astype(bf16)
         slope_ref[:, cs] = (phi + v * (jnp.exp(v * v * -0.5) * 0.3989422804014327)).astype(bf16)
 
 
-def up(info, own_att, got_att, tok, bo, ga, sa, bu, wo, wu):
+def up(info, own_att, got_att, tok, bo, ga, sa, bu, wu):
     tokens, width = tok.shape
-    ff, count = bu.shape[1], len(wu)
+    ff, count = bu.shape[0], len(wu)
     return pl.pallas_call(
-        functools.partial(up_kernel, n_o=len(wo), count=count),
+        functools.partial(up_kernel, count=count),
         out_shape=(
             shape_of((tokens, width), f32),
             shape_of((tokens, width), f32),
@@ -549,30 +589,34 @@
             shape_of((tokens, ff), bf16),
             shape_of((tokens, ff), bf16),
         ),
-        in_specs=[SM] + [VM] * 7 + [HB] * (len(wo) + count),
+        in_specs=[SM] + [HB] * 3 + [VM] * 4 + [HB] * count,
         out_specs=(VM,) * 5,
         scratch_shapes=[
             pltpu.VMEM((width, width), bf16),
             pltpu.VMEM((width, ff), bf16),
-            pltpu.SemaphoreType.DMA((count,)),
-            pltpu.SemaphoreType.DMA((ff // width, count)),
+            pltpu.VMEM((tokens, width // 2), bf16),
+            pltpu.VMEM((tokens, width // 2), bf16),
+            pltpu.VMEM((tokens, width), bf16),
+            pltpu.SemaphoreType.DMA((3,)),
+            pltpu.SemaphoreType.DMA((count - 2,)),
+            pltpu.SemaphoreType.DMA((UP_PARTS, count - 2)),
         ],
-        compiler_params=pltpu.CompilerParams(vmem_limit_bytes=50 << 20),
+        compiler_params=pltpu.CompilerParams(vmem_limit_bytes=55 << 20),
         name="up",
         cost_estimate=cost(10),
-    )(info, own_att, got_att, tok, bo, ga, sa, bu, *wo, *wu)
-
-
-def down_kernel(info, nrm_ref, hat_ref, inv_ref, act_ref, slope_ref, cot, bd, gf, sf, ga, *rest, n_o, count):
-    wo, wu, wd = rest[:n_o], rest[n_o : n_o + count], rest[n_o + count : n_o + 2 * count]
-    out_ref, gh_ref, keep_ref, send_ref, wo_s, wu_s, wd_s, sem_o, sem_u, sem_d = rest[n_o + 2 * count :]
+    )(info, own_att, got_att, tok, bo, ga, sa, bu, *wu)
+
+
+def down_kernel(info, nrm_ref, hat_ref, inv_ref, act_ref, slope_ref, cot, bd, gf, sf, ga, *rest, count):
+    wu, wd = rest[:count], rest[count : 2 * count - 2]
+    out_ref, gh_ref, keep_ref, send_ref, wo_s, wu_s, wd_s, sem_o, sem_u, sem_d = rest[2 * count - 2 :]
     width, ff = wu_s.shape
     half = keep_ref.shape[1]
     got_d = start_all(placed(wd, info, 1, ff // width, wd_s), sem_d)
-    got_u = start_all(placed(wu, info, 1, 1, wu_s), sem_u)
-    got_o = start_all(out_pairs(wo, info, width, wo_s), sem_o)
+    got_u = start_all(up_pairs(wu, info, wu_s, pl.ds(0, ff)), sem_u)
+    got_o = start_all(out_pairs(wu, info, ff, wo_s), sem_o)
     core = info[0]
-    summed = nrm_ref[...] + bd[...].astype(f32)
+    summed = nrm_ref[...] + bd[...].astype(f32)[None, :]
     for i, one in enumerate(got_d):
         one.wait()
         size = wd[i].shape[0]
@@ -580,8 +624,8 @@
         cols = pl.ds(pl.multiple_of(info[1 + i] * (ff // width), 128), size)
         summed = summed + dot(act_ref[:, cols], wd_s[at, :])
     n, inv = normalised(summed)
-    gain = gf[...].astype(f32)
-    out_ref[...] = (n * gain + sf[...].astype(f32)).astype(bf16)
+    gain = gf[...].astype(f32)[None, :]
+    out_ref[...] = (n * gain + sf[...].astype(f32)[None, :]).astype(bf16)
     gs = norm_back(cot[...].astype(f32) * gain, n, inv)
     low = gs.astype(bf16)
     wait_all(got_u)
@@ -590,7 +634,7 @@
         cs = pl.ds(j * CHUNK, CHUNK)
         gp = (dot(low, wd_s[cs, :], 1, 1) * slope_ref[:, cs].astype(f32)).astype(bf16)
         total = total + dot(gp, wu_s[:, cs], 1, 1)
-    gh = norm_back(total * ga[...].astype(f32), hat_ref[...], inv_ref[:, :1])
+    gh = norm_back(total * ga[...].astype(f32)[None, :], hat_ref[...], inv_ref[:, :1])
     gh_ref[...] = gh
     gh_low = gh.astype(bf16)
     wait_all(got_o)
@@ -598,31 +642,31 @@
     keep_ref[...] = dot(gh_low, wo_s[row_at(core * half, half), :], 1, 1).astype(bf16)
 
 
-def down(info, nrm, hat, inv, act, slope, cot, bd, gf, sf, ga, wo, wu, wd):
+def down(info, nrm, hat, inv, act, slope, cot, bd, gf, sf, ga, wu, wd):
     tokens, width = nrm.shape
     ff, count = act.shape[1], len(wu)
     return pl.pallas_call(
-        functools.partial(down_kernel, n_o=len(wo), count=count),
+        functools.partial(down_kernel, count=count),
         out_shape=(
             shape_of((tokens, width), bf16),
             shape_of((tokens, width), f32),
             shape_of((tokens, width // 2), bf16),
             shape_of((tokens, width // 2), bf16),
         ),
-        in_specs=[SM] + [VM] * 10 + [HB] * (len(wo) + 2 * count),
+        in_specs=[SM] + [VM] * 10 + [HB] * (2 * count - 2),
         out_specs=(VM,) * 4,
         scratch_shapes=[
             pltpu.VMEM((width, width), bf16),
             pltpu.VMEM((width, ff), bf16),
             pltpu.VMEM((ff, width), bf16),
-            pltpu.SemaphoreType.DMA((count,)),
-            pltpu.SemaphoreType.DMA((count,)),
-            pltpu.SemaphoreType.DMA((count,)),
+            pltpu.SemaphoreType.DMA((count - 2,)),
+            pltpu.SemaphoreType.DMA((count - 2,)),
+            pltpu.SemaphoreType.DMA((count - 2,)),
         ],
-        compiler_params=pltpu.CompilerParams(vmem_limit_bytes=58 << 20),
+        compiler_params=pltpu.CompilerParams(vmem_limit_bytes=47 << 20),
         name="down",
         cost_estimate=cost(16),
-    )(info, nrm, hat, inv, act, slope, cot, bd, gf, sf, ga, *wo, *wu, *wd)
+    )(info, nrm, hat, inv, act, slope, cot, bd, gf, sf, ga, *wu, *wd)
 
 
 def per_device(
@@ -647,13 +691,25 @@
         route = [(i * n_seq + j, (i ^ row_bit) * n_seq + (j ^ bit)) for i in range(n_row) for j in range(n_seq)]
         return lax.ppermute(a, ("row", "seq"), route)
 
-    def swapped(a, shift):
+    def here(z):
+        return z
+
+    def near(z):
+        return z ^ 1
+
+    def far(z):
+        to = z + 1 if z & 1 else z - 1
+        return to if 0 <= to < n_seq // 2 else z
+
+    def along(a, partner):
+        return lax.ppermute(a, "seq", [(j, 2 * partner(j // 2) + (j & 1)) for j in range(n_seq)])
+
+    def swapped(a, partner=here):
         route = []
         for i in range(n_row):
             for j in range(n_seq):
-                to = (j | 1) + 2 * shift - 1
-                if 0 <= to < n_seq:
-                    route.append((i * n_seq + j, ((i & ~1) | (j & 1)) * n_seq + to + (i & 1)))
+                to = ((i & ~1) | (j & 1)) * n_seq + 2 * partner(j // 2) + (i & 1)
+                route.append((i * n_seq + j, to))
         return lax.ppermute(a, ("row", "seq"), route)
 
     def after(a, *others):
@@ -661,34 +717,36 @@
 
     h = x ^ zbit
     first_q, second_q = 2 * h + x, 2 * h + 1 - x
-    which = jnp.stack([first_q, second_q]).astype(jnp.int32)
-    attn = (w_query, w_key, w_value, w_out)
+    m = w_query.shape[0]
+    others = [2 * (1 - h) + 1 - x, 2 * (1 - h) + x]
+    places = [r * m, (r ^ 1) * m]
+    halves = [(r ^ k) * m + j * (m // 4) for k in (2, 3) for j in [2 * h] + others]
+    quarters = [(r ^ k) * m + j * (m // 4) for k in (2, 3) for j in [first_q, second_q] + others]
+    odd = (s >> 1) & 1
+    info = jnp.stack([core] + places + quarters + halves + [first_q, second_q, h]).astype(jnp.int32)
+    attn = (w_query, w_key, w_value)
     short, ff = w_query.shape[0] // 4, w_up.shape[1]
-    (a_half,) = pack(h[None].astype(jnp.int32), attn, [(2 * short, 4 * width)], [(i, 0, 0, i * width) for i in range(4)])
-    plan = [(0, 0, 0, 0), (1, 0, 1, 0), (0, 1, 2, 0), (1, 1, 3, 0)]
-    shapes = [(short, ff), (w_down.shape[0] // 4, width)] * 2
+    plan = [(i, H_AT, 0, i * width) for i in range(3)] + [(3, Q_AT, 1, 0), (4, Q_AT, 1, ff)]
+    early, late = (w_query, w_key, w_value, w_up, w_out), (w_down, w_up, w_out)
+    a_half, u_one = pack(info, early, [(2 * short, 3 * width), (short, ff + width)], plan)
+    plan = [(0, Q_AT, 0, 0), (1, Q_AT + 1, 1, 0), (2, Q_AT + 1, 1, ff), (0, Q_AT + 1, 2, 0)]
+    low = (w_down.shape[0] // 4, width)
+    d_one, u_two, d_two = pack(after(info, u_one), late, [low, (short, ff + width), low], plan)
     a_half = by_y(a_half)
-    own, below, above = (swapped(tokens[0], k) for k in (0, 1, -1))
-    a_own = [by_core(a) for a in attn]
+    own, close, distant = (swapped(tokens[0], k) for k in (here, near, far))
+    a_own = [by_core(after(a, a_half)) for a in attn]
     mates = a_own
-    u_one, d_one, u_two, d_two = pack(after(which, below), (w_up, w_down), shapes, plan)
     a_part = lax.dynamic_slice_in_dim(a_half, x * short, short, 0)
     a_x, a_z = by_seq(a_part, 1), by_seq(a_part, 2)
-    u_one = by_y(after(u_one, a_half))
+    u_one = by_y(u_one)
     d_one = by_y(after(d_one, a_x))
     u_two = by_y(after(u_two, a_z))
-    toks = [below, own, above]
+    toks = [own, close, distant]
     toks = toks + [by_core(a) for a in toks]
     a_got = [a_half, a_x, a_z]
     a_got = a_got + [by_core(a_half), by_core(a_x), by_core(a_z)]
-    u_own = by_core(after(w_up, a_z))
-    m = w_query.shape[0]
-    far = [2 * (1 - h) + 1 - x, 2 * (1 - h) + x]
-    places = [r * m, (r ^ 1) * m]
-    halves = [(r ^ k) * m + j * (m // 4) for k in (2, 3) for j in [2 * h] + far]
-    quarters = [(r ^ k) * m + j * (m // 4) for k in (2, 3) for j in [first_q, second_q] + far]
-
-    theirs = by_core(after(pair_lengths, a_half))
+    u_own, o_own = by_core(after(w_up, a_z)), by_core(after(w_out, a_z))
+    theirs = by_core(after(pair_lengths, a_x))
     lengths = jnp.where(x == core, pair_lengths, theirs)[0]
     pairs = lengths.shape[0]
     later = jnp.arange(pairs)[:, None] >= jnp.arange(pairs)[None, :]
@@ -700,50 +758,35 @@
     first = jnp.max(jnp.where(passed, ends[:, None], 0), axis=0) - origin
     last = jnp.min(jnp.where(passed, n_seq * tok_count, ends[:, None]), axis=0) - origin
     bounds = jnp.stack([first[::TILE] // TILE, (last[TILE - 1 :: TILE] + TILE - 1) // TILE], 1)
-    tile_info = jnp.concatenate([core[None], bounds.reshape(-1)]).astype(jnp.int32)
-    info_a = jnp.stack([core] + places + halves).astype(jnp.int32)
-    info = jnp.stack([core] + places + quarters + halves).astype(jnp.int32)
+    tile_info = jnp.concatenate([odd[None], bounds.reshape(-1), core[None]]).astype(jnp.int32)
     first, last = first[None], last[None]
 
-    def row(a):
-        return a.reshape(1, -1)
-
-    (att_keep, att_send, ot, lse, pk, pkt, pv, q, qt, k, kt, v, w_half, _) = front(
-        info_a, tile_info, first, last, row(b_query), row(b_value), prefix_key, prefix_value, toks,
+    (att_keep, att_send, ot, lse, pk, pkt, pv, q, qt, k, kt, v, w_half) = front(
+        info, tile_info, first, last, b_query, b_value, prefix_key, prefix_value, toks,
         (w_query, w_key, w_value), mates[:3], a_got,
     )
     u_x, u_z = by_seq(u_one, 1), by_seq(u_one, 2)
     d_own = by_core(after(w_down, lse))
-    cot = swapped(after(cotangent[0], lse), 0)
+    cot = swapped(after(cotangent[0], lse))
     d_two = by_y(after(d_two, lse))
     d_one, lse = lax.optimization_barrier((d_one, lse))
     d_x, d_z = by_seq(d_one, 1), by_seq(d_one, 2)
     u_got = [u_one, u_two, u_x, u_z]
     u_got = u_got + [by_core(after(a, lse)) for a in u_got]
-    parts_o = [w_out, mates[3]] + a_got
-    parts_u = [w_up, u_own] + u_got
+    parts_u = [w_up, w_out, u_own, o_own] + u_got
     nrm, hat, inv, act, slope = up(
-        info, att_keep, by_core(att_send), own, row(b_out), row(gain_attn), row(shift_attn), row(b_up),
-        parts_o, parts_u,
+        info, att_keep, by_core(att_send), own, b_out, gain_attn, shift_attn, b_up,
+        parts_u,
     )
     d_got = [d_one, d_two, d_x, d_z]
     d_got = d_got + [by_core(a if a is d_one else after(a, inv, cot)) for a in d_got]
     parts_d = [w_down, d_own] + d_got
     result, gh, ga_keep, ga_send = down(
-        info, nrm, hat, inv, act, slope, cot, row(b_down), row(gain_ffn), row(shift_ffn), row(gain_attn),
-        parts_o, parts_u, parts_d,
+        info, nrm, hat, inv, act, slope, cot, b_down, gain_ffn, shift_ffn, gain_attn,
+        parts_u, parts_d,
     )
-    out_tokens = swapped(result, 0)
-    give, keep_lo, keep_hi, pre, dqt, do, dot_, inner = remote_grads(
-        tile_info, first, last, q, qt, k, kt, v, pk, pkt, pv, ga_keep, by_core(ga_send), ot, lse, w_half
-    )
-    got = by_core(after(give, out_tokens))
-    low_part = (keep_lo + got[:tok_count].astype(f32)).astype(bf16)
-    high_part = (keep_hi + got[tok_count:].astype(f32)).astype(bf16)
-    tile_info = after(tile_info, low_part, high_part)
-    pre = after(pre, low_part)
-    low_part = lax.ppermute(low_part, "seq", [(j + 2, j) for j in range(n_seq - 2)])
-    high_part = lax.ppermute(high_part, "seq", [(j, j + 2) for j in range(n_seq - 2)])
+    out_tokens = swapped(result)
+    pre, dqt, do, dot_, inner = prefix_grads(info, q, qt, pk, pkt, pv, ga_keep, by_core(ga_send), ot, lse)
 
     def summed(a, one, two):
         low = a.astype(bf16)
@@ -757,14 +800,24 @@
         pre = low.astype(f32) + by_both(low, *bits[0]).astype(f32)
         bits = bits[1:]
     pre = summed(pre, bits[0], bits[1])
+    give, keep_near, keep_far, dqt = remote_grads(
+        tile_info, first, last, q, qt, k, kt, v, do, dot_, lse, inner, dqt, w_half
+    )
+    give, out_tokens, pre = lax.optimization_barrier((give, out_tokens, pre))
+    got = by_core(give)
+    near_part = (keep_near.astype(f32) + got[:tok_count].astype(f32)).astype(bf16)
+    far_part = (keep_far.astype(f32) + got[tok_count:].astype(f32)).astype(bf16)
+    tile_info, near_part, far_part = lax.optimization_barrier((tile_info, near_part, far_part))
+    pre = after(pre, near_part)
+    near_part, far_part = along(near_part, near), along(far_part, far)
+    for i in range(2, len(bits), 2):
+        pre = summed(pre, bits[i], bits[i + 1])
     keep, give = local_grads(
         tile_info, first, last, q, qt, k, kt, v, do, dot_, lse, inner, dqt, gh, w_half
     )
-    pre, give, low_part, high_part = lax.optimization_barrier((pre, give, low_part, high_part))
-    mine = (keep + low_part.astype(f32)) + (by_core(give).astype(f32) + high_part.astype(f32))
-    grad_tokens = swapped(mine.astype(bf16), 0)
-    for i in range(2, len(bits), 2):
-        pre = summed(pre, bits[i], bits[i + 1])
+    pre, give, near_part, far_part = lax.optimization_barrier((pre, give, near_part, far_part))
+    mine = (keep + near_part.astype(f32)) + (by_core(give).astype(f32) + far_part.astype(f32))
+    grad_tokens = swapped(mine.astype(bf16))
     other = by_core(pre)
     pre = jnp.concatenate(
         [jnp.where(core == 0, pre, other), jnp.where(core == 0, other, pre)], axis=1

time: 200 us -> 183 us (0.915)
  local copies, waits for them, and re-layouts: 16 us -> 4.8 us
  Pallas kernels: 75.3 us -> 67.5 us
  waiting for transfers between devices: 44.2 us -> 48.3 us
    ppermute x5, waiting for transfers between devices: 1.64 us -> 16.9 us  [by_y(): return lax.ppermute(a, 'row', [(i, i ^ 2) for i in range(n_row)])]
    ppermute x26, starting transfers between devices: 13.7 us -> 23.1 us  [by_core(): return lax.ppermute(a, 'row', [(i, i ^ 1) for i in range(n_row)])]
    ppermute x2, waiting for transfers between devices: 1.02 us -> 10.1 us  [along(): lax.ppermute(a, 'seq', [(j, 2 * partner(j // 2) + (j & 1)) for j in range...]
    unnamed x106 -> x74, local copies, waits for them, and re-layouts: 11.8 us -> 3.77 us
    ppermute x6, waiting for transfers between devices: 15.6 us -> 7.69 us  [swapped(): return lax.ppermute(a, ('row', 'seq'), route)]
    ppermute x6, waiting for transfers between devices: 9.31 us -> 1.62 us  [by_both(): return lax.ppermute(a, ('row', 'seq'), route)]
    ppermute x6, waiting for transfers between devices: 8.89 us -> 1.53 us  [by_seq(): return lax.ppermute(a, 'seq', [(i, i ^ bit) for i in range(n_seq)])]
    ppermute x2, starting transfers between devices: 7.04 us -> 0.89 us  [along(): lax.ppermute(a, 'seq', [(j, 2 * partner(j // 2) + (j & 1)) for j in range...]
  transfers between devices with their start and end apart: 51 -> 51, of which waited for: 17 -> 18; matrix products, arithmetic and copies ran while one was open for 3% -> 1% of each run, Pallas kernels for 28% -> 27%
where the time goes in v3:
time: 183 us; the launch traced here: 182 us
  Pallas kernels  67.5 us (37%)
  starting transfers between devices  57.3 us (31%)
  waiting for transfers between devices  48.3 us (26%)
  local copies, waits for them, and re-layouts  4.8 us (3%)
  other arithmetic  2.62 us (1%)
    ppermute x26, starting transfers between devices, by_core(): return lax.ppermute(a, 'row', [(i, i ^ 1) for i in range(n_row)])  23.1 us
    pallas_call x1, Pallas kernels, front(): pl.pallas_call(functools.partial(front_kernel, count=count, half=half), o...  17.1 us
    ppermute x6, starting transfers between devices, swapped(): return lax.ppermute(a, ('row', 'seq'), route)  16.9 us
    ppermute x5, waiting for transfers between devices, by_y(): return lax.ppermute(a, 'row', [(i, i ^ 2) for i in range(n_row)])  16.9 us
    pallas_call x1, Pallas kernels, down(): pl.pallas_call(functools.partial(down_kernel, count=count), out_shape=(sh...  14.9 us
    pallas_call x1, Pallas kernels, up(): pl.pallas_call(functools.partial(up_kernel, count=count), out_shape=(shap...  13 us
    ppermute x26, waiting for transfers between devices, by_core(): return lax.ppermute(a, 'row', [(i, i ^ 1) for i in range(n_row)])  10.5 us
    ppermute x2, waiting for transfers between devices, along(): lax.ppermute(a, 'seq', [(j, 2 * partner(j // 2) + (j & 1)) for j in range...  10.1 us
  transfers between devices with their start and end apart: 51, of which 18 were waited for; matrix products, arithmetic and copies ran while one was open for 1% of the time, Pallas kernels for 27%

profile of v3, /device:TPU:1, one launch (start us, length us, event | category | flops | bytes accessed | tf_op | source)
XLA Modules:
  0.0 181.8 jit_solution(13917914467229712243)
XLA Ops:
  0.7 0.6 stack.80.info
  1.3 3.1 %pack.2 = (bf16[128,3072]{1,0:T(8,128)(2,1)}, bf16[64,5120]{1,0:T(8,128)(2,1)}) custom-call(s32[20]{0:T(128)} %stack.80.info, bf16[256,1024]{1,0:T(8,128)(2,1)} %rest_6_.1, bf16[256,1024]{1,0:T(8,128)(2,1)} %rest_7_.1, bf16[256,1024]{1,0:T(8,128)(2,1)} %rest_8_.1, bf16[256,4096]{1,0:T(8,128)(2,1)} %rest_0_.7, bf16[256,1024]{1,0:T(8,128)(2,1)} %rest_1_.7), custom_call_target="tpu_custom_call" | custom-call | flops 2000000000 | tf_op jit(solution)/shard_map/pack/pallas_call | solution.py:77
  4.4 2.1 %collective-permute-start = (bf16[128,3072]{1,0:T(8,128)(2,1)}, bf16[128,3072]{1,0:T(8,128)(2,1)S(1)}, u32[]{:S(2)}, u32[]{:S(2)}) collective-permute-start(bf16[128,3072]{1,0:T(8,128)(2,1)} %get-tuple-element.74), channel_id=1, source_target_pairs={{0,16},{8,24},{16,0},{24,8},{1,17},{9,25},{17,1},{25,9},{2,18},{10... | collective-permute-start | bytes 2359304 | tf_op jit(solution)/shard_map/ppermute | solution.py:685
  6.6 4.0 %collective-permute-start.5 = (bf16[256,1024]{1,0:T(8,128)(2,1)}, bf16[256,1024]{1,0:T(8,128)(2,1)}, u32[]{:S(2)}, u32[]{:S(2)}) collective-permute-start(bf16[256,1024]{1,0:T(8,128)(2,1)} %bitcast.22), channel_id=1, source_target_pairs={{0,0},{1,8},{2,4},{3,12},{4,2},{5,10},{6,6},{7,14},{8,1},{9,9},{10... | collective-permute-start | bytes 1572872 | tf_op jit(solution)/shard_map/ppermute | solution.py:713
  10.5 1.8 collective-permute-start.4
  12.3 4.0 %collective-permute-start.3 = (bf16[256,1024]{1,0:T(8,128)(2,1)}, bf16[256,1024]{1,0:T(8,128)(2,1)}, u32[]{:S(2)}, u32[]{:S(2)}) collective-permute-start(bf16[256,1024]{1,0:T(8,128)(2,1)} %bitcast.22), channel_id=1, source_target_pairs={{0,0},{1,8},{2,2},{3,10},{4,4},{5,12},{6,6},{7,14},{8,1},{9,9},{10... | collective-permute-start | bytes 1572872 | tf_op jit(solution)/shard_map/ppermute | solution.py:713
  16.3 7.9 %collective-permute-done.rest_12_ = bf16[128,3072]{1,0:T(8,128)(2,1)S(1)} collective-permute-done((bf16[128,3072]{1,0:T(8,128)(2,1)}, bf16[128,3072]{1,0:T(8,128)(2,1)S(1)}, u32[]{:S(2)}, u32[]{:S(2)}) %collective-permute-start) | collective-permute-done | bytes 786464 | tf_op jit(solution)/shard_map/ppermute | solution.py:685
  24.2 1.3 collective-permute-start.12
  25.5 1.2 collective-permute-start.1
  26.7 1.2 collective-permute-start.19
  27.9 3.5 %pack.3 = (bf16[256,1024]{1,0:T(8,128)(2,1)}, bf16[64,5120]{1,0:T(8,128)(2,1)}, bf16[256,1024]{1,0:T(8,128)(2,1)}) custom-call(s32[20]{0:T(128)} %stack.80.info, bf16[1024,1024]{1,0:T(8,128)(2,1)} %rest_12_.1, bf16[256,4096]{1,0:T(8,128)(2,1)} %rest_0_.7, bf16[256,1024]{1,0:T(8,128)(2,1)} %rest_1_.7), custom_call_target="tpu_custom_call" | custom-call | flops 2000000000 | tf_op jit(solution)/shard_map/pack/pallas_call | solution.py:77
  31.4 2.3 %collective-permute-start.8 = (bf16[256,1024]{1,0:T(8,128)(2,1)}, bf16[256,1024]{1,0:T(8,128)(2,1)}, u32[]{:S(2)}, u32[]{:S(2)}) collective-permute-start(bf16[256,1024]{1,0:T(8,128)(2,1)} %collective-permute-done.5.rest_2_), channel_id=1, source_target_pairs={{0,8},{8,0},{16,24},{24,16},{1,9},{9,1},{17,25},{25,17},{2,10},{10... | collective-permute-start | bytes 1572872 | tf_op jit(solution)/shard_map/ppermute | solution.py:682
  33.9 2.0 %collective-permute-start.6 = (bf16[256,1024]{1,0:T(8,128)(2,1)}, bf16[256,1024]{1,0:T(8,128)(2,1)}, u32[]{:S(2)}, u32[]{:S(2)}) collective-permute-start(bf16[256,1024]{1,0:T(8,128)(2,1)} %collective-permute-done.3.rest_0_.tok), channel_id=1, source_target_pairs={{0,8},{8,0},{16,24},{24,16},{1,9},{9,1},{17,25},{25,17},{2,10},{10... | collective-permute-start | bytes 1572872 | tf_op jit(solution)/shard_map/ppermute | solution.py:682
  35.9 0.5 collective-permute-done.1.rest_13_
  36.4 1.7 collective-permute-start.2
  38.1 0.8 collective-permute-done.2
  39.4 1.8 collective-permute-done.19.rest_4_
  41.2 2.9 %collective-permute-start.13 = (bf16[128,3072]{1,0:T(8,128)(2,1)S(1)}, bf16[128,3072]{1,0:T(8,128)(2,1)}, u32[]{:S(2)}, u32[]{:S(2)}) collective-permute-start(bf16[128,3072]{1,0:T(8,128)(2,1)S(1)} %collective-permute-done.rest_12_), channel_id=1, source_target_pairs={{0,8},{8,0},{16,24},{24,16},{1,9},{9,1},{17,25},{25,17},{2,10},{10... | collective-permute-start | bytes 2359304 | tf_op jit(solution)/shard_map/ppermute | solution.py:682
  44.3 0.5 collective-permute-start.11
  45.6 0.7 pad_add_fusion.1.tiles.info
  46.2 0.9 collective-permute-done.10.rest_10_
  47.3 0.6 collective-permute-done.11.rest_11_
  48.5 1.2 collective-permute-start.23
  49.7 0.6 collective-permute-start.20
  50.3 0.7 collective-permute-start.17
  50.9 17.1 %front.1 = (bf16[256,512]{1,0:T(8,128)(2,1)}, bf16[256,512]{1,0:T(8,128)(2,1)}, f32[512,512]{1,0:T(8,128)}, f32[8,512]{1,0:T(8,128)}, bf16[64,512]{1,0:T(8,128)(...) custom-call(s32[20]{0:T(128)} %stack.80.info, ...), custom_call_target="tpu_custom_call" | custom-call | flops 20000000000 | tf_op jit(solution)/shard_map/front/pallas_call | solution.py:270
  68.2 0.5 collective-permute-start.18
  68.8 7.2 %collective-permute-done.20.rest_5_ = bf16[64,5120]{1,0:T(8,128)(2,1)} collective-permute-done((bf16[64,5120]{1,0:T(8,128)(2,1)}, bf16[64,5120]{1,0:T(8,128)(2,1)}, u32[]{:S(2)}, u32[]{:S(2)}) %collective-permute-start.20) | collective-permute-done | bytes 655392 | tf_op jit(solution)/shard_map/ppermute | solution.py:685
  76.0 1.2 collective-permute-start.26
  77.8 1.5 collective-permute-done.26.rest_10_
  79.3 3.1 %collective-permute-start.28 = (bf16[256,1024]{1,0:T(8,128)(2,1)}, bf16[256,1024]{1,0:T(8,128)(2,1)S(1)}, u32[]{:S(2)}, u32[]{:S(2)}) collective-permute-start(bf16[256,1024]{1,0:T(8,128)(2,1)} %bitcast.37), channel_id=1, source_target_pairs={{0,0},{1,8},{2,2},{3,10},{4,4},{5,12},{6,6},{7,14},{8,1},{9,9},{10... | collective-permute-start | bytes 1572872 | tf_op jit(solution)/shard_map/ppermute | solution.py:713
  82.4 1.3 collective-permute-start.30
  83.7 0.7 collective-permute-start.32
  84.6 13.0 %up.1 = (f32[256,1024]{1,0:T(8,128)}, f32[256,1024]{1,0:T(8,128)}, f32[256,128]{1,0:T(8,128)}, bf16[256,4096]{1,0:T(8,128)(2,1)}, bf16[256,4096]{1,0:T(8,128)(2,1)}) custom-call(s32[20]{0:T(128)} %stack.80.info, bf16[256,512]{1,0:T(8,128)(2,1)} %get-tuple-element.87.own_att, bf16[256,512]{1,0:T(8,128)(2,1)} %copy-done.35, ...), custom_call_target="tpu_custom_call" | custom-call | flops 10000000000 | tf_op jit(solution)/shard_map/up/pallas_call | solution.py:583
  97.6 1.2 collective-permute-start.33
  98.8 1.0 collective-permute-done.31.rest_16_
  99.9 2.0 %collective-permute-start.34 = (bf16[256,1024]{1,0:T(8,128)(2,1)S(1)}, bf16[256,1024]{1,0:T(8,128)(2,1)S(1)}, u32[]{:S(2)}, u32[]{:S(2)}) collective-permute-start(bf16[256,1024]{1,0:T(8,128)(2,1)S(1)} %collective-permute-done.30.rest_15_), channel_id=1, source_target_pairs={{0,8},{8,0},{16,24},{24,16},{1,9},{9,1},{17,25},{25,17},{2,10},{10... | collective-permute-start | bytes 1572872 | tf_op jit(solution)/shard_map/ppermute | solution.py:682
  101.9 0.5 collective-permute-start.36
  102.4 1.0 collective-permute-done.34.rest_19_
  103.4 0.7 collective-permute-done.35.rest_20_
  104.2 0.7 collective-permute-done.36.rest_21_
  105.0 1.0 copy-done.9
  106.0 0.9 copy-done.25
  107.0 14.9 %down.1 = (bf16[256,1024]{1,0:T(8,128)(2,1)S(1)}, f32[256,1024]{1,0:T(8,128)}, bf16[256,512]{1,0:T(8,128)(2,1)S(1)}, bf16[256,512]{1,0:T(8,128)(2,1)S(1)}) custom-call(s32[20]{0:T(128)S(1)} %copy-done.5, f32[256,1024]{1,0:T(8,128)} %get-tuple-element.103.nrm_ref, f32[256,1024]{1,0:T(8,128)} %get-tuple-element.104.hat_ref, f32[256,128]{1,0:T(8,128)S(1)} %copy-done.25, ...), custom_call_target="tpu_custom_call" | custom-call | flops 16000000000 | tf_op jit(solution)/shard_map/down/pallas_call | solution.py:648
  122.3 2.2 %collective-permute-start.38 = (bf16[256,1024]{1,0:T(8,128)(2,1)S(1)}, bf16[256,1024]{1,0:T(8,128)(2,1)S(1)}, u32[]{:S(2)}, u32[]{:S(2)}) collective-permute-start(bf16[256,1024]{1,0:T(8,128)(2,1)S(1)} %get-tuple-element.125), channel_id=1, source_target_pairs={{0,0},{1,8},{2,2},{3,10},{4,4},{5,12},{6,6},{7,14},{8,1},{9,9},{10... | collective-permute-start | bytes 1572872 | tf_op jit(solution)/shard_map/ppermute | solution.py:713
  124.7 2.1 %prefix_grads.1 = (f32[128,512]{1,0:T(8,128)S(1)}, f32[512,512]{1,0:T(8,128)S(1)}, bf16[512,512]{1,0:T(8,128)(2,1)S(1)}, bf16[512,512]{1,0:T(8,128)(2,1)S(1)}, f32[8,512]{1,0:T(8,128)S(1)}) custom-call(s32[20]{0:T(128)S(1)} %copy-done.5, bf16[512,512]{1,0:T(8,128)(2,1)S(1)} %copy-done.15, bf16[512,512]{1,0:T(8,128)(2,1)S(1)} %copy-done.16, ...), custom_call_target="tpu_custom_call" | custom-call | flops 5000000000 | tf_op jit(solution)/shard_map/prefix_grads/pallas_call | solution.py:383
  126.9 1.3 collective-permute-start.39
  128.2 1.3 collective-permute-start.41
  129.6 5.0 %remote_grads.1 = (bf16[512,1024]{1,0:T(8,128)(2,1)S(1)}, bf16[256,1024]{1,0:T(8,128)(2,1)S(1)}, bf16[256,1024]{1,0:T(8,128)(2,1)S(1)}, f32[512,512]{1,0:T(8,128)S(1)}) custom-call(s32[6]{0:T(128)S(1)} %copy-done.4, s32[1,512]{1,0:T(1,128)S(1)} %bitcast.33, s32[1,512]{1,0:T(1,128)S(1)} %bitcast.30, bf16[512,512]{1,0:T(8,128)(2,1)S(1)} %copy-done.15, ...), custom_call_target="tpu_custom_call" | custom-call | flops 14000000000 | tf_op jit(solution)/shard_map/remote_grads/pallas_call | solution.py:439
  134.7 1.6 collective-permute-done.41
  136.3 3.9 %collective-permute-start.42 = (bf16[512,1024]{1,0:T(8,128)(2,1)S(1)}, bf16[512,1024]{1,0:T(8,128)(2,1)S(1)}, u32[]{:S(2)}, u32[]{:S(2)}) collective-permute-start(bf16[512,1024]{1,0:T(8,128)(2,1)S(1)} %get-tuple-element.129), channel_id=1, source_target_pairs={{0,8},{8,0},{16,24},{24,16},{1,9},{9,1},{17,25},{25,17},{2,10},{10... | collective-permute-start | bytes 3145736 | tf_op jit(solution)/shard_map/ppermute | solution.py:682
  140.2 2.3 %collective-permute-done.42 = bf16[512,1024]{1,0:T(8,128)(2,1)S(1)} collective-permute-done((bf16[512,1024]{1,0:T(8,128)(2,1)S(1)}, bf16[512,1024]{1,0:T(8,128)(2,1)S(1)}, u32[]{:S(2)}, u32[]{:S(2)}) %collective-permute-start.42) | collective-permute-done | bytes 1048608 | tf_op jit(solution)/shard_map/ppermute | solution.py:682
  142.9 2.4 %collective-permute-start.44 = (bf16[128,512]{1,0:T(8,128)(2,1)S(1)}, bf16[128,512]{1,0:T(8,128)(2,1)S(1)}, u32[]{:S(2)}, u32[]{:S(2)}) collective-permute-start(bf16[128,512]{1,0:T(8,128)(2,1)S(1)} %add_add_fusion.1), channel_id=1, source_target_pairs={{0,4},{1,5},{2,6},{3,7},{4,0},{5,1},{6,2},{7,3},{8,12},{9,13},{10,... | collective-permute-start | bytes 393224 | tf_op jit(solution)/shard_map/ppermute | solution.py:692
  145.6 1.0 collective-permute-start.45
  146.8 0.7 collective-permute-start.47
  147.5 8.7 %local_grads.1 = (f32[256,1024]{1,0:T(8,128)S(1)}, bf16[256,1024]{1,0:T(8,128)(2,1)S(1)}) custom-call(s32[6]{0:T(128)S(1)} %copy-done.4, s32[1,512]{1,0:T(1,128)S(1)} %bitcast.34, s32[1,512]{1,0:T(1,128)S(1)} %bitcast.31, bf16[512,512]{1,0:T(8,128)(2,1)S(1)} %copy-done.15, bf16[512,512]{1,0:T(8,128)(2,1)S(1)} %copy-done.16, ...), custom_call_target="tpu_custom_call" | custom-call | flops 14000000000 | tf_op jit(solution)/shard_map/local_grads/pallas_call | solution.py:505
  156.3 10.1 %collective-permute-done.46 = bf16[256,1024]{1,0:T(8,128)(2,1)S(1)} collective-permute-done((bf16[256,1024]{1,0:T(8,128)(2,1)S(1)}, bf16[256,1024]{1,0:T(8,128)(2,1)S(1)}, u32[]{:S(2)}, u32[]{:S(2)}) %collective-permute-start.46) | collective-permute-done | bytes 524320 | tf_op jit(solution)/shard_map/ppermute | solution.py:705
  166.4 1.4 collective-permute-start.48
  167.8 1.5 collective-permute-done.48
  169.7 1.9 %collective-permute-start.49 = (bf16[256,1024]{1,0:T(8,128)(2,1)S(1)}, bf16[256,1024]{1,0:T(8,128)(2,1)S(1)}, u32[]{:S(2)}, u32[]{:S(2)}) collective-permute-start(bf16[256,1024]{1,0:T(8,128)(2,1)S(1)} %add_convert_fusion), channel_id=1, source_target_pairs={{0,0},{1,8},{2,2},{3,10},{4,4},{5,12},{6,6},{7,14},{8,1},{9,9},{10... | collective-permute-start | bytes 1572872 | tf_op jit(solution)/shard_map/ppermute | solution.py:713
  171.7 0.8 pad_maximum_fusion
  172.5 7.7 %collective-permute-done.49 = bf16[256,1024]{1,0:T(8,128)(2,1)S(1)} collective-permute-done((bf16[256,1024]{1,0:T(8,128)(2,1)S(1)}, bf16[256,1024]{1,0:T(8,128)(2,1)S(1)}, u32[]{:S(2)}, u32[]{:S(2)}) %collective-permute-start.49) | collective-permute-done | bytes 524320 | tf_op jit(solution)/shard_map/ppermute | solution.py:713
  180.2 0.8 copy.28
  181.0 0.8 copy.29
  (142 shorter events, 5.4 us)
Async XLA Ops:
  4.4 19.7 %collective-permute-start = (bf16[128,3072]{1,0:T(8,128)(2,1)}, bf16[128,3072]{1,0:T(8,128)(2,1)S(1)}, u32[]{:S(2)}, u32[]{:S(2)}) collective-permute-start(bf16[128,3072]{1,0:T(8,128)(2,1)} %get-tuple-element.74), channel_id=1, source_target_pairs={{0,16},{8,24},{16,0},{24,8},{1,17},{9,25},{17,1},{25,9},{2,18},{10... | collective-permute-start | bytes 2359304 | tf_op jit(solution)/shard_map/ppermute | solution.py:685
  6.6 20.1 %collective-permute-start.5 = (bf16[256,1024]{1,0:T(8,128)(2,1)}, bf16[256,1024]{1,0:T(8,128)(2,1)}, u32[]{:S(2)}, u32[]{:S(2)}) collective-permute-start(bf16[256,1024]{1,0:T(8,128)(2,1)} %bitcast.22), channel_id=1, source_target_pairs={{0,0},{1,8},{2,4},{3,12},{4,2},{5,10},{6,6},{7,14},{8,1},{9,9},{10... | collective-permute-start | bytes 1572872 | tf_op jit(solution)/shard_map/ppermute | solution.py:713
  10.5 20.9 %collective-permute-start.4 = (bf16[256,1024]{1,0:T(8,128)(2,1)}, bf16[256,1024]{1,0:T(8,128)(2,1)}, u32[]{:S(2)}, u32[]{:S(2)}) collective-permute-start(bf16[256,1024]{1,0:T(8,128)(2,1)} %bitcast.22), channel_id=1, source_target_pairs={{0,2},{1,10},{2,0},{3,8},{4,6},{5,14},{6,4},{7,12},{8,3},{9,11},{1... | collective-permute-start | bytes 1572872 | tf_op jit(solution)/shard_map/ppermute | solution.py:713
  12.3 21.4 %collective-permute-start.3 = (bf16[256,1024]{1,0:T(8,128)(2,1)}, bf16[256,1024]{1,0:T(8,128)(2,1)}, u32[]{:S(2)}, u32[]{:S(2)}) collective-permute-start(bf16[256,1024]{1,0:T(8,128)(2,1)} %bitcast.22), channel_id=1, source_target_pairs={{0,0},{1,8},{2,2},{3,10},{4,4},{5,12},{6,6},{7,14},{8,1},{9,9},{10... | collective-permute-start | bytes 1572872 | tf_op jit(solution)/shard_map/ppermute | solution.py:713
  24.2 9.7 %collective-permute-start.12 = (bf16[64,3072]{1,0:T(8,128)(2,1)S(1)}, bf16[64,3072]{1,0:T(8,128)(2,1)}, u32[]{:S(2)}, u32[]{:S(2)}) collective-permute-start(bf16[64,3072]{1,0:T(8,128)(2,1)S(1)} %constant_dynamic-slice_fusion), channel_id=1, source_target_pairs={{0,2},{1,3},{2,0},{3,1},{4,6},{5,7},{6,4},{7,5},{8,10},{9,11},{10,... | collective-permute-start | bytes 1179656 | tf_op jit(solution)/shard_map/ppermute | solution.py:688
  25.5 10.9 %collective-permute-start.1 = (bf16[64,3072]{1,0:T(8,128)(2,1)S(1)}, bf16[64,3072]{1,0:T(8,128)(2,1)}, u32[]{:S(2)}, u32[]{:S(2)}) collective-permute-start(bf16[64,3072]{1,0:T(8,128)(2,1)S(1)} %constant_dynamic-slice_fusion), channel_id=1, source_target_pairs={{0,1},{1,0},{2,3},{3,2},{4,5},{5,4},{6,7},{7,6},{8,9},{9,8},{10,11... | collective-permute-start | bytes 1179656 | tf_op jit(solution)/shard_map/ppermute | solution.py:688
  26.7 14.5 %collective-permute-start.19 = (bf16[64,5120]{1,0:T(8,128)(2,1)}, bf16[64,5120]{1,0:T(8,128)(2,1)}, u32[]{:S(2)}, u32[]{:S(2)}) collective-permute-start(bf16[64,5120]{1,0:T(8,128)(2,1)} %get-tuple-element.91), channel_id=1, source_target_pairs={{0,16},{8,24},{16,0},{24,8},{1,17},{9,25},{17,1},{25,9},{2,18},{10... | collective-permute-start | bytes 1966088 | tf_op jit(solution)/shard_map/ppermute | solution.py:685
  27.9 22.3 %copy-start.29 = (bf16[256,4096]{1,0:T(8,128)(2,1)S(1)}, bf16[256,4096]{1,0:T(8,128)(2,1)}, u32[]{:S(2)}) copy-start(bf16[256,4096]{1,0:T(8,128)(2,1)} %rest_0_.7) | copy-start | bytes 6291460
  31.4 12.8 %collective-permute-start.8 = (bf16[256,1024]{1,0:T(8,128)(2,1)}, bf16[256,1024]{1,0:T(8,128)(2,1)}, u32[]{:S(2)}, u32[]{:S(2)}) collective-permute-start(bf16[256,1024]{1,0:T(8,128)(2,1)} %collective-permute-done.5.rest_2_), channel_id=1, source_target_pairs={{0,8},{8,0},{16,24},{24,16},{1,9},{9,1},{17,25},{25,17},{2,10},{10... | collective-permute-start | bytes 1572872 | tf_op jit(solution)/shard_map/ppermute | solution.py:682
  33.8 10.5 %collective-permute-start.7 = (bf16[256,1024]{1,0:T(8,128)(2,1)}, bf16[256,1024]{1,0:T(8,128)(2,1)}, u32[]{:S(2)}, u32[]{:S(2)}) collective-permute-start(bf16[256,1024]{1,0:T(8,128)(2,1)} %collective-permute-done.4.rest_1_), channel_id=1, source_target_pairs={{0,8},{8,0},{16,24},{24,16},{1,9},{9,1},{17,25},{25,17},{2,10},{10... | collective-permute-start | bytes 1572872 | tf_op jit(solution)/shard_map/ppermute | solution.py:682
  33.9 11.0 %collective-permute-start.6 = (bf16[256,1024]{1,0:T(8,128)(2,1)}, bf16[256,1024]{1,0:T(8,128)(2,1)}, u32[]{:S(2)}, u32[]{:S(2)}) collective-permute-start(bf16[256,1024]{1,0:T(8,128)(2,1)} %collective-permute-done.3.rest_0_.tok), channel_id=1, source_target_pairs={{0,8},{8,0},{16,24},{24,16},{1,9},{9,1},{17,25},{25,17},{2,10},{10... | collective-permute-start | bytes 1572872 | tf_op jit(solution)/shard_map/ppermute | solution.py:682
  36.4 2.5 %collective-permute-start.2 = (s32[1,8]{1,0:T(1,128)S(1)}, s32[1,8]{1,0:T(1,128)S(1)}, u32[]{:S(2)}, u32[]{:S(2)}) collective-permute-start(s32[1,8]{1,0:T(1,128)S(1)} %copy-done.28), channel_id=1, source_target_pairs={{0,8},{8,0},{16,24},{24,16},{1,9},{9,1},{17,25},{25,17},{2,10},{10... | collective-permute-start | bytes 104 | tf_op jit(solution)/shard_map/ppermute | solution.py:682
  38.9 6.1 %collective-permute-start.9 = (bf16[256,1024]{1,0:T(8,128)(2,1)}, bf16[256,1024]{1,0:T(8,128)(2,1)}, u32[]{:S(2)}, u32[]{:S(2)}) collective-permute-start(bf16[256,1024]{1,0:T(8,128)(2,1)} %rest_6_.1), channel_id=1, source_target_pairs={{0,8},{8,0},{16,24},{24,16},{1,9},{9,1},{17,25},{25,17},{2,10},{10... | collective-permute-start | bytes 1572872 | tf_op jit(solution)/shard_map/ppermute | solution.py:682
  41.2 9.0 %collective-permute-start.13 = (bf16[128,3072]{1,0:T(8,128)(2,1)S(1)}, bf16[128,3072]{1,0:T(8,128)(2,1)}, u32[]{:S(2)}, u32[]{:S(2)}) collective-permute-start(bf16[128,3072]{1,0:T(8,128)(2,1)S(1)} %collective-permute-done.rest_12_), channel_id=1, source_target_pairs={{0,8},{8,0},{16,24},{24,16},{1,9},{9,1},{17,25},{25,17},{2,10},{10... | collective-permute-start | bytes 2359304 | tf_op jit(solution)/shard_map/ppermute | solution.py:682
  44.2 2.9 %collective-permute-start.10 = (bf16[256,1024]{1,0:T(8,128)(2,1)}, bf16[256,1024]{1,0:T(8,128)(2,1)}, u32[]{:S(2)}, u32[]{:S(2)}) collective-permute-start(bf16[256,1024]{1,0:T(8,128)(2,1)} %rest_7_.1), channel_id=1, source_target_pairs={{0,8},{8,0},{16,24},{24,16},{1,9},{9,1},{17,25},{25,17},{2,10},{10... | collective-permute-start | bytes 1572872 | tf_op jit(solution)/shard_map/ppermute | solution.py:682
  44.3 3.6 %collective-permute-start.11 = (bf16[256,1024]{1,0:T(8,128)(2,1)}, bf16[256,1024]{1,0:T(8,128)(2,1)}, u32[]{:S(2)}, u32[]{:S(2)}) collective-permute-start(bf16[256,1024]{1,0:T(8,128)(2,1)} %rest_8_.1), channel_id=1, source_target_pairs={{0,8},{8,0},{16,24},{24,16},{1,9},{9,1},{17,25},{25,17},{2,10},{10... | collective-permute-start | bytes 1572872 | tf_op jit(solution)/shard_map/ppermute | solution.py:682
  44.9 3.6 %collective-permute-start.15 = (bf16[64,3072]{1,0:T(8,128)(2,1)}, bf16[64,3072]{1,0:T(8,128)(2,1)}, u32[]{:S(2)}, u32[]{:S(2)}) collective-permute-start(bf16[64,3072]{1,0:T(8,128)(2,1)} %collective-permute-done.12.rest_14_), channel_id=1, source_target_pairs={{0,8},{8,0},{16,24},{24,16},{1,9},{9,1},{17,25},{25,17},{2,10},{10... | collective-permute-start | bytes 1179656 | tf_op jit(solution)/shard_map/ppermute | solution.py:682
  45.0 4.7 %collective-permute-start.14 = (bf16[64,3072]{1,0:T(8,128)(2,1)}, bf16[64,3072]{1,0:T(8,128)(2,1)}, u32[]{:S(2)}, u32[]{:S(2)}) collective-permute-start(bf16[64,3072]{1,0:T(8,128)(2,1)} %collective-permute-done.1.rest_13_), channel_id=1, source_target_pairs={{0,8},{8,0},{16,24},{24,16},{1,9},{9,1},{17,25},{25,17},{2,10},{10... | collective-permute-start | bytes 1179656 | tf_op jit(solution)/shard_map/ppermute | solution.py:682
  47.1 21.1 %collective-permute-start.22 = (bf16[64,5120]{1,0:T(8,128)(2,1)}, bf16[64,5120]{1,0:T(8,128)(2,1)S(1)}, u32[]{:S(2)}, u32[]{:S(2)}) collective-permute-start(bf16[64,5120]{1,0:T(8,128)(2,1)} %collective-permute-done.19.rest_4_), channel_id=1, source_target_pairs={{0,2},{1,3},{2,0},{3,1},{4,6},{5,7},{6,4},{7,5},{8,10},{9,11},{10,... | collective-permute-start | bytes 1966088 | tf_op jit(solution)/shard_map/ppermute | solution.py:688
  47.9 20.8 %collective-permute-start.21 = (bf16[64,5120]{1,0:T(8,128)(2,1)}, bf16[64,5120]{1,0:T(8,128)(2,1)}, u32[]{:S(2)}, u32[]{:S(2)}) collective-permute-start(bf16[64,5120]{1,0:T(8,128)(2,1)} %collective-permute-done.19.rest_4_), channel_id=1, source_target_pairs={{0,1},{1,0},{2,3},{3,2},{4,5},{5,4},{6,7},{7,6},{8,9},{9,8},{10,11... | collective-permute-start | bytes 1966088 | tf_op jit(solution)/shard_map/ppermute | solution.py:688
  48.5 19.6 %collective-permute-start.23 = (bf16[256,1024]{1,0:T(8,128)(2,1)}, bf16[256,1024]{1,0:T(8,128)(2,1)S(1)}, u32[]{:S(2)}, u32[]{:S(2)}) collective-permute-start(bf16[256,1024]{1,0:T(8,128)(2,1)} %get-tuple-element.96), channel_id=1, source_target_pairs={{0,16},{8,24},{16,0},{24,8},{1,17},{9,25},{17,1},{25,9},{2,18},{10... | collective-permute-start | bytes 1572872 | tf_op jit(solution)/shard_map/ppermute | solution.py:685
  49.7 26.3 %collective-permute-start.20 = (bf16[64,5120]{1,0:T(8,128)(2,1)}, bf16[64,5120]{1,0:T(8,128)(2,1)}, u32[]{:S(2)}, u32[]{:S(2)}) collective-permute-start(bf16[64,5120]{1,0:T(8,128)(2,1)} %get-tuple-element.94), channel_id=1, source_target_pairs={{0,16},{8,24},{16,0},{24,8},{1,17},{9,25},{17,1},{25,9},{2,18},{10... | collective-permute-start | bytes 1966088 | tf_op jit(solution)/shard_map/ppermute | solution.py:685
  50.3 34.1 %collective-permute-start.17 = (bf16[256,4096]{1,0:T(8,128)(2,1)S(1)}, bf16[256,4096]{1,0:T(8,128)(2,1)}, u32[]{:S(2)}, u32[]{:S(2)}) collective-permute-start(bf16[256,4096]{1,0:T(8,128)(2,1)S(1)} %copy-done.29), channel_id=1, source_target_pairs={{0,8},{8,0},{16,24},{24,16},{1,9},{9,1},{17,25},{25,17},{2,10},{10... | collective-permute-start | bytes 6291464 | tf_op jit(solution)/shard_map/ppermute | solution.py:682
  68.1 9.6 %collective-permute-start.24 = (bf16[64,5120]{1,0:T(8,128)(2,1)}, bf16[64,5120]{1,0:T(8,128)(2,1)S(1)}, u32[]{:S(2)}, u32[]{:S(2)}) collective-permute-start(bf16[64,5120]{1,0:T(8,128)(2,1)} %collective-permute-done.19.rest_4_), channel_id=1, source_target_pairs={{0,8},{8,0},{16,24},{24,16},{1,9},{9,1},{17,25},{25,17},{2,10},{10... | collective-permute-start | bytes 1966088 | tf_op jit(solution)/shard_map/ppermute | solution.py:682
  68.2 8.9 %collective-permute-start.18 = (bf16[256,1024]{1,0:T(8,128)(2,1)S(1)}, bf16[256,1024]{1,0:T(8,128)(2,1)S(1)}, u32[]{:S(2)}, u32[]{:S(2)}) collective-permute-start(bf16[256,1024]{1,0:T(8,128)(2,1)S(1)} %copy-done.6), channel_id=1, source_target_pairs={{0,8},{8,0},{16,24},{24,16},{1,9},{9,1},{17,25},{25,17},{2,10},{10... | collective-permute-start | bytes 1572872 | tf_op jit(solution)/shard_map/ppermute | solution.py:682
  68.7 8.5 %collective-permute-start.16 = (bf16[256,512]{1,0:T(8,128)(2,1)}, bf16[256,512]{1,0:T(8,128)(2,1)S(1)}, u32[]{:S(2)}, u32[]{:S(2)}) collective-permute-start(bf16[256,512]{1,0:T(8,128)(2,1)} %get-tuple-element.88), channel_id=1, source_target_pairs={{0,8},{8,0},{16,24},{24,16},{1,9},{9,1},{17,25},{25,17},{2,10},{10... | collective-permute-start | bytes 786440 | tf_op jit(solution)/shard_map/ppermute | solution.py:682
  76.0 3.3 %collective-permute-start.26 = (bf16[64,5120]{1,0:T(8,128)(2,1)}, bf16[64,5120]{1,0:T(8,128)(2,1)S(1)}, u32[]{:S(2)}, u32[]{:S(2)}) collective-permute-start(bf16[64,5120]{1,0:T(8,128)(2,1)} %collective-permute-done.21.rest_6_), channel_id=1, source_target_pairs={{0,8},{8,0},{16,24},{24,16},{1,9},{9,1},{17,25},{25,17},{2,10},{10... | collective-permute-start | bytes 1966088 | tf_op jit(solution)/shard_map/ppermute | solution.py:682
  77.2 5.2 %collective-permute-start.27 = (bf16[64,5120]{1,0:T(8,128)(2,1)S(1)}, bf16[64,5120]{1,0:T(8,128)(2,1)S(1)}, u32[]{:S(2)}, u32[]{:S(2)}) collective-permute-start(bf16[64,5120]{1,0:T(8,128)(2,1)S(1)} %collective-permute-done.22.rest_7_), channel_id=1, source_target_pairs={{0,8},{8,0},{16,24},{24,16},{1,9},{9,1},{17,25},{25,17},{2,10},{10... | collective-permute-start | bytes 1966088 | tf_op jit(solution)/shard_map/ppermute | solution.py:682
  77.2 6.4 %collective-permute-start.25 = (bf16[64,5120]{1,0:T(8,128)(2,1)}, bf16[64,5120]{1,0:T(8,128)(2,1)S(1)}, u32[]{:S(2)}, u32[]{:S(2)}) collective-permute-start(bf16[64,5120]{1,0:T(8,128)(2,1)} %collective-permute-done.20.rest_5_), channel_id=1, source_target_pairs={{0,8},{8,0},{16,24},{24,16},{1,9},{9,1},{17,25},{25,17},{2,10},{10... | collective-permute-start | bytes 1966088 | tf_op jit(solution)/shard_map/ppermute | solution.py:682
  77.7 24.7 %collective-permute-start.29 = (bf16[1024,1024]{1,0:T(8,128)(2,1)}, bf16[1024,1024]{1,0:T(8,128)(2,1)}, u32[]{:S(2)}, u32[]{:S(2)}) collective-permute-start(bf16[1024,1024]{1,0:T(8,128)(2,1)} %rest_12_.1), channel_id=1, source_target_pairs={{0,8},{8,0},{16,24},{24,16},{1,9},{9,1},{17,25},{25,17},{2,10},{10... | collective-permute-start | bytes 6291464 | tf_op jit(solution)/shard_map/ppermute | solution.py:682
  79.3 18.4 %collective-permute-start.28 = (bf16[256,1024]{1,0:T(8,128)(2,1)}, bf16[256,1024]{1,0:T(8,128)(2,1)S(1)}, u32[]{:S(2)}, u32[]{:S(2)}) collective-permute-start(bf16[256,1024]{1,0:T(8,128)(2,1)} %bitcast.37), channel_id=1, source_target_pairs={{0,0},{1,8},{2,2},{3,10},{4,4},{5,12},{6,6},{7,14},{8,1},{9,9},{10... | collective-permute-start | bytes 1572872 | tf_op jit(solution)/shard_map/ppermute | solution.py:713
  82.4 17.5 %collective-permute-start.30 = (bf16[256,1024]{1,0:T(8,128)(2,1)}, bf16[256,1024]{1,0:T(8,128)(2,1)S(1)}, u32[]{:S(2)}, u32[]{:S(2)}) collective-permute-start(bf16[256,1024]{1,0:T(8,128)(2,1)} %get-tuple-element.112), channel_id=1, source_target_pairs={{0,16},{8,24},{16,0},{24,8},{1,17},{9,25},{17,1},{25,9},{2,18},{10... | collective-permute-start | bytes 1572872 | tf_op jit(solution)/shard_map/ppermute | solution.py:685
  83.7 15.2 %collective-permute-start.32 = (bf16[256,1024]{1,0:T(8,128)(2,1)S(1)}, bf16[256,1024]{1,0:T(8,128)(2,1)S(1)}, u32[]{:S(2)}, u32[]{:S(2)}) collective-permute-start(bf16[256,1024]{1,0:T(8,128)(2,1)S(1)} %collective-permute-done.23.rest_14_), channel_id=1, source_target_pairs={{0,2},{1,3},{2,0},{3,1},{4,6},{5,7},{6,4},{7,5},{8,10},{9,11},{10,... | collective-permute-start | bytes 1572872 | tf_op jit(solution)/shard_map/ppermute | solution.py:688
  84.4 15.5 %collective-permute-start.31 = (bf16[256,1024]{1,0:T(8,128)(2,1)S(1)}, bf16[256,1024]{1,0:T(8,128)(2,1)S(1)}, u32[]{:S(2)}, u32[]{:S(2)}) collective-permute-start(bf16[256,1024]{1,0:T(8,128)(2,1)S(1)} %collective-permute-done.23.rest_14_), channel_id=1, source_target_pairs={{0,1},{1,0},{2,3},{3,2},{4,5},{5,4},{6,7},{7,6},{8,9},{9,8},{10,11... | collective-permute-start | bytes 1572872 | tf_op jit(solution)/shard_map/ppermute | solution.py:688
  84.6 20.4 %copy-start.5 = (s32[20]{0:T(128)S(1)}, s32[20]{0:T(128)}, u32[]{:S(2)}) copy-start(s32[20]{0:T(128)} %stack.80.info) | copy-start | bytes 244
  84.6 20.4 %copy-start.7 = (bf16[256,1024]{1,0:T(8,128)(2,1)S(1)}, bf16[256,1024]{1,0:T(8,128)(2,1)}, u32[]{:S(2)}) copy-start(bf16[256,1024]{1,0:T(8,128)(2,1)} %rest_1_.7) | copy-start | bytes 1572868
  84.6 20.4 %copy-start.10 = (bf16[1024]{0:T(1024)(128)(2,1)S(1)}, bf16[1024]{0:T(1024)(128)(2,1)}, u32[]{:S(2)}) copy-start(bf16[1024]{0:T(1024)(128)(2,1)} %ga.3) | copy-start | bytes 6148
  84.6 20.4 %copy-start.11 = (bf16[1024]{0:T(1024)(128)(2,1)S(1)}, bf16[1024]{0:T(1024)(128)(2,1)}, u32[]{:S(2)}) copy-start(bf16[1024]{0:T(1024)(128)(2,1)} %bd.1) | copy-start | bytes 6148
  84.6 20.4 %copy-start.12 = (bf16[1024]{0:T(1024)(128)(2,1)S(1)}, bf16[1024]{0:T(1024)(128)(2,1)}, u32[]{:S(2)}) copy-start(bf16[1024]{0:T(1024)(128)(2,1)} %gf.1) | copy-start | bytes 6148
  84.6 20.4 %copy-start.13 = (bf16[1024]{0:T(1024)(128)(2,1)S(1)}, bf16[1024]{0:T(1024)(128)(2,1)}, u32[]{:S(2)}) copy-start(bf16[1024]{0:T(1024)(128)(2,1)} %sf.1) | copy-start | bytes 6148
  97.6 4.8 %collective-permute-start.33 = (bf16[256,1024]{1,0:T(8,128)(2,1)S(1)}, bf16[256,1024]{1,0:T(8,128)(2,1)S(1)}, u32[]{:S(2)}, u32[]{:S(2)}) collective-permute-start(bf16[256,1024]{1,0:T(8,128)(2,1)S(1)} %collective-permute-done.23.rest_14_), channel_id=1, source_target_pairs={{0,8},{8,0},{16,24},{24,16},{1,9},{9,1},{17,25},{25,17},{2,10},{10... | collective-permute-start | bytes 1572872 | tf_op jit(solution)/shard_map/ppermute | solution.py:682
  99.9 3.5 %collective-permute-start.34 = (bf16[256,1024]{1,0:T(8,128)(2,1)S(1)}, bf16[256,1024]{1,0:T(8,128)(2,1)S(1)}, u32[]{:S(2)}, u32[]{:S(2)}) collective-permute-start(bf16[256,1024]{1,0:T(8,128)(2,1)S(1)} %collective-permute-done.30.rest_15_), channel_id=1, source_target_pairs={{0,8},{8,0},{16,24},{24,16},{1,9},{9,1},{17,25},{25,17},{2,10},{10... | collective-permute-start | bytes 1572872 | tf_op jit(solution)/shard_map/ppermute | solution.py:682
  101.9 2.3 %collective-permute-start.35 = (bf16[256,1024]{1,0:T(8,128)(2,1)S(1)}, bf16[256,1024]{1,0:T(8,128)(2,1)S(1)}, u32[]{:S(2)}, u32[]{:S(2)}) collective-permute-start(bf16[256,1024]{1,0:T(8,128)(2,1)S(1)} %collective-permute-done.31.rest_16_), channel_id=1, source_target_pairs={{0,8},{8,0},{16,24},{24,16},{1,9},{9,1},{17,25},{25,17},{2,10},{10... | collective-permute-start | bytes 1572872 | tf_op jit(solution)/shard_map/ppermute | solution.py:682
  101.9 3.0 %collective-permute-start.36 = (bf16[256,1024]{1,0:T(8,128)(2,1)S(1)}, bf16[256,1024]{1,0:T(8,128)(2,1)S(1)}, u32[]{:S(2)}, u32[]{:S(2)}) collective-permute-start(bf16[256,1024]{1,0:T(8,128)(2,1)S(1)} %collective-permute-done.32.rest_17_), channel_id=1, source_target_pairs={{0,8},{8,0},{16,24},{24,16},{1,9},{9,1},{17,25},{25,17},{2,10},{10... | collective-permute-start | bytes 1572872 | tf_op jit(solution)/shard_map/ppermute | solution.py:682
  106.9 17.6 %copy-start.15 = (bf16[512,512]{1,0:T(8,128)(2,1)S(1)}, bf16[512,512]{1,0:T(8,128)(2,1)}, u32[]{:S(2)}) copy-start(bf16[512,512]{1,0:T(8,128)(2,1)} %get-tuple-element.79.q_ref) | copy-start | bytes 1572868
  106.9 17.6 %copy-start.16 = (bf16[512,512]{1,0:T(8,128)(2,1)S(1)}, bf16[512,512]{1,0:T(8,128)(2,1)}, u32[]{:S(2)}) copy-start(bf16[512,512]{1,0:T(8,128)(2,1)} %get-tuple-element.80.qt_ref) | copy-start | bytes 1572868
  106.9 17.7 %copy-start.22 = (bf16[512,64]{1,0:T(8,128)(2,1)S(1)}, bf16[512,64]{1,0:T(8,128)(2,1)}, u32[]{:S(2)}) copy-start(bf16[512,64]{1,0:T(8,128)(2,1)} %get-tuple-element.85.pkt_ref) | copy-start | bytes 196612
  106.9 17.7 %copy-start.23 = (bf16[64,512]{1,0:T(8,128)(2,1)S(1)}, bf16[64,512]{1,0:T(8,128)(2,1)}, u32[]{:S(2)}) copy-start(bf16[64,512]{1,0:T(8,128)(2,1)} %get-tuple-element.84.pk_ref) | copy-start | bytes 196612
  106.9 17.7 %copy-start.24 = (bf16[64,512]{1,0:T(8,128)(2,1)S(1)}, bf16[64,512]{1,0:T(8,128)(2,1)}, u32[]{:S(2)}) copy-start(bf16[64,512]{1,0:T(8,128)(2,1)} %get-tuple-element.86.pv_ref) | copy-start | bytes 196612
  106.9 17.7 %copy-start.26 = (f32[8,512]{1,0:T(8,128)S(1)}, f32[8,512]{1,0:T(8,128)}, u32[]{:S(2)}) copy-start(f32[8,512]{1,0:T(8,128)} %get-tuple-element.98.lse_ref) | copy-start | bytes 49156
  121.9 2.7 %collective-permute-start.37 = (bf16[256,512]{1,0:T(8,128)(2,1)S(1)}, bf16[256,512]{1,0:T(8,128)(2,1)S(1)}, u32[]{:S(2)}, u32[]{:S(2)}) collective-permute-start(bf16[256,512]{1,0:T(8,128)(2,1)S(1)} %get-tuple-element.117), channel_id=1, source_target_pairs={{0,8},{8,0},{16,24},{24,16},{1,9},{9,1},{17,25},{25,17},{2,10},{10... | collective-permute-start | bytes 786440 | tf_op jit(solution)/shard_map/ppermute | solution.py:682
  122.3 14.0 %collective-permute-start.38 = (bf16[256,1024]{1,0:T(8,128)(2,1)S(1)}, bf16[256,1024]{1,0:T(8,128)(2,1)S(1)}, u32[]{:S(2)}, u32[]{:S(2)}) collective-permute-start(bf16[256,1024]{1,0:T(8,128)(2,1)S(1)} %get-tuple-element.125), channel_id=1, source_target_pairs={{0,0},{1,8},{2,2},{3,10},{4,4},{5,12},{6,6},{7,14},{8,1},{9,9},{10... | collective-permute-start | bytes 1572872 | tf_op jit(solution)/shard_map/ppermute | solution.py:713
  126.9 7.8 %collective-permute-start.40 = (bf16[128,512]{1,0:T(8,128)(2,1)S(1)}, bf16[128,512]{1,0:T(8,128)(2,1)S(1)}, u32[]{:S(2)}, u32[]{:S(2)}) collective-permute-start(bf16[128,512]{1,0:T(8,128)(2,1)S(1)} %convert_element_type.60), channel_id=1, source_target_pairs={{0,1},{1,0},{2,3},{3,2},{4,5},{5,4},{6,7},{7,6},{8,9},{9,8},{10,11... | collective-permute-start | bytes 393224 | tf_op jit(solution)/shard_map/ppermute | solution.py:692
  126.9 7.7 %collective-permute-start.39 = (bf16[128,512]{1,0:T(8,128)(2,1)S(1)}, bf16[128,512]{1,0:T(8,128)(2,1)S(1)}, u32[]{:S(2)}, u32[]{:S(2)}) collective-permute-start(bf16[128,512]{1,0:T(8,128)(2,1)S(1)} %convert_element_type.60), channel_id=1, source_target_pairs={{0,16},{1,17},{2,18},{3,19},{4,20},{5,21},{6,22},{7,23},{8,24},{9,... | collective-permute-start | bytes 393224 | tf_op jit(solution)/shard_map/ppermute | solution.py:692
  128.2 8.0 %collective-permute-start.41 = (bf16[128,512]{1,0:T(8,128)(2,1)S(1)}, bf16[128,512]{1,0:T(8,128)(2,1)S(1)}, u32[]{:S(2)}, u32[]{:S(2)}) collective-permute-start(bf16[128,512]{1,0:T(8,128)(2,1)S(1)} %convert_element_type.60), channel_id=1, source_target_pairs={{0,17},{1,16},{2,19},{3,18},{4,21},{5,20},{6,23},{7,22},{8,25},{9,... | collective-permute-start | bytes 393224 | tf_op jit(solution)/shard_map/ppermute | solution.py:692
  136.3 6.2 %collective-permute-start.42 = (bf16[512,1024]{1,0:T(8,128)(2,1)S(1)}, bf16[512,1024]{1,0:T(8,128)(2,1)S(1)}, u32[]{:S(2)}, u32[]{:S(2)}) collective-permute-start(bf16[512,1024]{1,0:T(8,128)(2,1)S(1)} %get-tuple-element.129), channel_id=1, source_target_pairs={{0,8},{8,0},{16,24},{24,16},{1,9},{9,1},{17,25},{25,17},{2,10},{10... | collective-permute-start | bytes 3145736 | tf_op jit(solution)/shard_map/ppermute | solution.py:682
  142.9 13.3 %collective-permute-start.44 = (bf16[128,512]{1,0:T(8,128)(2,1)S(1)}, bf16[128,512]{1,0:T(8,128)(2,1)S(1)}, u32[]{:S(2)}, u32[]{:S(2)}) collective-permute-start(bf16[128,512]{1,0:T(8,128)(2,1)S(1)} %add_add_fusion.1), channel_id=1, source_target_pairs={{0,4},{1,5},{2,6},{3,7},{4,0},{5,1},{6,2},{7,3},{8,12},{9,13},{10,... | collective-permute-start | bytes 393224 | tf_op jit(solution)/shard_map/ppermute | solution.py:692
  145.3 10.9 %collective-permute-start.43 = (bf16[128,512]{1,0:T(8,128)(2,1)S(1)}, bf16[128,512]{1,0:T(8,128)(2,1)S(1)}, u32[]{:S(2)}, u32[]{:S(2)}) collective-permute-start(bf16[128,512]{1,0:T(8,128)(2,1)S(1)} %add_add_fusion.1), channel_id=1, source_target_pairs={{0,2},{1,3},{2,0},{3,1},{4,6},{5,7},{6,4},{7,5},{8,10},{9,11},{10,... | collective-permute-start | bytes 393224 | tf_op jit(solution)/shard_map/ppermute | solution.py:692
  145.6 10.6 %collective-permute-start.45 = (bf16[128,512]{1,0:T(8,128)(2,1)S(1)}, bf16[128,512]{1,0:T(8,128)(2,1)S(1)}, u32[]{:S(2)}, u32[]{:S(2)}) collective-permute-start(bf16[128,512]{1,0:T(8,128)(2,1)S(1)} %add_add_fusion.1), channel_id=1, source_target_pairs={{0,6},{1,7},{2,4},{3,5},{4,2},{5,3},{6,0},{7,1},{8,14},{9,15},{10,... | collective-permute-start | bytes 393224 | tf_op jit(solution)/shard_map/ppermute | solution.py:692
  146.6 19.9 %collective-permute-start.46 = (bf16[256,1024]{1,0:T(8,128)(2,1)S(1)}, bf16[256,1024]{1,0:T(8,128)(2,1)S(1)}, u32[]{:S(2)}, u32[]{:S(2)}) collective-permute-start(bf16[256,1024]{1,0:T(8,128)(2,1)S(1)} %get-tuple-element.136), channel_id=1, source_target_pairs={{0,2},{1,3},{2,0},{3,1},{4,6},{5,7},{6,4},{7,5},{8,10},{9,11},{10,... | collective-permute-start | bytes 1572872 | tf_op jit(solution)/shard_map/ppermute | solution.py:705
  146.8 9.5 %collective-permute-start.47 = (bf16[256,1024]{1,0:T(8,128)(2,1)S(1)}, bf16[256,1024]{1,0:T(8,128)(2,1)S(1)}, u32[]{:S(2)}, u32[]{:S(2)}) collective-permute-start(bf16[256,1024]{1,0:T(8,128)(2,1)S(1)} %get-tuple-element.139), channel_id=1, source_target_pairs={{0,0},{1,1},{2,4},{3,5},{4,2},{5,3},{6,6},{7,7},{8,8},{9,9},{10,12... | collective-permute-start | bytes 1572872 | tf_op jit(solution)/shard_map/ppermute | solution.py:705
  166.4 2.9 %collective-permute-start.48 = (bf16[256,1024]{1,0:T(8,128)(2,1)S(1)}, bf16[256,1024]{1,0:T(8,128)(2,1)S(1)}, u32[]{:S(2)}, u32[]{:S(2)}) collective-permute-start(bf16[256,1024]{1,0:T(8,128)(2,1)S(1)} %get-tuple-element.141), channel_id=1, source_target_pairs={{0,8},{8,0},{16,24},{24,16},{1,9},{9,1},{17,25},{25,17},{2,10},{10... | collective-permute-start | bytes 1572872 | tf_op jit(solution)/shard_map/ppermute | solution.py:682
  167.8 3.8 %collective-permute-start.50 = (f32[128,512]{1,0:T(8,128)S(1)}, f32[128,512]{1,0:T(8,128)S(1)}, u32[]{:S(2)}, u32[]{:S(2)}) collective-permute-start(f32[128,512]{1,0:T(8,128)S(1)} %add_add_fusion), channel_id=1, source_target_pairs={{0,8},{8,0},{16,24},{24,16},{1,9},{9,1},{17,25},{25,17},{2,10},{10... | collective-permute-start | bytes 786440 | tf_op jit(solution)/shard_map/ppermute | solution.py:682
  169.7 10.5 %collective-permute-start.49 = (bf16[256,1024]{1,0:T(8,128)(2,1)S(1)}, bf16[256,1024]{1,0:T(8,128)(2,1)S(1)}, u32[]{:S(2)}, u32[]{:S(2)}) collective-permute-start(bf16[256,1024]{1,0:T(8,128)(2,1)S(1)} %add_convert_fusion), channel_id=1, source_target_pairs={{0,0},{1,8},{2,2},{3,10},{4,4},{5,12},{6,6},{7,14},{8,1},{9,9},{10... | collective-permute-start | bytes 1572872 | tf_op jit(solution)/shard_map/ppermute | solution.py:713
  (23 other events, 168.9 us)

commit v4 on v3

--- a/solution.py
+++ b/solution.py
@@ -13,9 +13,9 @@
 MASKED = -1e30
 TILE = 256
 CHUNK = 512
-UP_PARTS = 4
+UP_PARTS = 1
 HALF_AT, Q_AT, H_AT = 11, 17, 19
-GRAD_LAGS = (0, 1, 2)
+GRAD_LAGS = (0, 2, 2)
 
 f32 = jnp.float32
 bf16 = jnp.bfloat16
@@ -543,7 +543,7 @@
 
 def up_kernel(info, own_att, got_att, tok, bo, ga, sa, bu, *rest, count):
     wu = rest[:count]
-    nrm_ref, hat_ref, inv_ref, act_ref, slope_ref, wo_s, wu_s, own_s, got_s, tok_s, sem_a, sem_o, sem_u = rest[count:]
+    hat_ref, inv_ref, act_ref, slope_ref, wo_s, wu_s, own_s, got_s, tok_s, sem_a, sem_o, sem_u = rest[count:]
     acts = start_all([(own_att, own_s), (got_att, got_s), (tok, tok_s)], sem_a)
     width, ff = wu_s.shape
     half = own_att.shape[1]
@@ -565,7 +565,6 @@
     hat_ref[...] = hat
     inv_ref[...] = jnp.broadcast_to(inv, inv_ref.shape)
     nrm = hat * ga[...].astype(f32)[None, :] + sa[...].astype(f32)[None, :]
-    nrm_ref[...] = nrm
     low = nrm.astype(bf16)
     for j in range(ff // CHUNK):
         if (j * CHUNK) % part == 0:
@@ -584,13 +583,12 @@
         functools.partial(up_kernel, count=count),
         out_shape=(
             shape_of((tokens, width), f32),
-            shape_of((tokens, width), f32),
             shape_of((tokens, 128), f32),
             shape_of((tokens, ff), bf16),
             shape_of((tokens, ff), bf16),
         ),
         in_specs=[SM] + [HB] * 3 + [VM] * 4 + [HB] * count,
-        out_specs=(VM,) * 5,
+        out_specs=(VM,) * 4,
         scratch_shapes=[
             pltpu.VMEM((width, width), bf16),
             pltpu.VMEM((width, ff), bf16),
@@ -607,7 +605,7 @@
     )(info, own_att, got_att, tok, bo, ga, sa, bu, *wu)
 
 
-def down_kernel(info, nrm_ref, hat_ref, inv_ref, act_ref, slope_ref, cot, bd, gf, sf, ga, *rest, count):
+def down_kernel(info, hat_ref, inv_ref, act_ref, slope_ref, cot, bd, gf, sf, ga, sa, *rest, count):
     wu, wd = rest[:count], rest[count : 2 * count - 2]
     out_ref, gh_ref, keep_ref, send_ref, wo_s, wu_s, wd_s, sem_o, sem_u, sem_d = rest[2 * count - 2 :]
     width, ff = wu_s.shape
@@ -616,7 +614,8 @@
     got_u = start_all(up_pairs(wu, info, wu_s, pl.ds(0, ff)), sem_u)
     got_o = start_all(out_pairs(wu, info, ff, wo_s), sem_o)
     core = info[0]
-    summed = nrm_ref[...] + bd[...].astype(f32)[None, :]
+    nrm = hat_ref[...] * ga[...].astype(f32)[None, :] + sa[...].astype(f32)[None, :]
+    summed = nrm + bd[...].astype(f32)[None, :]
     for i, one in enumerate(got_d):
         one.wait()
         size = wd[i].shape[0]
@@ -642,8 +641,8 @@
     keep_ref[...] = dot(gh_low, wo_s[row_at(core * half, half), :], 1, 1).astype(bf16)
 
 
-def down(info, nrm, hat, inv, act, slope, cot, bd, gf, sf, ga, wu, wd):
-    tokens, width = nrm.shape
+def down(info, hat, inv, act, slope, cot, bd, gf, sf, ga, sa, wu, wd):
+    tokens, width = hat.shape
     ff, count = act.shape[1], len(wu)
     return pl.pallas_call(
         functools.partial(down_kernel, count=count),
@@ -666,7 +665,7 @@
         compiler_params=pltpu.CompilerParams(vmem_limit_bytes=47 << 20),
         name="down",
         cost_estimate=cost(16),
-    )(info, nrm, hat, inv, act, slope, cot, bd, gf, sf, ga, *wu, *wd)
+    )(info, hat, inv, act, slope, cot, bd, gf, sf, ga, sa, *wu, *wd)
 
 
 def per_device(
@@ -739,8 +738,8 @@
     a_part = lax.dynamic_slice_in_dim(a_half, x * short, short, 0)
     a_x, a_z = by_seq(a_part, 1), by_seq(a_part, 2)
     u_one = by_y(u_one)
+    u_two = by_y(u_two)
     d_one = by_y(after(d_one, a_x))
-    u_two = by_y(after(u_two, a_z))
     toks = [own, close, distant]
     toks = toks + [by_core(a) for a in toks]
     a_got = [a_half, a_x, a_z]
@@ -774,7 +773,7 @@
     u_got = [u_one, u_two, u_x, u_z]
     u_got = u_got + [by_core(after(a, lse)) for a in u_got]
     parts_u = [w_up, w_out, u_own, o_own] + u_got
-    nrm, hat, inv, act, slope = up(
+    hat, inv, act, slope = up(
         info, att_keep, by_core(att_send), own, b_out, gain_attn, shift_attn, b_up,
         parts_u,
     )
@@ -782,24 +781,17 @@
     d_got = d_got + [by_core(a if a is d_one else after(a, inv, cot)) for a in d_got]
     parts_d = [w_down, d_own] + d_got
     result, gh, ga_keep, ga_send = down(
-        info, nrm, hat, inv, act, slope, cot, b_down, gain_ffn, shift_ffn, gain_attn,
+        info, hat, inv, act, slope, cot, b_down, gain_ffn, shift_ffn, gain_attn, shift_attn,
         parts_u, parts_d,
     )
     out_tokens = swapped(result)
     pre, dqt, do, dot_, inner = prefix_grads(info, q, qt, pk, pkt, pv, ga_keep, by_core(ga_send), ot, lse)
 
-    def summed(a, one, two):
+    def summed(a, row_bit, bit):
         low = a.astype(bf16)
-        sides = [by_both(low, *one), by_both(low, *two), by_both(low, one[0] | two[0], one[1] | two[1])]
-        low, p, q, r = (v.astype(f32) for v in [low] + sides)
-        return (low + p) + (q + r)
-
-    bits = [(2, 0)] + [(0, 1 << i) for i in range(n_seq.bit_length() - 1)]
-    if len(bits) % 2:
-        low = pre.astype(bf16)
-        pre = low.astype(f32) + by_both(low, *bits[0]).astype(f32)
-        bits = bits[1:]
-    pre = summed(pre, bits[0], bits[1])
+        return low.astype(f32) + by_both(low, row_bit, bit).astype(f32)
+
+    pre = summed(pre, 2, 0)
     give, keep_near, keep_far, dqt = remote_grads(
         tile_info, first, last, q, qt, k, kt, v, do, dot_, lse, inner, dqt, w_half
     )
@@ -808,17 +800,17 @@
     near_part = (keep_near.astype(f32) + got[:tok_count].astype(f32)).astype(bf16)
     far_part = (keep_far.astype(f32) + got[tok_count:].astype(f32)).astype(bf16)
     tile_info, near_part, far_part = lax.optimization_barrier((tile_info, near_part, far_part))
-    pre = after(pre, near_part)
+    pre = summed(pre, 0, 1)
     near_part, far_part = along(near_part, near), along(far_part, far)
-    for i in range(2, len(bits), 2):
-        pre = summed(pre, bits[i], bits[i + 1])
     keep, give = local_grads(
         tile_info, first, last, q, qt, k, kt, v, do, dot_, lse, inner, dqt, gh, w_half
     )
     pre, give, near_part, far_part = lax.optimization_barrier((pre, give, near_part, far_part))
+    for i in range(1, n_seq.bit_length() - 1):
+        pre = summed(pre, 0, 1 << i)
     mine = (keep + near_part.astype(f32)) + (by_core(give).astype(f32) + far_part.astype(f32))
     grad_tokens = swapped(mine.astype(bf16))
-    other = by_core(pre)
+    other = by_core(after(pre, grad_tokens))
     pre = jnp.concatenate(
         [jnp.where(core == 0, pre, other), jnp.where(core == 0, other, pre)], axis=1
     )

time: 183 us -> 180 us (0.984)
  waiting for transfers between devices: 48.3 us -> 38.9 us
  starting transfers between devices: 57.3 us -> 63.4 us
    ppermute x6 -> x4, waiting for transfers between devices: 1.62 us -> 10.1 us  [by_both(): return lax.ppermute(a, ('row', 'seq'), route)]
    ppermute x2, waiting for transfers between devices: 10.1 us -> 2 us  [along(): lax.ppermute(a, 'seq', [(j, 2 * partner(j // 2) + (j & 1)) for j in range...]
    ppermute x6, waiting for transfers between devices: 7.69 us -> 0.02 us  [swapped(): return lax.ppermute(a, ('row', 'seq'), route)]
    ppermute x6 -> x4, starting transfers between devices: 6.34 us -> 11.9 us  [by_both(): return lax.ppermute(a, ('row', 'seq'), route)]
    ppermute x26, waiting for transfers between devices: 10.5 us -> 8.42 us  [by_core(): return lax.ppermute(a, 'row', [(i, i ^ 1) for i in range(n_row)])]
    unnamed x74 -> x80, local copies, waits for them, and re-layouts: 3.77 us -> 5.13 us
  transfers between devices with their start and end apart: 51 -> 49, of which waited for: 18 -> 17; matrix products, arithmetic and copies ran while one was open for 1% -> 1% of each run, Pallas kernels for 27% -> 27%
where the time goes in v4:
time: 180 us; the launch traced here: 179 us
  Pallas kernels  66.2 us (37%)
  starting transfers between devices  63.4 us (35%)
  waiting for transfers between devices  38.9 us (22%)
  local copies, waits for them, and re-layouts  6.21 us (3%)
  other arithmetic  2.56 us (1%)
    ppermute x26, starting transfers between devices, by_core(): return lax.ppermute(a, 'row', [(i, i ^ 1) for i in range(n_row)])  22.8 us
    ppermute x6, starting transfers between devices, swapped(): return lax.ppermute(a, ('row', 'seq'), route)  17.1 us
    pallas_call x1, Pallas kernels, front(): pl.pallas_call(functools.partial(front_kernel, count=count, half=half), o...  17.1 us
    ppermute x5, waiting for transfers between devices, by_y(): return lax.ppermute(a, 'row', [(i, i ^ 2) for i in range(n_row)])  16.5 us
    pallas_call x1, Pallas kernels, down(): pl.pallas_call(functools.partial(down_kernel, count=count), out_shape=(sh...  14.6 us
    pallas_call x1, Pallas kernels, up(): pl.pallas_call(functools.partial(up_kernel, count=count), out_shape=(shap...  12.2 us
    ppermute x4, starting transfers between devices, by_both(): return lax.ppermute(a, ('row', 'seq'), route)  11.9 us
    ppermute x4, waiting for transfers between devices, by_both(): return lax.ppermute(a, ('row', 'seq'), route)  10.1 us
  transfers between devices with their start and end apart: 49, of which 17 were waited for; matrix products, arithmetic and copies ran while one was open for 1% of the time, Pallas kernels for 27%

profile of v4, /device:TPU:1, one launch (start us, length us, event | category | flops | bytes accessed | tf_op | source)
XLA Modules:
  0.0 178.6 jit_solution(5849794083284312851)
XLA Ops:
  0.7 0.7 stack.80.info
  1.3 3.1 %pack.2 = (bf16[128,3072]{1,0:T(8,128)(2,1)}, bf16[64,5120]{1,0:T(8,128)(2,1)}) custom-call(s32[20]{0:T(128)} %stack.80.info, bf16[256,1024]{1,0:T(8,128)(2,1)} %rest_6_.1, bf16[256,1024]{1,0:T(8,128)(2,1)} %rest_7_.1, bf16[256,1024]{1,0:T(8,128)(2,1)} %rest_8_.1, bf16[256,4096]{1,0:T(8,128)(2,1)} %rest_0_.7, bf16[256,1024]{1,0:T(8,128)(2,1)} %rest_1_.7), custom_call_target="tpu_custom_call" | custom-call | flops 2000000000 | tf_op jit(solution)/shard_map/pack/pallas_call | solution.py:77
  4.5 2.1 %collective-permute-start = (bf16[128,3072]{1,0:T(8,128)(2,1)}, bf16[128,3072]{1,0:T(8,128)(2,1)S(1)}, u32[]{:S(2)}, u32[]{:S(2)}) collective-permute-start(bf16[128,3072]{1,0:T(8,128)(2,1)} %get-tuple-element.72), channel_id=1, source_target_pairs={{0,16},{8,24},{16,0},{24,8},{1,17},{9,25},{17,1},{25,9},{2,18},{10... | collective-permute-start | bytes 2359304 | tf_op jit(solution)/shard_map/ppermute | solution.py:684
  6.6 4.0 %collective-permute-start.5 = (bf16[256,1024]{1,0:T(8,128)(2,1)}, bf16[256,1024]{1,0:T(8,128)(2,1)}, u32[]{:S(2)}, u32[]{:S(2)}) collective-permute-start(bf16[256,1024]{1,0:T(8,128)(2,1)} %bitcast.22), channel_id=1, source_target_pairs={{0,0},{1,8},{2,4},{3,12},{4,2},{5,10},{6,6},{7,14},{8,1},{9,9},{10... | collective-permute-start | bytes 1572872 | tf_op jit(solution)/shard_map/ppermute | solution.py:712
  10.6 1.8 collective-permute-start.4
  12.4 4.0 %collective-permute-start.3 = (bf16[256,1024]{1,0:T(8,128)(2,1)}, bf16[256,1024]{1,0:T(8,128)(2,1)}, u32[]{:S(2)}, u32[]{:S(2)}) collective-permute-start(bf16[256,1024]{1,0:T(8,128)(2,1)} %bitcast.22), channel_id=1, source_target_pairs={{0,0},{1,8},{2,2},{3,10},{4,4},{5,12},{6,6},{7,14},{8,1},{9,9},{10... | collective-permute-start | bytes 1572872 | tf_op jit(solution)/shard_map/ppermute | solution.py:712
  16.3 7.9 %collective-permute-done.rest_12_ = bf16[128,3072]{1,0:T(8,128)(2,1)S(1)} collective-permute-done((bf16[128,3072]{1,0:T(8,128)(2,1)}, bf16[128,3072]{1,0:T(8,128)(2,1)S(1)}, u32[]{:S(2)}, u32[]{:S(2)}) %collective-permute-start) | collective-permute-done | bytes 786464 | tf_op jit(solution)/shard_map/ppermute | solution.py:684
  24.2 1.3 collective-permute-start.12
  25.5 1.2 collective-permute-start.1
  26.7 1.2 collective-permute-start.19
  28.0 3.4 %pack.3 = (bf16[256,1024]{1,0:T(8,128)(2,1)}, bf16[64,5120]{1,0:T(8,128)(2,1)}, bf16[256,1024]{1,0:T(8,128)(2,1)}) custom-call(s32[20]{0:T(128)} %stack.80.info, bf16[1024,1024]{1,0:T(8,128)(2,1)} %rest_12_.1, bf16[256,4096]{1,0:T(8,128)(2,1)} %rest_0_.7, bf16[256,1024]{1,0:T(8,128)(2,1)} %rest_1_.7), custom_call_target="tpu_custom_call" | custom-call | flops 2000000000 | tf_op jit(solution)/shard_map/pack/pallas_call | solution.py:77
  31.4 2.3 %collective-permute-start.8 = (bf16[256,1024]{1,0:T(8,128)(2,1)}, bf16[256,1024]{1,0:T(8,128)(2,1)}, u32[]{:S(2)}, u32[]{:S(2)}) collective-permute-start(bf16[256,1024]{1,0:T(8,128)(2,1)} %collective-permute-done.5.rest_2_), channel_id=1, source_target_pairs={{0,8},{8,0},{16,24},{24,16},{1,9},{9,1},{17,25},{25,17},{2,10},{10... | collective-permute-start | bytes 1572872 | tf_op jit(solution)/shard_map/ppermute | solution.py:681
  33.9 2.0 %collective-permute-start.6 = (bf16[256,1024]{1,0:T(8,128)(2,1)}, bf16[256,1024]{1,0:T(8,128)(2,1)}, u32[]{:S(2)}, u32[]{:S(2)}) collective-permute-start(bf16[256,1024]{1,0:T(8,128)(2,1)} %collective-permute-done.3.rest_0_.tok), channel_id=1, source_target_pairs={{0,8},{8,0},{16,24},{24,16},{1,9},{9,1},{17,25},{25,17},{2,10},{10... | collective-permute-start | bytes 1572872 | tf_op jit(solution)/shard_map/ppermute | solution.py:681
  36.0 0.5 collective-permute-done.1.rest_13_
  36.4 1.7 collective-permute-start.2
  38.1 0.8 collective-permute-done.2
  39.5 1.8 %collective-permute-done.19.rest_4_ = bf16[64,5120]{1,0:T(8,128)(2,1)} collective-permute-done((bf16[64,5120]{1,0:T(8,128)(2,1)}, bf16[64,5120]{1,0:T(8,128)(2,1)}, u32[]{:S(2)}, u32[]{:S(2)}) %collective-permute-start.19) | collective-permute-done | bytes 655392 | tf_op jit(solution)/shard_map/ppermute | solution.py:684
  41.3 2.9 %collective-permute-start.13 = (bf16[128,3072]{1,0:T(8,128)(2,1)S(1)}, bf16[128,3072]{1,0:T(8,128)(2,1)}, u32[]{:S(2)}, u32[]{:S(2)}) collective-permute-start(bf16[128,3072]{1,0:T(8,128)(2,1)S(1)} %collective-permute-done.rest_12_), channel_id=1, source_target_pairs={{0,8},{8,0},{16,24},{24,16},{1,9},{9,1},{17,25},{25,17},{2,10},{10... | collective-permute-start | bytes 2359304 | tf_op jit(solution)/shard_map/ppermute | solution.py:681
  44.3 0.5 collective-permute-start.11
  45.6 0.6 pad_add_fusion.1.tiles.info
  46.2 1.6 collective-permute-done.10.rest_10_
  47.8 0.8 copy-done.37
  48.6 1.2 collective-permute-start.20
  50.6 1.5 collective-permute-start.17
  52.1 17.1 %front.1 = (bf16[256,512]{1,0:T(8,128)(2,1)}, bf16[256,512]{1,0:T(8,128)(2,1)}, f32[512,512]{1,0:T(8,128)}, f32[8,512]{1,0:T(8,128)}, bf16[64,512]{1,0:T(8,128)(...) custom-call(s32[20]{0:T(128)} %stack.80.info, ...), custom_call_target="tpu_custom_call" | custom-call | flops 20000000000 | tf_op jit(solution)/shard_map/front/pallas_call | solution.py:270
  69.2 6.8 %collective-permute-done.23.rest_14_ = bf16[256,1024]{1,0:T(8,128)(2,1)S(1)} collective-permute-done((bf16[256,1024]{1,0:T(8,128)(2,1)}, bf16[256,1024]{1,0:T(8,128)(2,1)S(1)}, u32[]{:S(2)}, u32[]{:S(2)}) %collective-permute-start.23) | collective-permute-done | bytes 524320 | tf_op jit(solution)/shard_map/ppermute | solution.py:684
  76.0 1.2 collective-permute-start.24
  77.3 0.4 collective-permute-start.16
  77.8 2.2 %collective-permute-done.18.rest_3_ = bf16[256,1024]{1,0:T(8,128)(2,1)S(1)} collective-permute-done((bf16[256,1024]{1,0:T(8,128)(2,1)S(1)}, bf16[256,1024]{1,0:T(8,128)(2,1)S(1)}, u32[]{:S(2)}, u32[]{:S(2)}) %collective-permute-start.18) | collective-permute-done | bytes 524320 | tf_op jit(solution)/shard_map/ppermute | solution.py:681
  81.0 2.4 %collective-permute-start.28 = (bf16[256,1024]{1,0:T(8,128)(2,1)}, bf16[256,1024]{1,0:T(8,128)(2,1)S(1)}, u32[]{:S(2)}, u32[]{:S(2)}) collective-permute-start(bf16[256,1024]{1,0:T(8,128)(2,1)} %bitcast.37), channel_id=1, source_target_pairs={{0,0},{1,8},{2,2},{3,10},{4,4},{5,12},{6,6},{7,14},{8,1},{9,9},{10... | collective-permute-start | bytes 1572872 | tf_op jit(solution)/shard_map/ppermute | solution.py:712
  83.4 1.3 collective-permute-start.30
  85.0 0.7 copy-done.36
  85.7 12.2 %up.1 = (f32[256,1024]{1,0:T(8,128)}, f32[256,128]{1,0:T(8,128)}, bf16[256,4096]{1,0:T(8,128)(2,1)}, bf16[256,4096]{1,0:T(8,128)(2,1)}) custom-call(s32[20]{0:T(128)} %stack.80.info, bf16[256,512]{1,0:T(8,128)(2,1)} %get-tuple-element.85.own_att, bf16[256,512]{1,0:T(8,128)(2,1)} %copy-done.38, bf16[256,1024]{1,0:T(8,128)(2,1)} %collective-permute-done.3.rest_0_.tok, ...), custom_call_target="tpu_custom_call" | custom-call | flops 10000000000 | tf_op jit(solution)/shard_map/up/pallas_call | solution.py:582
  98.0 1.6 collective-permute-start.33
  99.6 1.4 collective-permute-done.31.rest_16_
  101.0 2.7 %collective-permute-start.34 = (bf16[256,1024]{1,0:T(8,128)(2,1)S(1)}, bf16[256,1024]{1,0:T(8,128)(2,1)S(1)}, u32[]{:S(2)}, u32[]{:S(2)}) collective-permute-start(bf16[256,1024]{1,0:T(8,128)(2,1)S(1)} %collective-permute-done.30.rest_15_), channel_id=1, source_target_pairs={{0,8},{8,0},{16,24},{24,16},{1,9},{9,1},{17,25},{25,17},{2,10},{10... | collective-permute-start | bytes 1572872 | tf_op jit(solution)/shard_map/ppermute | solution.py:681
  103.6 0.5 collective-permute-start.36
  104.1 1.0 collective-permute-done.34.rest_19_
  105.2 0.7 collective-permute-done.35.rest_20_
  105.9 0.7 collective-permute-done.36.rest_21_
  106.7 1.0 copy-done.9
  107.8 0.9 copy-done.26
  108.7 14.6 %down.1 = (bf16[256,1024]{1,0:T(8,128)(2,1)S(1)}, f32[256,1024]{1,0:T(8,128)}, bf16[256,512]{1,0:T(8,128)(2,1)S(1)}, bf16[256,512]{1,0:T(8,128)(2,1)S(1)}) custom-call(s32[20]{0:T(128)S(1)} %copy-done.5, f32[256,1024]{1,0:T(8,128)} %get-tuple-element.100.hat_ref, f32[256,128]{1,0:T(8,128)S(1)} %copy-done.26, bf16[256,4096]{1,0:T(8,128)(2,1)} %get-tuple-element.102.act_ref, ...), custom_call_target="tpu_custom_call" | custom-call | flops 16000000000 | tf_op jit(solution)/shard_map/down/pallas_call | solution.py:647
  123.3 0.4 collective-permute-start.37
  123.8 1.9 %collective-permute-start.38 = (bf16[256,1024]{1,0:T(8,128)(2,1)S(1)}, bf16[256,1024]{1,0:T(8,128)(2,1)S(1)}, u32[]{:S(2)}, u32[]{:S(2)}) collective-permute-start(bf16[256,1024]{1,0:T(8,128)(2,1)S(1)} %get-tuple-element.121), channel_id=1, source_target_pairs={{0,0},{1,8},{2,2},{3,10},{4,4},{5,12},{6,6},{7,14},{8,1},{9,9},{10... | collective-permute-start | bytes 1572872 | tf_op jit(solution)/shard_map/ppermute | solution.py:712
  125.8 2.1 %prefix_grads.1 = (f32[128,512]{1,0:T(8,128)S(1)}, f32[512,512]{1,0:T(8,128)S(1)}, bf16[512,512]{1,0:T(8,128)(2,1)S(1)}, bf16[512,512]{1,0:T(8,128)(2,1)S(1)}, f32[8,512]{1,0:T(8,128)S(1)}) custom-call(s32[20]{0:T(128)S(1)} %copy-done.5, bf16[512,512]{1,0:T(8,128)(2,1)S(1)} %copy-done.16, bf16[512,512]{1,0:T(8,128)(2,1)S(1)} %copy-done.17, ...), custom_call_target="tpu_custom_call" | custom-call | flops 5000000000 | tf_op jit(solution)/shard_map/prefix_grads/pallas_call | solution.py:383
  127.9 1.3 collective-permute-start.39
  129.3 5.0 %remote_grads.1 = (bf16[512,1024]{1,0:T(8,128)(2,1)S(1)}, bf16[256,1024]{1,0:T(8,128)(2,1)S(1)}, bf16[256,1024]{1,0:T(8,128)(2,1)S(1)}, f32[512,512]{1,0:T(8,128)S(1)}) custom-call(s32[6]{0:T(128)S(1)} %copy-done.4, s32[1,512]{1,0:T(1,128)S(1)} %bitcast.33, s32[1,512]{1,0:T(1,128)S(1)} %bitcast.30, bf16[512,512]{1,0:T(8,128)(2,1)S(1)} %copy-done.16, ...), custom_call_target="tpu_custom_call" | custom-call | flops 14000000000 | tf_op jit(solution)/shard_map/remote_grads/pallas_call | solution.py:439
  134.4 3.5 %collective-permute-start.41 = (bf16[128,512]{1,0:T(8,128)(2,1)S(1)}, bf16[128,512]{1,0:T(8,128)(2,1)S(1)}, u32[]{:S(2)}, u32[]{:S(2)}) collective-permute-start(bf16[128,512]{1,0:T(8,128)(2,1)S(1)} %convert_add_fusion.2), channel_id=1, source_target_pairs={{0,1},{1,0},{2,3},{3,2},{4,5},{5,4},{6,7},{7,6},{8,9},{9,8},{10,11... | collective-permute-start | bytes 393224 | tf_op jit(solution)/shard_map/ppermute | solution.py:691
  137.9 3.8 %collective-permute-done.41 = bf16[128,512]{1,0:T(8,128)(2,1)S(1)} collective-permute-done((bf16[128,512]{1,0:T(8,128)(2,1)S(1)}, bf16[128,512]{1,0:T(8,128)(2,1)S(1)}, u32[]{:S(2)}, u32[]{:S(2)}) %collective-permute-start.41) | collective-permute-done | bytes 131104 | tf_op jit(solution)/shard_map/ppermute | solution.py:691
  142.1 1.6 collective-permute-start.42
  143.7 0.7 collective-permute-start.43
  144.4 8.7 %local_grads.1 = (f32[256,1024]{1,0:T(8,128)S(1)}, bf16[256,1024]{1,0:T(8,128)(2,1)S(1)}) custom-call(s32[6]{0:T(128)S(1)} %copy-done.4, s32[1,512]{1,0:T(1,128)S(1)} %bitcast.34, s32[1,512]{1,0:T(1,128)S(1)} %bitcast.31, bf16[512,512]{1,0:T(8,128)(2,1)S(1)} %copy-done.16, bf16[512,512]{1,0:T(8,128)(2,1)S(1)} %copy-done.17, ...), custom_call_target="tpu_custom_call" | custom-call | flops 14000000000 | tf_op jit(solution)/shard_map/local_grads/pallas_call | solution.py:505
  153.1 2.0 %collective-permute-done.42 = bf16[256,1024]{1,0:T(8,128)(2,1)S(1)} collective-permute-done((bf16[256,1024]{1,0:T(8,128)(2,1)S(1)}, bf16[256,1024]{1,0:T(8,128)(2,1)S(1)}, u32[]{:S(2)}, u32[]{:S(2)}) %collective-permute-start.42) | collective-permute-done | bytes 524320 | tf_op jit(solution)/shard_map/ppermute | solution.py:704
  155.1 1.5 collective-permute-start.44
  156.6 4.6 %collective-permute-start.46 = (bf16[128,512]{1,0:T(8,128)(2,1)S(1)}, bf16[128,512]{1,0:T(8,128)(2,1)S(1)}, u32[]{:S(2)}, u32[]{:S(2)}) collective-permute-start(bf16[128,512]{1,0:T(8,128)(2,1)S(1)} %convert_add_fusion.1), channel_id=1, source_target_pairs={{0,2},{1,3},{2,0},{3,1},{4,6},{5,7},{6,4},{7,5},{8,10},{9,11},{10,... | collective-permute-start | bytes 393224 | tf_op jit(solution)/shard_map/ppermute | solution.py:691
  161.5 3.1 %collective-permute-start.45 = (bf16[256,1024]{1,0:T(8,128)(2,1)S(1)}, bf16[256,1024]{1,0:T(8,128)(2,1)S(1)}, u32[]{:S(2)}, u32[]{:S(2)}) collective-permute-start(bf16[256,1024]{1,0:T(8,128)(2,1)S(1)} %add_convert_fusion), channel_id=1, source_target_pairs={{0,0},{1,8},{2,2},{3,10},{4,4},{5,12},{6,6},{7,14},{8,1},{9,9},{10... | collective-permute-start | bytes 1572872 | tf_op jit(solution)/shard_map/ppermute | solution.py:712
  165.1 2.5 %collective-permute-start.47 = (bf16[128,512]{1,0:T(8,128)(2,1)S(1)}, bf16[128,512]{1,0:T(8,128)(2,1)S(1)}, u32[]{:S(2)}, u32[]{:S(2)}) collective-permute-start(bf16[128,512]{1,0:T(8,128)(2,1)S(1)} %add_convert_fusion.3), channel_id=1, source_target_pairs={{0,4},{1,5},{2,6},{3,7},{4,0},{5,1},{6,2},{7,3},{8,12},{9,13},{10,... | collective-permute-start | bytes 393224 | tf_op jit(solution)/shard_map/ppermute | solution.py:691
  167.6 5.9 %collective-permute-done.47 = bf16[128,512]{1,0:T(8,128)(2,1)S(1)} collective-permute-done((bf16[128,512]{1,0:T(8,128)(2,1)S(1)}, bf16[128,512]{1,0:T(8,128)(2,1)S(1)}, u32[]{:S(2)}, u32[]{:S(2)}) %collective-permute-start.47) | collective-permute-done | bytes 131104 | tf_op jit(solution)/shard_map/ppermute | solution.py:691
  173.5 1.4 collective-permute-start.48
  174.9 1.2 collective-permute-done.48
  176.2 0.8 pad_maximum_fusion
  177.0 0.8 copy.28
  177.8 0.8 copy.29
  (146 shorter events, 5.3 us)
Async XLA Ops:
  4.5 19.7 %collective-permute-start = (bf16[128,3072]{1,0:T(8,128)(2,1)}, bf16[128,3072]{1,0:T(8,128)(2,1)S(1)}, u32[]{:S(2)}, u32[]{:S(2)}) collective-permute-start(bf16[128,3072]{1,0:T(8,128)(2,1)} %get-tuple-element.72), channel_id=1, source_target_pairs={{0,16},{8,24},{16,0},{24,8},{1,17},{9,25},{17,1},{25,9},{2,18},{10... | collective-permute-start | bytes 2359304 | tf_op jit(solution)/shard_map/ppermute | solution.py:684
  6.6 20.1 %collective-permute-start.5 = (bf16[256,1024]{1,0:T(8,128)(2,1)}, bf16[256,1024]{1,0:T(8,128)(2,1)}, u32[]{:S(2)}, u32[]{:S(2)}) collective-permute-start(bf16[256,1024]{1,0:T(8,128)(2,1)} %bitcast.22), channel_id=1, source_target_pairs={{0,0},{1,8},{2,4},{3,12},{4,2},{5,10},{6,6},{7,14},{8,1},{9,9},{10... | collective-permute-start | bytes 1572872 | tf_op jit(solution)/shard_map/ppermute | solution.py:712
  10.6 20.8 %collective-permute-start.4 = (bf16[256,1024]{1,0:T(8,128)(2,1)}, bf16[256,1024]{1,0:T(8,128)(2,1)}, u32[]{:S(2)}, u32[]{:S(2)}) collective-permute-start(bf16[256,1024]{1,0:T(8,128)(2,1)} %bitcast.22), channel_id=1, source_target_pairs={{0,2},{1,10},{2,0},{3,8},{4,6},{5,14},{6,4},{7,12},{8,3},{9,11},{1... | collective-permute-start | bytes 1572872 | tf_op jit(solution)/shard_map/ppermute | solution.py:712
  12.4 21.4 %collective-permute-start.3 = (bf16[256,1024]{1,0:T(8,128)(2,1)}, bf16[256,1024]{1,0:T(8,128)(2,1)}, u32[]{:S(2)}, u32[]{:S(2)}) collective-permute-start(bf16[256,1024]{1,0:T(8,128)(2,1)} %bitcast.22), channel_id=1, source_target_pairs={{0,0},{1,8},{2,2},{3,10},{4,4},{5,12},{6,6},{7,14},{8,1},{9,9},{10... | collective-permute-start | bytes 1572872 | tf_op jit(solution)/shard_map/ppermute | solution.py:712
  24.2 17.1 %copy-start.28 = (bf16[128,3072]{1,0:T(8,128)(2,1)}, bf16[128,3072]{1,0:T(8,128)(2,1)S(1)}, u32[]{:S(2)}) copy-start(bf16[128,3072]{1,0:T(8,128)(2,1)S(1)} %collective-permute-done.rest_12_) | copy-start | bytes 2359300
  24.2 9.7 %collective-permute-start.12 = (bf16[64,3072]{1,0:T(8,128)(2,1)S(1)}, bf16[64,3072]{1,0:T(8,128)(2,1)}, u32[]{:S(2)}, u32[]{:S(2)}) collective-permute-start(bf16[64,3072]{1,0:T(8,128)(2,1)S(1)} %constant_dynamic-slice_fusion), channel_id=1, source_target_pairs={{0,2},{1,3},{2,0},{3,1},{4,6},{5,7},{6,4},{7,5},{8,10},{9,11},{10,... | collective-permute-start | bytes 1179656 | tf_op jit(solution)/shard_map/ppermute | solution.py:687
  25.5 10.9 %collective-permute-start.1 = (bf16[64,3072]{1,0:T(8,128)(2,1)S(1)}, bf16[64,3072]{1,0:T(8,128)(2,1)}, u32[]{:S(2)}, u32[]{:S(2)}) collective-permute-start(bf16[64,3072]{1,0:T(8,128)(2,1)S(1)} %constant_dynamic-slice_fusion), channel_id=1, source_target_pairs={{0,1},{1,0},{2,3},{3,2},{4,5},{5,4},{6,7},{7,6},{8,9},{9,8},{10,11... | collective-permute-start | bytes 1179656 | tf_op jit(solution)/shard_map/ppermute | solution.py:687
  26.7 14.5 %collective-permute-start.19 = (bf16[64,5120]{1,0:T(8,128)(2,1)}, bf16[64,5120]{1,0:T(8,128)(2,1)}, u32[]{:S(2)}, u32[]{:S(2)}) collective-permute-start(bf16[64,5120]{1,0:T(8,128)(2,1)} %get-tuple-element.89), channel_id=1, source_target_pairs={{0,16},{8,24},{16,0},{24,8},{1,17},{9,25},{17,1},{25,9},{2,18},{10... | collective-permute-start | bytes 1966088 | tf_op jit(solution)/shard_map/ppermute | solution.py:684
  28.0 22.6 %copy-start.30 = (bf16[256,4096]{1,0:T(8,128)(2,1)S(1)}, bf16[256,4096]{1,0:T(8,128)(2,1)}, u32[]{:S(2)}) copy-start(bf16[256,4096]{1,0:T(8,128)(2,1)} %rest_0_.7) | copy-start | bytes 6291460
  31.4 12.9 %collective-permute-start.8 = (bf16[256,1024]{1,0:T(8,128)(2,1)}, bf16[256,1024]{1,0:T(8,128)(2,1)}, u32[]{:S(2)}, u32[]{:S(2)}) collective-permute-start(bf16[256,1024]{1,0:T(8,128)(2,1)} %collective-permute-done.5.rest_2_), channel_id=1, source_target_pairs={{0,8},{8,0},{16,24},{24,16},{1,9},{9,1},{17,25},{25,17},{2,10},{10... | collective-permute-start | bytes 1572872 | tf_op jit(solution)/shard_map/ppermute | solution.py:681
  33.8 10.6 %collective-permute-start.7 = (bf16[256,1024]{1,0:T(8,128)(2,1)}, bf16[256,1024]{1,0:T(8,128)(2,1)}, u32[]{:S(2)}, u32[]{:S(2)}) collective-permute-start(bf16[256,1024]{1,0:T(8,128)(2,1)} %collective-permute-done.4.rest_1_), channel_id=1, source_target_pairs={{0,8},{8,0},{16,24},{24,16},{1,9},{9,1},{17,25},{25,17},{2,10},{10... | collective-permute-start | bytes 1572872 | tf_op jit(solution)/shard_map/ppermute | solution.py:681
  33.9 11.0 %collective-permute-start.6 = (bf16[256,1024]{1,0:T(8,128)(2,1)}, bf16[256,1024]{1,0:T(8,128)(2,1)}, u32[]{:S(2)}, u32[]{:S(2)}) collective-permute-start(bf16[256,1024]{1,0:T(8,128)(2,1)} %collective-permute-done.3.rest_0_.tok), channel_id=1, source_target_pairs={{0,8},{8,0},{16,24},{24,16},{1,9},{9,1},{17,25},{25,17},{2,10},{10... | collective-permute-start | bytes 1572872 | tf_op jit(solution)/shard_map/ppermute | solution.py:681
  36.4 2.5 %collective-permute-start.2 = (s32[1,8]{1,0:T(1,128)S(1)}, s32[1,8]{1,0:T(1,128)S(1)}, u32[]{:S(2)}, u32[]{:S(2)}) collective-permute-start(s32[1,8]{1,0:T(1,128)S(1)} %copy-done.29), channel_id=1, source_target_pairs={{0,8},{8,0},{16,24},{24,16},{1,9},{9,1},{17,25},{25,17},{2,10},{10... | collective-permute-start | bytes 104 | tf_op jit(solution)/shard_map/ppermute | solution.py:681
  38.9 6.1 %collective-permute-start.9 = (bf16[256,1024]{1,0:T(8,128)(2,1)}, bf16[256,1024]{1,0:T(8,128)(2,1)}, u32[]{:S(2)}, u32[]{:S(2)}) collective-permute-start(bf16[256,1024]{1,0:T(8,128)(2,1)} %rest_6_.1), channel_id=1, source_target_pairs={{0,8},{8,0},{16,24},{24,16},{1,9},{9,1},{17,25},{25,17},{2,10},{10... | collective-permute-start | bytes 1572872 | tf_op jit(solution)/shard_map/ppermute | solution.py:681
  41.3 9.3 %collective-permute-start.13 = (bf16[128,3072]{1,0:T(8,128)(2,1)S(1)}, bf16[128,3072]{1,0:T(8,128)(2,1)}, u32[]{:S(2)}, u32[]{:S(2)}) collective-permute-start(bf16[128,3072]{1,0:T(8,128)(2,1)S(1)} %collective-permute-done.rest_12_), channel_id=1, source_target_pairs={{0,8},{8,0},{16,24},{24,16},{1,9},{9,1},{17,25},{25,17},{2,10},{10... | collective-permute-start | bytes 2359304 | tf_op jit(solution)/shard_map/ppermute | solution.py:681
  44.3 3.5 %collective-permute-start.10 = (bf16[256,1024]{1,0:T(8,128)(2,1)}, bf16[256,1024]{1,0:T(8,128)(2,1)S(1)}, u32[]{:S(2)}, u32[]{:S(2)}) collective-permute-start(bf16[256,1024]{1,0:T(8,128)(2,1)} %rest_7_.1), channel_id=1, source_target_pairs={{0,8},{8,0},{16,24},{24,16},{1,9},{9,1},{17,25},{25,17},{2,10},{10... | collective-permute-start | bytes 1572872 | tf_op jit(solution)/shard_map/ppermute | solution.py:681
  44.3 5.5 %collective-permute-start.11 = (bf16[256,1024]{1,0:T(8,128)(2,1)}, bf16[256,1024]{1,0:T(8,128)(2,1)}, u32[]{:S(2)}, u32[]{:S(2)}) collective-permute-start(bf16[256,1024]{1,0:T(8,128)(2,1)} %rest_8_.1), channel_id=1, source_target_pairs={{0,8},{8,0},{16,24},{24,16},{1,9},{9,1},{17,25},{25,17},{2,10},{10... | collective-permute-start | bytes 1572872 | tf_op jit(solution)/shard_map/ppermute | solution.py:681
  44.9 5.1 %collective-permute-start.15 = (bf16[64,3072]{1,0:T(8,128)(2,1)}, bf16[64,3072]{1,0:T(8,128)(2,1)}, u32[]{:S(2)}, u32[]{:S(2)}) collective-permute-start(bf16[64,3072]{1,0:T(8,128)(2,1)} %collective-permute-done.12.rest_14_), channel_id=1, source_target_pairs={{0,8},{8,0},{16,24},{24,16},{1,9},{9,1},{17,25},{25,17},{2,10},{10... | collective-permute-start | bytes 1179656 | tf_op jit(solution)/shard_map/ppermute | solution.py:681
  45.0 5.3 %collective-permute-start.14 = (bf16[64,3072]{1,0:T(8,128)(2,1)}, bf16[64,3072]{1,0:T(8,128)(2,1)}, u32[]{:S(2)}, u32[]{:S(2)}) collective-permute-start(bf16[64,3072]{1,0:T(8,128)(2,1)} %collective-permute-done.1.rest_13_), channel_id=1, source_target_pairs={{0,8},{8,0},{16,24},{24,16},{1,9},{9,1},{17,25},{25,17},{2,10},{10... | collective-permute-start | bytes 1179656 | tf_op jit(solution)/shard_map/ppermute | solution.py:681
  48.6 29.1 %collective-permute-start.20 = (bf16[64,5120]{1,0:T(8,128)(2,1)}, bf16[64,5120]{1,0:T(8,128)(2,1)S(1)}, u32[]{:S(2)}, u32[]{:S(2)}) collective-permute-start(bf16[64,5120]{1,0:T(8,128)(2,1)} %get-tuple-element.91), channel_id=1, source_target_pairs={{0,16},{8,24},{16,0},{24,8},{1,17},{9,25},{17,1},{25,9},{2,18},{10... | collective-permute-start | bytes 1966088 | tf_op jit(solution)/shard_map/ppermute | solution.py:684
  49.9 27.4 %collective-permute-start.22 = (bf16[64,5120]{1,0:T(8,128)(2,1)}, bf16[64,5120]{1,0:T(8,128)(2,1)}, u32[]{:S(2)}, u32[]{:S(2)}) collective-permute-start(bf16[64,5120]{1,0:T(8,128)(2,1)} %collective-permute-done.19.rest_4_), channel_id=1, source_target_pairs={{0,2},{1,3},{2,0},{3,1},{4,6},{5,7},{6,4},{7,5},{8,10},{9,11},{10,... | collective-permute-start | bytes 1966088 | tf_op jit(solution)/shard_map/ppermute | solution.py:687
  50.0 27.3 %collective-permute-start.21 = (bf16[64,5120]{1,0:T(8,128)(2,1)}, bf16[64,5120]{1,0:T(8,128)(2,1)}, u32[]{:S(2)}, u32[]{:S(2)}) collective-permute-start(bf16[64,5120]{1,0:T(8,128)(2,1)} %collective-permute-done.19.rest_4_), channel_id=1, source_target_pairs={{0,1},{1,0},{2,3},{3,2},{4,5},{5,4},{6,7},{7,6},{8,9},{9,8},{10,11... | collective-permute-start | bytes 1966088 | tf_op jit(solution)/shard_map/ppermute | solution.py:687
  50.3 25.7 %collective-permute-start.23 = (bf16[256,1024]{1,0:T(8,128)(2,1)}, bf16[256,1024]{1,0:T(8,128)(2,1)S(1)}, u32[]{:S(2)}, u32[]{:S(2)}) collective-permute-start(bf16[256,1024]{1,0:T(8,128)(2,1)} %get-tuple-element.93), channel_id=1, source_target_pairs={{0,16},{8,24},{16,0},{24,8},{1,17},{9,25},{17,1},{25,9},{2,18},{10... | collective-permute-start | bytes 1572872 | tf_op jit(solution)/shard_map/ppermute | solution.py:684
  50.6 34.4 %collective-permute-start.17 = (bf16[256,4096]{1,0:T(8,128)(2,1)S(1)}, bf16[256,4096]{1,0:T(8,128)(2,1)}, u32[]{:S(2)}, u32[]{:S(2)}) collective-permute-start(bf16[256,4096]{1,0:T(8,128)(2,1)S(1)} %copy-done.30), channel_id=1, source_target_pairs={{0,8},{8,0},{16,24},{24,16},{1,9},{9,1},{17,25},{25,17},{2,10},{10... | collective-permute-start | bytes 6291464 | tf_op jit(solution)/shard_map/ppermute | solution.py:681
  52.1 25.1 %copy-start.6 = (bf16[256,1024]{1,0:T(8,128)(2,1)S(1)}, bf16[256,1024]{1,0:T(8,128)(2,1)}, u32[]{:S(2)}) copy-start(bf16[256,1024]{1,0:T(8,128)(2,1)} %rest_1_.7) | copy-start | bytes 1572868
  76.0 4.6 %collective-permute-start.24 = (bf16[64,5120]{1,0:T(8,128)(2,1)}, bf16[64,5120]{1,0:T(8,128)(2,1)S(1)}, u32[]{:S(2)}, u32[]{:S(2)}) collective-permute-start(bf16[64,5120]{1,0:T(8,128)(2,1)} %collective-permute-done.19.rest_4_), channel_id=1, source_target_pairs={{0,8},{8,0},{16,24},{24,16},{1,9},{9,1},{17,25},{25,17},{2,10},{10... | collective-permute-start | bytes 1966088 | tf_op jit(solution)/shard_map/ppermute | solution.py:681
  77.2 2.8 %collective-permute-start.18 = (bf16[256,1024]{1,0:T(8,128)(2,1)S(1)}, bf16[256,1024]{1,0:T(8,128)(2,1)S(1)}, u32[]{:S(2)}, u32[]{:S(2)}) collective-permute-start(bf16[256,1024]{1,0:T(8,128)(2,1)S(1)} %copy-done.6), channel_id=1, source_target_pairs={{0,8},{8,0},{16,24},{24,16},{1,9},{9,1},{17,25},{25,17},{2,10},{10... | collective-permute-start | bytes 1572872 | tf_op jit(solution)/shard_map/ppermute | solution.py:681
  77.3 3.1 %collective-permute-start.16 = (bf16[256,512]{1,0:T(8,128)(2,1)}, bf16[256,512]{1,0:T(8,128)(2,1)S(1)}, u32[]{:S(2)}, u32[]{:S(2)}) collective-permute-start(bf16[256,512]{1,0:T(8,128)(2,1)} %get-tuple-element.86), channel_id=1, source_target_pairs={{0,8},{8,0},{16,24},{24,16},{1,9},{9,1},{17,25},{25,17},{2,10},{10... | collective-permute-start | bytes 786440 | tf_op jit(solution)/shard_map/ppermute | solution.py:681
  77.7 3.3 %collective-permute-start.25 = (bf16[64,5120]{1,0:T(8,128)(2,1)S(1)}, bf16[64,5120]{1,0:T(8,128)(2,1)S(1)}, u32[]{:S(2)}, u32[]{:S(2)}) collective-permute-start(bf16[64,5120]{1,0:T(8,128)(2,1)S(1)} %collective-permute-done.20.rest_5_), channel_id=1, source_target_pairs={{0,8},{8,0},{16,24},{24,16},{1,9},{9,1},{17,25},{25,17},{2,10},{10... | collective-permute-start | bytes 1966088 | tf_op jit(solution)/shard_map/ppermute | solution.py:681
  80.1 3.4 %collective-permute-start.26 = (bf16[64,5120]{1,0:T(8,128)(2,1)}, bf16[64,5120]{1,0:T(8,128)(2,1)S(1)}, u32[]{:S(2)}, u32[]{:S(2)}) collective-permute-start(bf16[64,5120]{1,0:T(8,128)(2,1)} %collective-permute-done.21.rest_6_), channel_id=1, source_target_pairs={{0,8},{8,0},{16,24},{24,16},{1,9},{9,1},{17,25},{25,17},{2,10},{10... | collective-permute-start | bytes 1966088 | tf_op jit(solution)/shard_map/ppermute | solution.py:681
  80.4 4.3 %collective-permute-start.27 = (bf16[64,5120]{1,0:T(8,128)(2,1)}, bf16[64,5120]{1,0:T(8,128)(2,1)S(1)}, u32[]{:S(2)}, u32[]{:S(2)}) collective-permute-start(bf16[64,5120]{1,0:T(8,128)(2,1)} %collective-permute-done.22.rest_7_), channel_id=1, source_target_pairs={{0,8},{8,0},{16,24},{24,16},{1,9},{9,1},{17,25},{25,17},{2,10},{10... | collective-permute-start | bytes 1966088 | tf_op jit(solution)/shard_map/ppermute | solution.py:681
  80.6 23.6 %collective-permute-start.29 = (bf16[1024,1024]{1,0:T(8,128)(2,1)}, bf16[1024,1024]{1,0:T(8,128)(2,1)S(1)}, u32[]{:S(2)}, u32[]{:S(2)}) collective-permute-start(bf16[1024,1024]{1,0:T(8,128)(2,1)} %rest_12_.1), channel_id=1, source_target_pairs={{0,8},{8,0},{16,24},{24,16},{1,9},{9,1},{17,25},{25,17},{2,10},{10... | collective-permute-start | bytes 6291464 | tf_op jit(solution)/shard_map/ppermute | solution.py:681
  81.0 17.0 %collective-permute-start.28 = (bf16[256,1024]{1,0:T(8,128)(2,1)}, bf16[256,1024]{1,0:T(8,128)(2,1)S(1)}, u32[]{:S(2)}, u32[]{:S(2)}) collective-permute-start(bf16[256,1024]{1,0:T(8,128)(2,1)} %bitcast.37), channel_id=1, source_target_pairs={{0,0},{1,8},{2,2},{3,10},{4,4},{5,12},{6,6},{7,14},{8,1},{9,9},{10... | collective-permute-start | bytes 1572872 | tf_op jit(solution)/shard_map/ppermute | solution.py:712
  83.4 17.5 %collective-permute-start.30 = (bf16[256,1024]{1,0:T(8,128)(2,1)}, bf16[256,1024]{1,0:T(8,128)(2,1)S(1)}, u32[]{:S(2)}, u32[]{:S(2)}) collective-permute-start(bf16[256,1024]{1,0:T(8,128)(2,1)} %get-tuple-element.108), channel_id=1, source_target_pairs={{0,16},{8,24},{16,0},{24,8},{1,17},{9,25},{17,1},{25,9},{2,18},{10... | collective-permute-start | bytes 1572872 | tf_op jit(solution)/shard_map/ppermute | solution.py:684
  84.8 14.8 %collective-permute-start.32 = (bf16[256,1024]{1,0:T(8,128)(2,1)S(1)}, bf16[256,1024]{1,0:T(8,128)(2,1)S(1)}, u32[]{:S(2)}, u32[]{:S(2)}) collective-permute-start(bf16[256,1024]{1,0:T(8,128)(2,1)S(1)} %collective-permute-done.23.rest_14_), channel_id=1, source_target_pairs={{0,2},{1,3},{2,0},{3,1},{4,6},{5,7},{6,4},{7,5},{8,10},{9,11},{10,... | collective-permute-start | bytes 1572872 | tf_op jit(solution)/shard_map/ppermute | solution.py:687
  85.0 16.0 %collective-permute-start.31 = (bf16[256,1024]{1,0:T(8,128)(2,1)S(1)}, bf16[256,1024]{1,0:T(8,128)(2,1)S(1)}, u32[]{:S(2)}, u32[]{:S(2)}) collective-permute-start(bf16[256,1024]{1,0:T(8,128)(2,1)S(1)} %collective-permute-done.23.rest_14_), channel_id=1, source_target_pairs={{0,1},{1,0},{2,3},{3,2},{4,5},{5,4},{6,7},{7,6},{8,9},{9,8},{10,11... | collective-permute-start | bytes 1572872 | tf_op jit(solution)/shard_map/ppermute | solution.py:687
  85.7 21.0 %copy-start.5 = (s32[20]{0:T(128)S(1)}, s32[20]{0:T(128)}, u32[]{:S(2)}) copy-start(s32[20]{0:T(128)} %stack.80.info) | copy-start | bytes 244
  85.7 21.0 %copy-start.7 = (bf16[256,1024]{1,0:T(8,128)(2,1)S(1)}, bf16[256,1024]{1,0:T(8,128)(2,1)}, u32[]{:S(2)}) copy-start(bf16[256,1024]{1,0:T(8,128)(2,1)} %rest_1_.7) | copy-start | bytes 1572868
  85.7 21.0 %copy-start.10 = (bf16[1024]{0:T(1024)(128)(2,1)S(1)}, bf16[1024]{0:T(1024)(128)(2,1)}, u32[]{:S(2)}) copy-start(bf16[1024]{0:T(1024)(128)(2,1)} %ga.3) | copy-start | bytes 6148
  85.7 21.0 %copy-start.11 = (bf16[1024]{0:T(1024)(128)(2,1)S(1)}, bf16[1024]{0:T(1024)(128)(2,1)}, u32[]{:S(2)}) copy-start(bf16[1024]{0:T(1024)(128)(2,1)} %sa.3) | copy-start | bytes 6148
  85.7 21.0 %copy-start.12 = (bf16[1024]{0:T(1024)(128)(2,1)S(1)}, bf16[1024]{0:T(1024)(128)(2,1)}, u32[]{:S(2)}) copy-start(bf16[1024]{0:T(1024)(128)(2,1)} %bd.1) | copy-start | bytes 6148
  85.7 21.0 %copy-start.13 = (bf16[1024]{0:T(1024)(128)(2,1)S(1)}, bf16[1024]{0:T(1024)(128)(2,1)}, u32[]{:S(2)}) copy-start(bf16[1024]{0:T(1024)(128)(2,1)} %gf.1) | copy-start | bytes 6148
  85.7 21.0 %copy-start.14 = (bf16[1024]{0:T(1024)(128)(2,1)S(1)}, bf16[1024]{0:T(1024)(128)(2,1)}, u32[]{:S(2)}) copy-start(bf16[1024]{0:T(1024)(128)(2,1)} %sf.1) | copy-start | bytes 6148
  98.0 6.2 %collective-permute-start.33 = (bf16[256,1024]{1,0:T(8,128)(2,1)S(1)}, bf16[256,1024]{1,0:T(8,128)(2,1)S(1)}, u32[]{:S(2)}, u32[]{:S(2)}) collective-permute-start(bf16[256,1024]{1,0:T(8,128)(2,1)S(1)} %collective-permute-done.23.rest_14_), channel_id=1, source_target_pairs={{0,8},{8,0},{16,24},{24,16},{1,9},{9,1},{17,25},{25,17},{2,10},{10... | collective-permute-start | bytes 1572872 | tf_op jit(solution)/shard_map/ppermute | solution.py:681
  101.0 4.2 %collective-permute-start.34 = (bf16[256,1024]{1,0:T(8,128)(2,1)S(1)}, bf16[256,1024]{1,0:T(8,128)(2,1)S(1)}, u32[]{:S(2)}, u32[]{:S(2)}) collective-permute-start(bf16[256,1024]{1,0:T(8,128)(2,1)S(1)} %collective-permute-done.30.rest_15_), channel_id=1, source_target_pairs={{0,8},{8,0},{16,24},{24,16},{1,9},{9,1},{17,25},{25,17},{2,10},{10... | collective-permute-start | bytes 1572872 | tf_op jit(solution)/shard_map/ppermute | solution.py:681
  103.6 2.3 %collective-permute-start.35 = (bf16[256,1024]{1,0:T(8,128)(2,1)S(1)}, bf16[256,1024]{1,0:T(8,128)(2,1)S(1)}, u32[]{:S(2)}, u32[]{:S(2)}) collective-permute-start(bf16[256,1024]{1,0:T(8,128)(2,1)S(1)} %collective-permute-done.31.rest_16_), channel_id=1, source_target_pairs={{0,8},{8,0},{16,24},{24,16},{1,9},{9,1},{17,25},{25,17},{2,10},{10... | collective-permute-start | bytes 1572872 | tf_op jit(solution)/shard_map/ppermute | solution.py:681
  103.6 3.0 %collective-permute-start.36 = (bf16[256,1024]{1,0:T(8,128)(2,1)S(1)}, bf16[256,1024]{1,0:T(8,128)(2,1)S(1)}, u32[]{:S(2)}, u32[]{:S(2)}) collective-permute-start(bf16[256,1024]{1,0:T(8,128)(2,1)S(1)} %collective-permute-done.32.rest_17_), channel_id=1, source_target_pairs={{0,8},{8,0},{16,24},{24,16},{1,9},{9,1},{17,25},{25,17},{2,10},{10... | collective-permute-start | bytes 1572872 | tf_op jit(solution)/shard_map/ppermute | solution.py:681
  108.7 17.0 %copy-start.17 = (bf16[512,512]{1,0:T(8,128)(2,1)S(1)}, bf16[512,512]{1,0:T(8,128)(2,1)}, u32[]{:S(2)}) copy-start(bf16[512,512]{1,0:T(8,128)(2,1)} %get-tuple-element.78.qt_ref) | copy-start | bytes 1572868
  108.7 17.0 %copy-start.23 = (bf16[512,64]{1,0:T(8,128)(2,1)S(1)}, bf16[512,64]{1,0:T(8,128)(2,1)}, u32[]{:S(2)}) copy-start(bf16[512,64]{1,0:T(8,128)(2,1)} %get-tuple-element.83.pkt_ref) | copy-start | bytes 196612
  108.7 17.1 %copy-start.24 = (bf16[64,512]{1,0:T(8,128)(2,1)S(1)}, bf16[64,512]{1,0:T(8,128)(2,1)}, u32[]{:S(2)}) copy-start(bf16[64,512]{1,0:T(8,128)(2,1)} %get-tuple-element.82.pk_ref) | copy-start | bytes 196612
  108.7 17.1 %copy-start.25 = (bf16[64,512]{1,0:T(8,128)(2,1)S(1)}, bf16[64,512]{1,0:T(8,128)(2,1)}, u32[]{:S(2)}) copy-start(bf16[64,512]{1,0:T(8,128)(2,1)} %get-tuple-element.84.pv_ref) | copy-start | bytes 196612
  108.7 17.1 %copy-start.27 = (f32[8,512]{1,0:T(8,128)S(1)}, f32[8,512]{1,0:T(8,128)}, u32[]{:S(2)}) copy-start(f32[8,512]{1,0:T(8,128)} %get-tuple-element.95.lse_ref) | copy-start | bytes 49156
  123.3 2.4 %collective-permute-start.37 = (bf16[256,512]{1,0:T(8,128)(2,1)S(1)}, bf16[256,512]{1,0:T(8,128)(2,1)S(1)}, u32[]{:S(2)}, u32[]{:S(2)}) collective-permute-start(bf16[256,512]{1,0:T(8,128)(2,1)S(1)} %get-tuple-element.113), channel_id=1, source_target_pairs={{0,8},{8,0},{16,24},{24,16},{1,9},{9,1},{17,25},{25,17},{2,10},{10... | collective-permute-start | bytes 786440 | tf_op jit(solution)/shard_map/ppermute | solution.py:681
  123.8 10.6 %collective-permute-start.38 = (bf16[256,1024]{1,0:T(8,128)(2,1)S(1)}, bf16[256,1024]{1,0:T(8,128)(2,1)S(1)}, u32[]{:S(2)}, u32[]{:S(2)}) collective-permute-start(bf16[256,1024]{1,0:T(8,128)(2,1)S(1)} %get-tuple-element.121), channel_id=1, source_target_pairs={{0,0},{1,8},{2,2},{3,10},{4,4},{5,12},{6,6},{7,14},{8,1},{9,9},{10... | collective-permute-start | bytes 1572872 | tf_op jit(solution)/shard_map/ppermute | solution.py:712
  127.9 6.4 %collective-permute-start.39 = (bf16[128,512]{1,0:T(8,128)(2,1)S(1)}, bf16[128,512]{1,0:T(8,128)(2,1)S(1)}, u32[]{:S(2)}, u32[]{:S(2)}) collective-permute-start(bf16[128,512]{1,0:T(8,128)(2,1)S(1)} %convert_element_type.66), channel_id=1, source_target_pairs={{0,16},{1,17},{2,18},{3,19},{4,20},{5,21},{6,22},{7,23},{8,24},{9,... | collective-permute-start | bytes 393224 | tf_op jit(solution)/shard_map/ppermute | solution.py:691
  134.3 7.4 %collective-permute-start.40 = (bf16[512,1024]{1,0:T(8,128)(2,1)S(1)}, bf16[512,1024]{1,0:T(8,128)(2,1)S(1)}, u32[]{:S(2)}, u32[]{:S(2)}) collective-permute-start(bf16[512,1024]{1,0:T(8,128)(2,1)S(1)} %get-tuple-element.125), channel_id=1, source_target_pairs={{0,8},{8,0},{16,24},{24,16},{1,9},{9,1},{17,25},{25,17},{2,10},{10... | collective-permute-start | bytes 3145736 | tf_op jit(solution)/shard_map/ppermute | solution.py:681
  134.4 7.3 %collective-permute-start.41 = (bf16[128,512]{1,0:T(8,128)(2,1)S(1)}, bf16[128,512]{1,0:T(8,128)(2,1)S(1)}, u32[]{:S(2)}, u32[]{:S(2)}) collective-permute-start(bf16[128,512]{1,0:T(8,128)(2,1)S(1)} %convert_add_fusion.2), channel_id=1, source_target_pairs={{0,1},{1,0},{2,3},{3,2},{4,5},{5,4},{6,7},{7,6},{8,9},{9,8},{10,11... | collective-permute-start | bytes 393224 | tf_op jit(solution)/shard_map/ppermute | solution.py:691
  142.1 13.0 %collective-permute-start.42 = (bf16[256,1024]{1,0:T(8,128)(2,1)S(1)}, bf16[256,1024]{1,0:T(8,128)(2,1)S(1)}, u32[]{:S(2)}, u32[]{:S(2)}) collective-permute-start(bf16[256,1024]{1,0:T(8,128)(2,1)S(1)} %get-tuple-element.133), channel_id=1, source_target_pairs={{0,2},{1,3},{2,0},{3,1},{4,6},{5,7},{6,4},{7,5},{8,10},{9,11},{10,... | collective-permute-start | bytes 1572872 | tf_op jit(solution)/shard_map/ppermute | solution.py:704
  143.7 11.4 %collective-permute-start.43 = (bf16[256,1024]{1,0:T(8,128)(2,1)S(1)}, bf16[256,1024]{1,0:T(8,128)(2,1)S(1)}, u32[]{:S(2)}, u32[]{:S(2)}) collective-permute-start(bf16[256,1024]{1,0:T(8,128)(2,1)S(1)} %get-tuple-element.134), channel_id=1, source_target_pairs={{0,0},{1,1},{2,4},{3,5},{4,2},{5,3},{6,6},{7,7},{8,8},{9,9},{10,12... | collective-permute-start | bytes 1572872 | tf_op jit(solution)/shard_map/ppermute | solution.py:704
  155.1 6.1 %collective-permute-start.44 = (bf16[256,1024]{1,0:T(8,128)(2,1)S(1)}, bf16[256,1024]{1,0:T(8,128)(2,1)S(1)}, u32[]{:S(2)}, u32[]{:S(2)}) collective-permute-start(bf16[256,1024]{1,0:T(8,128)(2,1)S(1)} %get-tuple-element.136), channel_id=1, source_target_pairs={{0,8},{8,0},{16,24},{24,16},{1,9},{9,1},{17,25},{25,17},{2,10},{10... | collective-permute-start | bytes 1572872 | tf_op jit(solution)/shard_map/ppermute | solution.py:681
  156.6 8.4 %collective-permute-start.46 = (bf16[128,512]{1,0:T(8,128)(2,1)S(1)}, bf16[128,512]{1,0:T(8,128)(2,1)S(1)}, u32[]{:S(2)}, u32[]{:S(2)}) collective-permute-start(bf16[128,512]{1,0:T(8,128)(2,1)S(1)} %convert_add_fusion.1), channel_id=1, source_target_pairs={{0,2},{1,3},{2,0},{3,1},{4,6},{5,7},{6,4},{7,5},{8,10},{9,11},{10,... | collective-permute-start | bytes 393224 | tf_op jit(solution)/shard_map/ppermute | solution.py:691
  161.5 12.0 %collective-permute-start.45 = (bf16[256,1024]{1,0:T(8,128)(2,1)S(1)}, bf16[256,1024]{1,0:T(8,128)(2,1)S(1)}, u32[]{:S(2)}, u32[]{:S(2)}) collective-permute-start(bf16[256,1024]{1,0:T(8,128)(2,1)S(1)} %add_convert_fusion), channel_id=1, source_target_pairs={{0,0},{1,8},{2,2},{3,10},{4,4},{5,12},{6,6},{7,14},{8,1},{9,9},{10... | collective-permute-start | bytes 1572872 | tf_op jit(solution)/shard_map/ppermute | solution.py:712
  165.1 8.4 %collective-permute-start.47 = (bf16[128,512]{1,0:T(8,128)(2,1)S(1)}, bf16[128,512]{1,0:T(8,128)(2,1)S(1)}, u32[]{:S(2)}, u32[]{:S(2)}) collective-permute-start(bf16[128,512]{1,0:T(8,128)(2,1)S(1)} %add_convert_fusion.3), channel_id=1, source_target_pairs={{0,4},{1,5},{2,6},{3,7},{4,0},{5,1},{6,2},{7,3},{8,12},{9,13},{10,... | collective-permute-start | bytes 393224 | tf_op jit(solution)/shard_map/ppermute | solution.py:691
  173.5 2.6 %collective-permute-start.48 = (f32[128,512]{1,0:T(8,128)S(1)}, f32[128,512]{1,0:T(8,128)S(1)}, u32[]{:S(2)}, u32[]{:S(2)}) collective-permute-start(f32[128,512]{1,0:T(8,128)S(1)} %convert_add_fusion), channel_id=1, source_target_pairs={{0,8},{8,0},{16,24},{24,16},{1,9},{9,1},{17,25},{25,17},{2,10},{10... | collective-permute-start | bytes 786440 | tf_op jit(solution)/shard_map/ppermute | solution.py:681
  (24 other events, 127.3 us)

commit v5 on v4

--- a/solution.py
+++ b/solution.py
@@ -599,7 +599,7 @@
             pltpu.SemaphoreType.DMA((count - 2,)),
             pltpu.SemaphoreType.DMA((UP_PARTS, count - 2)),
         ],
-        compiler_params=pltpu.CompilerParams(vmem_limit_bytes=55 << 20),
+        compiler_params=pltpu.CompilerParams(vmem_limit_bytes=50 << 20),
         name="up",
         cost_estimate=cost(10),
     )(info, own_att, got_att, tok, bo, ga, sa, bu, *wu)
@@ -662,7 +662,7 @@
             pltpu.SemaphoreType.DMA((count - 2,)),
             pltpu.SemaphoreType.DMA((count - 2,)),
         ],
-        compiler_params=pltpu.CompilerParams(vmem_limit_bytes=47 << 20),
+        compiler_params=pltpu.CompilerParams(vmem_limit_bytes=46 << 20),
         name="down",
         cost_estimate=cost(16),
     )(info, hat, inv, act, slope, cot, bd, gf, sf, ga, sa, *wu, *wd)
@@ -800,7 +800,7 @@
     near_part = (keep_near.astype(f32) + got[:tok_count].astype(f32)).astype(bf16)
     far_part = (keep_far.astype(f32) + got[tok_count:].astype(f32)).astype(bf16)
     tile_info, near_part, far_part = lax.optimization_barrier((tile_info, near_part, far_part))
-    pre = summed(pre, 0, 1)
+    pre = summed(after(pre, near_part), 0, 1)
     near_part, far_part = along(near_part, near), along(far_part, far)
     keep, give = local_grads(
         tile_info, first, last, q, qt, k, kt, v, do, dot_, lse, inner, dqt, gh, w_half

time: 180 us -> 175 us (0.972)
  waiting for transfers between devices: 38.9 us -> 36.7 us
  starting transfers between devices: 63.4 us -> 61.4 us
    ppermute x4, waiting for transfers between devices: 10.1 us -> 7.35 us  [by_both(): return lax.ppermute(a, ('row', 'seq'), route)]
    ppermute x26, waiting for transfers between devices: 8.42 us -> 10.6 us  [by_core(): return lax.ppermute(a, 'row', [(i, i ^ 1) for i in range(n_row)])]
    ppermute x4, starting transfers between devices: 11.9 us -> 10 us  [by_both(): return lax.ppermute(a, ('row', 'seq'), route)]
    pallas_call x1, Pallas kernels: 12.2 us -> 10.4 us  [up(): pl.pallas_call(functools.partial(up_kernel, count=count), out_shape=(shap...]
    unnamed x80 -> x82, local copies, waits for them, and re-layouts: 5.13 us -> 4.57 us
  transfers between devices with their start and end apart: 49 -> 49, of which waited for: 17 -> 17; matrix products, arithmetic and copies ran while one was open for 1% -> 1% of each run, Pallas kernels for 27% -> 28%
where the time goes in v5:
time: 175 us
  Pallas kernels  67.3 us (38%)
  starting transfers between devices  61.4 us (35%)
  waiting for transfers between devices  36.7 us (21%)
  local copies, waits for them, and re-layouts  5.59 us (3%)
  other arithmetic  2.65 us (2%)
    ppermute x26, starting transfers between devices, by_core(): return lax.ppermute(a, 'row', [(i, i ^ 1) for i in range(n_row)])  21.4 us
    pallas_call x1, Pallas kernels, front(): pl.pallas_call(functools.partial(front_kernel, count=count, half=half), o...  18.2 us
    ppermute x6, starting transfers between devices, swapped(): return lax.ppermute(a, ('row', 'seq'), route)  16.3 us
    ppermute x5, waiting for transfers between devices, by_y(): return lax.ppermute(a, 'row', [(i, i ^ 2) for i in range(n_row)])  15 us
    pallas_call x1, Pallas kernels, down(): pl.pallas_call(functools.partial(down_kernel, count=count), out_shape=(sh...  14.6 us
    ppermute x26, waiting for transfers between devices, by_core(): return lax.ppermute(a, 'row', [(i, i ^ 1) for i in range(n_row)])  10.6 us
    pallas_call x1, Pallas kernels, up(): pl.pallas_call(functools.partial(up_kernel, count=count), out_shape=(shap...  10.4 us
    ppermute x4, starting transfers between devices, by_both(): return lax.ppermute(a, ('row', 'seq'), route)  10 us
  transfers between devices with their start and end apart: 49, of which 17 were waited for; matrix products, arithmetic and copies ran while one was open for 1% of the time, Pallas kernels for 28%

profile of v5, /device:TPU:1, one launch (start us, length us, event | category | flops | bytes accessed | tf_op | source)
XLA Modules:
  0.0 174.9 jit_solution(12741123153154286965)
XLA Ops:
  0.7 0.6 stack.80.info
  1.3 3.3 %pack.2 = (bf16[128,3072]{1,0:T(8,128)(2,1)}, bf16[64,5120]{1,0:T(8,128)(2,1)}) custom-call(s32[20]{0:T(128)} %stack.80.info, bf16[256,1024]{1,0:T(8,128)(2,1)} %rest_6_.1, bf16[256,1024]{1,0:T(8,128)(2,1)} %rest_7_.1, bf16[256,1024]{1,0:T(8,128)(2,1)} %rest_8_.1, bf16[256,4096]{1,0:T(8,128)(2,1)} %rest_0_.7, bf16[256,1024]{1,0:T(8,128)(2,1)} %rest_1_.7), custom_call_target="tpu_custom_call" | custom-call | flops 2000000000 | tf_op jit(solution)/shard_map/pack/pallas_call | solution.py:77
  4.6 2.1 %collective-permute-start = (bf16[128,3072]{1,0:T(8,128)(2,1)}, bf16[128,3072]{1,0:T(8,128)(2,1)S(1)}, u32[]{:S(2)}, u32[]{:S(2)}) collective-permute-start(bf16[128,3072]{1,0:T(8,128)(2,1)} %get-tuple-element.73), channel_id=1, source_target_pairs={{0,16},{8,24},{16,0},{24,8},{1,17},{9,25},{17,1},{25,9},{2,18},{10... | collective-permute-start | bytes 2359304 | tf_op jit(solution)/shard_map/ppermute | solution.py:684
  6.7 3.9 %collective-permute-start.5 = (bf16[256,1024]{1,0:T(8,128)(2,1)S(1)}, bf16[256,1024]{1,0:T(8,128)(2,1)}, u32[]{:S(2)}, u32[]{:S(2)}) collective-permute-start(bf16[256,1024]{1,0:T(8,128)(2,1)S(1)} %bitcast.37), channel_id=1, source_target_pairs={{0,0},{1,8},{2,4},{3,12},{4,2},{5,10},{6,6},{7,14},{8,1},{9,9},{10... | collective-permute-start | bytes 1572872 | tf_op jit(solution)/shard_map/ppermute | solution.py:712
  10.7 1.8 %collective-permute-start.4 = (bf16[256,1024]{1,0:T(8,128)(2,1)S(1)}, bf16[256,1024]{1,0:T(8,128)(2,1)}, u32[]{:S(2)}, u32[]{:S(2)}) collective-permute-start(bf16[256,1024]{1,0:T(8,128)(2,1)S(1)} %bitcast.38), channel_id=1, source_target_pairs={{0,2},{1,10},{2,0},{3,8},{4,6},{5,14},{6,4},{7,12},{8,3},{9,11},{1... | collective-permute-start | bytes 1572872 | tf_op jit(solution)/shard_map/ppermute | solution.py:712
  12.4 3.9 %collective-permute-start.3 = (bf16[256,1024]{1,0:T(8,128)(2,1)S(1)}, bf16[256,1024]{1,0:T(8,128)(2,1)S(1)}, u32[]{:S(2)}, u32[]{:S(2)}) collective-permute-start(bf16[256,1024]{1,0:T(8,128)(2,1)S(1)} %bitcast.39), channel_id=1, source_target_pairs={{0,0},{1,8},{2,2},{3,10},{4,4},{5,12},{6,6},{7,14},{8,1},{9,9},{10... | collective-permute-start | bytes 1572872 | tf_op jit(solution)/shard_map/ppermute | solution.py:712
  16.4 7.9 %collective-permute-done.rest_12_ = bf16[128,3072]{1,0:T(8,128)(2,1)S(1)} collective-permute-done((bf16[128,3072]{1,0:T(8,128)(2,1)}, bf16[128,3072]{1,0:T(8,128)(2,1)S(1)}, u32[]{:S(2)}, u32[]{:S(2)}) %collective-permute-start) | collective-permute-done | bytes 786464 | tf_op jit(solution)/shard_map/ppermute | solution.py:684
  24.3 1.3 collective-permute-start.12
  25.6 1.2 collective-permute-start.1
  26.8 1.1 collective-permute-start.19
  27.9 3.5 %pack.3 = (bf16[256,1024]{1,0:T(8,128)(2,1)}, bf16[64,5120]{1,0:T(8,128)(2,1)}, bf16[256,1024]{1,0:T(8,128)(2,1)}) custom-call(s32[20]{0:T(128)} %stack.80.info, bf16[1024,1024]{1,0:T(8,128)(2,1)} %rest_12_.1, bf16[256,4096]{1,0:T(8,128)(2,1)} %rest_0_.7, bf16[256,1024]{1,0:T(8,128)(2,1)} %rest_1_.7), custom_call_target="tpu_custom_call" | custom-call | flops 2000000000 | tf_op jit(solution)/shard_map/pack/pallas_call | solution.py:77
  31.4 2.5 %collective-permute-start.8 = (bf16[256,1024]{1,0:T(8,128)(2,1)}, bf16[256,1024]{1,0:T(8,128)(2,1)}, u32[]{:S(2)}, u32[]{:S(2)}) collective-permute-start(bf16[256,1024]{1,0:T(8,128)(2,1)} %collective-permute-done.5.rest_2_), channel_id=1, source_target_pairs={{0,8},{8,0},{16,24},{24,16},{1,9},{9,1},{17,25},{25,17},{2,10},{10... | collective-permute-start | bytes 1572872 | tf_op jit(solution)/shard_map/ppermute | solution.py:681
  34.0 1.9 %collective-permute-start.6 = (bf16[256,1024]{1,0:T(8,128)(2,1)S(1)}, bf16[256,1024]{1,0:T(8,128)(2,1)}, u32[]{:S(2)}, u32[]{:S(2)}) collective-permute-start(bf16[256,1024]{1,0:T(8,128)(2,1)S(1)} %collective-permute-done.3.rest_0_.tok), channel_id=1, source_target_pairs={{0,8},{8,0},{16,24},{24,16},{1,9},{9,1},{17,25},{25,17},{2,10},{10... | collective-permute-start | bytes 1572872 | tf_op jit(solution)/shard_map/ppermute | solution.py:681
  36.1 1.9 %collective-permute-start.2 = (s32[1,8]{1,0:T(1,128)S(1)}, s32[1,8]{1,0:T(1,128)S(1)}, u32[]{:S(2)}, u32[]{:S(2)}) collective-permute-start(s32[1,8]{1,0:T(1,128)S(1)} %copy-done.30), channel_id=1, source_target_pairs={{0,8},{8,0},{16,24},{24,16},{1,9},{9,1},{17,25},{25,17},{2,10},{10... | collective-permute-start | bytes 104 | tf_op jit(solution)/shard_map/ppermute | solution.py:681
  38.0 0.8 collective-permute-done.2
  39.3 1.9 %collective-permute-done.19.rest_4_ = bf16[64,5120]{1,0:T(8,128)(2,1)S(1)} collective-permute-done((bf16[64,5120]{1,0:T(8,128)(2,1)}, bf16[64,5120]{1,0:T(8,128)(2,1)S(1)}, u32[]{:S(2)}, u32[]{:S(2)}) %collective-permute-start.19) | collective-permute-done | bytes 655392 | tf_op jit(solution)/shard_map/ppermute | solution.py:684
  41.2 2.9 %collective-permute-start.13 = (bf16[128,3072]{1,0:T(8,128)(2,1)S(1)}, bf16[128,3072]{1,0:T(8,128)(2,1)S(1)}, u32[]{:S(2)}, u32[]{:S(2)}) collective-permute-start(bf16[128,3072]{1,0:T(8,128)(2,1)S(1)} %collective-permute-done.rest_12_), channel_id=1, source_target_pairs={{0,8},{8,0},{16,24},{24,16},{1,9},{9,1},{17,25},{25,17},{2,10},{10... | collective-permute-start | bytes 2359304 | tf_op jit(solution)/shard_map/ppermute | solution.py:681
  44.3 0.5 collective-permute-start.11
  45.0 0.4 collective-permute-start.14
  45.6 0.7 pad_add_fusion.1.tiles.info
  46.3 0.9 collective-permute-done.10.rest_10_
  47.2 1.1 collective-permute-start.20
  49.0 1.1 collective-permute-start.23
  50.2 0.7 collective-permute-start.17
  51.1 18.2 %front.1 = (bf16[256,512]{1,0:T(8,128)(2,1)}, bf16[256,512]{1,0:T(8,128)(2,1)}, f32[512,512]{1,0:T(8,128)}, f32[8,512]{1,0:T(8,128)}, bf16[64,512]{1,0:T(8,128)(...) custom-call(s32[20]{0:T(128)} %stack.80.info, ...), custom_call_target="tpu_custom_call" | custom-call | flops 20000000000 | tf_op jit(solution)/shard_map/front/pallas_call | solution.py:270
  69.3 5.2 %collective-permute-done.23.rest_14_ = bf16[256,1024]{1,0:T(8,128)(2,1)S(1)} collective-permute-done((bf16[256,1024]{1,0:T(8,128)(2,1)}, bf16[256,1024]{1,0:T(8,128)(2,1)S(1)}, u32[]{:S(2)}, u32[]{:S(2)}) %collective-permute-start.23) | collective-permute-done | bytes 524320 | tf_op jit(solution)/shard_map/ppermute | solution.py:684
  74.6 1.2 collective-permute-start.24
  75.8 0.4 collective-permute-start.16
  76.4 2.2 %collective-permute-done.18.rest_3_ = bf16[256,1024]{1,0:T(8,128)(2,1)S(1)} collective-permute-done((bf16[256,1024]{1,0:T(8,128)(2,1)S(1)}, bf16[256,1024]{1,0:T(8,128)(2,1)S(1)}, u32[]{:S(2)}, u32[]{:S(2)}) %collective-permute-start.18) | collective-permute-done | bytes 524320 | tf_op jit(solution)/shard_map/ppermute | solution.py:681
  79.5 2.6 %collective-permute-start.28 = (bf16[256,1024]{1,0:T(8,128)(2,1)}, bf16[256,1024]{1,0:T(8,128)(2,1)S(1)}, u32[]{:S(2)}, u32[]{:S(2)}) collective-permute-start(bf16[256,1024]{1,0:T(8,128)(2,1)} %bitcast.40), channel_id=1, source_target_pairs={{0,0},{1,8},{2,2},{3,10},{4,4},{5,12},{6,6},{7,14},{8,1},{9,9},{10... | collective-permute-start | bytes 1572872 | tf_op jit(solution)/shard_map/ppermute | solution.py:712
  82.2 1.3 collective-permute-start.30
  83.6 0.7 copy-done.36
  84.3 1.0 copy-done.8
  85.4 0.9 copy-done.25
  86.3 10.4 %up.1 = (f32[256,1024]{1,0:T(8,128)}, f32[256,128]{1,0:T(8,128)S(1)}, bf16[256,4096]{1,0:T(8,128)(2,1)}, bf16[256,4096]{1,0:T(8,128)(2,1)}) custom-call(s32[20]{0:T(128)S(1)} %copy-done.5, bf16[256,512]{1,0:T(8,128)(2,1)S(1)} %copy-done.25, bf16[256,512]{1,0:T(8,128)(2,1)S(1)} %collective-permute-done.16.got_att, bf16[256,1024]{1,0:T(8,128)(2,1)S(1)} %copy-done.8, ...), custom_call_target="tpu_custom_call" | custom-call | flops 10000000000 | tf_op jit(solution)/shard_map/up/pallas_call | solution.py:582
  96.7 1.6 collective-permute-start.33
  98.4 1.1 collective-permute-done.31.rest_16_
  99.5 2.7 %collective-permute-start.34 = (bf16[256,1024]{1,0:T(8,128)(2,1)S(1)}, bf16[256,1024]{1,0:T(8,128)(2,1)S(1)}, u32[]{:S(2)}, u32[]{:S(2)}) collective-permute-start(bf16[256,1024]{1,0:T(8,128)(2,1)S(1)} %collective-permute-done.30.rest_15_), channel_id=1, source_target_pairs={{0,8},{8,0},{16,24},{24,16},{1,9},{9,1},{17,25},{25,17},{2,10},{10... | collective-permute-start | bytes 1572872 | tf_op jit(solution)/shard_map/ppermute | solution.py:681
  102.2 0.5 collective-permute-start.36
  102.7 1.0 collective-permute-done.34.rest_19_
  103.7 0.7 collective-permute-done.35.rest_20_
  104.5 0.7 collective-permute-done.36.rest_21_
  105.3 14.6 %down.1 = (bf16[256,1024]{1,0:T(8,128)(2,1)S(1)}, f32[256,1024]{1,0:T(8,128)}, bf16[256,512]{1,0:T(8,128)(2,1)S(1)}, bf16[256,512]{1,0:T(8,128)(2,1)S(1)}) custom-call(s32[20]{0:T(128)S(1)} %copy-done.5, f32[256,1024]{1,0:T(8,128)} %get-tuple-element.101.hat_ref, f32[256,128]{1,0:T(8,128)S(1)} %get-tuple-element.102.inv_ref, ...), custom_call_target="tpu_custom_call" | custom-call | flops 16000000000 | tf_op jit(solution)/shard_map/down/pallas_call | solution.py:647
  119.9 0.4 collective-permute-start.37
  120.4 1.9 %collective-permute-start.38 = (bf16[256,1024]{1,0:T(8,128)(2,1)S(1)}, bf16[256,1024]{1,0:T(8,128)(2,1)S(1)}, u32[]{:S(2)}, u32[]{:S(2)}) collective-permute-start(bf16[256,1024]{1,0:T(8,128)(2,1)S(1)} %get-tuple-element.122), channel_id=1, source_target_pairs={{0,0},{1,8},{2,2},{3,10},{4,4},{5,12},{6,6},{7,14},{8,1},{9,9},{10... | collective-permute-start | bytes 1572872 | tf_op jit(solution)/shard_map/ppermute | solution.py:712
  122.4 2.1 %prefix_grads.1 = (f32[128,512]{1,0:T(8,128)S(1)}, f32[512,512]{1,0:T(8,128)S(1)}, bf16[512,512]{1,0:T(8,128)(2,1)S(1)}, bf16[512,512]{1,0:T(8,128)(2,1)S(1)}, f32[8,512]{1,0:T(8,128)S(1)}) custom-call(s32[20]{0:T(128)S(1)} %copy-done.5, bf16[512,512]{1,0:T(8,128)(2,1)S(1)} %copy-done.17, bf16[512,512]{1,0:T(8,128)(2,1)S(1)} %copy-done.18, ...), custom_call_target="tpu_custom_call" | custom-call | flops 5000000000 | tf_op jit(solution)/shard_map/prefix_grads/pallas_call | solution.py:383
  124.6 1.2 collective-permute-start.39
  125.8 6.4 %remote_grads.1 = (bf16[512,1024]{1,0:T(8,128)(2,1)S(1)}, bf16[256,1024]{1,0:T(8,128)(2,1)S(1)}, bf16[256,1024]{1,0:T(8,128)(2,1)S(1)}, f32[512,512]{1,0:T(8,128)S(1)}) custom-call(s32[6]{0:T(128)S(1)} %copy-done.4, s32[1,512]{1,0:T(1,128)S(1)} %bitcast.33, s32[1,512]{1,0:T(1,128)S(1)} %bitcast.30, bf16[512,512]{1,0:T(8,128)(2,1)S(1)} %copy-done.17, ...), custom_call_target="tpu_custom_call" | custom-call | flops 14000000000 | tf_op jit(solution)/shard_map/remote_grads/pallas_call | solution.py:439
  132.4 2.6 %collective-permute-done.40 = bf16[512,1024]{1,0:T(8,128)(2,1)S(1)} collective-permute-done((bf16[512,1024]{1,0:T(8,128)(2,1)S(1)}, bf16[512,1024]{1,0:T(8,128)(2,1)S(1)}, u32[]{:S(2)}, u32[]{:S(2)}) %collective-permute-start.40) | collective-permute-done | bytes 1048608 | tf_op jit(solution)/shard_map/ppermute | solution.py:681
  135.5 3.2 %collective-permute-start.42 = (bf16[256,1024]{1,0:T(8,128)(2,1)S(1)}, bf16[256,1024]{1,0:T(8,128)(2,1)S(1)}, u32[]{:S(2)}, u32[]{:S(2)}) collective-permute-start(bf16[256,1024]{1,0:T(8,128)(2,1)S(1)} %get-tuple-element.133), channel_id=1, source_target_pairs={{0,2},{1,3},{2,0},{3,1},{4,6},{5,7},{6,4},{7,5},{8,10},{9,11},{10,... | collective-permute-start | bytes 1572872 | tf_op jit(solution)/shard_map/ppermute | solution.py:704
  138.9 0.7 collective-permute-start.43
  139.6 8.8 %local_grads.1 = (f32[256,1024]{1,0:T(8,128)S(1)}, bf16[256,1024]{1,0:T(8,128)(2,1)S(1)}) custom-call(s32[6]{0:T(128)S(1)} %copy-done.4, s32[1,512]{1,0:T(1,128)S(1)} %bitcast.34, s32[1,512]{1,0:T(1,128)S(1)} %bitcast.31, bf16[512,512]{1,0:T(8,128)(2,1)S(1)} %copy-done.17, bf16[512,512]{1,0:T(8,128)(2,1)S(1)} %copy-done.18, ...), custom_call_target="tpu_custom_call" | custom-call | flops 14000000000 | tf_op jit(solution)/shard_map/local_grads/pallas_call | solution.py:505
  148.5 2.3 %collective-permute-done.42 = bf16[256,1024]{1,0:T(8,128)(2,1)S(1)} collective-permute-done((bf16[256,1024]{1,0:T(8,128)(2,1)S(1)}, bf16[256,1024]{1,0:T(8,128)(2,1)S(1)}, u32[]{:S(2)}, u32[]{:S(2)}) %collective-permute-start.42) | collective-permute-done | bytes 524320 | tf_op jit(solution)/shard_map/ppermute | solution.py:704
  150.8 0.7 collective-permute-start.44
  151.5 6.0 %collective-permute-start.46 = (bf16[128,512]{1,0:T(8,128)(2,1)S(1)}, bf16[128,512]{1,0:T(8,128)(2,1)S(1)}, u32[]{:S(2)}, u32[]{:S(2)}) collective-permute-start(bf16[128,512]{1,0:T(8,128)(2,1)S(1)} %convert_add_fusion.1), channel_id=1, source_target_pairs={{0,2},{1,3},{2,0},{3,1},{4,6},{5,7},{6,4},{7,5},{8,10},{9,11},{10,... | collective-permute-start | bytes 393224 | tf_op jit(solution)/shard_map/ppermute | solution.py:691
  157.8 2.1 %collective-permute-start.45 = (bf16[256,1024]{1,0:T(8,128)(2,1)S(1)}, bf16[256,1024]{1,0:T(8,128)(2,1)S(1)}, u32[]{:S(2)}, u32[]{:S(2)}) collective-permute-start(bf16[256,1024]{1,0:T(8,128)(2,1)S(1)} %add_convert_fusion), channel_id=1, source_target_pairs={{0,0},{1,8},{2,2},{3,10},{4,4},{5,12},{6,6},{7,14},{8,1},{9,9},{10... | collective-permute-start | bytes 1572872 | tf_op jit(solution)/shard_map/ppermute | solution.py:712
  160.0 1.4 collective-permute-done.46
  161.4 2.5 %collective-permute-start.47 = (bf16[128,512]{1,0:T(8,128)(2,1)S(1)}, bf16[128,512]{1,0:T(8,128)(2,1)S(1)}, u32[]{:S(2)}, u32[]{:S(2)}) collective-permute-start(bf16[128,512]{1,0:T(8,128)(2,1)S(1)} %add_convert_fusion.3), channel_id=1, source_target_pairs={{0,4},{1,5},{2,6},{3,7},{4,0},{5,1},{6,2},{7,3},{8,12},{9,13},{10,... | collective-permute-start | bytes 393224 | tf_op jit(solution)/shard_map/ppermute | solution.py:691
  163.9 5.9 %collective-permute-done.47 = bf16[128,512]{1,0:T(8,128)(2,1)S(1)} collective-permute-done((bf16[128,512]{1,0:T(8,128)(2,1)S(1)}, bf16[128,512]{1,0:T(8,128)(2,1)S(1)}, u32[]{:S(2)}, u32[]{:S(2)}) %collective-permute-start.47) | collective-permute-done | bytes 131104 | tf_op jit(solution)/shard_map/ppermute | solution.py:691
  169.9 1.4 collective-permute-start.48
  171.3 1.2 collective-permute-done.48
  172.5 0.8 pad_maximum_fusion
  173.3 0.8 copy.28
  174.1 0.8 copy.29
  (148 shorter events, 4.8 us)
Async XLA Ops:
  4.6 19.7 %collective-permute-start = (bf16[128,3072]{1,0:T(8,128)(2,1)}, bf16[128,3072]{1,0:T(8,128)(2,1)S(1)}, u32[]{:S(2)}, u32[]{:S(2)}) collective-permute-start(bf16[128,3072]{1,0:T(8,128)(2,1)} %get-tuple-element.73), channel_id=1, source_target_pairs={{0,16},{8,24},{16,0},{24,8},{1,17},{9,25},{17,1},{25,9},{2,18},{10... | collective-permute-start | bytes 2359304 | tf_op jit(solution)/shard_map/ppermute | solution.py:684
  6.7 20.1 %collective-permute-start.5 = (bf16[256,1024]{1,0:T(8,128)(2,1)S(1)}, bf16[256,1024]{1,0:T(8,128)(2,1)}, u32[]{:S(2)}, u32[]{:S(2)}) collective-permute-start(bf16[256,1024]{1,0:T(8,128)(2,1)S(1)} %bitcast.37), channel_id=1, source_target_pairs={{0,0},{1,8},{2,4},{3,12},{4,2},{5,10},{6,6},{7,14},{8,1},{9,9},{10... | collective-permute-start | bytes 1572872 | tf_op jit(solution)/shard_map/ppermute | solution.py:712
  10.7 20.8 %collective-permute-start.4 = (bf16[256,1024]{1,0:T(8,128)(2,1)S(1)}, bf16[256,1024]{1,0:T(8,128)(2,1)}, u32[]{:S(2)}, u32[]{:S(2)}) collective-permute-start(bf16[256,1024]{1,0:T(8,128)(2,1)S(1)} %bitcast.38), channel_id=1, source_target_pairs={{0,2},{1,10},{2,0},{3,8},{4,6},{5,14},{6,4},{7,12},{8,3},{9,11},{1... | collective-permute-start | bytes 1572872 | tf_op jit(solution)/shard_map/ppermute | solution.py:712
  12.4 21.5 %collective-permute-start.3 = (bf16[256,1024]{1,0:T(8,128)(2,1)S(1)}, bf16[256,1024]{1,0:T(8,128)(2,1)S(1)}, u32[]{:S(2)}, u32[]{:S(2)}) collective-permute-start(bf16[256,1024]{1,0:T(8,128)(2,1)S(1)} %bitcast.39), channel_id=1, source_target_pairs={{0,0},{1,8},{2,2},{3,10},{4,4},{5,12},{6,6},{7,14},{8,1},{9,9},{10... | collective-permute-start | bytes 1572872 | tf_op jit(solution)/shard_map/ppermute | solution.py:712
  24.3 9.7 %collective-permute-start.12 = (bf16[64,3072]{1,0:T(8,128)(2,1)S(1)}, bf16[64,3072]{1,0:T(8,128)(2,1)S(1)}, u32[]{:S(2)}, u32[]{:S(2)}) collective-permute-start(bf16[64,3072]{1,0:T(8,128)(2,1)S(1)} %constant_dynamic-slice_fusion), channel_id=1, source_target_pairs={{0,2},{1,3},{2,0},{3,1},{4,6},{5,7},{6,4},{7,5},{8,10},{9,11},{10,... | collective-permute-start | bytes 1179656 | tf_op jit(solution)/shard_map/ppermute | solution.py:687
  25.6 10.5 %collective-permute-start.1 = (bf16[64,3072]{1,0:T(8,128)(2,1)S(1)}, bf16[64,3072]{1,0:T(8,128)(2,1)}, u32[]{:S(2)}, u32[]{:S(2)}) collective-permute-start(bf16[64,3072]{1,0:T(8,128)(2,1)S(1)} %constant_dynamic-slice_fusion), channel_id=1, source_target_pairs={{0,1},{1,0},{2,3},{3,2},{4,5},{5,4},{6,7},{7,6},{8,9},{9,8},{10,11... | collective-permute-start | bytes 1179656 | tf_op jit(solution)/shard_map/ppermute | solution.py:687
  26.8 14.4 %collective-permute-start.19 = (bf16[64,5120]{1,0:T(8,128)(2,1)}, bf16[64,5120]{1,0:T(8,128)(2,1)S(1)}, u32[]{:S(2)}, u32[]{:S(2)}) collective-permute-start(bf16[64,5120]{1,0:T(8,128)(2,1)} %get-tuple-element.90), channel_id=1, source_target_pairs={{0,16},{8,24},{16,0},{24,8},{1,17},{9,25},{17,1},{25,9},{2,18},{10... | collective-permute-start | bytes 1966088 | tf_op jit(solution)/shard_map/ppermute | solution.py:684
  31.4 12.8 %collective-permute-start.8 = (bf16[256,1024]{1,0:T(8,128)(2,1)}, bf16[256,1024]{1,0:T(8,128)(2,1)}, u32[]{:S(2)}, u32[]{:S(2)}) collective-permute-start(bf16[256,1024]{1,0:T(8,128)(2,1)} %collective-permute-done.5.rest_2_), channel_id=1, source_target_pairs={{0,8},{8,0},{16,24},{24,16},{1,9},{9,1},{17,25},{25,17},{2,10},{10... | collective-permute-start | bytes 1572872 | tf_op jit(solution)/shard_map/ppermute | solution.py:681
  33.9 10.4 %collective-permute-start.7 = (bf16[256,1024]{1,0:T(8,128)(2,1)}, bf16[256,1024]{1,0:T(8,128)(2,1)}, u32[]{:S(2)}, u32[]{:S(2)}) collective-permute-start(bf16[256,1024]{1,0:T(8,128)(2,1)} %collective-permute-done.4.rest_1_), channel_id=1, source_target_pairs={{0,8},{8,0},{16,24},{24,16},{1,9},{9,1},{17,25},{25,17},{2,10},{10... | collective-permute-start | bytes 1572872 | tf_op jit(solution)/shard_map/ppermute | solution.py:681
  34.0 10.9 %collective-permute-start.6 = (bf16[256,1024]{1,0:T(8,128)(2,1)S(1)}, bf16[256,1024]{1,0:T(8,128)(2,1)}, u32[]{:S(2)}, u32[]{:S(2)}) collective-permute-start(bf16[256,1024]{1,0:T(8,128)(2,1)S(1)} %collective-permute-done.3.rest_0_.tok), channel_id=1, source_target_pairs={{0,8},{8,0},{16,24},{24,16},{1,9},{9,1},{17,25},{25,17},{2,10},{10... | collective-permute-start | bytes 1572872 | tf_op jit(solution)/shard_map/ppermute | solution.py:681
  36.1 2.7 %collective-permute-start.2 = (s32[1,8]{1,0:T(1,128)S(1)}, s32[1,8]{1,0:T(1,128)S(1)}, u32[]{:S(2)}, u32[]{:S(2)}) collective-permute-start(s32[1,8]{1,0:T(1,128)S(1)} %copy-done.30), channel_id=1, source_target_pairs={{0,8},{8,0},{16,24},{24,16},{1,9},{9,1},{17,25},{25,17},{2,10},{10... | collective-permute-start | bytes 104 | tf_op jit(solution)/shard_map/ppermute | solution.py:681
  38.8 6.2 %collective-permute-start.9 = (bf16[256,1024]{1,0:T(8,128)(2,1)}, bf16[256,1024]{1,0:T(8,128)(2,1)S(1)}, u32[]{:S(2)}, u32[]{:S(2)}) collective-permute-start(bf16[256,1024]{1,0:T(8,128)(2,1)} %rest_6_.1), channel_id=1, source_target_pairs={{0,8},{8,0},{16,24},{24,16},{1,9},{9,1},{17,25},{25,17},{2,10},{10... | collective-permute-start | bytes 1572872 | tf_op jit(solution)/shard_map/ppermute | solution.py:681
  41.2 8.9 %collective-permute-start.13 = (bf16[128,3072]{1,0:T(8,128)(2,1)S(1)}, bf16[128,3072]{1,0:T(8,128)(2,1)S(1)}, u32[]{:S(2)}, u32[]{:S(2)}) collective-permute-start(bf16[128,3072]{1,0:T(8,128)(2,1)S(1)} %collective-permute-done.rest_12_), channel_id=1, source_target_pairs={{0,8},{8,0},{16,24},{24,16},{1,9},{9,1},{17,25},{25,17},{2,10},{10... | collective-permute-start | bytes 2359304 | tf_op jit(solution)/shard_map/ppermute | solution.py:681
  44.3 2.9 %collective-permute-start.10 = (bf16[256,1024]{1,0:T(8,128)(2,1)}, bf16[256,1024]{1,0:T(8,128)(2,1)}, u32[]{:S(2)}, u32[]{:S(2)}) collective-permute-start(bf16[256,1024]{1,0:T(8,128)(2,1)} %rest_7_.1), channel_id=1, source_target_pairs={{0,8},{8,0},{16,24},{24,16},{1,9},{9,1},{17,25},{25,17},{2,10},{10... | collective-permute-start | bytes 1572872 | tf_op jit(solution)/shard_map/ppermute | solution.py:681
  44.3 4.0 %collective-permute-start.11 = (bf16[256,1024]{1,0:T(8,128)(2,1)}, bf16[256,1024]{1,0:T(8,128)(2,1)}, u32[]{:S(2)}, u32[]{:S(2)}) collective-permute-start(bf16[256,1024]{1,0:T(8,128)(2,1)} %rest_8_.1), channel_id=1, source_target_pairs={{0,8},{8,0},{16,24},{24,16},{1,9},{9,1},{17,25},{25,17},{2,10},{10... | collective-permute-start | bytes 1572872 | tf_op jit(solution)/shard_map/ppermute | solution.py:681
  44.9 3.7 %collective-permute-start.15 = (bf16[64,3072]{1,0:T(8,128)(2,1)}, bf16[64,3072]{1,0:T(8,128)(2,1)}, u32[]{:S(2)}, u32[]{:S(2)}) collective-permute-start(bf16[64,3072]{1,0:T(8,128)(2,1)} %copy-done.39), channel_id=1, source_target_pairs={{0,8},{8,0},{16,24},{24,16},{1,9},{9,1},{17,25},{25,17},{2,10},{10... | collective-permute-start | bytes 1179656 | tf_op jit(solution)/shard_map/ppermute | solution.py:681
  45.0 4.1 %collective-permute-start.14 = (bf16[64,3072]{1,0:T(8,128)(2,1)}, bf16[64,3072]{1,0:T(8,128)(2,1)}, u32[]{:S(2)}, u32[]{:S(2)}) collective-permute-start(bf16[64,3072]{1,0:T(8,128)(2,1)} %collective-permute-done.1.rest_13_), channel_id=1, source_target_pairs={{0,8},{8,0},{16,24},{24,16},{1,9},{9,1},{17,25},{25,17},{2,10},{10... | collective-permute-start | bytes 1179656 | tf_op jit(solution)/shard_map/ppermute | solution.py:681
  47.2 29.1 %collective-permute-start.20 = (bf16[64,5120]{1,0:T(8,128)(2,1)}, bf16[64,5120]{1,0:T(8,128)(2,1)S(1)}, u32[]{:S(2)}, u32[]{:S(2)}) collective-permute-start(bf16[64,5120]{1,0:T(8,128)(2,1)} %get-tuple-element.92), channel_id=1, source_target_pairs={{0,16},{8,24},{16,0},{24,8},{1,17},{9,25},{17,1},{25,9},{2,18},{10... | collective-permute-start | bytes 1966088 | tf_op jit(solution)/shard_map/ppermute | solution.py:684
  48.3 27.5 %collective-permute-start.22 = (bf16[64,5120]{1,0:T(8,128)(2,1)S(1)}, bf16[64,5120]{1,0:T(8,128)(2,1)}, u32[]{:S(2)}, u32[]{:S(2)}) collective-permute-start(bf16[64,5120]{1,0:T(8,128)(2,1)S(1)} %collective-permute-done.19.rest_4_), channel_id=1, source_target_pairs={{0,2},{1,3},{2,0},{3,1},{4,6},{5,7},{6,4},{7,5},{8,10},{9,11},{10,... | collective-permute-start | bytes 1966088 | tf_op jit(solution)/shard_map/ppermute | solution.py:687
  48.6 27.3 %collective-permute-start.21 = (bf16[64,5120]{1,0:T(8,128)(2,1)S(1)}, bf16[64,5120]{1,0:T(8,128)(2,1)}, u32[]{:S(2)}, u32[]{:S(2)}) collective-permute-start(bf16[64,5120]{1,0:T(8,128)(2,1)S(1)} %collective-permute-done.19.rest_4_), channel_id=1, source_target_pairs={{0,1},{1,0},{2,3},{3,2},{4,5},{5,4},{6,7},{7,6},{8,9},{9,8},{10,11... | collective-permute-start | bytes 1966088 | tf_op jit(solution)/shard_map/ppermute | solution.py:687
  49.0 25.5 %collective-permute-start.23 = (bf16[256,1024]{1,0:T(8,128)(2,1)}, bf16[256,1024]{1,0:T(8,128)(2,1)S(1)}, u32[]{:S(2)}, u32[]{:S(2)}) collective-permute-start(bf16[256,1024]{1,0:T(8,128)(2,1)} %get-tuple-element.94), channel_id=1, source_target_pairs={{0,16},{8,24},{16,0},{24,8},{1,17},{9,25},{17,1},{25,9},{2,18},{10... | collective-permute-start | bytes 1572872 | tf_op jit(solution)/shard_map/ppermute | solution.py:684
  50.2 33.4 %collective-permute-start.17 = (bf16[256,4096]{1,0:T(8,128)(2,1)}, bf16[256,4096]{1,0:T(8,128)(2,1)}, u32[]{:S(2)}, u32[]{:S(2)}) collective-permute-start(bf16[256,4096]{1,0:T(8,128)(2,1)} %rest_0_.7), channel_id=1, source_target_pairs={{0,8},{8,0},{16,24},{24,16},{1,9},{9,1},{17,25},{25,17},{2,10},{10... | collective-permute-start | bytes 6291464 | tf_op jit(solution)/shard_map/ppermute | solution.py:681
  51.1 24.7 %copy-start.6 = (bf16[256,1024]{1,0:T(8,128)(2,1)S(1)}, bf16[256,1024]{1,0:T(8,128)(2,1)}, u32[]{:S(2)}) copy-start(bf16[256,1024]{1,0:T(8,128)(2,1)} %rest_1_.7) | copy-start | bytes 1572868
  51.1 33.2 %copy-start.5 = (s32[20]{0:T(128)S(1)}, s32[20]{0:T(128)}, u32[]{:S(2)}) copy-start(s32[20]{0:T(128)} %stack.80.info) | copy-start | bytes 244
  51.1 33.2 %copy-start.9 = (bf16[4096]{0:T(1024)(128)(2,1)S(1)}, bf16[4096]{0:T(1024)(128)(2,1)}, u32[]{:S(2)}) copy-start(bf16[4096]{0:T(1024)(128)(2,1)} %bu.1) | copy-start | bytes 24580
  51.1 33.2 %copy-start.10 = (bf16[1024]{0:T(1024)(128)(2,1)S(1)}, bf16[1024]{0:T(1024)(128)(2,1)}, u32[]{:S(2)}) copy-start(bf16[1024]{0:T(1024)(128)(2,1)} %bo.1) | copy-start | bytes 6148
  51.1 33.2 %copy-start.11 = (bf16[1024]{0:T(1024)(128)(2,1)S(1)}, bf16[1024]{0:T(1024)(128)(2,1)}, u32[]{:S(2)}) copy-start(bf16[1024]{0:T(1024)(128)(2,1)} %ga.3) | copy-start | bytes 6148
  51.1 33.2 %copy-start.12 = (bf16[1024]{0:T(1024)(128)(2,1)S(1)}, bf16[1024]{0:T(1024)(128)(2,1)}, u32[]{:S(2)}) copy-start(bf16[1024]{0:T(1024)(128)(2,1)} %sa.3) | copy-start | bytes 6148
  74.6 4.6 %collective-permute-start.24 = (bf16[64,5120]{1,0:T(8,128)(2,1)S(1)}, bf16[64,5120]{1,0:T(8,128)(2,1)S(1)}, u32[]{:S(2)}, u32[]{:S(2)}) collective-permute-start(bf16[64,5120]{1,0:T(8,128)(2,1)S(1)} %collective-permute-done.19.rest_4_), channel_id=1, source_target_pairs={{0,8},{8,0},{16,24},{24,16},{1,9},{9,1},{17,25},{25,17},{2,10},{10... | collective-permute-start | bytes 1966088 | tf_op jit(solution)/shard_map/ppermute | solution.py:681
  75.8 2.8 %collective-permute-start.18 = (bf16[256,1024]{1,0:T(8,128)(2,1)S(1)}, bf16[256,1024]{1,0:T(8,128)(2,1)S(1)}, u32[]{:S(2)}, u32[]{:S(2)}) collective-permute-start(bf16[256,1024]{1,0:T(8,128)(2,1)S(1)} %copy-done.6), channel_id=1, source_target_pairs={{0,8},{8,0},{16,24},{24,16},{1,9},{9,1},{17,25},{25,17},{2,10},{10... | collective-permute-start | bytes 1572872 | tf_op jit(solution)/shard_map/ppermute | solution.py:681
  75.8 3.1 %collective-permute-start.16 = (bf16[256,512]{1,0:T(8,128)(2,1)}, bf16[256,512]{1,0:T(8,128)(2,1)S(1)}, u32[]{:S(2)}, u32[]{:S(2)}) collective-permute-start(bf16[256,512]{1,0:T(8,128)(2,1)} %get-tuple-element.87), channel_id=1, source_target_pairs={{0,8},{8,0},{16,24},{24,16},{1,9},{9,1},{17,25},{25,17},{2,10},{10... | collective-permute-start | bytes 786440 | tf_op jit(solution)/shard_map/ppermute | solution.py:681
  76.3 3.3 %collective-permute-start.25 = (bf16[64,5120]{1,0:T(8,128)(2,1)S(1)}, bf16[64,5120]{1,0:T(8,128)(2,1)S(1)}, u32[]{:S(2)}, u32[]{:S(2)}) collective-permute-start(bf16[64,5120]{1,0:T(8,128)(2,1)S(1)} %collective-permute-done.20.rest_5_), channel_id=1, source_target_pairs={{0,8},{8,0},{16,24},{24,16},{1,9},{9,1},{17,25},{25,17},{2,10},{10... | collective-permute-start | bytes 1966088 | tf_op jit(solution)/shard_map/ppermute | solution.py:681
  78.6 3.5 %collective-permute-start.26 = (bf16[64,5120]{1,0:T(8,128)(2,1)}, bf16[64,5120]{1,0:T(8,128)(2,1)S(1)}, u32[]{:S(2)}, u32[]{:S(2)}) collective-permute-start(bf16[64,5120]{1,0:T(8,128)(2,1)} %collective-permute-done.21.rest_6_), channel_id=1, source_target_pairs={{0,8},{8,0},{16,24},{24,16},{1,9},{9,1},{17,25},{25,17},{2,10},{10... | collective-permute-start | bytes 1966088 | tf_op jit(solution)/shard_map/ppermute | solution.py:681
  79.0 4.5 %collective-permute-start.27 = (bf16[64,5120]{1,0:T(8,128)(2,1)}, bf16[64,5120]{1,0:T(8,128)(2,1)S(1)}, u32[]{:S(2)}, u32[]{:S(2)}) collective-permute-start(bf16[64,5120]{1,0:T(8,128)(2,1)} %collective-permute-done.22.rest_7_), channel_id=1, source_target_pairs={{0,8},{8,0},{16,24},{24,16},{1,9},{9,1},{17,25},{25,17},{2,10},{10... | collective-permute-start | bytes 1966088 | tf_op jit(solution)/shard_map/ppermute | solution.py:681
  79.1 23.6 %collective-permute-start.29 = (bf16[1024,1024]{1,0:T(8,128)(2,1)}, bf16[1024,1024]{1,0:T(8,128)(2,1)S(1)}, u32[]{:S(2)}, u32[]{:S(2)}) collective-permute-start(bf16[1024,1024]{1,0:T(8,128)(2,1)} %rest_12_.1), channel_id=1, source_target_pairs={{0,8},{8,0},{16,24},{24,16},{1,9},{9,1},{17,25},{25,17},{2,10},{10... | collective-permute-start | bytes 6291464 | tf_op jit(solution)/shard_map/ppermute | solution.py:681
  79.5 17.2 %collective-permute-start.28 = (bf16[256,1024]{1,0:T(8,128)(2,1)}, bf16[256,1024]{1,0:T(8,128)(2,1)S(1)}, u32[]{:S(2)}, u32[]{:S(2)}) collective-permute-start(bf16[256,1024]{1,0:T(8,128)(2,1)} %bitcast.40), channel_id=1, source_target_pairs={{0,0},{1,8},{2,2},{3,10},{4,4},{5,12},{6,6},{7,14},{8,1},{9,9},{10... | collective-permute-start | bytes 1572872 | tf_op jit(solution)/shard_map/ppermute | solution.py:712
  82.2 17.4 %collective-permute-start.30 = (bf16[256,1024]{1,0:T(8,128)(2,1)}, bf16[256,1024]{1,0:T(8,128)(2,1)S(1)}, u32[]{:S(2)}, u32[]{:S(2)}) collective-permute-start(bf16[256,1024]{1,0:T(8,128)(2,1)} %get-tuple-element.109), channel_id=1, source_target_pairs={{0,16},{8,24},{16,0},{24,8},{1,17},{9,25},{17,1},{25,9},{2,18},{10... | collective-permute-start | bytes 1572872 | tf_op jit(solution)/shard_map/ppermute | solution.py:684
  83.5 14.9 %collective-permute-start.32 = (bf16[256,1024]{1,0:T(8,128)(2,1)S(1)}, bf16[256,1024]{1,0:T(8,128)(2,1)S(1)}, u32[]{:S(2)}, u32[]{:S(2)}) collective-permute-start(bf16[256,1024]{1,0:T(8,128)(2,1)S(1)} %collective-permute-done.23.rest_14_), channel_id=1, source_target_pairs={{0,2},{1,3},{2,0},{3,1},{4,6},{5,7},{6,4},{7,5},{8,10},{9,11},{10,... | collective-permute-start | bytes 1572872 | tf_op jit(solution)/shard_map/ppermute | solution.py:687
  83.6 16.0 %collective-permute-start.31 = (bf16[256,1024]{1,0:T(8,128)(2,1)S(1)}, bf16[256,1024]{1,0:T(8,128)(2,1)S(1)}, u32[]{:S(2)}, u32[]{:S(2)}) collective-permute-start(bf16[256,1024]{1,0:T(8,128)(2,1)S(1)} %collective-permute-done.23.rest_14_), channel_id=1, source_target_pairs={{0,1},{1,0},{2,3},{3,2},{4,5},{5,4},{6,7},{7,6},{8,9},{9,8},{10,11... | collective-permute-start | bytes 1572872 | tf_op jit(solution)/shard_map/ppermute | solution.py:687
  86.3 18.9 %copy-start.13 = (bf16[1024]{0:T(1024)(128)(2,1)S(1)}, bf16[1024]{0:T(1024)(128)(2,1)}, u32[]{:S(2)}) copy-start(bf16[1024]{0:T(1024)(128)(2,1)} %bd.1) | copy-start | bytes 6148
  86.3 18.9 %copy-start.14 = (bf16[1024]{0:T(1024)(128)(2,1)S(1)}, bf16[1024]{0:T(1024)(128)(2,1)}, u32[]{:S(2)}) copy-start(bf16[1024]{0:T(1024)(128)(2,1)} %gf.1) | copy-start | bytes 6148
  86.3 18.9 %copy-start.15 = (bf16[1024]{0:T(1024)(128)(2,1)S(1)}, bf16[1024]{0:T(1024)(128)(2,1)}, u32[]{:S(2)}) copy-start(bf16[1024]{0:T(1024)(128)(2,1)} %sf.1) | copy-start | bytes 6148
  96.7 6.0 %collective-permute-start.33 = (bf16[256,1024]{1,0:T(8,128)(2,1)S(1)}, bf16[256,1024]{1,0:T(8,128)(2,1)S(1)}, u32[]{:S(2)}, u32[]{:S(2)}) collective-permute-start(bf16[256,1024]{1,0:T(8,128)(2,1)S(1)} %collective-permute-done.23.rest_14_), channel_id=1, source_target_pairs={{0,8},{8,0},{16,24},{24,16},{1,9},{9,1},{17,25},{25,17},{2,10},{10... | collective-permute-start | bytes 1572872 | tf_op jit(solution)/shard_map/ppermute | solution.py:681
  99.5 4.2 %collective-permute-start.34 = (bf16[256,1024]{1,0:T(8,128)(2,1)S(1)}, bf16[256,1024]{1,0:T(8,128)(2,1)S(1)}, u32[]{:S(2)}, u32[]{:S(2)}) collective-permute-start(bf16[256,1024]{1,0:T(8,128)(2,1)S(1)} %collective-permute-done.30.rest_15_), channel_id=1, source_target_pairs={{0,8},{8,0},{16,24},{24,16},{1,9},{9,1},{17,25},{25,17},{2,10},{10... | collective-permute-start | bytes 1572872 | tf_op jit(solution)/shard_map/ppermute | solution.py:681
  102.2 2.3 %collective-permute-start.35 = (bf16[256,1024]{1,0:T(8,128)(2,1)S(1)}, bf16[256,1024]{1,0:T(8,128)(2,1)S(1)}, u32[]{:S(2)}, u32[]{:S(2)}) collective-permute-start(bf16[256,1024]{1,0:T(8,128)(2,1)S(1)} %collective-permute-done.31.rest_16_), channel_id=1, source_target_pairs={{0,8},{8,0},{16,24},{24,16},{1,9},{9,1},{17,25},{25,17},{2,10},{10... | collective-permute-start | bytes 1572872 | tf_op jit(solution)/shard_map/ppermute | solution.py:681
  102.2 3.0 %collective-permute-start.36 = (bf16[256,1024]{1,0:T(8,128)(2,1)S(1)}, bf16[256,1024]{1,0:T(8,128)(2,1)S(1)}, u32[]{:S(2)}, u32[]{:S(2)}) collective-permute-start(bf16[256,1024]{1,0:T(8,128)(2,1)S(1)} %collective-permute-done.32.rest_17_), channel_id=1, source_target_pairs={{0,8},{8,0},{16,24},{24,16},{1,9},{9,1},{17,25},{25,17},{2,10},{10... | collective-permute-start | bytes 1572872 | tf_op jit(solution)/shard_map/ppermute | solution.py:681
  105.2 17.1 %copy-start.16 = (f32[512,512]{1,0:T(8,128)S(1)}, f32[512,512]{1,0:T(8,128)}, u32[]{:S(2)}) copy-start(f32[512,512]{1,0:T(8,128)} %get-tuple-element.115.ot_ref) | copy-start | bytes 3145732
  105.2 17.1 %copy-start.17 = (bf16[512,512]{1,0:T(8,128)(2,1)S(1)}, bf16[512,512]{1,0:T(8,128)(2,1)}, u32[]{:S(2)}) copy-start(bf16[512,512]{1,0:T(8,128)(2,1)} %get-tuple-element.78.q_ref) | copy-start | bytes 1572868
  105.2 17.1 %copy-start.18 = (bf16[512,512]{1,0:T(8,128)(2,1)S(1)}, bf16[512,512]{1,0:T(8,128)(2,1)}, u32[]{:S(2)}) copy-start(bf16[512,512]{1,0:T(8,128)(2,1)} %get-tuple-element.79.qt_ref) | copy-start | bytes 1572868
  105.3 17.1 %copy-start.24 = (bf16[512,64]{1,0:T(8,128)(2,1)S(1)}, bf16[512,64]{1,0:T(8,128)(2,1)}, u32[]{:S(2)}) copy-start(bf16[512,64]{1,0:T(8,128)(2,1)} %get-tuple-element.84.pkt_ref) | copy-start | bytes 196612
  105.3 17.1 %copy-start.26 = (bf16[64,512]{1,0:T(8,128)(2,1)S(1)}, bf16[64,512]{1,0:T(8,128)(2,1)}, u32[]{:S(2)}) copy-start(bf16[64,512]{1,0:T(8,128)(2,1)} %get-tuple-element.83.pk_ref) | copy-start | bytes 196612
  105.3 17.1 %copy-start.27 = (bf16[64,512]{1,0:T(8,128)(2,1)S(1)}, bf16[64,512]{1,0:T(8,128)(2,1)}, u32[]{:S(2)}) copy-start(bf16[64,512]{1,0:T(8,128)(2,1)} %get-tuple-element.85.pv_ref) | copy-start | bytes 196612
  119.9 2.4 %collective-permute-start.37 = (bf16[256,512]{1,0:T(8,128)(2,1)S(1)}, bf16[256,512]{1,0:T(8,128)(2,1)S(1)}, u32[]{:S(2)}, u32[]{:S(2)}) collective-permute-start(bf16[256,512]{1,0:T(8,128)(2,1)S(1)} %get-tuple-element.114), channel_id=1, source_target_pairs={{0,8},{8,0},{16,24},{24,16},{1,9},{9,1},{17,25},{25,17},{2,10},{10... | collective-permute-start | bytes 786440 | tf_op jit(solution)/shard_map/ppermute | solution.py:681
  120.4 12.0 %collective-permute-start.38 = (bf16[256,1024]{1,0:T(8,128)(2,1)S(1)}, bf16[256,1024]{1,0:T(8,128)(2,1)S(1)}, u32[]{:S(2)}, u32[]{:S(2)}) collective-permute-start(bf16[256,1024]{1,0:T(8,128)(2,1)S(1)} %get-tuple-element.122), channel_id=1, source_target_pairs={{0,0},{1,8},{2,2},{3,10},{4,4},{5,12},{6,6},{7,14},{8,1},{9,9},{10... | collective-permute-start | bytes 1572872 | tf_op jit(solution)/shard_map/ppermute | solution.py:712
  124.6 7.7 %collective-permute-start.39 = (bf16[128,512]{1,0:T(8,128)(2,1)S(1)}, bf16[128,512]{1,0:T(8,128)(2,1)S(1)}, u32[]{:S(2)}, u32[]{:S(2)}) collective-permute-start(bf16[128,512]{1,0:T(8,128)(2,1)S(1)} %convert_element_type.66), channel_id=1, source_target_pairs={{0,16},{1,17},{2,18},{3,19},{4,20},{5,21},{6,22},{7,23},{8,24},{9,... | collective-permute-start | bytes 393224 | tf_op jit(solution)/shard_map/ppermute | solution.py:691
  132.3 2.7 %collective-permute-start.40 = (bf16[512,1024]{1,0:T(8,128)(2,1)S(1)}, bf16[512,1024]{1,0:T(8,128)(2,1)S(1)}, u32[]{:S(2)}, u32[]{:S(2)}) collective-permute-start(bf16[512,1024]{1,0:T(8,128)(2,1)S(1)} %get-tuple-element.126), channel_id=1, source_target_pairs={{0,8},{8,0},{16,24},{24,16},{1,9},{9,1},{17,25},{25,17},{2,10},{10... | collective-permute-start | bytes 3145736 | tf_op jit(solution)/shard_map/ppermute | solution.py:681
  135.5 15.3 %collective-permute-start.42 = (bf16[256,1024]{1,0:T(8,128)(2,1)S(1)}, bf16[256,1024]{1,0:T(8,128)(2,1)S(1)}, u32[]{:S(2)}, u32[]{:S(2)}) collective-permute-start(bf16[256,1024]{1,0:T(8,128)(2,1)S(1)} %get-tuple-element.133), channel_id=1, source_target_pairs={{0,2},{1,3},{2,0},{3,1},{4,6},{5,7},{6,4},{7,5},{8,10},{9,11},{10,... | collective-permute-start | bytes 1572872 | tf_op jit(solution)/shard_map/ppermute | solution.py:704
  138.6 9.8 %collective-permute-start.41 = (bf16[128,512]{1,0:T(8,128)(2,1)S(1)}, bf16[128,512]{1,0:T(8,128)(2,1)S(1)}, u32[]{:S(2)}, u32[]{:S(2)}) collective-permute-start(bf16[128,512]{1,0:T(8,128)(2,1)S(1)} %convert_add_fusion.2), channel_id=1, source_target_pairs={{0,1},{1,0},{2,3},{3,2},{4,5},{5,4},{6,7},{7,6},{8,9},{9,8},{10,11... | collective-permute-start | bytes 393224 | tf_op jit(solution)/shard_map/ppermute | solution.py:691
  138.9 9.6 %collective-permute-start.43 = (bf16[256,1024]{1,0:T(8,128)(2,1)S(1)}, bf16[256,1024]{1,0:T(8,128)(2,1)S(1)}, u32[]{:S(2)}, u32[]{:S(2)}) collective-permute-start(bf16[256,1024]{1,0:T(8,128)(2,1)S(1)} %get-tuple-element.136), channel_id=1, source_target_pairs={{0,0},{1,1},{2,4},{3,5},{4,2},{5,3},{6,6},{7,7},{8,8},{9,9},{10,12... | collective-permute-start | bytes 1572872 | tf_op jit(solution)/shard_map/ppermute | solution.py:704
  150.8 6.7 %collective-permute-start.44 = (bf16[256,1024]{1,0:T(8,128)(2,1)S(1)}, bf16[256,1024]{1,0:T(8,128)(2,1)S(1)}, u32[]{:S(2)}, u32[]{:S(2)}) collective-permute-start(bf16[256,1024]{1,0:T(8,128)(2,1)S(1)} %get-tuple-element.138), channel_id=1, source_target_pairs={{0,8},{8,0},{16,24},{24,16},{1,9},{9,1},{17,25},{25,17},{2,10},{10... | collective-permute-start | bytes 1572872 | tf_op jit(solution)/shard_map/ppermute | solution.py:681
  151.5 9.9 %collective-permute-start.46 = (bf16[128,512]{1,0:T(8,128)(2,1)S(1)}, bf16[128,512]{1,0:T(8,128)(2,1)S(1)}, u32[]{:S(2)}, u32[]{:S(2)}) collective-permute-start(bf16[128,512]{1,0:T(8,128)(2,1)S(1)} %convert_add_fusion.1), channel_id=1, source_target_pairs={{0,2},{1,3},{2,0},{3,1},{4,6},{5,7},{6,4},{7,5},{8,10},{9,11},{10,... | collective-permute-start | bytes 393224 | tf_op jit(solution)/shard_map/ppermute | solution.py:691
  157.8 12.0 %collective-permute-start.45 = (bf16[256,1024]{1,0:T(8,128)(2,1)S(1)}, bf16[256,1024]{1,0:T(8,128)(2,1)S(1)}, u32[]{:S(2)}, u32[]{:S(2)}) collective-permute-start(bf16[256,1024]{1,0:T(8,128)(2,1)S(1)} %add_convert_fusion), channel_id=1, source_target_pairs={{0,0},{1,8},{2,2},{3,10},{4,4},{5,12},{6,6},{7,14},{8,1},{9,9},{10... | collective-permute-start | bytes 1572872 | tf_op jit(solution)/shard_map/ppermute | solution.py:712
  161.4 8.4 %collective-permute-start.47 = (bf16[128,512]{1,0:T(8,128)(2,1)S(1)}, bf16[128,512]{1,0:T(8,128)(2,1)S(1)}, u32[]{:S(2)}, u32[]{:S(2)}) collective-permute-start(bf16[128,512]{1,0:T(8,128)(2,1)S(1)} %add_convert_fusion.3), channel_id=1, source_target_pairs={{0,4},{1,5},{2,6},{3,7},{4,0},{5,1},{6,2},{7,3},{8,12},{9,13},{10,... | collective-permute-start | bytes 393224 | tf_op jit(solution)/shard_map/ppermute | solution.py:691
  169.9 2.6 %collective-permute-start.48 = (f32[128,512]{1,0:T(8,128)S(1)}, f32[128,512]{1,0:T(8,128)S(1)}, u32[]{:S(2)}, u32[]{:S(2)}) collective-permute-start(f32[128,512]{1,0:T(8,128)S(1)} %convert_add_fusion), channel_id=1, source_target_pairs={{0,8},{8,0},{16,24},{24,16},{1,9},{9,1},{17,25},{25,17},{2,10},{10... | collective-permute-start | bytes 786440 | tf_op jit(solution)/shard_map/ppermute | solution.py:681
  (25 other events, 133.0 us)

commit v6 on v5

--- a/solution.py
+++ b/solution.py
@@ -167,7 +167,7 @@
         kt_ref[:, at] = full.T.astype(bf16)
         return carry
 
-    lax.fori_loop(0, blocks, key_block, 0, unroll=2)
+    lax.fori_loop(0, blocks, key_block, 0, unroll=3)
     wait_all(got_w[1])
 
     def value_block(b, carry):
@@ -177,7 +177,7 @@
         vt_ref[:, at] = full.T.astype(bf16)
         return carry
 
-    lax.fori_loop(0, blocks, value_block, 0, unroll=2)
+    lax.fori_loop(0, blocks, value_block, 0, unroll=3)
     wait_all(got_w[2])
 
     def query_block(b, carry):
@@ -405,8 +405,9 @@
     n_q = q_ref.shape[0]
     tokens = n_q // 2
     core = info[1 + 2 * (n_q // TILE)]
-    dk[...] = jnp.zeros_like(dk)
-    dv[...] = jnp.zeros_like(dv)
+    for ref in (dk, dv):
+        for low in (0, 2 * n_q):
+            ref[pl.ds(low, n_q), :] = jnp.zeros((n_q, ref.shape[1]), f32)
     dqt[...] = dqt_in[...]
 
     def one_query_tile(t, carry):
@@ -468,8 +469,8 @@
     n_q = q_ref.shape[0]
     tokens = n_q // 2
     dqt[...] = dqt_in[...]
-    dk[...] = jnp.zeros_like(dk)
-    dv[...] = jnp.zeros_like(dv)
+    for ref in (dk, dv):
+        ref[pl.ds(n_q, n_q), :] = jnp.zeros((n_q, ref.shape[1]), f32)
     side = 2 * tokens // TILE
 
     def one_query_tile(t, carry):

time: 175 us -> 174 us (level)
    ppermute x4, starting transfers between devices: 10 us -> 12.3 us  [by_both(): return lax.ppermute(a, ('row', 'seq'), route)]
    ppermute x2, waiting for transfers between devices: 2.31 us -> 0.01 us  [along(): lax.ppermute(a, 'seq', [(j, 2 * partner(j // 2) + (j & 1)) for j in range...]
  transfers between devices with their start and end apart: 49 -> 49, of which waited for: 17 -> 16; matrix products, arithmetic and copies ran while one was open for 1% -> 1% of each run, Pallas kernels for 28% -> 28%
where the time goes in v6:
time: 174 us
  Pallas kernels  66.4 us (38%)
  starting transfers between devices  62.7 us (36%)
  waiting for transfers between devices  35.2 us (20%)
  local copies, waits for them, and re-layouts  5.59 us (3%)
  other arithmetic  2.65 us (2%)
    ppermute x26, starting transfers between devices, by_core(): return lax.ppermute(a, 'row', [(i, i ^ 1) for i in range(n_row)])  21.8 us
    pallas_call x1, Pallas kernels, front(): pl.pallas_call(functools.partial(front_kernel, count=count, half=half), o...  17.8 us
    ppermute x6, starting transfers between devices, swapped(): return lax.ppermute(a, ('row', 'seq'), route)  16.3 us
    ppermute x5, waiting for transfers between devices, by_y(): return lax.ppermute(a, 'row', [(i, i ^ 2) for i in range(n_row)])  15.5 us
    pallas_call x1, Pallas kernels, down(): pl.pallas_call(functools.partial(down_kernel, count=count), out_shape=(sh...  14.6 us
    ppermute x4, starting transfers between devices, by_both(): return lax.ppermute(a, ('row', 'seq'), route)  12.3 us
    ppermute x26, waiting for transfers between devices, by_core(): return lax.ppermute(a, 'row', [(i, i ^ 1) for i in range(n_row)])  10.6 us
    pallas_call x1, Pallas kernels, up(): pl.pallas_call(functools.partial(up_kernel, count=count), out_shape=(shap...  10.4 us
  transfers between devices with their start and end apart: 49, of which 16 were waited for; matrix products, arithmetic and copies ran while one was open for 1% of the time, Pallas kernels for 28%

profile of v6, /device:TPU:1, one launch (start us, length us, event | category | flops | bytes accessed | tf_op | source)
XLA Modules:
  0.0 173.9 jit_solution(2006462548407594719)
XLA Ops:
  0.7 0.6 stack.80.info
  1.3 3.3 %pack.2 = (bf16[128,3072]{1,0:T(8,128)(2,1)}, bf16[64,5120]{1,0:T(8,128)(2,1)}) custom-call(s32[20]{0:T(128)} %stack.80.info, bf16[256,1024]{1,0:T(8,128)(2,1)} %rest_6_.1, bf16[256,1024]{1,0:T(8,128)(2,1)} %rest_7_.1, bf16[256,1024]{1,0:T(8,128)(2,1)} %rest_8_.1, bf16[256,4096]{1,0:T(8,128)(2,1)} %rest_0_.7, bf16[256,1024]{1,0:T(8,128)(2,1)} %rest_1_.7), custom_call_target="tpu_custom_call" | custom-call | flops 2000000000 | tf_op jit(solution)/shard_map/pack/pallas_call | solution.py:77
  4.6 2.1 %collective-permute-start = (bf16[128,3072]{1,0:T(8,128)(2,1)}, bf16[128,3072]{1,0:T(8,128)(2,1)S(1)}, u32[]{:S(2)}, u32[]{:S(2)}) collective-permute-start(bf16[128,3072]{1,0:T(8,128)(2,1)} %get-tuple-element.73), channel_id=1, source_target_pairs={{0,16},{8,24},{16,0},{24,8},{1,17},{9,25},{17,1},{25,9},{2,18},{10... | collective-permute-start | bytes 2359304 | tf_op jit(solution)/shard_map/ppermute | solution.py:685
  6.7 3.9 %collective-permute-start.5 = (bf16[256,1024]{1,0:T(8,128)(2,1)S(1)}, bf16[256,1024]{1,0:T(8,128)(2,1)}, u32[]{:S(2)}, u32[]{:S(2)}) collective-permute-start(bf16[256,1024]{1,0:T(8,128)(2,1)S(1)} %bitcast.37), channel_id=1, source_target_pairs={{0,0},{1,8},{2,4},{3,12},{4,2},{5,10},{6,6},{7,14},{8,1},{9,9},{10... | collective-permute-start | bytes 1572872 | tf_op jit(solution)/shard_map/ppermute | solution.py:713
  10.7 1.8 %collective-permute-start.4 = (bf16[256,1024]{1,0:T(8,128)(2,1)S(1)}, bf16[256,1024]{1,0:T(8,128)(2,1)}, u32[]{:S(2)}, u32[]{:S(2)}) collective-permute-start(bf16[256,1024]{1,0:T(8,128)(2,1)S(1)} %bitcast.38), channel_id=1, source_target_pairs={{0,2},{1,10},{2,0},{3,8},{4,6},{5,14},{6,4},{7,12},{8,3},{9,11},{1... | collective-permute-start | bytes 1572872 | tf_op jit(solution)/shard_map/ppermute | solution.py:713
  12.4 3.9 %collective-permute-start.3 = (bf16[256,1024]{1,0:T(8,128)(2,1)S(1)}, bf16[256,1024]{1,0:T(8,128)(2,1)S(1)}, u32[]{:S(2)}, u32[]{:S(2)}) collective-permute-start(bf16[256,1024]{1,0:T(8,128)(2,1)S(1)} %bitcast.39), channel_id=1, source_target_pairs={{0,0},{1,8},{2,2},{3,10},{4,4},{5,12},{6,6},{7,14},{8,1},{9,9},{10... | collective-permute-start | bytes 1572872 | tf_op jit(solution)/shard_map/ppermute | solution.py:713
  16.4 7.9 %collective-permute-done.rest_12_ = bf16[128,3072]{1,0:T(8,128)(2,1)S(1)} collective-permute-done((bf16[128,3072]{1,0:T(8,128)(2,1)}, bf16[128,3072]{1,0:T(8,128)(2,1)S(1)}, u32[]{:S(2)}, u32[]{:S(2)}) %collective-permute-start) | collective-permute-done | bytes 786464 | tf_op jit(solution)/shard_map/ppermute | solution.py:685
  24.3 1.3 collective-permute-start.12
  25.6 1.2 collective-permute-start.1
  26.8 1.1 collective-permute-start.19
  27.9 3.5 %pack.3 = (bf16[256,1024]{1,0:T(8,128)(2,1)}, bf16[64,5120]{1,0:T(8,128)(2,1)}, bf16[256,1024]{1,0:T(8,128)(2,1)}) custom-call(s32[20]{0:T(128)} %stack.80.info, bf16[1024,1024]{1,0:T(8,128)(2,1)} %rest_12_.1, bf16[256,4096]{1,0:T(8,128)(2,1)} %rest_0_.7, bf16[256,1024]{1,0:T(8,128)(2,1)} %rest_1_.7), custom_call_target="tpu_custom_call" | custom-call | flops 2000000000 | tf_op jit(solution)/shard_map/pack/pallas_call | solution.py:77
  31.4 2.5 %collective-permute-start.8 = (bf16[256,1024]{1,0:T(8,128)(2,1)}, bf16[256,1024]{1,0:T(8,128)(2,1)}, u32[]{:S(2)}, u32[]{:S(2)}) collective-permute-start(bf16[256,1024]{1,0:T(8,128)(2,1)} %collective-permute-done.5.rest_2_), channel_id=1, source_target_pairs={{0,8},{8,0},{16,24},{24,16},{1,9},{9,1},{17,25},{25,17},{2,10},{10... | collective-permute-start | bytes 1572872 | tf_op jit(solution)/shard_map/ppermute | solution.py:682
  34.0 1.9 %collective-permute-start.6 = (bf16[256,1024]{1,0:T(8,128)(2,1)S(1)}, bf16[256,1024]{1,0:T(8,128)(2,1)}, u32[]{:S(2)}, u32[]{:S(2)}) collective-permute-start(bf16[256,1024]{1,0:T(8,128)(2,1)S(1)} %collective-permute-done.3.rest_0_.tok), channel_id=1, source_target_pairs={{0,8},{8,0},{16,24},{24,16},{1,9},{9,1},{17,25},{25,17},{2,10},{10... | collective-permute-start | bytes 1572872 | tf_op jit(solution)/shard_map/ppermute | solution.py:682
  36.1 1.9 %collective-permute-start.2 = (s32[1,8]{1,0:T(1,128)S(1)}, s32[1,8]{1,0:T(1,128)S(1)}, u32[]{:S(2)}, u32[]{:S(2)}) collective-permute-start(s32[1,8]{1,0:T(1,128)S(1)} %copy-done.30), channel_id=1, source_target_pairs={{0,8},{8,0},{16,24},{24,16},{1,9},{9,1},{17,25},{25,17},{2,10},{10... | collective-permute-start | bytes 104 | tf_op jit(solution)/shard_map/ppermute | solution.py:682
  38.0 0.8 collective-permute-done.2
  39.3 1.9 %collective-permute-done.19.rest_4_ = bf16[64,5120]{1,0:T(8,128)(2,1)S(1)} collective-permute-done((bf16[64,5120]{1,0:T(8,128)(2,1)}, bf16[64,5120]{1,0:T(8,128)(2,1)S(1)}, u32[]{:S(2)}, u32[]{:S(2)}) %collective-permute-start.19) | collective-permute-done | bytes 655392 | tf_op jit(solution)/shard_map/ppermute | solution.py:685
  41.2 2.9 %collective-permute-start.13 = (bf16[128,3072]{1,0:T(8,128)(2,1)S(1)}, bf16[128,3072]{1,0:T(8,128)(2,1)S(1)}, u32[]{:S(2)}, u32[]{:S(2)}) collective-permute-start(bf16[128,3072]{1,0:T(8,128)(2,1)S(1)} %collective-permute-done.rest_12_), channel_id=1, source_target_pairs={{0,8},{8,0},{16,24},{24,16},{1,9},{9,1},{17,25},{25,17},{2,10},{10... | collective-permute-start | bytes 2359304 | tf_op jit(solution)/shard_map/ppermute | solution.py:682
  44.3 0.5 collective-permute-start.11
  45.0 0.4 collective-permute-start.14
  45.6 0.7 pad_add_fusion.1.tiles.info
  46.3 0.9 collective-permute-done.10.rest_10_
  47.2 1.1 collective-permute-start.20
  49.0 1.1 collective-permute-start.23
  50.2 0.7 collective-permute-start.17
  51.1 17.8 %front.1 = (bf16[256,512]{1,0:T(8,128)(2,1)}, bf16[256,512]{1,0:T(8,128)(2,1)}, f32[512,512]{1,0:T(8,128)}, f32[8,512]{1,0:T(8,128)}, bf16[64,512]{1,0:T(8,128)(...) custom-call(s32[20]{0:T(128)} %stack.80.info, ...), custom_call_target="tpu_custom_call" | custom-call | flops 20000000000 | tf_op jit(solution)/shard_map/front/pallas_call | solution.py:270
  68.9 5.7 %collective-permute-done.23.rest_14_ = bf16[256,1024]{1,0:T(8,128)(2,1)S(1)} collective-permute-done((bf16[256,1024]{1,0:T(8,128)(2,1)}, bf16[256,1024]{1,0:T(8,128)(2,1)S(1)}, u32[]{:S(2)}, u32[]{:S(2)}) %collective-permute-start.23) | collective-permute-done | bytes 524320 | tf_op jit(solution)/shard_map/ppermute | solution.py:685
  74.6 1.2 collective-permute-start.24
  75.8 0.4 collective-permute-start.16
  76.4 2.2 %collective-permute-done.18.rest_3_ = bf16[256,1024]{1,0:T(8,128)(2,1)S(1)} collective-permute-done((bf16[256,1024]{1,0:T(8,128)(2,1)S(1)}, bf16[256,1024]{1,0:T(8,128)(2,1)S(1)}, u32[]{:S(2)}, u32[]{:S(2)}) %collective-permute-start.18) | collective-permute-done | bytes 524320 | tf_op jit(solution)/shard_map/ppermute | solution.py:682
  79.5 2.6 %collective-permute-start.28 = (bf16[256,1024]{1,0:T(8,128)(2,1)}, bf16[256,1024]{1,0:T(8,128)(2,1)S(1)}, u32[]{:S(2)}, u32[]{:S(2)}) collective-permute-start(bf16[256,1024]{1,0:T(8,128)(2,1)} %bitcast.40), channel_id=1, source_target_pairs={{0,0},{1,8},{2,2},{3,10},{4,4},{5,12},{6,6},{7,14},{8,1},{9,9},{10... | collective-permute-start | bytes 1572872 | tf_op jit(solution)/shard_map/ppermute | solution.py:713
  82.2 1.3 collective-permute-start.30
  83.6 0.7 copy-done.36
  84.3 1.0 copy-done.8
  85.4 0.9 copy-done.25
  86.3 10.4 %up.1 = (f32[256,1024]{1,0:T(8,128)}, f32[256,128]{1,0:T(8,128)S(1)}, bf16[256,4096]{1,0:T(8,128)(2,1)}, bf16[256,4096]{1,0:T(8,128)(2,1)}) custom-call(s32[20]{0:T(128)S(1)} %copy-done.5, bf16[256,512]{1,0:T(8,128)(2,1)S(1)} %copy-done.25, bf16[256,512]{1,0:T(8,128)(2,1)S(1)} %collective-permute-done.16.got_att, bf16[256,1024]{1,0:T(8,128)(2,1)S(1)} %copy-done.8, ...), custom_call_target="tpu_custom_call" | custom-call | flops 10000000000 | tf_op jit(solution)/shard_map/up/pallas_call | solution.py:583
  96.7 1.6 collective-permute-start.33
  98.4 1.1 collective-permute-done.31.rest_16_
  99.5 2.7 %collective-permute-start.34 = (bf16[256,1024]{1,0:T(8,128)(2,1)S(1)}, bf16[256,1024]{1,0:T(8,128)(2,1)S(1)}, u32[]{:S(2)}, u32[]{:S(2)}) collective-permute-start(bf16[256,1024]{1,0:T(8,128)(2,1)S(1)} %collective-permute-done.30.rest_15_), channel_id=1, source_target_pairs={{0,8},{8,0},{16,24},{24,16},{1,9},{9,1},{17,25},{25,17},{2,10},{10... | collective-permute-start | bytes 1572872 | tf_op jit(solution)/shard_map/ppermute | solution.py:682
  102.2 0.5 collective-permute-start.36
  102.7 1.0 collective-permute-done.34.rest_19_
  103.7 0.7 collective-permute-done.35.rest_20_
  104.5 0.7 collective-permute-done.36.rest_21_
  105.3 14.6 %down.1 = (bf16[256,1024]{1,0:T(8,128)(2,1)S(1)}, f32[256,1024]{1,0:T(8,128)}, bf16[256,512]{1,0:T(8,128)(2,1)S(1)}, bf16[256,512]{1,0:T(8,128)(2,1)S(1)}) custom-call(s32[20]{0:T(128)S(1)} %copy-done.5, f32[256,1024]{1,0:T(8,128)} %get-tuple-element.101.hat_ref, f32[256,128]{1,0:T(8,128)S(1)} %get-tuple-element.102.inv_ref, ...), custom_call_target="tpu_custom_call" | custom-call | flops 16000000000 | tf_op jit(solution)/shard_map/down/pallas_call | solution.py:648
  119.9 0.4 collective-permute-start.37
  120.4 1.9 %collective-permute-start.38 = (bf16[256,1024]{1,0:T(8,128)(2,1)S(1)}, bf16[256,1024]{1,0:T(8,128)(2,1)S(1)}, u32[]{:S(2)}, u32[]{:S(2)}) collective-permute-start(bf16[256,1024]{1,0:T(8,128)(2,1)S(1)} %get-tuple-element.122), channel_id=1, source_target_pairs={{0,0},{1,8},{2,2},{3,10},{4,4},{5,12},{6,6},{7,14},{8,1},{9,9},{10... | collective-permute-start | bytes 1572872 | tf_op jit(solution)/shard_map/ppermute | solution.py:713
  122.4 2.1 %prefix_grads.1 = (f32[128,512]{1,0:T(8,128)S(1)}, f32[512,512]{1,0:T(8,128)S(1)}, bf16[512,512]{1,0:T(8,128)(2,1)S(1)}, bf16[512,512]{1,0:T(8,128)(2,1)S(1)}, f32[8,512]{1,0:T(8,128)S(1)}) custom-call(s32[20]{0:T(128)S(1)} %copy-done.5, bf16[512,512]{1,0:T(8,128)(2,1)S(1)} %copy-done.17, bf16[512,512]{1,0:T(8,128)(2,1)S(1)} %copy-done.18, ...), custom_call_target="tpu_custom_call" | custom-call | flops 5000000000 | tf_op jit(solution)/shard_map/prefix_grads/pallas_call | solution.py:383
  124.6 1.2 collective-permute-start.39
  125.8 6.3 %remote_grads.1 = (bf16[512,1024]{1,0:T(8,128)(2,1)S(1)}, bf16[256,1024]{1,0:T(8,128)(2,1)S(1)}, bf16[256,1024]{1,0:T(8,128)(2,1)S(1)}, f32[512,512]{1,0:T(8,128)S(1)}) custom-call(s32[6]{0:T(128)S(1)} %copy-done.4, s32[1,512]{1,0:T(1,128)S(1)} %bitcast.33, s32[1,512]{1,0:T(1,128)S(1)} %bitcast.30, bf16[512,512]{1,0:T(8,128)(2,1)S(1)} %copy-done.17, ...), custom_call_target="tpu_custom_call" | custom-call | flops 14000000000 | tf_op jit(solution)/shard_map/remote_grads/pallas_call | solution.py:440
  132.2 2.6 %collective-permute-done.40 = bf16[512,1024]{1,0:T(8,128)(2,1)S(1)} collective-permute-done((bf16[512,1024]{1,0:T(8,128)(2,1)S(1)}, bf16[512,1024]{1,0:T(8,128)(2,1)S(1)}, u32[]{:S(2)}, u32[]{:S(2)}) %collective-permute-start.40) | collective-permute-done | bytes 1048608 | tf_op jit(solution)/shard_map/ppermute | solution.py:682
  135.3 1.7 collective-permute-start.42
  137.0 3.2 %collective-permute-start.41 = (bf16[128,512]{1,0:T(8,128)(2,1)S(1)}, bf16[128,512]{1,0:T(8,128)(2,1)S(1)}, u32[]{:S(2)}, u32[]{:S(2)}) collective-permute-start(bf16[128,512]{1,0:T(8,128)(2,1)S(1)} %convert_add_fusion.2), channel_id=1, source_target_pairs={{0,1},{1,0},{2,3},{3,2},{4,5},{5,4},{6,7},{7,6},{8,9},{9,8},{10,11... | collective-permute-start | bytes 393224 | tf_op jit(solution)/shard_map/ppermute | solution.py:692
  140.3 0.7 collective-permute-start.43
  141.0 8.5 %local_grads.1 = (f32[256,1024]{1,0:T(8,128)S(1)}, bf16[256,1024]{1,0:T(8,128)(2,1)S(1)}) custom-call(s32[6]{0:T(128)S(1)} %copy-done.4, s32[1,512]{1,0:T(1,128)S(1)} %bitcast.34, s32[1,512]{1,0:T(1,128)S(1)} %bitcast.31, bf16[512,512]{1,0:T(8,128)(2,1)S(1)} %copy-done.17, bf16[512,512]{1,0:T(8,128)(2,1)S(1)} %copy-done.18, ...), custom_call_target="tpu_custom_call" | custom-call | flops 14000000000 | tf_op jit(solution)/shard_map/local_grads/pallas_call | solution.py:506
  149.6 1.0 collective-permute-start.44
  150.5 6.0 %collective-permute-start.46 = (bf16[128,512]{1,0:T(8,128)(2,1)S(1)}, bf16[128,512]{1,0:T(8,128)(2,1)S(1)}, u32[]{:S(2)}, u32[]{:S(2)}) collective-permute-start(bf16[128,512]{1,0:T(8,128)(2,1)S(1)} %convert_add_fusion.1), channel_id=1, source_target_pairs={{0,2},{1,3},{2,0},{3,1},{4,6},{5,7},{6,4},{7,5},{8,10},{9,11},{10,... | collective-permute-start | bytes 393224 | tf_op jit(solution)/shard_map/ppermute | solution.py:692
  156.9 2.1 %collective-permute-start.45 = (bf16[256,1024]{1,0:T(8,128)(2,1)S(1)}, bf16[256,1024]{1,0:T(8,128)(2,1)S(1)}, u32[]{:S(2)}, u32[]{:S(2)}) collective-permute-start(bf16[256,1024]{1,0:T(8,128)(2,1)S(1)} %add_convert_fusion), channel_id=1, source_target_pairs={{0,0},{1,8},{2,2},{3,10},{4,4},{5,12},{6,6},{7,14},{8,1},{9,9},{10... | collective-permute-start | bytes 1572872 | tf_op jit(solution)/shard_map/ppermute | solution.py:713
  159.0 1.4 collective-permute-done.46
  160.5 1.9 %collective-permute-start.47 = (bf16[128,512]{1,0:T(8,128)(2,1)S(1)}, bf16[128,512]{1,0:T(8,128)(2,1)S(1)}, u32[]{:S(2)}, u32[]{:S(2)}) collective-permute-start(bf16[128,512]{1,0:T(8,128)(2,1)S(1)} %add_convert_fusion.3), channel_id=1, source_target_pairs={{0,4},{1,5},{2,6},{3,7},{4,0},{5,1},{6,2},{7,3},{8,12},{9,13},{10,... | collective-permute-start | bytes 393224 | tf_op jit(solution)/shard_map/ppermute | solution.py:692
  162.4 6.3 %collective-permute-done.47 = bf16[128,512]{1,0:T(8,128)(2,1)S(1)} collective-permute-done((bf16[128,512]{1,0:T(8,128)(2,1)S(1)}, bf16[128,512]{1,0:T(8,128)(2,1)S(1)}, u32[]{:S(2)}, u32[]{:S(2)}) %collective-permute-start.47) | collective-permute-done | bytes 131104 | tf_op jit(solution)/shard_map/ppermute | solution.py:692
  168.8 1.5 collective-permute-start.48
  170.3 1.2 collective-permute-done.48
  171.5 0.8 pad_maximum_fusion
  172.3 0.8 copy.28
  173.1 0.8 copy.29
  (148 shorter events, 4.6 us)
Async XLA Ops:
  4.6 19.7 %collective-permute-start = (bf16[128,3072]{1,0:T(8,128)(2,1)}, bf16[128,3072]{1,0:T(8,128)(2,1)S(1)}, u32[]{:S(2)}, u32[]{:S(2)}) collective-permute-start(bf16[128,3072]{1,0:T(8,128)(2,1)} %get-tuple-element.73), channel_id=1, source_target_pairs={{0,16},{8,24},{16,0},{24,8},{1,17},{9,25},{17,1},{25,9},{2,18},{10... | collective-permute-start | bytes 2359304 | tf_op jit(solution)/shard_map/ppermute | solution.py:685
  6.7 20.1 %collective-permute-start.5 = (bf16[256,1024]{1,0:T(8,128)(2,1)S(1)}, bf16[256,1024]{1,0:T(8,128)(2,1)}, u32[]{:S(2)}, u32[]{:S(2)}) collective-permute-start(bf16[256,1024]{1,0:T(8,128)(2,1)S(1)} %bitcast.37), channel_id=1, source_target_pairs={{0,0},{1,8},{2,4},{3,12},{4,2},{5,10},{6,6},{7,14},{8,1},{9,9},{10... | collective-permute-start | bytes 1572872 | tf_op jit(solution)/shard_map/ppermute | solution.py:713
  10.7 20.8 %collective-permute-start.4 = (bf16[256,1024]{1,0:T(8,128)(2,1)S(1)}, bf16[256,1024]{1,0:T(8,128)(2,1)}, u32[]{:S(2)}, u32[]{:S(2)}) collective-permute-start(bf16[256,1024]{1,0:T(8,128)(2,1)S(1)} %bitcast.38), channel_id=1, source_target_pairs={{0,2},{1,10},{2,0},{3,8},{4,6},{5,14},{6,4},{7,12},{8,3},{9,11},{1... | collective-permute-start | bytes 1572872 | tf_op jit(solution)/shard_map/ppermute | solution.py:713
  12.4 21.5 %collective-permute-start.3 = (bf16[256,1024]{1,0:T(8,128)(2,1)S(1)}, bf16[256,1024]{1,0:T(8,128)(2,1)S(1)}, u32[]{:S(2)}, u32[]{:S(2)}) collective-permute-start(bf16[256,1024]{1,0:T(8,128)(2,1)S(1)} %bitcast.39), channel_id=1, source_target_pairs={{0,0},{1,8},{2,2},{3,10},{4,4},{5,12},{6,6},{7,14},{8,1},{9,9},{10... | collective-permute-start | bytes 1572872 | tf_op jit(solution)/shard_map/ppermute | solution.py:713
  24.3 9.7 %collective-permute-start.12 = (bf16[64,3072]{1,0:T(8,128)(2,1)S(1)}, bf16[64,3072]{1,0:T(8,128)(2,1)S(1)}, u32[]{:S(2)}, u32[]{:S(2)}) collective-permute-start(bf16[64,3072]{1,0:T(8,128)(2,1)S(1)} %constant_dynamic-slice_fusion), channel_id=1, source_target_pairs={{0,2},{1,3},{2,0},{3,1},{4,6},{5,7},{6,4},{7,5},{8,10},{9,11},{10,... | collective-permute-start | bytes 1179656 | tf_op jit(solution)/shard_map/ppermute | solution.py:688
  25.6 10.5 %collective-permute-start.1 = (bf16[64,3072]{1,0:T(8,128)(2,1)S(1)}, bf16[64,3072]{1,0:T(8,128)(2,1)}, u32[]{:S(2)}, u32[]{:S(2)}) collective-permute-start(bf16[64,3072]{1,0:T(8,128)(2,1)S(1)} %constant_dynamic-slice_fusion), channel_id=1, source_target_pairs={{0,1},{1,0},{2,3},{3,2},{4,5},{5,4},{6,7},{7,6},{8,9},{9,8},{10,11... | collective-permute-start | bytes 1179656 | tf_op jit(solution)/shard_map/ppermute | solution.py:688
  26.8 14.4 %collective-permute-start.19 = (bf16[64,5120]{1,0:T(8,128)(2,1)}, bf16[64,5120]{1,0:T(8,128)(2,1)S(1)}, u32[]{:S(2)}, u32[]{:S(2)}) collective-permute-start(bf16[64,5120]{1,0:T(8,128)(2,1)} %get-tuple-element.90), channel_id=1, source_target_pairs={{0,16},{8,24},{16,0},{24,8},{1,17},{9,25},{17,1},{25,9},{2,18},{10... | collective-permute-start | bytes 1966088 | tf_op jit(solution)/shard_map/ppermute | solution.py:685
  31.4 12.8 %collective-permute-start.8 = (bf16[256,1024]{1,0:T(8,128)(2,1)}, bf16[256,1024]{1,0:T(8,128)(2,1)}, u32[]{:S(2)}, u32[]{:S(2)}) collective-permute-start(bf16[256,1024]{1,0:T(8,128)(2,1)} %collective-permute-done.5.rest_2_), channel_id=1, source_target_pairs={{0,8},{8,0},{16,24},{24,16},{1,9},{9,1},{17,25},{25,17},{2,10},{10... | collective-permute-start | bytes 1572872 | tf_op jit(solution)/shard_map/ppermute | solution.py:682
  33.9 10.4 %collective-permute-start.7 = (bf16[256,1024]{1,0:T(8,128)(2,1)}, bf16[256,1024]{1,0:T(8,128)(2,1)}, u32[]{:S(2)}, u32[]{:S(2)}) collective-permute-start(bf16[256,1024]{1,0:T(8,128)(2,1)} %collective-permute-done.4.rest_1_), channel_id=1, source_target_pairs={{0,8},{8,0},{16,24},{24,16},{1,9},{9,1},{17,25},{25,17},{2,10},{10... | collective-permute-start | bytes 1572872 | tf_op jit(solution)/shard_map/ppermute | solution.py:682
  34.0 10.9 %collective-permute-start.6 = (bf16[256,1024]{1,0:T(8,128)(2,1)S(1)}, bf16[256,1024]{1,0:T(8,128)(2,1)}, u32[]{:S(2)}, u32[]{:S(2)}) collective-permute-start(bf16[256,1024]{1,0:T(8,128)(2,1)S(1)} %collective-permute-done.3.rest_0_.tok), channel_id=1, source_target_pairs={{0,8},{8,0},{16,24},{24,16},{1,9},{9,1},{17,25},{25,17},{2,10},{10... | collective-permute-start | bytes 1572872 | tf_op jit(solution)/shard_map/ppermute | solution.py:682
  36.1 2.7 %collective-permute-start.2 = (s32[1,8]{1,0:T(1,128)S(1)}, s32[1,8]{1,0:T(1,128)S(1)}, u32[]{:S(2)}, u32[]{:S(2)}) collective-permute-start(s32[1,8]{1,0:T(1,128)S(1)} %copy-done.30), channel_id=1, source_target_pairs={{0,8},{8,0},{16,24},{24,16},{1,9},{9,1},{17,25},{25,17},{2,10},{10... | collective-permute-start | bytes 104 | tf_op jit(solution)/shard_map/ppermute | solution.py:682
  38.8 6.2 %collective-permute-start.9 = (bf16[256,1024]{1,0:T(8,128)(2,1)}, bf16[256,1024]{1,0:T(8,128)(2,1)S(1)}, u32[]{:S(2)}, u32[]{:S(2)}) collective-permute-start(bf16[256,1024]{1,0:T(8,128)(2,1)} %rest_6_.1), channel_id=1, source_target_pairs={{0,8},{8,0},{16,24},{24,16},{1,9},{9,1},{17,25},{25,17},{2,10},{10... | collective-permute-start | bytes 1572872 | tf_op jit(solution)/shard_map/ppermute | solution.py:682
  41.2 8.9 %collective-permute-start.13 = (bf16[128,3072]{1,0:T(8,128)(2,1)S(1)}, bf16[128,3072]{1,0:T(8,128)(2,1)S(1)}, u32[]{:S(2)}, u32[]{:S(2)}) collective-permute-start(bf16[128,3072]{1,0:T(8,128)(2,1)S(1)} %collective-permute-done.rest_12_), channel_id=1, source_target_pairs={{0,8},{8,0},{16,24},{24,16},{1,9},{9,1},{17,25},{25,17},{2,10},{10... | collective-permute-start | bytes 2359304 | tf_op jit(solution)/shard_map/ppermute | solution.py:682
  44.3 2.9 %collective-permute-start.10 = (bf16[256,1024]{1,0:T(8,128)(2,1)}, bf16[256,1024]{1,0:T(8,128)(2,1)}, u32[]{:S(2)}, u32[]{:S(2)}) collective-permute-start(bf16[256,1024]{1,0:T(8,128)(2,1)} %rest_7_.1), channel_id=1, source_target_pairs={{0,8},{8,0},{16,24},{24,16},{1,9},{9,1},{17,25},{25,17},{2,10},{10... | collective-permute-start | bytes 1572872 | tf_op jit(solution)/shard_map/ppermute | solution.py:682
  44.3 4.0 %collective-permute-start.11 = (bf16[256,1024]{1,0:T(8,128)(2,1)}, bf16[256,1024]{1,0:T(8,128)(2,1)}, u32[]{:S(2)}, u32[]{:S(2)}) collective-permute-start(bf16[256,1024]{1,0:T(8,128)(2,1)} %rest_8_.1), channel_id=1, source_target_pairs={{0,8},{8,0},{16,24},{24,16},{1,9},{9,1},{17,25},{25,17},{2,10},{10... | collective-permute-start | bytes 1572872 | tf_op jit(solution)/shard_map/ppermute | solution.py:682
  44.9 3.7 %collective-permute-start.15 = (bf16[64,3072]{1,0:T(8,128)(2,1)}, bf16[64,3072]{1,0:T(8,128)(2,1)}, u32[]{:S(2)}, u32[]{:S(2)}) collective-permute-start(bf16[64,3072]{1,0:T(8,128)(2,1)} %copy-done.39), channel_id=1, source_target_pairs={{0,8},{8,0},{16,24},{24,16},{1,9},{9,1},{17,25},{25,17},{2,10},{10... | collective-permute-start | bytes 1179656 | tf_op jit(solution)/shard_map/ppermute | solution.py:682
  45.0 4.1 %collective-permute-start.14 = (bf16[64,3072]{1,0:T(8,128)(2,1)}, bf16[64,3072]{1,0:T(8,128)(2,1)}, u32[]{:S(2)}, u32[]{:S(2)}) collective-permute-start(bf16[64,3072]{1,0:T(8,128)(2,1)} %collective-permute-done.1.rest_13_), channel_id=1, source_target_pairs={{0,8},{8,0},{16,24},{24,16},{1,9},{9,1},{17,25},{25,17},{2,10},{10... | collective-permute-start | bytes 1179656 | tf_op jit(solution)/shard_map/ppermute | solution.py:682
  47.2 29.1 %collective-permute-start.20 = (bf16[64,5120]{1,0:T(8,128)(2,1)}, bf16[64,5120]{1,0:T(8,128)(2,1)S(1)}, u32[]{:S(2)}, u32[]{:S(2)}) collective-permute-start(bf16[64,5120]{1,0:T(8,128)(2,1)} %get-tuple-element.92), channel_id=1, source_target_pairs={{0,16},{8,24},{16,0},{24,8},{1,17},{9,25},{17,1},{25,9},{2,18},{10... | collective-permute-start | bytes 1966088 | tf_op jit(solution)/shard_map/ppermute | solution.py:685
  48.3 27.5 %collective-permute-start.22 = (bf16[64,5120]{1,0:T(8,128)(2,1)S(1)}, bf16[64,5120]{1,0:T(8,128)(2,1)}, u32[]{:S(2)}, u32[]{:S(2)}) collective-permute-start(bf16[64,5120]{1,0:T(8,128)(2,1)S(1)} %collective-permute-done.19.rest_4_), channel_id=1, source_target_pairs={{0,2},{1,3},{2,0},{3,1},{4,6},{5,7},{6,4},{7,5},{8,10},{9,11},{10,... | collective-permute-start | bytes 1966088 | tf_op jit(solution)/shard_map/ppermute | solution.py:688
  48.6 27.3 %collective-permute-start.21 = (bf16[64,5120]{1,0:T(8,128)(2,1)S(1)}, bf16[64,5120]{1,0:T(8,128)(2,1)}, u32[]{:S(2)}, u32[]{:S(2)}) collective-permute-start(bf16[64,5120]{1,0:T(8,128)(2,1)S(1)} %collective-permute-done.19.rest_4_), channel_id=1, source_target_pairs={{0,1},{1,0},{2,3},{3,2},{4,5},{5,4},{6,7},{7,6},{8,9},{9,8},{10,11... | collective-permute-start | bytes 1966088 | tf_op jit(solution)/shard_map/ppermute | solution.py:688
  49.0 25.5 %collective-permute-start.23 = (bf16[256,1024]{1,0:T(8,128)(2,1)}, bf16[256,1024]{1,0:T(8,128)(2,1)S(1)}, u32[]{:S(2)}, u32[]{:S(2)}) collective-permute-start(bf16[256,1024]{1,0:T(8,128)(2,1)} %get-tuple-element.94), channel_id=1, source_target_pairs={{0,16},{8,24},{16,0},{24,8},{1,17},{9,25},{17,1},{25,9},{2,18},{10... | collective-permute-start | bytes 1572872 | tf_op jit(solution)/shard_map/ppermute | solution.py:685
  50.2 33.4 %collective-permute-start.17 = (bf16[256,4096]{1,0:T(8,128)(2,1)}, bf16[256,4096]{1,0:T(8,128)(2,1)}, u32[]{:S(2)}, u32[]{:S(2)}) collective-permute-start(bf16[256,4096]{1,0:T(8,128)(2,1)} %rest_0_.7), channel_id=1, source_target_pairs={{0,8},{8,0},{16,24},{24,16},{1,9},{9,1},{17,25},{25,17},{2,10},{10... | collective-permute-start | bytes 6291464 | tf_op jit(solution)/shard_map/ppermute | solution.py:682
  51.1 24.7 %copy-start.6 = (bf16[256,1024]{1,0:T(8,128)(2,1)S(1)}, bf16[256,1024]{1,0:T(8,128)(2,1)}, u32[]{:S(2)}) copy-start(bf16[256,1024]{1,0:T(8,128)(2,1)} %rest_1_.7) | copy-start | bytes 1572868
  51.1 33.2 %copy-start.5 = (s32[20]{0:T(128)S(1)}, s32[20]{0:T(128)}, u32[]{:S(2)}) copy-start(s32[20]{0:T(128)} %stack.80.info) | copy-start | bytes 244
  51.1 33.2 %copy-start.9 = (bf16[4096]{0:T(1024)(128)(2,1)S(1)}, bf16[4096]{0:T(1024)(128)(2,1)}, u32[]{:S(2)}) copy-start(bf16[4096]{0:T(1024)(128)(2,1)} %bu.1) | copy-start | bytes 24580
  51.1 33.2 %copy-start.10 = (bf16[1024]{0:T(1024)(128)(2,1)S(1)}, bf16[1024]{0:T(1024)(128)(2,1)}, u32[]{:S(2)}) copy-start(bf16[1024]{0:T(1024)(128)(2,1)} %bo.1) | copy-start | bytes 6148
  51.1 33.2 %copy-start.11 = (bf16[1024]{0:T(1024)(128)(2,1)S(1)}, bf16[1024]{0:T(1024)(128)(2,1)}, u32[]{:S(2)}) copy-start(bf16[1024]{0:T(1024)(128)(2,1)} %ga.3) | copy-start | bytes 6148
  51.1 33.2 %copy-start.12 = (bf16[1024]{0:T(1024)(128)(2,1)S(1)}, bf16[1024]{0:T(1024)(128)(2,1)}, u32[]{:S(2)}) copy-start(bf16[1024]{0:T(1024)(128)(2,1)} %sa.3) | copy-start | bytes 6148
  74.6 4.6 %collective-permute-start.24 = (bf16[64,5120]{1,0:T(8,128)(2,1)S(1)}, bf16[64,5120]{1,0:T(8,128)(2,1)S(1)}, u32[]{:S(2)}, u32[]{:S(2)}) collective-permute-start(bf16[64,5120]{1,0:T(8,128)(2,1)S(1)} %collective-permute-done.19.rest_4_), channel_id=1, source_target_pairs={{0,8},{8,0},{16,24},{24,16},{1,9},{9,1},{17,25},{25,17},{2,10},{10... | collective-permute-start | bytes 1966088 | tf_op jit(solution)/shard_map/ppermute | solution.py:682
  75.8 2.8 %collective-permute-start.18 = (bf16[256,1024]{1,0:T(8,128)(2,1)S(1)}, bf16[256,1024]{1,0:T(8,128)(2,1)S(1)}, u32[]{:S(2)}, u32[]{:S(2)}) collective-permute-start(bf16[256,1024]{1,0:T(8,128)(2,1)S(1)} %copy-done.6), channel_id=1, source_target_pairs={{0,8},{8,0},{16,24},{24,16},{1,9},{9,1},{17,25},{25,17},{2,10},{10... | collective-permute-start | bytes 1572872 | tf_op jit(solution)/shard_map/ppermute | solution.py:682
  75.8 3.1 %collective-permute-start.16 = (bf16[256,512]{1,0:T(8,128)(2,1)}, bf16[256,512]{1,0:T(8,128)(2,1)S(1)}, u32[]{:S(2)}, u32[]{:S(2)}) collective-permute-start(bf16[256,512]{1,0:T(8,128)(2,1)} %get-tuple-element.87), channel_id=1, source_target_pairs={{0,8},{8,0},{16,24},{24,16},{1,9},{9,1},{17,25},{25,17},{2,10},{10... | collective-permute-start | bytes 786440 | tf_op jit(solution)/shard_map/ppermute | solution.py:682
  76.3 3.3 %collective-permute-start.25 = (bf16[64,5120]{1,0:T(8,128)(2,1)S(1)}, bf16[64,5120]{1,0:T(8,128)(2,1)S(1)}, u32[]{:S(2)}, u32[]{:S(2)}) collective-permute-start(bf16[64,5120]{1,0:T(8,128)(2,1)S(1)} %collective-permute-done.20.rest_5_), channel_id=1, source_target_pairs={{0,8},{8,0},{16,24},{24,16},{1,9},{9,1},{17,25},{25,17},{2,10},{10... | collective-permute-start | bytes 1966088 | tf_op jit(solution)/shard_map/ppermute | solution.py:682
  78.6 3.5 %collective-permute-start.26 = (bf16[64,5120]{1,0:T(8,128)(2,1)}, bf16[64,5120]{1,0:T(8,128)(2,1)S(1)}, u32[]{:S(2)}, u32[]{:S(2)}) collective-permute-start(bf16[64,5120]{1,0:T(8,128)(2,1)} %collective-permute-done.21.rest_6_), channel_id=1, source_target_pairs={{0,8},{8,0},{16,24},{24,16},{1,9},{9,1},{17,25},{25,17},{2,10},{10... | collective-permute-start | bytes 1966088 | tf_op jit(solution)/shard_map/ppermute | solution.py:682
  79.0 4.5 %collective-permute-start.27 = (bf16[64,5120]{1,0:T(8,128)(2,1)}, bf16[64,5120]{1,0:T(8,128)(2,1)S(1)}, u32[]{:S(2)}, u32[]{:S(2)}) collective-permute-start(bf16[64,5120]{1,0:T(8,128)(2,1)} %collective-permute-done.22.rest_7_), channel_id=1, source_target_pairs={{0,8},{8,0},{16,24},{24,16},{1,9},{9,1},{17,25},{25,17},{2,10},{10... | collective-permute-start | bytes 1966088 | tf_op jit(solution)/shard_map/ppermute | solution.py:682
  79.1 23.6 %collective-permute-start.29 = (bf16[1024,1024]{1,0:T(8,128)(2,1)}, bf16[1024,1024]{1,0:T(8,128)(2,1)S(1)}, u32[]{:S(2)}, u32[]{:S(2)}) collective-permute-start(bf16[1024,1024]{1,0:T(8,128)(2,1)} %rest_12_.1), channel_id=1, source_target_pairs={{0,8},{8,0},{16,24},{24,16},{1,9},{9,1},{17,25},{25,17},{2,10},{10... | collective-permute-start | bytes 6291464 | tf_op jit(solution)/shard_map/ppermute | solution.py:682
  79.5 17.2 %collective-permute-start.28 = (bf16[256,1024]{1,0:T(8,128)(2,1)}, bf16[256,1024]{1,0:T(8,128)(2,1)S(1)}, u32[]{:S(2)}, u32[]{:S(2)}) collective-permute-start(bf16[256,1024]{1,0:T(8,128)(2,1)} %bitcast.40), channel_id=1, source_target_pairs={{0,0},{1,8},{2,2},{3,10},{4,4},{5,12},{6,6},{7,14},{8,1},{9,9},{10... | collective-permute-start | bytes 1572872 | tf_op jit(solution)/shard_map/ppermute | solution.py:713
  82.2 17.4 %collective-permute-start.30 = (bf16[256,1024]{1,0:T(8,128)(2,1)}, bf16[256,1024]{1,0:T(8,128)(2,1)S(1)}, u32[]{:S(2)}, u32[]{:S(2)}) collective-permute-start(bf16[256,1024]{1,0:T(8,128)(2,1)} %get-tuple-element.109), channel_id=1, source_target_pairs={{0,16},{8,24},{16,0},{24,8},{1,17},{9,25},{17,1},{25,9},{2,18},{10... | collective-permute-start | bytes 1572872 | tf_op jit(solution)/shard_map/ppermute | solution.py:685
  83.5 14.9 %collective-permute-start.32 = (bf16[256,1024]{1,0:T(8,128)(2,1)S(1)}, bf16[256,1024]{1,0:T(8,128)(2,1)S(1)}, u32[]{:S(2)}, u32[]{:S(2)}) collective-permute-start(bf16[256,1024]{1,0:T(8,128)(2,1)S(1)} %collective-permute-done.23.rest_14_), channel_id=1, source_target_pairs={{0,2},{1,3},{2,0},{3,1},{4,6},{5,7},{6,4},{7,5},{8,10},{9,11},{10,... | collective-permute-start | bytes 1572872 | tf_op jit(solution)/shard_map/ppermute | solution.py:688
  83.6 16.0 %collective-permute-start.31 = (bf16[256,1024]{1,0:T(8,128)(2,1)S(1)}, bf16[256,1024]{1,0:T(8,128)(2,1)S(1)}, u32[]{:S(2)}, u32[]{:S(2)}) collective-permute-start(bf16[256,1024]{1,0:T(8,128)(2,1)S(1)} %collective-permute-done.23.rest_14_), channel_id=1, source_target_pairs={{0,1},{1,0},{2,3},{3,2},{4,5},{5,4},{6,7},{7,6},{8,9},{9,8},{10,11... | collective-permute-start | bytes 1572872 | tf_op jit(solution)/shard_map/ppermute | solution.py:688
  86.3 18.9 %copy-start.13 = (bf16[1024]{0:T(1024)(128)(2,1)S(1)}, bf16[1024]{0:T(1024)(128)(2,1)}, u32[]{:S(2)}) copy-start(bf16[1024]{0:T(1024)(128)(2,1)} %bd.1) | copy-start | bytes 6148
  86.3 18.9 %copy-start.14 = (bf16[1024]{0:T(1024)(128)(2,1)S(1)}, bf16[1024]{0:T(1024)(128)(2,1)}, u32[]{:S(2)}) copy-start(bf16[1024]{0:T(1024)(128)(2,1)} %gf.1) | copy-start | bytes 6148
  86.3 18.9 %copy-start.15 = (bf16[1024]{0:T(1024)(128)(2,1)S(1)}, bf16[1024]{0:T(1024)(128)(2,1)}, u32[]{:S(2)}) copy-start(bf16[1024]{0:T(1024)(128)(2,1)} %sf.1) | copy-start | bytes 6148
  96.7 6.0 %collective-permute-start.33 = (bf16[256,1024]{1,0:T(8,128)(2,1)S(1)}, bf16[256,1024]{1,0:T(8,128)(2,1)S(1)}, u32[]{:S(2)}, u32[]{:S(2)}) collective-permute-start(bf16[256,1024]{1,0:T(8,128)(2,1)S(1)} %collective-permute-done.23.rest_14_), channel_id=1, source_target_pairs={{0,8},{8,0},{16,24},{24,16},{1,9},{9,1},{17,25},{25,17},{2,10},{10... | collective-permute-start | bytes 1572872 | tf_op jit(solution)/shard_map/ppermute | solution.py:682
  99.5 4.2 %collective-permute-start.34 = (bf16[256,1024]{1,0:T(8,128)(2,1)S(1)}, bf16[256,1024]{1,0:T(8,128)(2,1)S(1)}, u32[]{:S(2)}, u32[]{:S(2)}) collective-permute-start(bf16[256,1024]{1,0:T(8,128)(2,1)S(1)} %collective-permute-done.30.rest_15_), channel_id=1, source_target_pairs={{0,8},{8,0},{16,24},{24,16},{1,9},{9,1},{17,25},{25,17},{2,10},{10... | collective-permute-start | bytes 1572872 | tf_op jit(solution)/shard_map/ppermute | solution.py:682
  102.2 2.3 %collective-permute-start.35 = (bf16[256,1024]{1,0:T(8,128)(2,1)S(1)}, bf16[256,1024]{1,0:T(8,128)(2,1)S(1)}, u32[]{:S(2)}, u32[]{:S(2)}) collective-permute-start(bf16[256,1024]{1,0:T(8,128)(2,1)S(1)} %collective-permute-done.31.rest_16_), channel_id=1, source_target_pairs={{0,8},{8,0},{16,24},{24,16},{1,9},{9,1},{17,25},{25,17},{2,10},{10... | collective-permute-start | bytes 1572872 | tf_op jit(solution)/shard_map/ppermute | solution.py:682
  102.2 3.0 %collective-permute-start.36 = (bf16[256,1024]{1,0:T(8,128)(2,1)S(1)}, bf16[256,1024]{1,0:T(8,128)(2,1)S(1)}, u32[]{:S(2)}, u32[]{:S(2)}) collective-permute-start(bf16[256,1024]{1,0:T(8,128)(2,1)S(1)} %collective-permute-done.32.rest_17_), channel_id=1, source_target_pairs={{0,8},{8,0},{16,24},{24,16},{1,9},{9,1},{17,25},{25,17},{2,10},{10... | collective-permute-start | bytes 1572872 | tf_op jit(solution)/shard_map/ppermute | solution.py:682
  105.2 17.1 %copy-start.16 = (f32[512,512]{1,0:T(8,128)S(1)}, f32[512,512]{1,0:T(8,128)}, u32[]{:S(2)}) copy-start(f32[512,512]{1,0:T(8,128)} %get-tuple-element.115.ot_ref) | copy-start | bytes 3145732
  105.2 17.1 %copy-start.17 = (bf16[512,512]{1,0:T(8,128)(2,1)S(1)}, bf16[512,512]{1,0:T(8,128)(2,1)}, u32[]{:S(2)}) copy-start(bf16[512,512]{1,0:T(8,128)(2,1)} %get-tuple-element.78.q_ref) | copy-start | bytes 1572868
  105.2 17.1 %copy-start.18 = (bf16[512,512]{1,0:T(8,128)(2,1)S(1)}, bf16[512,512]{1,0:T(8,128)(2,1)}, u32[]{:S(2)}) copy-start(bf16[512,512]{1,0:T(8,128)(2,1)} %get-tuple-element.79.qt_ref) | copy-start | bytes 1572868
  105.3 17.1 %copy-start.24 = (bf16[512,64]{1,0:T(8,128)(2,1)S(1)}, bf16[512,64]{1,0:T(8,128)(2,1)}, u32[]{:S(2)}) copy-start(bf16[512,64]{1,0:T(8,128)(2,1)} %get-tuple-element.84.pkt_ref) | copy-start | bytes 196612
  105.3 17.1 %copy-start.26 = (bf16[64,512]{1,0:T(8,128)(2,1)S(1)}, bf16[64,512]{1,0:T(8,128)(2,1)}, u32[]{:S(2)}) copy-start(bf16[64,512]{1,0:T(8,128)(2,1)} %get-tuple-element.83.pk_ref) | copy-start | bytes 196612
  105.3 17.1 %copy-start.27 = (bf16[64,512]{1,0:T(8,128)(2,1)S(1)}, bf16[64,512]{1,0:T(8,128)(2,1)}, u32[]{:S(2)}) copy-start(bf16[64,512]{1,0:T(8,128)(2,1)} %get-tuple-element.85.pv_ref) | copy-start | bytes 196612
  119.9 2.4 %collective-permute-start.37 = (bf16[256,512]{1,0:T(8,128)(2,1)S(1)}, bf16[256,512]{1,0:T(8,128)(2,1)S(1)}, u32[]{:S(2)}, u32[]{:S(2)}) collective-permute-start(bf16[256,512]{1,0:T(8,128)(2,1)S(1)} %get-tuple-element.114), channel_id=1, source_target_pairs={{0,8},{8,0},{16,24},{24,16},{1,9},{9,1},{17,25},{25,17},{2,10},{10... | collective-permute-start | bytes 786440 | tf_op jit(solution)/shard_map/ppermute | solution.py:682
  120.4 11.8 %collective-permute-start.38 = (bf16[256,1024]{1,0:T(8,128)(2,1)S(1)}, bf16[256,1024]{1,0:T(8,128)(2,1)S(1)}, u32[]{:S(2)}, u32[]{:S(2)}) collective-permute-start(bf16[256,1024]{1,0:T(8,128)(2,1)S(1)} %get-tuple-element.122), channel_id=1, source_target_pairs={{0,0},{1,8},{2,2},{3,10},{4,4},{5,12},{6,6},{7,14},{8,1},{9,9},{10... | collective-permute-start | bytes 1572872 | tf_op jit(solution)/shard_map/ppermute | solution.py:713
  124.6 7.5 %collective-permute-start.39 = (bf16[128,512]{1,0:T(8,128)(2,1)S(1)}, bf16[128,512]{1,0:T(8,128)(2,1)S(1)}, u32[]{:S(2)}, u32[]{:S(2)}) collective-permute-start(bf16[128,512]{1,0:T(8,128)(2,1)S(1)} %convert_element_type.66), channel_id=1, source_target_pairs={{0,16},{1,17},{2,18},{3,19},{4,20},{5,21},{6,22},{7,23},{8,24},{9,... | collective-permute-start | bytes 393224 | tf_op jit(solution)/shard_map/ppermute | solution.py:692
  132.2 2.7 %collective-permute-start.40 = (bf16[512,1024]{1,0:T(8,128)(2,1)S(1)}, bf16[512,1024]{1,0:T(8,128)(2,1)S(1)}, u32[]{:S(2)}, u32[]{:S(2)}) collective-permute-start(bf16[512,1024]{1,0:T(8,128)(2,1)S(1)} %get-tuple-element.126), channel_id=1, source_target_pairs={{0,8},{8,0},{16,24},{24,16},{1,9},{9,1},{17,25},{25,17},{2,10},{10... | collective-permute-start | bytes 3145736 | tf_op jit(solution)/shard_map/ppermute | solution.py:682
  135.3 14.2 %collective-permute-start.42 = (bf16[256,1024]{1,0:T(8,128)(2,1)S(1)}, bf16[256,1024]{1,0:T(8,128)(2,1)S(1)}, u32[]{:S(2)}, u32[]{:S(2)}) collective-permute-start(bf16[256,1024]{1,0:T(8,128)(2,1)S(1)} %get-tuple-element.133), channel_id=1, source_target_pairs={{0,2},{1,3},{2,0},{3,1},{4,6},{5,7},{6,4},{7,5},{8,10},{9,11},{10,... | collective-permute-start | bytes 1572872 | tf_op jit(solution)/shard_map/ppermute | solution.py:705
  137.0 12.4 %collective-permute-start.41 = (bf16[128,512]{1,0:T(8,128)(2,1)S(1)}, bf16[128,512]{1,0:T(8,128)(2,1)S(1)}, u32[]{:S(2)}, u32[]{:S(2)}) collective-permute-start(bf16[128,512]{1,0:T(8,128)(2,1)S(1)} %convert_add_fusion.2), channel_id=1, source_target_pairs={{0,1},{1,0},{2,3},{3,2},{4,5},{5,4},{6,7},{7,6},{8,9},{9,8},{10,11... | collective-permute-start | bytes 393224 | tf_op jit(solution)/shard_map/ppermute | solution.py:692
  140.3 9.3 %collective-permute-start.43 = (bf16[256,1024]{1,0:T(8,128)(2,1)S(1)}, bf16[256,1024]{1,0:T(8,128)(2,1)S(1)}, u32[]{:S(2)}, u32[]{:S(2)}) collective-permute-start(bf16[256,1024]{1,0:T(8,128)(2,1)S(1)} %get-tuple-element.136), channel_id=1, source_target_pairs={{0,0},{1,1},{2,4},{3,5},{4,2},{5,3},{6,6},{7,7},{8,8},{9,9},{10,12... | collective-permute-start | bytes 1572872 | tf_op jit(solution)/shard_map/ppermute | solution.py:705
  149.6 7.0 %collective-permute-start.44 = (bf16[256,1024]{1,0:T(8,128)(2,1)S(1)}, bf16[256,1024]{1,0:T(8,128)(2,1)S(1)}, u32[]{:S(2)}, u32[]{:S(2)}) collective-permute-start(bf16[256,1024]{1,0:T(8,128)(2,1)S(1)} %get-tuple-element.138), channel_id=1, source_target_pairs={{0,8},{8,0},{16,24},{24,16},{1,9},{9,1},{17,25},{25,17},{2,10},{10... | collective-permute-start | bytes 1572872 | tf_op jit(solution)/shard_map/ppermute | solution.py:682
  150.5 9.9 %collective-permute-start.46 = (bf16[128,512]{1,0:T(8,128)(2,1)S(1)}, bf16[128,512]{1,0:T(8,128)(2,1)S(1)}, u32[]{:S(2)}, u32[]{:S(2)}) collective-permute-start(bf16[128,512]{1,0:T(8,128)(2,1)S(1)} %convert_add_fusion.1), channel_id=1, source_target_pairs={{0,2},{1,3},{2,0},{3,1},{4,6},{5,7},{6,4},{7,5},{8,10},{9,11},{10,... | collective-permute-start | bytes 393224 | tf_op jit(solution)/shard_map/ppermute | solution.py:692
  156.9 11.9 %collective-permute-start.45 = (bf16[256,1024]{1,0:T(8,128)(2,1)S(1)}, bf16[256,1024]{1,0:T(8,128)(2,1)S(1)}, u32[]{:S(2)}, u32[]{:S(2)}) collective-permute-start(bf16[256,1024]{1,0:T(8,128)(2,1)S(1)} %add_convert_fusion), channel_id=1, source_target_pairs={{0,0},{1,8},{2,2},{3,10},{4,4},{5,12},{6,6},{7,14},{8,1},{9,9},{10... | collective-permute-start | bytes 1572872 | tf_op jit(solution)/shard_map/ppermute | solution.py:713
  160.5 8.3 %collective-permute-start.47 = (bf16[128,512]{1,0:T(8,128)(2,1)S(1)}, bf16[128,512]{1,0:T(8,128)(2,1)S(1)}, u32[]{:S(2)}, u32[]{:S(2)}) collective-permute-start(bf16[128,512]{1,0:T(8,128)(2,1)S(1)} %add_convert_fusion.3), channel_id=1, source_target_pairs={{0,4},{1,5},{2,6},{3,7},{4,0},{5,1},{6,2},{7,3},{8,12},{9,13},{10,... | collective-permute-start | bytes 393224 | tf_op jit(solution)/shard_map/ppermute | solution.py:692
  168.8 2.7 %collective-permute-start.48 = (f32[128,512]{1,0:T(8,128)S(1)}, f32[128,512]{1,0:T(8,128)S(1)}, u32[]{:S(2)}, u32[]{:S(2)}) collective-permute-start(f32[128,512]{1,0:T(8,128)S(1)} %convert_add_fusion), channel_id=1, source_target_pairs={{0,8},{8,0},{16,24},{24,16},{1,9},{9,1},{17,25},{25,17},{2,10},{10... | collective-permute-start | bytes 786440 | tf_op jit(solution)/shard_map/ppermute | solution.py:682
  (25 other events, 134.5 us)
